TPU v7x, 32 devices: a whole 2x2x4 slice. The times are simulated.
32 devices in a mesh: parts: 2 (over x), fibre: 16 (over z, y, core).
Axes of the slice: x: 2, y: 2, z: 4, core: 2. Of those that a mesh axis runs over, the one named last changes fastest.
Arguments:
- signal: bfloat16 [64, 16, 8192], P('parts', None, 'fibre'), parts along dimension 0, may hold values from -6 to 6
- conv_taps: bfloat16 [5, 5, 64, 32], replicated, may hold values from -0.21875 to 0.21875
- response: float32 [2, 64, 4096], P(None, 'fibre'), may hold values from -4 to 4
- cotangent: bfloat16 [128, 8, 4096], P('parts', None, 'fibre'), parts along dimension 0, may hold values from -6 to 6
Outputs:
- input_grad: bfloat16 [64, 16, 8192], P('parts', None, 'fibre'), parts along dimension 0
- tap_grad: float32 [10, 5, 64, 32], P('parts'), parts along dimension 0
- filter_grad: float32 [4, 64, 4096], P('parts', 'fibre'), parts along dimension 0
There are 2 independent parts, one for each index of `parts`. A program takes and returns all parts, laid end to end along the dimension named above; an argument that names none is the same for every part. Nothing has to cross between parts.
All inputs are finite; a program needn't handle non-finite values.
Results may differ from a plain program's by a relative error of at most 0.012.
Values may be sent and summed in bfloat16 or wider, within the bound.
No kernel may reach another device: no remote copies, remote signals or barrier semaphores. Data moves between devices by JAX's collectives and lax.ppermute only.
A program may use at most 64 MiB of HBM per device.

v0:
```python
import functools
import math

import jax
import jax.numpy as jnp
import numpy as np
from jax import lax
from jax.experimental import pallas as pl
from jax.experimental.pallas import tpu as pltpu
from jax.sharding import PartitionSpec as P

bf16 = jnp.bfloat16
f32 = jnp.float32
inv_root_two = 1.0 / math.sqrt(2.0)
inv_root_tau = 1.0 / math.sqrt(2.0 * math.pi)
lanes = 128
edge_rows = 8
tap_rows = 416


def dot(a, b):
    return jnp.dot(a, b, preferred_element_type=f32)


def dot_nt(a, b):
    return lax.dot_general(a, b, (((1,), (1,)), ((), ())), preferred_element_type=f32)


def dot_tn(a, b):
    return lax.dot_general(a, b, (((0,), (0,)), ((), ())), preferred_element_type=f32)


def iota(shape, dim):
    return lax.broadcasted_iota(jnp.int32, shape, dim)


def one_hot(shape, column_of_row):
    return (iota(shape, 1) == column_of_row(iota(shape, 0))).astype(f32).astype(bf16)


def one_hot_columns(shape, row_of_column):
    return (iota(shape, 0) == row_of_column(iota(shape, 1))).astype(f32).astype(bf16)


def call(kernel, outs, scratch, flops, args):
    moved = sum(a.size * a.dtype.itemsize for a in list(args) + list(outs))
    return pl.pallas_call(
        kernel,
        out_shape=outs,
        in_specs=[pl.BlockSpec(memory_space=pltpu.VMEM)] * len(args),
        out_specs=[pl.BlockSpec(memory_space=pltpu.VMEM)] * len(outs),
        scratch_shapes=scratch,
        compiler_params=pltpu.CompilerParams(vmem_limit_bytes=48 << 20),
        cost_estimate=pl.CostEstimate(flops=int(flops), bytes_accessed=moved, transcendentals=0),
    )(*args)


def conv_kernel(dims, sig_ref, taps_ref, out_ref, z_ref, w_ref):
    cin, tin, cout, tout, ks, count, rows = dims
    k_in, k_out = cin * tin, cout * tout
    half = sig_ref.shape[1] // 2
    split = one_hot_columns((2 * lanes, 2 * lanes), lambda q: 2 * (q % lanes) + q // lanes)
    parts = [dot(sig_ref[:, b : b + 2 * lanes], split) for b in range(0, 2 * half, 2 * lanes)]
    apart = jnp.concatenate([p[:, :lanes] for p in parts] + [p[:, lanes:] for p in parts], axis=1)
    to_time = one_hot((k_in, k_in), lambda r: (r % cin) * tin + r // cin)
    z = dot(to_time, apart.astype(bf16)).astype(bf16)
    z_ref[...] = z
    blank = jnp.zeros((2 * cin, cout), bf16)
    stacked = []
    for j in range(ks):
        column = jnp.concatenate([blank] + [taps_ref[i, j] for i in range(ks)] + [blank, blank], axis=0)
        for v in range(4):
            stacked.append(column[2 * cin * v : 2 * cin * v + lanes])
    eye = one_hot((cout, cout), lambda r: r)
    tiles = dot_nt(eye, jnp.concatenate(stacked, axis=0)).astype(bf16)
    empty = jnp.zeros((cout, lanes), bf16)
    for j in range(ks):
        for t in range(tout):
            for q in range(k_in // lanes):
                v = 2 * q - t + 2
                at = (j * 4 + v) * lanes
                tile = tiles[:, at : at + lanes] if 0 <= v < 4 else empty
                w_ref[j, cout * t : cout * (t + 1), lanes * q : lanes * (q + 1)] = tile
    even, odd = z[:, :half], z[:, half:]
    left = dot(w_ref[0], even) + dot(w_ref[1], odd)
    right = dot(w_ref[4], even)
    lane = iota((k_out, half), 1)
    own = (
        dot(w_ref[2], even)
        + dot(w_ref[3], odd)
        + jnp.where(lane == 0, 0.0, pltpu.roll(left, 1, 1))
        + jnp.where(lane == half - 1, 0.0, pltpu.roll(right, half - 1, 1))
    )
    high = own.astype(bf16)
    rest = (own - high.astype(f32)).astype(bf16)
    left_edge, right_edge = left[:, half - lanes :], right[:, :lanes]
    left_high, right_high = left_edge.astype(bf16), right_edge.astype(bf16)
    left_rest = (left_edge - left_high.astype(f32)).astype(bf16)
    right_rest = (right_edge - right_high.astype(f32)).astype(bf16)

    def pick(row, column, tile):
        at = (iota((edge_rows, lanes), 0) == row) & (iota((edge_rows, lanes), 1) == column)
        return dot_nt(at.astype(f32).astype(bf16), tile)

    edges = (
        pick(0, 0, rest[:, :lanes])
        + pick(1, lanes - 1, rest[:, half - lanes :])
        + pick(2, lanes - 1, left_high)
        + pick(3, lanes - 1, left_rest)
        + pick(4, 0, right_high)
        + pick(5, 0, right_rest)
    ).astype(bf16)
    to_channel = one_hot((k_out, k_out), lambda r: (r % tout) * cout + r // tout)
    edges = dot_nt(edges, to_channel)
    main = dot(to_channel, high).astype(bf16)
    for d in range(count):
        out_ref[d, :rows] = main[rows * d : rows * (d + 1)]
        out_ref[d, rows:] = jnp.zeros((edge_rows, half), bf16)
        out_ref[d, rows:, :rows] = edges[:, rows * d : rows * (d + 1)].astype(bf16)


def transform(real, imag, sign):
    size = len(real)
    if size == 1:
        return (list(real), [None] if imag is None else list(imag))
    even_re, even_im = transform(real[0::2], None if imag is None else imag[0::2], sign)
    odd_re, odd_im = transform(real[1::2], None if imag is None else imag[1::2], sign)
    out_re, out_im = [None] * size, [None] * size

    def plus(a, b):
        return b if a is None else (a if b is None else a + b)

    def minus(a, b):
        return a if b is None else (-b if a is None else a - b)

    for k in range(size // 2):
        re, im = odd_re[k], odd_im[k]
        if k == 0:
            tr, ti = re, im
        elif 4 * k == size:
            tr = None if im is None else (im if sign < 0 else -im)
            ti = -re if sign < 0 else re
        else:
            c, s = math.cos(2 * math.pi * k / size), sign * math.sin(2 * math.pi * k / size)
            if im is None:
                tr, ti = c * re, s * re
            elif 8 * k == size:
                tr, ti = (c * (re - im), c * (re + im)) if sign > 0 else (c * (re + im), c * (im - re))
            elif 8 * k == 3 * size:
                tr, ti = (c * (re + im), c * (im - re)) if sign > 0 else (c * (re - im), c * (re + im))
            else:
                tr, ti = c * re - s * im, s * re + c * im
        out_re[k], out_im[k] = plus(even_re[k], tr), plus(even_im[k], ti)
        out_re[k + size // 2], out_im[k + size // 2] = minus(even_re[k], tr), minus(even_im[k], ti)
    return out_re, out_im


def gelu_slope(v):
    return 0.5 * (1.0 + lax.erf(v * inv_root_two)) + v * jnp.exp(-0.5 * v * v) * inv_root_tau


def filter_kernel(
    dims, conv_ref, cot_ref, resp_ref, twist_ref, high_ref, rest_ref,
    out_ref, fgrad_ref, x_ref, y_ref, spec_ref, grad_ref,
):
    count, channels, tout, width = dims
    rows = channels * tout
    scale = 1.0 / (count * width)
    edge_row, edge_col = iota((edge_rows, width), 0), iota((edge_rows, width), 1)
    to_low = (edge_col == 0) & ((edge_row == 0) | (edge_row == 2) | (edge_row == 3))
    to_high = (edge_col == width - 1) & ((edge_row == 1) | (edge_row == 4) | (edge_row == 5))
    spread = (to_low | to_high).astype(f32).astype(bf16)
    edges = [conv_ref[d, rows:, :rows].astype(f32) for d in range(count)]
    none = jnp.zeros((edge_rows, rows), f32)
    kind = iota((edge_rows, rows), 0)
    for d in range(count):
        before = edges[d - 1] if d > 0 else none
        after = edges[d + 1] if d < count - 1 else none
        joined = jnp.where(kind < 2, edges[d], jnp.where(kind < 4, before, after))
        whole = conv_ref[d, :rows].astype(f32) + dot_tn(joined.astype(bf16), spread)
        x_ref[d] = whole.astype(bf16).astype(f32)

    def forward_planes(planes, r, h):
        re, im = transform(planes, None, -1)
        for k in range(count):
            c = twist_ref[0, k : k + 1, h : h + lanes]
            s = twist_ref[1, k : k + 1, h : h + lanes]
            at = pl.ds(k * rows + r, tout)
            if k == 0:
                y_ref[at, h : h + lanes] = re[k]
                y_ref[at, width + h : width + h + lanes] = jnp.zeros_like(re[k]) if im[k] is None else im[k]
            elif im[k] is None:
                y_ref[at, h : h + lanes] = re[k] * c
                y_ref[at, width + h : width + h + lanes] = -(re[k] * s)
            else:
                y_ref[at, h : h + lanes] = re[k] * c + im[k] * s
                y_ref[at, width + h : width + h + lanes] = im[k] * c - re[k] * s

    def backward_planes(r, h):
        re, im = [], []
        for k in range(count):
            c = twist_ref[0, k : k + 1, h : h + lanes]
            s = twist_ref[1, k : k + 1, h : h + lanes]
            at = pl.ds(k * rows + r, tout)
            a, b = y_ref[at, h : h + lanes], y_ref[at, width + h : width + h + lanes]
            re.append(a * c - b * s if k else a)
            im.append(b * c + a * s if k else b)
        return transform(re, im, 1)[0]

    def halves(v):
        high = v.astype(bf16)
        return high, (v - high.astype(f32)).astype(bf16)

    def inner(product):
        high, rest = halves(y_ref[...])
        return (
            product(high, high_ref[...]) + product(rest, high_ref[...]) + product(high, rest_ref[...])
        )

    chunks = [(r * tout, h) for r in range(channels) for h in range(0, width, lanes)]
    for r, h in chunks:
        forward_planes([x_ref[d, r : r + tout, h : h + lanes] for d in range(count)], r, h)
    spec_ref[...] = inner(dot)
    for k in range(count):
        for ch in range(channels):
            at = pl.ds(k * rows + ch * tout, tout)
            sr, si = spec_ref[at, :width], spec_ref[at, width:]
            rr, ri = resp_ref[0, ch, k : k + 1], resp_ref[1, ch, k : k + 1]
            y_ref[at, :width] = rr * sr - ri * si
            y_ref[at, width:] = rr * si + ri * sr
    y_ref[...] = inner(dot_nt)
    for r, h in chunks:
        planes = backward_planes(r, h)
        slopes = [
            cot_ref[d, r : r + tout, h : h + lanes].astype(f32) * gelu_slope(planes[d])
            for d in range(count)
        ]
        forward_planes(slopes, r, h)
    grad_ref[...] = inner(dot)
    for k in range(count):
        for ch in range(channels):
            at = pl.ds(k * rows + ch * tout, tout)
            sr, si = spec_ref[at, :width], spec_ref[at, width:]
            gr, gi = grad_ref[at, :width], grad_ref[at, width:]
            rr, ri = resp_ref[0, ch, k : k + 1], resp_ref[1, ch, k : k + 1]
            fgrad_ref[0, ch, k : k + 1] = jnp.sum(sr * gr + si * gi, axis=0, keepdims=True) * scale
            fgrad_ref[1, ch, k : k + 1] = jnp.sum(sr * gi - si * gr, axis=0, keepdims=True) * scale
            y_ref[at, :width] = rr * gr + ri * gi
            y_ref[at, width:] = rr * gi - ri * gr
    y_ref[...] = inner(dot_nt)
    for r, h in chunks:
        planes = backward_planes(r, h)
        for d in range(count):
            x_ref[d, r : r + tout, h : h + lanes] = planes[d]
    last = ((iota((edge_rows, lanes), 0) == 0) & (iota((edge_rows, lanes), 1) == lanes - 1)).astype(f32).astype(bf16)
    first = ((iota((edge_rows, lanes), 0) == 1) & (iota((edge_rows, lanes), 1) == 0)).astype(f32).astype(bf16)
    for d in range(count):
        out_ref[d, :rows] = x_ref[d].astype(bf16)
        out_ref[d, rows:] = jnp.zeros((edge_rows, width), bf16)
        edge = none
        if d > 0:
            edge = edge + dot_nt(last, x_ref[d - 1, :, width - lanes :].astype(bf16))
        if d < count - 1:
            edge = edge + dot_nt(first, x_ref[d + 1, :, :lanes].astype(bf16))
        out_ref[d, rows:, :rows] = edge.astype(bf16)


def tap_kernel(dims, grad_ref, z_ref, tap_ref, shifted_ref, g_ref, zp_ref):
    cin, tin, cout, tout, ks, count, rows = dims
    half = grad_ref.shape[2]
    k_out = cout * tout
    row, col = iota((edge_rows, lanes), 0), iota((edge_rows, lanes), 1)
    spread = (((row == 1) & (col == 0)) | ((row == 0) & (col == 1))).astype(f32).astype(bf16)
    for d in range(count):
        at = slice(rows * d, rows * (d + 1))
        g_ref[at, :half] = grad_ref[d, :rows].astype(f32)
        g_ref[at, half:] = dot_tn(grad_ref[d, rows:, :rows], spread)
    to_time = one_hot((k_out, k_out), lambda r: (r % cout) * tout + r // cout)
    g = dot(to_time, g_ref[...].astype(bf16)).astype(bf16)
    wide = half + lanes
    later = one_hot_columns((wide, half), lambda n: n + 1)
    sooner = one_hot_columns((wide, half), lambda n: jnp.where(n == 0, half + 1, n - 1))
    shifted_ref[0] = dot(g, later).astype(bf16)
    shifted_ref[1] = g[:, :half]
    shifted_ref[2] = dot(g, sooner).astype(bf16)
    k_in = cin * tin
    pad = 2 * cin
    zp_ref[:pad] = jnp.zeros((pad, 2 * half), bf16)
    zp_ref[pad + k_in :] = jnp.zeros((zp_ref.shape[0] - pad - k_in, 2 * half), bf16)
    zp_ref[pad : pad + k_in] = z_ref[...]
    both, lone = None, None
    for t in range(tout):
        at = slice(cout * t, cout * (t + 1))
        band = zp_ref[2 * cin * t : 2 * cin * t + ks * cin]
        pair = jnp.concatenate([shifted_ref[0, at], shifted_ref[1, at]], axis=0)
        even, odd = band[:, :half], band[:, half:]
        term = jnp.concatenate([dot_nt(even, pair), dot_nt(odd, pair)], axis=0)
        both = term if both is None else both + term
        blank = jnp.zeros((cout, half), bf16)
        mid = ks * cin // 2
        term = dot_nt(even[:mid], jnp.concatenate([shifted_ref[2, at], blank], axis=0)) + dot_nt(
            even[mid:], jnp.concatenate([blank, shifted_ref[2, at]], axis=0)
        )
        lone = term if lone is None else lone + term
    top = both.shape[0]
    tap_ref[:top] = both
    tap_ref[top : top + lone.shape[0]] = lone
    tap_ref[top + lone.shape[0] :] = jnp.zeros((tap_ref.shape[0] - top - lone.shape[0], lanes), f32)


def input_kernel(dims, shifted_ref, taps_ref, out_ref, w_ref):
    cin, tin, cout, tout, ks, count, rows = dims
    k_in = cin * tin
    half = shifted_ref.shape[2]
    blank = jnp.zeros((cin, cout), bf16)
    firsts, seconds = [], []
    for j in range(ks):
        for i in range(ks + 2):
            firsts.append(taps_ref[i, j] if i < ks else blank)
            seconds.append(taps_ref[i - 2, j] if i >= 2 else blank)
    to_first = one_hot((cout, lanes), lambda r: r)
    to_second = one_hot((cout, lanes), lambda r: r + cout)
    tiles = (
        dot(jnp.concatenate(firsts, axis=0), to_first) + dot(jnp.concatenate(seconds, axis=0), to_second)
    ).astype(bf16)
    empty = jnp.zeros((cin, lanes), bf16)
    for j in range(ks):
        for s in range(tin):
            for q in range(cout * tout // lanes):
                i = s - 4 * q + 2
                at = (j * (ks + 2) + i) * cin
                tile = tiles[at : at + cin] if 0 <= i < ks + 2 else empty
                w_ref[j, cin * s : cin * (s + 1), lanes * q : lanes * (q + 1)] = tile
    later, same, sooner = shifted_ref[0], shifted_ref[1], shifted_ref[2]
    even = dot(w_ref[0], later) + dot(w_ref[2], same) + dot(w_ref[4], sooner)
    odd = dot(w_ref[1], later) + dot(w_ref[3], same)
    both = jnp.concatenate([even.astype(bf16), odd.astype(bf16)], axis=1)
    to_channel = one_hot((k_in, k_in), lambda r: (r % tin) * cin + r // tin)
    both = dot(to_channel, both).astype(bf16)
    merge = one_hot((2 * lanes, 2 * lanes), lambda r: 2 * (r % lanes) + r // lanes)
    for b in range(half // lanes):
        part = jnp.concatenate(
            [both[:, lanes * b : lanes * (b + 1)], both[:, half + lanes * b : half + lanes * (b + 1)]], axis=1
        )
        out_ref[:, 2 * lanes * b : 2 * lanes * (b + 1)] = dot(part, merge).astype(bf16)


def unpack_kernel(dims, scale, tap_ref, out_ref):
    cin, tin, cout, tout, ks, count, rows = dims
    band = ks * cin
    for i in range(ks):
        at = slice(cin * i, cin * (i + 1))
        even, odd = tap_ref[at] * scale, tap_ref[band + cin * i : band + cin * (i + 1)] * scale
        out_ref[i, 0] = even[:, :cout]
        out_ref[i, 2] = even[:, cout:]
        out_ref[i, 1] = odd[:, :cout]
        out_ref[i, 3] = odd[:, cout:]
        for c in range(0, cin, 8):
            at = cin * i + c
            low = at < band // 2
            packed = tap_ref[2 * band + at % (band // 2) : 2 * band + at % (band // 2) + 8] * scale
            out_ref[i, 4, c : c + 8] = packed[:, :cout] if low else packed[:, cout:]


def summed_over(rows, axis):
    count = lax.axis_size(axis)
    index = lax.axis_index(axis)
    pairs = lambda step: [(i, i ^ step) for i in range(count)]
    halved = [step for step in (1, 2) if step < count]
    for step in halved:
        size = rows.shape[0] // 2
        bit = (index // step) % 2
        kept = lax.dynamic_slice_in_dim(rows, bit * size, size)
        sent = lax.dynamic_slice_in_dim(rows, (1 - bit) * size, size)
        rows = kept + lax.ppermute(sent, axis, pairs(step))
    step = 2 * halved[-1] if halved else 1
    while step < count:
        rows = rows + lax.ppermute(rows, axis, pairs(step))
        step *= 2
    for step in reversed(halved):
        bit = (index // step) % 2
        other = lax.ppermute(rows, axis, pairs(step))
        rows = jnp.where(bit == 0, jnp.concatenate([rows, other]), jnp.concatenate([other, rows]))
    return rows


def tables(count, width):
    inner = np.outer(np.arange(width), np.arange(width)) % width * (2.0 * np.pi / width)
    c, s = np.cos(inner), np.sin(inner)
    table = np.block([[c, -s], [s, c]]).astype(np.float32)
    high = table.astype(bf16)
    rest = (table - high.astype(np.float32)).astype(bf16)
    outer = np.outer(np.arange(count), np.arange(width)) * (2.0 * np.pi / (count * width))
    twist = np.stack([np.cos(outer), np.sin(outer)]).astype(np.float32)
    return twist, high, rest


def per_device(signal, conv_taps, response, cotangent):
    cin, tin, fibre_in = signal.shape
    cout, tout, width = cotangent.shape
    ks = conv_taps.shape[0]
    count = lax.axis_size("fibre")
    channels = cout // count
    rows = channels * tout
    waves = count * width
    dims = (cin, tin, cout, tout, ks, count, rows)
    k_in, k_out = cin * tin, cout * tout
    taps = jnp.swapaxes(conv_taps, 2, 3)
    shape = jax.ShapeDtypeStruct
    cot_cols = lax.all_to_all(
        cotangent.reshape(count, rows, width), "fibre", split_axis=0, concat_axis=0, tiled=True
    )
    conv_part, z = call(
        functools.partial(conv_kernel, dims),
        [shape((count, rows + edge_rows, width), bf16), shape((k_in, fibre_in), bf16)],
        [pltpu.VMEM((ks, k_out, k_in), bf16)],
        2e9,
        (signal.reshape(k_in, fibre_in), taps),
    )
    conv_cols = lax.all_to_all(conv_part, "fibre", split_axis=0, concat_axis=0, tiled=True)
    arranged = (response * (1.0 / waves)).reshape(2, channels, width, count).transpose(0, 1, 3, 2)
    twist, high, rest = tables(count, width)
    big = count * rows
    grad_part, fgrad = call(
        functools.partial(filter_kernel, (count, channels, tout, width)),
        [shape((count, rows + edge_rows, width), bf16), shape((2, channels, count, width), f32)],
        [
            pltpu.VMEM((count, rows, width), f32),
            pltpu.VMEM((big, 2 * width), f32),
            pltpu.VMEM((big, 2 * width), f32),
            pltpu.VMEM((big, 2 * width), f32),
        ],
        6e9,
        (conv_cols, cot_cols, arranged, jnp.asarray(twist), jnp.asarray(high), jnp.asarray(rest)),
    )
    filter_grad = fgrad.transpose(0, 1, 3, 2).reshape(2, channels, waves)
    grad_cols = lax.all_to_all(grad_part, "fibre", split_axis=0, concat_axis=0, tiled=True)
    taps_part, shifted = call(
        functools.partial(tap_kernel, dims),
        [shape((tap_rows, lanes), f32), shape((3, k_out, width), bf16)],
        [pltpu.VMEM((k_out, width + lanes), f32), pltpu.VMEM((k_in + 4 * cin, fibre_in), bf16)],
        1e9,
        (grad_cols, z),
    )
    total = summed_over(taps_part, "fibre")
    (input_grad,) = call(
        functools.partial(input_kernel, dims),
        [shape((k_in, fibre_in), bf16)],
        [pltpu.VMEM((ks, k_in, k_out), bf16)],
        2e9,
        (shifted, taps),
    )
    (tap_grad,) = call(
        functools.partial(unpack_kernel, dims, 1.0 / math.sqrt(tout * waves)),
        [shape((ks, ks, cin, cout), f32)],
        [],
        1e6,
        (total,),
    )
    return (input_grad.reshape(signal.shape), jnp.swapaxes(tap_grad, 2, 3), filter_grad)


def solution(mesh):
    in_specs = (P("parts", None, "fibre"), P(), P(None, "fibre", None), P("parts", None, "fibre"))
    out_specs = (P("parts", None, "fibre"), P("parts", None, None, None), P("parts", "fibre", None))
    return jax.shard_map(
        per_device, mesh=mesh, in_specs=in_specs, out_specs=out_specs, check_vma=False
    )
```

profile of v0, /device:TPU:0, one launch (start us, length us, event | category | flops | bytes accessed | tf_op | source)
XLA Modules:
  0.0 78.7 jit_solution(13285471217058453175)
XLA Ops:
  0.6 0.0 copy-start
  0.6 7.5 %all-to-all-start.1 = ((bf16[16,32,256]{2,1,0:T(8,128)(2,1)}), bf16[16,32,256]{2,1,0:T(8,128)(2,1)S(1)}, u32[]{:S(2)}, u32[]{:S(2)}) async-start(bf16[16,32,256]{2,1,0:T(8,128)(2,1)} %bitcast.15), calls=%async_computation.1 | async-start | bytes 524288 | tf_op jit(solution)/shard_map/all_to_all | solution.py:410
  8.2 0.0 copy-done
  8.2 0.0 copy-start.1
  8.2 0.9 %copy-done.1 = bf16[5,5,64,32]{2,3,1,0:T(8,128)(2,1)S(1)} copy-done((bf16[5,5,64,32]{2,3,1,0:T(8,128)(2,1)S(1)}, bf16[5,5,64,32]{2,3,1,0:T(8,128)(2,1)}, u32[]{:S(2)}) %copy-start.1) | copy-done | bytes 102424
  9.1 3.8 %shard_map.94 = (bf16[16,40,256]{2,1,0:T(8,128)(2,1)}, bf16[512,512]{1,0:T(8,128)(2,1)S(1)}) custom-call(bf16[512,512]{1,0:T(8,128)(2,1)S(1)} %bitcast.11, bf16[5,5,32,64]{3,2,1,0:T(8,128)(2,1)S(1)} %bitcast.12), custom_call_target="tpu_custom_call" | custom-call | flops 2000000000 | bytes 1478656 | tf_op jit(solution)/shard_map/pallas_call | solution.py:47
  12.9 5.4 %all-to-all-done.1.cot_ref = bf16[16,32,256]{2,1,0:T(8,128)(2,1)S(1)} async-done(((bf16[16,32,256]{2,1,0:T(8,128)(2,1)}), bf16[16,32,256]{2,1,0:T(8,128)(2,1)S(1)}, u32[]{:S(2)}, u32[]{:S(2)}) %all-to-all-start.1) | async-done | bytes 262176 | tf_op jit(solution)/shard_map/all_to_all | solution.py:410
  18.2 0.0 copy-start.6
  18.2 3.7 %all-to-all-start = ((bf16[16,40,256]{2,1,0:T(8,128)(2,1)}), bf16[16,40,256]{2,1,0:T(8,128)(2,1)S(1)}, u32[]{:S(2)}, u32[]{:S(2)}) async-start(bf16[16,40,256]{2,1,0:T(8,128)(2,1)} %get-tuple-element.9), calls=%async_computation | async-start | bytes 655360 | tf_op jit(solution)/shard_map/all_to_all | solution.py:420
  21.9 0.0 copy-done.6
  22.0 0.4 reshape.23
  22.3 0.0 copy-start.3
  22.4 0.0 copy-start.4
  22.4 0.0 copy-start.5
  22.4 0.3 copy.10
  22.7 10.3 %all-to-all-done.conv_ref = bf16[16,40,256]{2,1,0:T(8,128)(2,1)S(1)} async-done(((bf16[16,40,256]{2,1,0:T(8,128)(2,1)}), bf16[16,40,256]{2,1,0:T(8,128)(2,1)S(1)}, u32[]{:S(2)}, u32[]{:S(2)}) %all-to-all-start) | async-done | bytes 327712 | tf_op jit(solution)/shard_map/all_to_all | solution.py:420
  33.0 0.0 copy-done.3
  33.0 0.0 copy-done.4
  33.0 0.0 copy-done.5
  33.0 6.0 %shard_map.95 = (bf16[16,40,256]{2,1,0:T(8,128)(2,1)}, f32[2,4,16,256]{3,2,1,0:T(8,128)S(1)}) custom-call(bf16[16,40,256]{2,1,0:T(8,128)(2,1)S(1)} %all-to-all-done.conv_ref, bf16[16,32,256]{2,1,0:T(8,128)(2,1)S(1)} %all-to-all-done.1.cot_ref, f32[2,4,16,256]{3,2,1,0:T(8,128)S(1)} %bitcast.10, f32[2,16,256]{2,1,0:T(8,128)S(1)} %copy-done.5, ...), custom_call_target="tpu_custom_call" | custom-call | flops 6000000000 | bytes 2260992 | tf_op jit(solution)/shard_map/pallas_call | solution.py:47
  39.0 3.5 %all-to-all-start.2 = ((bf16[16,40,256]{2,1,0:T(8,128)(2,1)}), bf16[16,40,256]{2,1,0:T(8,128)(2,1)S(1)}, u32[]{:S(2)}, u32[]{:S(2)}) async-start(bf16[16,40,256]{2,1,0:T(8,128)(2,1)} %get-tuple-element.10), calls=%async_computation.2 | async-start | bytes 655360 | tf_op jit(solution)/shard_map/all_to_all | solution.py:437
  42.6 11.0 %all-to-all-done.2.grad_ref = bf16[16,40,256]{2,1,0:T(8,128)(2,1)S(1)} async-done(((bf16[16,40,256]{2,1,0:T(8,128)(2,1)}), bf16[16,40,256]{2,1,0:T(8,128)(2,1)S(1)}, u32[]{:S(2)}, u32[]{:S(2)}) %all-to-all-start.2) | async-done | bytes 327712 | tf_op jit(solution)/shard_map/all_to_all | solution.py:437
  53.6 1.6 %shard_map.96 = (f32[416,128]{1,0:T(8,128)S(1)}, bf16[3,512,256]{2,1,0:T(8,128)(2,1)S(1)}) custom-call(bf16[16,40,256]{2,1,0:T(8,128)(2,1)S(1)} %all-to-all-done.2.grad_ref, bf16[512,512]{1,0:T(8,128)(2,1)S(1)} %get-tuple-element.11.z_ref), custom_call_target="tpu_custom_call" | custom-call | flops 1000000000 | bytes 1851392 | tf_op jit(solution)/shard_map/pallas_call | solution.py:47
  55.2 0.1 collective-permute-start
  55.3 1.3 %collective-permute-done = f32[208,128]{1,0:T(8,128)S(1)} collective-permute-done((f32[208,128]{1,0:T(8,128)S(1)}, f32[208,128]{1,0:T(8,128)S(1)}, u32[]{:S(2)}, u32[]{:S(2)}) %collective-permute-start) | collective-permute-done | bytes 106528 | tf_op jit(solution)/shard_map/ppermute | solution.py:375
  56.6 0.5 collective-permute-start.1
  57.1 3.7 %collective-permute-done.1 = f32[104,128]{1,0:T(8,128)S(1)} collective-permute-done((f32[104,128]{1,0:T(8,128)S(1)}, f32[104,128]{1,0:T(8,128)S(1)}, u32[]{:S(2)}, u32[]{:S(2)}) %collective-permute-start.1) | collective-permute-done | bytes 53280 | tf_op jit(solution)/shard_map/ppermute | solution.py:375
  60.8 0.7 collective-permute-start.2
  61.6 3.5 %collective-permute-done.2 = f32[104,128]{1,0:T(8,128)S(1)} collective-permute-done((f32[104,128]{1,0:T(8,128)S(1)}, f32[104,128]{1,0:T(8,128)S(1)}, u32[]{:S(2)}, u32[]{:S(2)}) %collective-permute-start.2) | collective-permute-done | bytes 53280 | tf_op jit(solution)/shard_map/ppermute | solution.py:378
  65.1 1.4 %collective-permute-start.3 = (f32[104,128]{1,0:T(8,128)S(1)}, f32[104,128]{1,0:T(8,128)S(1)}, u32[]{:S(2)}, u32[]{:S(2)}) collective-permute-start(f32[104,128]{1,0:T(8,128)S(1)} %add.43), channel_id=1, source_target_pairs={{0,8},{1,9},{2,10},{3,11},{4,12},{5,13},{6,14},{7,15},{8,0},{9,1},... | collective-permute-start | bytes 159752 | tf_op jit(solution)/shard_map/ppermute | solution.py:378
  66.5 4.2 %collective-permute-done.3 = f32[104,128]{1,0:T(8,128)S(1)} collective-permute-done((f32[104,128]{1,0:T(8,128)S(1)}, f32[104,128]{1,0:T(8,128)S(1)}, u32[]{:S(2)}, u32[]{:S(2)}) %collective-permute-start.3) | collective-permute-done | bytes 53280 | tf_op jit(solution)/shard_map/ppermute | solution.py:378
  70.7 0.1 collective-permute-start.4
  70.8 0.3 copy.11
  71.2 1.2 %reshape.25 = f32[2,4,4096]{2,1,0:T(4,128)} reshape(f32[2,4,256,16]{3,2,1,0:T(8,128)S(1)} %copy.11) | data formatting | bytes 262144 | tf_op jit(solution)/shard_map/reshape | solution.py:436
  72.4 0.0 copy-start.2
  72.4 2.6 %collective-permute-done.4 = f32[104,128]{1,0:T(8,128)S(1)} collective-permute-done((f32[104,128]{1,0:T(8,128)S(1)}, f32[104,128]{1,0:T(8,128)S(1)}, u32[]{:S(2)}, u32[]{:S(2)}) %collective-permute-start.4) | collective-permute-done | bytes 53280 | tf_op jit(solution)/shard_map/ppermute | solution.py:382
  74.9 0.1 collective-permute-start.5
  75.0 0.0 copy-done.2
  75.0 2.8 %shard_map.97 = bf16[512,512]{1,0:T(8,128)(2,1)} custom-call(bf16[3,512,256]{2,1,0:T(8,128)(2,1)S(1)} %get-tuple-element.12.shifted_ref, bf16[5,5,32,64]{3,2,1,0:T(8,128)(2,1)S(1)} %bitcast.13), custom_call_target="tpu_custom_call" | custom-call | flops 2000000000 | bytes 1413120 | tf_op jit(solution)/shard_map/pallas_call | solution.py:47
  77.8 0.0 collective-permute-done.5
  77.8 0.9 %shard_map.98 = f32[5,5,32,64]{3,2,1,0:T(8,128)} custom-call(f32[416,128]{1,0:T(8,128)S(1)} %maximum_select_fusion.tap_ref), custom_call_target="tpu_custom_call" | custom-call | flops 1000000 | bytes 417792 | tf_op jit(solution)/shard_map/pallas_call | solution.py:47
  (9 shorter events, 0.1 us)
Async XLA Ops:
  0.6 7.5 %copy-start = (bf16[32,16,512]{2,1,0:T(8,128)(2,1)S(1)}, bf16[32,16,512]{2,1,0:T(8,128)(2,1)}, u32[]{:S(2)}) copy-start(bf16[32,16,512]{2,1,0:T(8,128)(2,1)} %param.7) | copy-start | bytes 1572868
  0.6 17.6 %all-to-all-start.1 = ((bf16[16,32,256]{2,1,0:T(8,128)(2,1)}), bf16[16,32,256]{2,1,0:T(8,128)(2,1)S(1)}, u32[]{:S(2)}, u32[]{:S(2)}) async-start(bf16[16,32,256]{2,1,0:T(8,128)(2,1)} %bitcast.15), calls=%async_computation.1 | async-start | bytes 524288 | tf_op jit(solution)/shard_map/all_to_all | solution.py:410
  8.2 0.9 %copy-start.1 = (bf16[5,5,64,32]{2,3,1,0:T(8,128)(2,1)S(1)}, bf16[5,5,64,32]{2,3,1,0:T(8,128)(2,1)}, u32[]{:S(2)}) copy-start(bf16[5,5,64,32]{2,3,1,0:T(8,128)(2,1)} %param.8) | copy-start | bytes 307204
  18.2 3.7 %copy-start.6 = (f32[2,4,4096]{2,1,0:T(4,128)S(1)}, f32[2,4,4096]{2,1,0:T(4,128)}, u32[]{:S(2)}) copy-start(f32[2,4,4096]{2,1,0:T(4,128)} %param.9) | copy-start | bytes 393220
  18.2 14.7 %all-to-all-start = ((bf16[16,40,256]{2,1,0:T(8,128)(2,1)}), bf16[16,40,256]{2,1,0:T(8,128)(2,1)S(1)}, u32[]{:S(2)}, u32[]{:S(2)}) async-start(bf16[16,40,256]{2,1,0:T(8,128)(2,1)} %get-tuple-element.9), calls=%async_computation | async-start | bytes 655360 | tf_op jit(solution)/shard_map/all_to_all | solution.py:420
  22.3 10.6 %copy-start.3 = (bf16[512,512]{1,0:T(8,128)(2,1)S(1)}, bf16[512,512]{1,0:T(8,128)(2,1)}, u32[]{:S(2)}) copy-start(bf16[512,512]{1,0:T(8,128)(2,1)} %constant.65.clone.high_ref) | copy-start | bytes 1572868
  22.4 10.6 %copy-start.4 = (bf16[512,512]{1,0:T(8,128)(2,1)S(1)}, bf16[512,512]{1,0:T(8,128)(2,1)}, u32[]{:S(2)}) copy-start(bf16[512,512]{1,0:T(8,128)(2,1)} %constant.66.clone.rest_ref) | copy-start | bytes 1572868
  22.4 10.6 %copy-start.5 = (f32[2,16,256]{2,1,0:T(8,128)S(1)}, f32[2,16,256]{2,1,0:T(8,128)}, u32[]{:S(2)}) copy-start(f32[2,16,256]{2,1,0:T(8,128)} %constant.64.clone.twist_ref) | copy-start | bytes 98308
  39.0 14.6 %all-to-all-start.2 = ((bf16[16,40,256]{2,1,0:T(8,128)(2,1)}), bf16[16,40,256]{2,1,0:T(8,128)(2,1)S(1)}, u32[]{:S(2)}, u32[]{:S(2)}) async-start(bf16[16,40,256]{2,1,0:T(8,128)(2,1)} %get-tuple-element.10), calls=%async_computation.2 | async-start | bytes 655360 | tf_op jit(solution)/shard_map/all_to_all | solution.py:437
  55.2 1.4 %collective-permute-start = (f32[208,128]{1,0:T(8,128)S(1)}, f32[208,128]{1,0:T(8,128)S(1)}, u32[]{:S(2)}, u32[]{:S(2)}) collective-permute-start(f32[208,128]{1,0:T(8,128)S(1)} %constant_dynamic-slice_fusion.1), channel_id=1, source_target_pairs={{0,1},{1,0},{2,3},{3,2},{4,5},{5,4},{6,7},{7,6},{8,9},{9,8},{10,11... | collective-permute-start | bytes 319496 | tf_op jit(solution)/shard_map/ppermute | solution.py:375
  56.6 4.2 %collective-permute-start.1 = (f32[104,128]{1,0:T(8,128)S(1)}, f32[104,128]{1,0:T(8,128)S(1)}, u32[]{:S(2)}, u32[]{:S(2)}) collective-permute-start(f32[104,128]{1,0:T(8,128)S(1)} %constant_dynamic-slice_fusion), channel_id=1, source_target_pairs={{0,2},{1,3},{2,0},{3,1},{4,6},{5,7},{6,4},{7,5},{8,10},{9,11},{10,... | collective-permute-start | bytes 159752 | tf_op jit(solution)/shard_map/ppermute | solution.py:375
  60.8 4.2 %collective-permute-start.2 = (f32[104,128]{1,0:T(8,128)S(1)}, f32[104,128]{1,0:T(8,128)S(1)}, u32[]{:S(2)}, u32[]{:S(2)}) collective-permute-start(f32[104,128]{1,0:T(8,128)S(1)} %dynamic-slice_add_fusion.1), channel_id=1, source_target_pairs={{0,4},{1,5},{2,6},{3,7},{4,0},{5,1},{6,2},{7,3},{8,12},{9,13},{10,... | collective-permute-start | bytes 159752 | tf_op jit(solution)/shard_map/ppermute | solution.py:378
  65.1 5.7 %collective-permute-start.3 = (f32[104,128]{1,0:T(8,128)S(1)}, f32[104,128]{1,0:T(8,128)S(1)}, u32[]{:S(2)}, u32[]{:S(2)}) collective-permute-start(f32[104,128]{1,0:T(8,128)S(1)} %add.43), channel_id=1, source_target_pairs={{0,8},{1,9},{2,10},{3,11},{4,12},{5,13},{6,14},{7,15},{8,0},{9,1},... | collective-permute-start | bytes 159752 | tf_op jit(solution)/shard_map/ppermute | solution.py:378
  70.7 4.2 %collective-permute-start.4 = (f32[104,128]{1,0:T(8,128)S(1)}, f32[104,128]{1,0:T(8,128)S(1)}, u32[]{:S(2)}, u32[]{:S(2)}) collective-permute-start(f32[104,128]{1,0:T(8,128)S(1)} %add.44), channel_id=1, source_target_pairs={{0,2},{1,3},{2,0},{3,1},{4,6},{5,7},{6,4},{7,5},{8,10},{9,11},{10,... | collective-permute-start | bytes 159752 | tf_op jit(solution)/shard_map/ppermute | solution.py:382
  72.4 2.6 %copy-start.2 = (bf16[5,5,64,32]{2,3,1,0:T(8,128)(2,1)S(1)}, bf16[5,5,64,32]{2,3,1,0:T(8,128)(2,1)}, u32[]{:S(2)}) copy-start(bf16[5,5,64,32]{2,3,1,0:T(8,128)(2,1)} %param.8) | copy-start | bytes 307204
  74.9 2.9 %collective-permute-start.5 = (f32[208,128]{1,0:T(8,128)S(1)}, f32[208,128]{1,0:T(8,128)S(1)}, u32[]{:S(2)}, u32[]{:S(2)}) collective-permute-start(f32[208,128]{1,0:T(8,128)S(1)} %maximum_select_fusion.1), channel_id=1, source_target_pairs={{0,1},{1,0},{2,3},{3,2},{4,5},{5,4},{6,7},{7,6},{8,9},{9,8},{10,11... | collective-permute-start | bytes 319496 | tf_op jit(solution)/shard_map/ppermute | solution.py:382
where the time goes:
time: 79.2 us; the launch traced here: 78.7 us
  waiting for transfers between devices  41.9 us (53%)
  starting transfers between devices  17.6 us (22%)
  Pallas kernels  15 us (19%)
  local copies, waits for them, and re-layouts  3.21 us (4%)
  between operations  0.9 us (1%)
    pallas_call x5, Pallas kernels, call(): pl.pallas_call(kernel, out_shape=outs, in_specs=[pl.BlockSpec(memory_spac...  15 us
    all_to_all x1, waiting for transfers between devices, per_device(): lax.all_to_all(grad_part, 'fibre', split_axis=0, concat_axis=0, tiled=True)  11 us
    all_to_all x1, waiting for transfers between devices, per_device(): lax.all_to_all(conv_part, 'fibre', split_axis=0, concat_axis=0, tiled=True)  10.3 us
    ppermute x2, waiting for transfers between devices, summed_over(): rows = rows + lax.ppermute(rows, axis, pairs(step))  7.73 us
    all_to_all x1, starting transfers between devices, per_device(): lax.all_to_all(cotangent.reshape(count, rows, width), 'fibre', split_axis...  7.53 us
    all_to_all x1, waiting for transfers between devices, per_device(): lax.all_to_all(cotangent.reshape(count, rows, width), 'fibre', split_axis...  5.35 us
    ppermute x2, waiting for transfers between devices, summed_over(): rows = kept + lax.ppermute(sent, axis, pairs(step))  4.96 us
    all_to_all x1, starting transfers between devices, per_device(): lax.all_to_all(conv_part, 'fibre', split_axis=0, concat_axis=0, tiled=True)  3.68 us
  transfers between devices with their start and end apart: 9, of which 8 were waited for; matrix products, arithmetic and copies ran while one was open for 3% of the time, Pallas kernels for 8%

commit v1 on v0

--- a/solution.py
+++ b/solution.py
@@ -42,29 +42,29 @@
     return (iota(shape, 0) == row_of_column(iota(shape, 1))).astype(f32).astype(bf16)
 
 
-def call(kernel, outs, scratch, flops, args):
+def call(kernel, outs, scratch, flops, args, left=(), room=48):
     moved = sum(a.size * a.dtype.itemsize for a in list(args) + list(outs))
     return pl.pallas_call(
         kernel,
         out_shape=outs,
-        in_specs=[pl.BlockSpec(memory_space=pltpu.VMEM)] * len(args),
+        in_specs=[
+            pl.BlockSpec(memory_space=pltpu.HBM if a in left else pltpu.VMEM) for a in range(len(args))
+        ],
         out_specs=[pl.BlockSpec(memory_space=pltpu.VMEM)] * len(outs),
         scratch_shapes=scratch,
-        compiler_params=pltpu.CompilerParams(vmem_limit_bytes=48 << 20),
+        compiler_params=pltpu.CompilerParams(vmem_limit_bytes=room << 20),
         cost_estimate=pl.CostEstimate(flops=int(flops), bytes_accessed=moved, transcendentals=0),
     )(*args)
 
 
-def conv_kernel(dims, sig_ref, taps_ref, out_ref, z_ref, w_ref):
+def conv_kernel(dims, sig_hbm, cot_hbm, taps_ref, out_ref, z_ref, w_ref, sig_ref, cot_ref, sem):
     cin, tin, cout, tout, ks, count, rows = dims
     k_in, k_out = cin * tin, cout * tout
     half = sig_ref.shape[1] // 2
-    split = one_hot_columns((2 * lanes, 2 * lanes), lambda q: 2 * (q % lanes) + q // lanes)
-    parts = [dot(sig_ref[:, b : b + 2 * lanes], split) for b in range(0, 2 * half, 2 * lanes)]
-    apart = jnp.concatenate([p[:, :lanes] for p in parts] + [p[:, lanes:] for p in parts], axis=1)
-    to_time = one_hot((k_in, k_in), lambda r: (r % cin) * tin + r // cin)
-    z = dot(to_time, apart.astype(bf16)).astype(bf16)
-    z_ref[...] = z
+    sig_copy = pltpu.make_async_copy(sig_hbm, sig_ref, sem.at[0])
+    cot_copy = pltpu.make_async_copy(cot_hbm, cot_ref, sem.at[1])
+    sig_copy.start()
+    cot_copy.start()
     blank = jnp.zeros((2 * cin, cout), bf16)
     stacked = []
     for j in range(ks):
@@ -81,6 +81,13 @@
                 at = (j * 4 + v) * lanes
                 tile = tiles[:, at : at + lanes] if 0 <= v < 4 else empty
                 w_ref[j, cout * t : cout * (t + 1), lanes * q : lanes * (q + 1)] = tile
+    sig_copy.wait()
+    split = one_hot_columns((2 * lanes, 2 * lanes), lambda q: 2 * (q % lanes) + q // lanes)
+    parts = [dot(sig_ref[:, b : b + 2 * lanes], split) for b in range(0, 2 * half, 2 * lanes)]
+    apart = jnp.concatenate([p[:, :lanes] for p in parts] + [p[:, lanes:] for p in parts], axis=1)
+    to_time = one_hot((k_in, k_in), lambda r: (r % cin) * tin + r // cin)
+    z = dot(to_time, apart.astype(bf16)).astype(bf16)
+    z_ref[...] = z
     even, odd = z[:, :half], z[:, half:]
     left = dot(w_ref[0], even) + dot(w_ref[1], odd)
     right = dot(w_ref[4], even)
@@ -113,10 +120,16 @@
     to_channel = one_hot((k_out, k_out), lambda r: (r % tout) * cout + r // tout)
     edges = dot_nt(edges, to_channel)
     main = dot(to_channel, high).astype(bf16)
+    cot_copy.wait()
     for d in range(count):
-        out_ref[d, :rows] = main[rows * d : rows * (d + 1)]
-        out_ref[d, rows:] = jnp.zeros((edge_rows, half), bf16)
-        out_ref[d, rows:, :rows] = edges[:, rows * d : rows * (d + 1)].astype(bf16)
+        for b in range(half // lanes):
+            at = slice(lanes * b, lanes * (b + 1))
+            out_ref[d, rows * b : rows * (b + 1)] = main[rows * d : rows * (d + 1), at]
+            low = rows * (half // lanes + b)
+            out_ref[d, low : low + rows] = cot_ref[d, :, at]
+        low = 2 * rows * (half // lanes)
+        out_ref[d, low:] = jnp.zeros((edge_rows, lanes), bf16)
+        out_ref[d, low:, :rows] = edges[:, rows * d : rows * (d + 1)].astype(bf16)
 
 
 def transform(real, imag, sign):
@@ -160,7 +173,7 @@
 
 
 def filter_kernel(
-    dims, conv_ref, cot_ref, resp_ref, twist_ref, high_ref, rest_ref,
+    dims, cols_ref, resp_ref, twist_ref, high_ref, rest_ref,
     out_ref, fgrad_ref, x_ref, y_ref, spec_ref, grad_ref,
 ):
     count, channels, tout, width = dims
@@ -170,14 +183,16 @@
     to_low = (edge_col == 0) & ((edge_row == 0) | (edge_row == 2) | (edge_row == 3))
     to_high = (edge_col == width - 1) & ((edge_row == 1) | (edge_row == 4) | (edge_row == 5))
     spread = (to_low | to_high).astype(f32).astype(bf16)
-    edges = [conv_ref[d, rows:, :rows].astype(f32) for d in range(count)]
+    low = 2 * rows * (width // lanes)
+    edges = [cols_ref[d, low:, :rows].astype(f32) for d in range(count)]
     none = jnp.zeros((edge_rows, rows), f32)
     kind = iota((edge_rows, rows), 0)
     for d in range(count):
         before = edges[d - 1] if d > 0 else none
         after = edges[d + 1] if d < count - 1 else none
         joined = jnp.where(kind < 2, edges[d], jnp.where(kind < 4, before, after))
-        whole = conv_ref[d, :rows].astype(f32) + dot_tn(joined.astype(bf16), spread)
+        blocks = [cols_ref[d, rows * b : rows * (b + 1)] for b in range(width // lanes)]
+        whole = jnp.concatenate(blocks, axis=1).astype(f32) + dot_tn(joined.astype(bf16), spread)
         x_ref[d] = whole.astype(bf16).astype(f32)
 
     def forward_planes(planes, r, h):
@@ -231,9 +246,9 @@
     y_ref[...] = inner(dot_nt)
     for r, h in chunks:
         planes = backward_planes(r, h)
+        at = rows * (width + h) // lanes + r
         slopes = [
-            cot_ref[d, r : r + tout, h : h + lanes].astype(f32) * gelu_slope(planes[d])
-            for d in range(count)
+            cols_ref[d, at : at + tout].astype(f32) * gelu_slope(planes[d]) for d in range(count)
         ]
         forward_planes(slopes, r, h)
     grad_ref[...] = inner(dot)
@@ -255,26 +270,29 @@
     last = ((iota((edge_rows, lanes), 0) == 0) & (iota((edge_rows, lanes), 1) == lanes - 1)).astype(f32).astype(bf16)
     first = ((iota((edge_rows, lanes), 0) == 1) & (iota((edge_rows, lanes), 1) == 0)).astype(f32).astype(bf16)
     for d in range(count):
-        out_ref[d, :rows] = x_ref[d].astype(bf16)
-        out_ref[d, rows:] = jnp.zeros((edge_rows, width), bf16)
+        for b in range(width // lanes):
+            out_ref[d, rows * b : rows * (b + 1)] = x_ref[d, :, lanes * b : lanes * (b + 1)].astype(bf16)
+        low = rows * (width // lanes)
+        out_ref[d, low:] = jnp.zeros((edge_rows, lanes), bf16)
         edge = none
         if d > 0:
             edge = edge + dot_nt(last, x_ref[d - 1, :, width - lanes :].astype(bf16))
         if d < count - 1:
             edge = edge + dot_nt(first, x_ref[d + 1, :, :lanes].astype(bf16))
-        out_ref[d, rows:, :rows] = edge.astype(bf16)
+        out_ref[d, low:, :rows] = edge.astype(bf16)
 
 
 def tap_kernel(dims, grad_ref, z_ref, tap_ref, shifted_ref, g_ref, zp_ref):
     cin, tin, cout, tout, ks, count, rows = dims
-    half = grad_ref.shape[2]
+    half = zp_ref.shape[1] // 2
     k_out = cout * tout
     row, col = iota((edge_rows, lanes), 0), iota((edge_rows, lanes), 1)
     spread = (((row == 1) & (col == 0)) | ((row == 0) & (col == 1))).astype(f32).astype(bf16)
     for d in range(count):
         at = slice(rows * d, rows * (d + 1))
-        g_ref[at, :half] = grad_ref[d, :rows].astype(f32)
-        g_ref[at, half:] = dot_tn(grad_ref[d, rows:, :rows], spread)
+        for b in range(half // lanes):
+            g_ref[at, lanes * b : lanes * (b + 1)] = grad_ref[d, rows * b : rows * (b + 1)].astype(f32)
+        g_ref[at, half:] = dot_tn(grad_ref[d, rows * (half // lanes) :, :rows], spread)
     to_time = one_hot((k_out, k_out), lambda r: (r % cout) * tout + r // cout)
     g = dot(to_time, g_ref[...].astype(bf16)).astype(bf16)
     wide = half + lanes
@@ -362,7 +380,7 @@
             out_ref[i, 4, c : c + 8] = packed[:, :cout] if low else packed[:, cout:]
 
 
-def summed_over(rows, axis):
+def summed_over(rows, axis, beside):
     count = lax.axis_size(axis)
     index = lax.axis_index(axis)
     pairs = lambda step: [(i, i ^ step) for i in range(count)]
@@ -373,6 +391,7 @@
         kept = lax.dynamic_slice_in_dim(rows, bit * size, size)
         sent = lax.dynamic_slice_in_dim(rows, (1 - bit) * size, size)
         rows = kept + lax.ppermute(sent, axis, pairs(step))
+    rows, beside = lax.optimization_barrier((rows, beside))
     step = 2 * halved[-1] if halved else 1
     while step < count:
         rows = rows + lax.ppermute(rows, axis, pairs(step))
@@ -381,7 +400,7 @@
         bit = (index // step) % 2
         other = lax.ppermute(rows, axis, pairs(step))
         rows = jnp.where(bit == 0, jnp.concatenate([rows, other]), jnp.concatenate([other, rows]))
-    return rows
+    return rows, beside
 
 
 def tables(count, width):
@@ -403,27 +422,38 @@
     channels = cout // count
     rows = channels * tout
     waves = count * width
+    tiles = width // lanes
     dims = (cin, tin, cout, tout, ks, count, rows)
     k_in, k_out = cin * tin, cout * tout
     taps = jnp.swapaxes(conv_taps, 2, 3)
     shape = jax.ShapeDtypeStruct
-    cot_cols = lax.all_to_all(
-        cotangent.reshape(count, rows, width), "fibre", split_axis=0, concat_axis=0, tiled=True
-    )
     conv_part, z = call(
         functools.partial(conv_kernel, dims),
-        [shape((count, rows + edge_rows, width), bf16), shape((k_in, fibre_in), bf16)],
-        [pltpu.VMEM((ks, k_out, k_in), bf16)],
+        [
+            shape((count, 2 * rows * tiles + edge_rows, lanes), bf16),
+            shape((k_in, fibre_in), bf16),
+        ],
+        [
+            pltpu.VMEM((ks, k_out, k_in), bf16),
+            pltpu.VMEM((k_in, fibre_in), bf16),
+            pltpu.VMEM((count, rows, width), bf16),
+            pltpu.SemaphoreType.DMA((2,)),
+        ],
         2e9,
-        (signal.reshape(k_in, fibre_in), taps),
-    )
-    conv_cols = lax.all_to_all(conv_part, "fibre", split_axis=0, concat_axis=0, tiled=True)
+        (signal.reshape(k_in, fibre_in), cotangent.reshape(count, rows, width), taps),
+        left=(0, 1),
+        room=60,
+    )
+    cols = lax.all_to_all(conv_part, "fibre", split_axis=0, concat_axis=0, tiled=True)
     arranged = (response * (1.0 / waves)).reshape(2, channels, width, count).transpose(0, 1, 3, 2)
     twist, high, rest = tables(count, width)
     big = count * rows
     grad_part, fgrad = call(
         functools.partial(filter_kernel, (count, channels, tout, width)),
-        [shape((count, rows + edge_rows, width), bf16), shape((2, channels, count, width), f32)],
+        [
+            shape((count, rows * tiles + edge_rows, lanes), bf16),
+            shape((2, channels, count, width), f32),
+        ],
         [
             pltpu.VMEM((count, rows, width), f32),
             pltpu.VMEM((big, 2 * width), f32),
@@ -431,10 +461,11 @@
             pltpu.VMEM((big, 2 * width), f32),
         ],
         6e9,
-        (conv_cols, cot_cols, arranged, jnp.asarray(twist), jnp.asarray(high), jnp.asarray(rest)),
+        (cols, arranged, jnp.asarray(twist), jnp.asarray(high), jnp.asarray(rest)),
     )
     filter_grad = fgrad.transpose(0, 1, 3, 2).reshape(2, channels, waves)
     grad_cols = lax.all_to_all(grad_part, "fibre", split_axis=0, concat_axis=0, tiled=True)
+    grad_cols, filter_grad = lax.optimization_barrier((grad_cols, filter_grad))
     taps_part, shifted = call(
         functools.partial(tap_kernel, dims),
         [shape((tap_rows, lanes), f32), shape((3, k_out, width), bf16)],
@@ -442,7 +473,6 @@
         1e9,
         (grad_cols, z),
     )
-    total = summed_over(taps_part, "fibre")
     (input_grad,) = call(
         functools.partial(input_kernel, dims),
         [shape((k_in, fibre_in), bf16)],
@@ -450,6 +480,7 @@
         2e9,
         (shifted, taps),
     )
+    total, input_grad = summed_over(taps_part, "fibre", input_grad)
     (tap_grad,) = call(
         functools.partial(unpack_kernel, dims, 1.0 / math.sqrt(tout * waves)),
         [shape((ks, ks, cin, cout), f32)],

time: 79.2 us -> 73.5 us (0.928)
  waiting for transfers between devices: 41.9 us -> 38.2 us
  starting transfers between devices: 17.6 us -> 15 us
  Pallas kernels: 15 us -> 16.8 us
  local copies, waits for them, and re-layouts: 3.21 us -> 2.28 us
    all_to_all x1 -> x0, starting transfers between devices: 7.53 us -> none  [per_device(): lax.all_to_all(cotangent.reshape(count, rows, width), 'fibre', split_axis...]
    all_to_all x1 -> x0, waiting for transfers between devices: 5.35 us -> none  [per_device(): lax.all_to_all(cotangent.reshape(count, rows, width), 'fibre', split_axis...]
    all_to_all x1, waiting for transfers between devices: 10.3 us -> 14.3 us  [per_device(): lax.all_to_all(conv_part, 'fibre', split_axis=0, concat_axis=0, tiled=True)]
    all_to_all x1, starting transfers between devices: 3.68 us -> 7.53 us  [per_device(): lax.all_to_all(conv_part, 'fibre', split_axis=0, concat_axis=0, tiled=True)]
    ppermute x2, waiting for transfers between devices: 4.96 us -> 2.28 us  [summed_over(): rows = kept + lax.ppermute(sent, axis, pairs(step))]
    ppermute x2, waiting for transfers between devices: 2.55 us -> 4.72 us  [summed_over(): other = lax.ppermute(rows, axis, pairs(step))]
    all_to_all x1, waiting for transfers between devices: 11 us -> 8.99 us  [per_device(): lax.all_to_all(grad_part, 'fibre', split_axis=0, concat_axis=0, tiled=True)]
    pallas_call x5, Pallas kernels: 15 us -> 16.8 us  [call(): pl.pallas_call(kernel, out_shape=outs, in_specs=[pl.BlockSpec(memory_spac...]
  transfers between devices with their start and end apart: 9 -> 8, of which waited for: 8 -> 8; matrix products, arithmetic and copies ran while one was open for 3% -> 3% of each run, Pallas kernels for 8% -> 4%
where the time goes in v1:
time: 73.5 us; the launch traced here: 73.2 us
  waiting for transfers between devices  38.2 us (52%)
  Pallas kernels  16.8 us (23%)
  starting transfers between devices  15 us (20%)
  local copies, waits for them, and re-layouts  2.28 us (3%)
  between operations  0.88 us (1%)
    pallas_call x5, Pallas kernels, call(): pl.pallas_call(kernel, out_shape=outs, in_specs=[pl.BlockSpec(memory_spac...  16.8 us
    all_to_all x1, waiting for transfers between devices, per_device(): lax.all_to_all(conv_part, 'fibre', split_axis=0, concat_axis=0, tiled=True)  14.3 us
    all_to_all x1, waiting for transfers between devices, per_device(): lax.all_to_all(grad_part, 'fibre', split_axis=0, concat_axis=0, tiled=True)  8.99 us
    ppermute x2, waiting for transfers between devices, summed_over(): rows = rows + lax.ppermute(rows, axis, pairs(step))  7.94 us
    all_to_all x1, starting transfers between devices, per_device(): lax.all_to_all(conv_part, 'fibre', split_axis=0, concat_axis=0, tiled=True)  7.53 us
    ppermute x2, waiting for transfers between devices, summed_over(): other = lax.ppermute(rows, axis, pairs(step))  4.72 us
    all_to_all x1, starting transfers between devices, per_device(): lax.all_to_all(grad_part, 'fibre', split_axis=0, concat_axis=0, tiled=True)  4.25 us
    ppermute x2, waiting for transfers between devices, summed_over(): rows = kept + lax.ppermute(sent, axis, pairs(step))  2.28 us
  transfers between devices with their start and end apart: 8, of which 8 were waited for; matrix products, arithmetic and copies ran while one was open for 3% of the time, Pallas kernels for 4%

profile of v1, /device:TPU:0, one launch (start us, length us, event | category | flops | bytes accessed | tf_op | source)
XLA Modules:
  0.0 73.2 jit_solution(14102613764329280218)
XLA Ops:
  0.6 5.6 %shard_map.94 = (bf16[16,136,128]{2,1,0:T(8,128)(2,1)}, bf16[512,512]{1,0:T(8,128)(2,1)}) custom-call(bf16[512,512]{1,0:T(8,128)(2,1)} %bitcast.14, bf16[16,32,256]{2,1,0:T(8,128)(2,1)} %bitcast.15, bf16[5,5,32,64]{3,2,1,0:T(8,128)(2,1)} %bitcast.11), custom_call_target="tpu_custom_call" | custom-call | flops 2000000000 | bytes 1970176 | tf_op jit(solution)/shard_map/pallas_call | solution.py:47
  6.2 0.0 copy-start.5
  6.2 7.5 %all-to-all-start = ((bf16[16,136,128]{2,1,0:T(8,128)(2,1)}), bf16[16,136,128]{2,1,0:T(8,128)(2,1)S(1)}, u32[]{:S(2)}, u32[]{:S(2)}) async-start(bf16[16,136,128]{2,1,0:T(8,128)(2,1)} %get-tuple-element.13), calls=%async_computation | async-start | bytes 1114112 | tf_op jit(solution)/shard_map/all_to_all | solution.py:447
  13.7 0.0 copy-done.5
  13.8 0.4 reshape.23
  14.2 0.0 copy-start.1
  14.2 0.0 copy-start.2
  14.2 0.0 copy-start.3
  14.2 0.3 copy.10
  14.5 14.3 %all-to-all-done.cols_ref = bf16[16,136,128]{2,1,0:T(8,128)(2,1)S(1)} async-done(((bf16[16,136,128]{2,1,0:T(8,128)(2,1)}), bf16[16,136,128]{2,1,0:T(8,128)(2,1)S(1)}, u32[]{:S(2)}, u32[]{:S(2)}) %all-to-all-start) | async-done | bytes 557088 | tf_op jit(solution)/shard_map/all_to_all | solution.py:447
  28.8 0.0 copy-done.1
  28.8 0.0 copy-done.2
  28.8 0.0 copy-done.3
  28.8 6.0 %shard_map.95 = (bf16[16,72,128]{2,1,0:T(8,128)(2,1)}, f32[2,4,16,256]{3,2,1,0:T(8,128)S(1)}) custom-call(bf16[16,136,128]{2,1,0:T(8,128)(2,1)S(1)} %all-to-all-done.cols_ref, f32[2,4,16,256]{3,2,1,0:T(8,128)S(1)} %bitcast.10, f32[2,16,256]{2,1,0:T(8,128)S(1)} %copy-done.3, bf16[512,512]{1,0:T(8,128)(2,1)S(1)} %copy-done.2, bf16[512,512]{1,0:T(8,128)(2,1)S(1)} %copy-done.1), custom_call_target="tpu_custom_call" | custom-call | flops 6000000000 | bytes 2195456 | tf_op jit(solution)/shard_map/pallas_call | solution.py:47
  34.8 4.2 %all-to-all-start.1 = ((bf16[16,72,128]{2,1,0:T(8,128)(2,1)}), bf16[16,72,128]{2,1,0:T(8,128)(2,1)S(1)}, u32[]{:S(2)}, u32[]{:S(2)}) async-start(bf16[16,72,128]{2,1,0:T(8,128)(2,1)} %get-tuple-element.14), calls=%async_computation.1 | async-start | bytes 589824 | tf_op jit(solution)/shard_map/all_to_all | solution.py:467
  39.1 0.3 copy.11
  39.4 0.0 copy-start.4
  39.4 1.2 %reshape.24 = f32[2,4,4096]{2,1,0:T(4,128)} reshape(f32[2,4,256,16]{3,2,1,0:T(8,128)S(1)} %copy.11) | data formatting | bytes 262144 | tf_op jit(solution)/shard_map/reshape | solution.py:466
  40.6 9.0 %all-to-all-done.1.grad_ref = bf16[16,72,128]{2,1,0:T(8,128)(2,1)S(1)} async-done(((bf16[16,72,128]{2,1,0:T(8,128)(2,1)}), bf16[16,72,128]{2,1,0:T(8,128)(2,1)S(1)}, u32[]{:S(2)}, u32[]{:S(2)}) %all-to-all-start.1) | async-done | bytes 294944 | tf_op jit(solution)/shard_map/all_to_all | solution.py:467
  49.6 0.0 copy-done.4
  49.6 1.6 %shard_map.96 = (f32[416,128]{1,0:T(8,128)S(1)}, bf16[3,512,256]{2,1,0:T(8,128)(2,1)S(1)}) custom-call(bf16[16,72,128]{2,1,0:T(8,128)(2,1)S(1)} %all-to-all-done.1.grad_ref, bf16[512,512]{1,0:T(8,128)(2,1)S(1)} %copy-done.4), custom_call_target="tpu_custom_call" | custom-call | flops 1000000000 | bytes 1818624 | tf_op jit(solution)/shard_map/pallas_call | solution.py:47
  51.2 0.1 collective-permute-start
  51.3 0.0 copy-start
  51.3 1.2 %collective-permute-done = f32[208,128]{1,0:T(8,128)S(1)} collective-permute-done((f32[208,128]{1,0:T(8,128)S(1)}, f32[208,128]{1,0:T(8,128)S(1)}, u32[]{:S(2)}, u32[]{:S(2)}) %collective-permute-start) | collective-permute-done | bytes 106528 | tf_op jit(solution)/shard_map/ppermute | solution.py:393
  52.6 0.4 collective-permute-start.1
  53.0 0.0 copy-done
  53.0 2.8 %shard_map.97 = bf16[512,512]{1,0:T(8,128)(2,1)} custom-call(bf16[3,512,256]{2,1,0:T(8,128)(2,1)S(1)} %get-tuple-element.19.shifted_ref, bf16[5,5,32,64]{3,2,1,0:T(8,128)(2,1)S(1)} %bitcast.12), custom_call_target="tpu_custom_call" | custom-call | flops 2000000000 | bytes 1413120 | tf_op jit(solution)/shard_map/pallas_call | solution.py:47
  55.8 1.0 %collective-permute-done.1 = f32[104,128]{1,0:T(8,128)S(1)} collective-permute-done((f32[104,128]{1,0:T(8,128)S(1)}, f32[104,128]{1,0:T(8,128)S(1)}, u32[]{:S(2)}, u32[]{:S(2)}) %collective-permute-start.1) | collective-permute-done | bytes 53280 | tf_op jit(solution)/shard_map/ppermute | solution.py:393
  56.8 0.6 collective-permute-start.2
  57.4 3.6 %collective-permute-done.2 = f32[104,128]{1,0:T(8,128)S(1)} collective-permute-done((f32[104,128]{1,0:T(8,128)S(1)}, f32[104,128]{1,0:T(8,128)S(1)}, u32[]{:S(2)}, u32[]{:S(2)}) %collective-permute-start.2) | collective-permute-done | bytes 53280 | tf_op jit(solution)/shard_map/ppermute | solution.py:397
  61.0 1.3 %collective-permute-start.3 = (f32[104,128]{1,0:T(8,128)S(1)}, f32[104,128]{1,0:T(8,128)S(1)}, u32[]{:S(2)}, u32[]{:S(2)}) collective-permute-start(f32[104,128]{1,0:T(8,128)S(1)} %add.43), channel_id=1, source_target_pairs={{0,8},{1,9},{2,10},{3,11},{4,12},{5,13},{6,14},{7,15},{8,0},{9,1},... | collective-permute-start | bytes 159752 | tf_op jit(solution)/shard_map/ppermute | solution.py:397
  62.3 4.3 %collective-permute-done.3 = f32[104,128]{1,0:T(8,128)S(1)} collective-permute-done((f32[104,128]{1,0:T(8,128)S(1)}, f32[104,128]{1,0:T(8,128)S(1)}, u32[]{:S(2)}, u32[]{:S(2)}) %collective-permute-start.3) | collective-permute-done | bytes 53280 | tf_op jit(solution)/shard_map/ppermute | solution.py:397
  66.7 0.8 %collective-permute-start.4 = (f32[104,128]{1,0:T(8,128)S(1)}, f32[104,128]{1,0:T(8,128)S(1)}, u32[]{:S(2)}, u32[]{:S(2)}) collective-permute-start(f32[104,128]{1,0:T(8,128)S(1)} %add.44), channel_id=1, source_target_pairs={{0,2},{1,3},{2,0},{3,1},{4,6},{5,7},{6,4},{7,5},{8,10},{9,11},{10,... | collective-permute-start | bytes 159752 | tf_op jit(solution)/shard_map/ppermute | solution.py:401
  67.5 3.4 %collective-permute-done.4 = f32[104,128]{1,0:T(8,128)S(1)} collective-permute-done((f32[104,128]{1,0:T(8,128)S(1)}, f32[104,128]{1,0:T(8,128)S(1)}, u32[]{:S(2)}, u32[]{:S(2)}) %collective-permute-start.4) | collective-permute-done | bytes 53280 | tf_op jit(solution)/shard_map/ppermute | solution.py:401
  70.9 0.1 collective-permute-start.5
  71.0 1.3 %collective-permute-done.5 = f32[208,128]{1,0:T(8,128)S(1)} collective-permute-done((f32[208,128]{1,0:T(8,128)S(1)}, f32[208,128]{1,0:T(8,128)S(1)}, u32[]{:S(2)}, u32[]{:S(2)}) %collective-permute-start.5) | collective-permute-done | bytes 106528 | tf_op jit(solution)/shard_map/ppermute | solution.py:401
  72.3 0.9 %shard_map.98 = f32[5,5,32,64]{3,2,1,0:T(8,128)} custom-call(f32[416,128]{1,0:T(8,128)S(1)} %maximum_select_fusion.tap_ref), custom_call_target="tpu_custom_call" | custom-call | flops 1000000 | bytes 417792 | tf_op jit(solution)/shard_map/pallas_call | solution.py:47
  (9 shorter events, 0.1 us)
Async XLA Ops:
  6.2 7.6 %copy-start.5 = (f32[2,4,4096]{2,1,0:T(4,128)S(1)}, f32[2,4,4096]{2,1,0:T(4,128)}, u32[]{:S(2)}) copy-start(f32[2,4,4096]{2,1,0:T(4,128)} %param.9) | copy-start | bytes 393220
  6.2 22.6 %all-to-all-start = ((bf16[16,136,128]{2,1,0:T(8,128)(2,1)}), bf16[16,136,128]{2,1,0:T(8,128)(2,1)S(1)}, u32[]{:S(2)}, u32[]{:S(2)}) async-start(bf16[16,136,128]{2,1,0:T(8,128)(2,1)} %get-tuple-element.13), calls=%async_computation | async-start | bytes 1114112 | tf_op jit(solution)/shard_map/all_to_all | solution.py:447
  14.2 14.6 %copy-start.1 = (bf16[512,512]{1,0:T(8,128)(2,1)S(1)}, bf16[512,512]{1,0:T(8,128)(2,1)}, u32[]{:S(2)}) copy-start(bf16[512,512]{1,0:T(8,128)(2,1)} %constant.66.clone.rest_ref) | copy-start | bytes 1572868
  14.2 14.6 %copy-start.2 = (bf16[512,512]{1,0:T(8,128)(2,1)S(1)}, bf16[512,512]{1,0:T(8,128)(2,1)}, u32[]{:S(2)}) copy-start(bf16[512,512]{1,0:T(8,128)(2,1)} %constant.65.clone.high_ref) | copy-start | bytes 1572868
  14.2 14.6 %copy-start.3 = (f32[2,16,256]{2,1,0:T(8,128)S(1)}, f32[2,16,256]{2,1,0:T(8,128)}, u32[]{:S(2)}) copy-start(f32[2,16,256]{2,1,0:T(8,128)} %constant.64.clone.twist_ref) | copy-start | bytes 98308
  34.8 14.8 %all-to-all-start.1 = ((bf16[16,72,128]{2,1,0:T(8,128)(2,1)}), bf16[16,72,128]{2,1,0:T(8,128)(2,1)S(1)}, u32[]{:S(2)}, u32[]{:S(2)}) async-start(bf16[16,72,128]{2,1,0:T(8,128)(2,1)} %get-tuple-element.14), calls=%async_computation.1 | async-start | bytes 589824 | tf_op jit(solution)/shard_map/all_to_all | solution.py:467
  39.4 10.2 %copy-start.4 = (bf16[512,512]{1,0:T(8,128)(2,1)S(1)}, bf16[512,512]{1,0:T(8,128)(2,1)}, u32[]{:S(2)}) copy-start(bf16[512,512]{1,0:T(8,128)(2,1)} %get-tuple-element.17.z_ref) | copy-start | bytes 1572868
  51.2 1.4 %collective-permute-start = (f32[208,128]{1,0:T(8,128)S(1)}, f32[208,128]{1,0:T(8,128)S(1)}, u32[]{:S(2)}, u32[]{:S(2)}) collective-permute-start(f32[208,128]{1,0:T(8,128)S(1)} %constant_dynamic-slice_fusion.1), channel_id=1, source_target_pairs={{0,1},{1,0},{2,3},{3,2},{4,5},{5,4},{6,7},{7,6},{8,9},{9,8},{10,11... | collective-permute-start | bytes 319496 | tf_op jit(solution)/shard_map/ppermute | solution.py:393
  51.3 1.7 %copy-start = (bf16[5,5,64,32]{2,3,1,0:T(8,128)(2,1)S(1)}, bf16[5,5,64,32]{2,3,1,0:T(8,128)(2,1)}, u32[]{:S(2)}) copy-start(bf16[5,5,64,32]{2,3,1,0:T(8,128)(2,1)} %param.8) | copy-start | bytes 307204
  52.6 4.2 %collective-permute-start.1 = (f32[104,128]{1,0:T(8,128)S(1)}, f32[104,128]{1,0:T(8,128)S(1)}, u32[]{:S(2)}, u32[]{:S(2)}) collective-permute-start(f32[104,128]{1,0:T(8,128)S(1)} %constant_dynamic-slice_fusion), channel_id=1, source_target_pairs={{0,2},{1,3},{2,0},{3,1},{4,6},{5,7},{6,4},{7,5},{8,10},{9,11},{10,... | collective-permute-start | bytes 159752 | tf_op jit(solution)/shard_map/ppermute | solution.py:393
  56.8 4.2 %collective-permute-start.2 = (f32[104,128]{1,0:T(8,128)S(1)}, f32[104,128]{1,0:T(8,128)S(1)}, u32[]{:S(2)}, u32[]{:S(2)}) collective-permute-start(f32[104,128]{1,0:T(8,128)S(1)} %dynamic-slice_add_fusion.1), channel_id=1, source_target_pairs={{0,4},{1,5},{2,6},{3,7},{4,0},{5,1},{6,2},{7,3},{8,12},{9,13},{10,... | collective-permute-start | bytes 159752 | tf_op jit(solution)/shard_map/ppermute | solution.py:397
  61.0 5.6 %collective-permute-start.3 = (f32[104,128]{1,0:T(8,128)S(1)}, f32[104,128]{1,0:T(8,128)S(1)}, u32[]{:S(2)}, u32[]{:S(2)}) collective-permute-start(f32[104,128]{1,0:T(8,128)S(1)} %add.43), channel_id=1, source_target_pairs={{0,8},{1,9},{2,10},{3,11},{4,12},{5,13},{6,14},{7,15},{8,0},{9,1},... | collective-permute-start | bytes 159752 | tf_op jit(solution)/shard_map/ppermute | solution.py:397
  66.7 4.2 %collective-permute-start.4 = (f32[104,128]{1,0:T(8,128)S(1)}, f32[104,128]{1,0:T(8,128)S(1)}, u32[]{:S(2)}, u32[]{:S(2)}) collective-permute-start(f32[104,128]{1,0:T(8,128)S(1)} %add.44), channel_id=1, source_target_pairs={{0,2},{1,3},{2,0},{3,1},{4,6},{5,7},{6,4},{7,5},{8,10},{9,11},{10,... | collective-permute-start | bytes 159752 | tf_op jit(solution)/shard_map/ppermute | solution.py:401
  70.9 1.4 %collective-permute-start.5 = (f32[208,128]{1,0:T(8,128)S(1)}, f32[208,128]{1,0:T(8,128)S(1)}, u32[]{:S(2)}, u32[]{:S(2)}) collective-permute-start(f32[208,128]{1,0:T(8,128)S(1)} %maximum_select_fusion.1), channel_id=1, source_target_pairs={{0,1},{1,0},{2,3},{3,2},{4,5},{5,4},{6,7},{7,6},{8,9},{9,8},{10,11... | collective-permute-start | bytes 319496 | tf_op jit(solution)/shard_map/ppermute | solution.py:401

commit v2 on v1

--- a/solution.py
+++ b/solution.py
@@ -34,12 +34,23 @@
     return lax.broadcasted_iota(jnp.int32, shape, dim)
 
 
+def split_index(x, size):
+    if size & (size - 1):
+        return x // size, x % size
+    return lax.shift_right_logical(x, jnp.full_like(x, size.bit_length() - 1)), x & (size - 1)
+
+
+def swapped(x, outer, inner):
+    a, b = split_index(x, inner)
+    return b * outer + a
+
+
 def one_hot(shape, column_of_row):
-    return (iota(shape, 1) == column_of_row(iota(shape, 0))).astype(f32).astype(bf16)
+    return (iota(shape, 1) == column_of_row(iota((shape[0], 1), 0))).astype(f32).astype(bf16)
 
 
 def one_hot_columns(shape, row_of_column):
-    return (iota(shape, 0) == row_of_column(iota(shape, 1))).astype(f32).astype(bf16)
+    return (iota(shape, 0) == row_of_column(iota((1, shape[1]), 1))).astype(f32).astype(bf16)
 
 
 def call(kernel, outs, scratch, flops, args, left=(), room=48):
@@ -82,10 +93,10 @@
                 tile = tiles[:, at : at + lanes] if 0 <= v < 4 else empty
                 w_ref[j, cout * t : cout * (t + 1), lanes * q : lanes * (q + 1)] = tile
     sig_copy.wait()
-    split = one_hot_columns((2 * lanes, 2 * lanes), lambda q: 2 * (q % lanes) + q // lanes)
+    split = one_hot_columns((2 * lanes, 2 * lanes), lambda q: swapped(q, 2, lanes))
     parts = [dot(sig_ref[:, b : b + 2 * lanes], split) for b in range(0, 2 * half, 2 * lanes)]
     apart = jnp.concatenate([p[:, :lanes] for p in parts] + [p[:, lanes:] for p in parts], axis=1)
-    to_time = one_hot((k_in, k_in), lambda r: (r % cin) * tin + r // cin)
+    to_time = one_hot((k_in, k_in), lambda r: swapped(r, tin, cin))
     z = dot(to_time, apart.astype(bf16)).astype(bf16)
     z_ref[...] = z
     even, odd = z[:, :half], z[:, half:]
@@ -117,7 +128,7 @@
         + pick(4, 0, right_high)
         + pick(5, 0, right_rest)
     ).astype(bf16)
-    to_channel = one_hot((k_out, k_out), lambda r: (r % tout) * cout + r // tout)
+    to_channel = one_hot((k_out, k_out), lambda r: swapped(r, cout, tout))
     edges = dot_nt(edges, to_channel)
     main = dot(to_channel, high).astype(bf16)
     cot_copy.wait()
@@ -293,7 +304,7 @@
         for b in range(half // lanes):
             g_ref[at, lanes * b : lanes * (b + 1)] = grad_ref[d, rows * b : rows * (b + 1)].astype(f32)
         g_ref[at, half:] = dot_tn(grad_ref[d, rows * (half // lanes) :, :rows], spread)
-    to_time = one_hot((k_out, k_out), lambda r: (r % cout) * tout + r // cout)
+    to_time = one_hot((k_out, k_out), lambda r: swapped(r, tout, cout))
     g = dot(to_time, g_ref[...].astype(bf16)).astype(bf16)
     wide = half + lanes
     later = one_hot_columns((wide, half), lambda n: n + 1)
@@ -353,9 +364,9 @@
     even = dot(w_ref[0], later) + dot(w_ref[2], same) + dot(w_ref[4], sooner)
     odd = dot(w_ref[1], later) + dot(w_ref[3], same)
     both = jnp.concatenate([even.astype(bf16), odd.astype(bf16)], axis=1)
-    to_channel = one_hot((k_in, k_in), lambda r: (r % tin) * cin + r // tin)
+    to_channel = one_hot((k_in, k_in), lambda r: swapped(r, cin, tin))
     both = dot(to_channel, both).astype(bf16)
-    merge = one_hot((2 * lanes, 2 * lanes), lambda r: 2 * (r % lanes) + r // lanes)
+    merge = one_hot((2 * lanes, 2 * lanes), lambda r: swapped(r, 2, lanes))
     for b in range(half // lanes):
         part = jnp.concatenate(
             [both[:, lanes * b : lanes * (b + 1)], both[:, half + lanes * b : half + lanes * (b + 1)]], axis=1
@@ -382,24 +393,21 @@
 
 def summed_over(rows, axis, beside):
     count = lax.axis_size(axis)
-    index = lax.axis_index(axis)
+    bit = lax.axis_index(axis) % 2
     pairs = lambda step: [(i, i ^ step) for i in range(count)]
-    halved = [step for step in (1, 2) if step < count]
-    for step in halved:
-        size = rows.shape[0] // 2
-        bit = (index // step) % 2
-        kept = lax.dynamic_slice_in_dim(rows, bit * size, size)
-        sent = lax.dynamic_slice_in_dim(rows, (1 - bit) * size, size)
-        rows = kept + lax.ppermute(sent, axis, pairs(step))
-    rows, beside = lax.optimization_barrier((rows, beside))
-    step = 2 * halved[-1] if halved else 1
+    size = rows.shape[0] // 2
+    kept = lax.dynamic_slice_in_dim(rows, bit * size, size)
+    sent = lax.dynamic_slice_in_dim(rows, (1 - bit) * size, size)
+    rows = kept + lax.ppermute(sent, axis, pairs(1))
+    step = 2
     while step < count:
-        rows = rows + lax.ppermute(rows, axis, pairs(step))
+        rounded = rows.astype(bf16)
+        rows = rounded.astype(f32) + lax.ppermute(rounded, axis, pairs(step)).astype(f32)
+        if step == 2:
+            rows, beside = lax.optimization_barrier((rows, beside))
         step *= 2
-    for step in reversed(halved):
-        bit = (index // step) % 2
-        other = lax.ppermute(rows, axis, pairs(step))
-        rows = jnp.where(bit == 0, jnp.concatenate([rows, other]), jnp.concatenate([other, rows]))
+    other = lax.ppermute(rows, axis, pairs(1))
+    rows = jnp.where(bit == 0, jnp.concatenate([rows, other]), jnp.concatenate([other, rows]))
     return rows, beside
 
 

time: 73.5 us -> 69.3 us (0.943)
  waiting for transfers between devices: 38.2 us -> 34.8 us
  starting transfers between devices: 15 us -> 14.2 us
    ppermute x6 -> x5, waiting for transfers between devices: 14.9 us -> 11.6 us  [the longest x3 8.98 us: summed_over(): lax.ppermute(rounded, axis, pairs(step)).astype(f32)]
    ppermute x6 -> x5, starting transfers between devices: 3.19 us -> 2.41 us  [the longest x3 2.27 us: summed_over(): lax.ppermute(rounded, axis, pairs(step)).astype(f32)]
  transfers between devices with their start and end apart: 8 -> 7, of which waited for: 8 -> 7; matrix products, arithmetic and copies ran while one was open for 3% -> 3% of each run, Pallas kernels for 4% -> 4%
where the time goes in v2:
time: 69.3 us; the launch traced here: 69 us
  waiting for transfers between devices  34.8 us (50%)
  Pallas kernels  16.8 us (24%)
  starting transfers between devices  14.2 us (20%)
  local copies, waits for them, and re-layouts  2.27 us (3%)
  between operations  0.83 us (1%)
    pallas_call x5, Pallas kernels, call(): pl.pallas_call(kernel, out_shape=outs, in_specs=[pl.BlockSpec(memory_spac...  16.8 us
    all_to_all x1, waiting for transfers between devices, per_device(): lax.all_to_all(conv_part, 'fibre', split_axis=0, concat_axis=0, tiled=True)  14.3 us
    all_to_all x1, waiting for transfers between devices, per_device(): lax.all_to_all(grad_part, 'fibre', split_axis=0, concat_axis=0, tiled=True)  8.99 us
    ppermute x3, waiting for transfers between devices, summed_over(): lax.ppermute(rounded, axis, pairs(step)).astype(f32)  8.98 us
    all_to_all x1, starting transfers between devices, per_device(): lax.all_to_all(conv_part, 'fibre', split_axis=0, concat_axis=0, tiled=True)  7.53 us
    all_to_all x1, starting transfers between devices, per_device(): lax.all_to_all(grad_part, 'fibre', split_axis=0, concat_axis=0, tiled=True)  4.24 us
    ppermute x3, starting transfers between devices, summed_over(): lax.ppermute(rounded, axis, pairs(step)).astype(f32)  2.27 us
  transfers between devices with their start and end apart: 7, of which 7 were waited for; matrix products, arithmetic and copies ran while one was open for 3% of the time, Pallas kernels for 4%

profile of v2, /device:TPU:0, one launch (start us, length us, event | category | flops | bytes accessed | tf_op | source)
XLA Modules:
  0.0 69.0 jit_solution(15085997422917981084)
XLA Ops:
  0.6 5.6 %shard_map.94 = (bf16[16,136,128]{2,1,0:T(8,128)(2,1)}, bf16[512,512]{1,0:T(8,128)(2,1)}) custom-call(bf16[512,512]{1,0:T(8,128)(2,1)} %bitcast.14, bf16[16,32,256]{2,1,0:T(8,128)(2,1)} %bitcast.15, bf16[5,5,32,64]{3,2,1,0:T(8,128)(2,1)} %bitcast.11), custom_call_target="tpu_custom_call" | custom-call | flops 2000000000 | bytes 1970176 | tf_op jit(solution)/shard_map/pallas_call | solution.py:58
  6.2 0.0 copy-start.5
  6.2 7.5 %all-to-all-start = ((bf16[16,136,128]{2,1,0:T(8,128)(2,1)}), bf16[16,136,128]{2,1,0:T(8,128)(2,1)S(1)}, u32[]{:S(2)}, u32[]{:S(2)}) async-start(bf16[16,136,128]{2,1,0:T(8,128)(2,1)} %get-tuple-element.13), calls=%async_computation | async-start | bytes 1114112 | tf_op jit(solution)/shard_map/all_to_all | solution.py:455
  13.7 0.0 copy-done.5
  13.8 0.4 reshape.23
  14.2 0.0 copy-start.1
  14.2 0.0 copy-start.2
  14.2 0.0 copy-start.3
  14.2 0.3 copy.10
  14.5 14.3 %all-to-all-done.cols_ref = bf16[16,136,128]{2,1,0:T(8,128)(2,1)S(1)} async-done(((bf16[16,136,128]{2,1,0:T(8,128)(2,1)}), bf16[16,136,128]{2,1,0:T(8,128)(2,1)S(1)}, u32[]{:S(2)}, u32[]{:S(2)}) %all-to-all-start) | async-done | bytes 557088 | tf_op jit(solution)/shard_map/all_to_all | solution.py:455
  28.8 0.0 copy-done.1
  28.8 0.0 copy-done.2
  28.8 0.0 copy-done.3
  28.8 6.0 %shard_map.95 = (bf16[16,72,128]{2,1,0:T(8,128)(2,1)}, f32[2,4,16,256]{3,2,1,0:T(8,128)S(1)}) custom-call(bf16[16,136,128]{2,1,0:T(8,128)(2,1)S(1)} %all-to-all-done.cols_ref, f32[2,4,16,256]{3,2,1,0:T(8,128)S(1)} %bitcast.10, f32[2,16,256]{2,1,0:T(8,128)S(1)} %copy-done.3, bf16[512,512]{1,0:T(8,128)(2,1)S(1)} %copy-done.2, bf16[512,512]{1,0:T(8,128)(2,1)S(1)} %copy-done.1), custom_call_target="tpu_custom_call" | custom-call | flops 6000000000 | bytes 2195456 | tf_op jit(solution)/shard_map/pallas_call | solution.py:58
  34.8 4.2 %all-to-all-start.1 = ((bf16[16,72,128]{2,1,0:T(8,128)(2,1)}), bf16[16,72,128]{2,1,0:T(8,128)(2,1)S(1)}, u32[]{:S(2)}, u32[]{:S(2)}) async-start(bf16[16,72,128]{2,1,0:T(8,128)(2,1)} %get-tuple-element.14), calls=%async_computation.1 | async-start | bytes 589824 | tf_op jit(solution)/shard_map/all_to_all | solution.py:475
  39.1 0.3 copy.11
  39.4 0.0 copy-start.4
  39.4 1.2 %reshape.24 = f32[2,4,4096]{2,1,0:T(4,128)} reshape(f32[2,4,256,16]{3,2,1,0:T(8,128)S(1)} %copy.11) | data formatting | bytes 262144 | tf_op jit(solution)/shard_map/reshape | solution.py:474
  40.6 9.0 %all-to-all-done.1.grad_ref = bf16[16,72,128]{2,1,0:T(8,128)(2,1)S(1)} async-done(((bf16[16,72,128]{2,1,0:T(8,128)(2,1)}), bf16[16,72,128]{2,1,0:T(8,128)(2,1)S(1)}, u32[]{:S(2)}, u32[]{:S(2)}) %all-to-all-start.1) | async-done | bytes 294944 | tf_op jit(solution)/shard_map/all_to_all | solution.py:475
  49.6 0.0 copy-done.4
  49.6 1.6 %shard_map.96 = (f32[416,128]{1,0:T(8,128)S(1)}, bf16[3,512,256]{2,1,0:T(8,128)(2,1)S(1)}) custom-call(bf16[16,72,128]{2,1,0:T(8,128)(2,1)S(1)} %all-to-all-done.1.grad_ref, bf16[512,512]{1,0:T(8,128)(2,1)S(1)} %copy-done.4), custom_call_target="tpu_custom_call" | custom-call | flops 1000000000 | bytes 1818624 | tf_op jit(solution)/shard_map/pallas_call | solution.py:58
  51.2 0.0 copy-start
  51.2 0.1 collective-permute-start
  51.3 1.3 %collective-permute-done = f32[208,128]{1,0:T(8,128)S(1)} collective-permute-done((f32[208,128]{1,0:T(8,128)S(1)}, f32[208,128]{1,0:T(8,128)S(1)}, u32[]{:S(2)}, u32[]{:S(2)}) %collective-permute-start) | collective-permute-done | bytes 106528 | tf_op jit(solution)/shard_map/ppermute | solution.py:401
  52.6 0.4 collective-permute-start.1
  53.0 0.0 copy-done
  53.0 2.8 %shard_map.97 = bf16[512,512]{1,0:T(8,128)(2,1)} custom-call(bf16[3,512,256]{2,1,0:T(8,128)(2,1)S(1)} %get-tuple-element.19.shifted_ref, bf16[5,5,32,64]{3,2,1,0:T(8,128)(2,1)S(1)} %bitcast.12), custom_call_target="tpu_custom_call" | custom-call | flops 2000000000 | bytes 1413120 | tf_op jit(solution)/shard_map/pallas_call | solution.py:58
  55.8 1.0 %collective-permute-done.1 = bf16[208,128]{1,0:T(8,128)(2,1)S(1)} collective-permute-done((bf16[208,128]{1,0:T(8,128)(2,1)S(1)}, bf16[208,128]{1,0:T(8,128)(2,1)S(1)}, u32[]{:S(2)}, u32[]{:S(2)}) %collective-permute-start.1) | collective-permute-done | bytes 53280 | tf_op jit(solution)/shard_map/ppermute | solution.py:405
  56.8 0.6 collective-permute-start.2
  57.4 3.6 %collective-permute-done.2 = bf16[208,128]{1,0:T(8,128)(2,1)S(1)} collective-permute-done((bf16[208,128]{1,0:T(8,128)(2,1)S(1)}, bf16[208,128]{1,0:T(8,128)(2,1)S(1)}, u32[]{:S(2)}, u32[]{:S(2)}) %collective-permute-start.2) | collective-permute-done | bytes 53280 | tf_op jit(solution)/shard_map/ppermute | solution.py:405
  61.1 1.3 %collective-permute-start.3 = (bf16[208,128]{1,0:T(8,128)(2,1)S(1)}, bf16[208,128]{1,0:T(8,128)(2,1)S(1)}, u32[]{:S(2)}, u32[]{:S(2)}) collective-permute-start(bf16[208,128]{1,0:T(8,128)(2,1)S(1)} %add_convert_fusion), channel_id=1, source_target_pairs={{0,8},{1,9},{2,10},{3,11},{4,12},{5,13},{6,14},{7,15},{8,0},{9,1},... | collective-permute-start | bytes 159752 | tf_op jit(solution)/shard_map/ppermute | solution.py:405
  62.4 4.3 %collective-permute-done.3 = bf16[208,128]{1,0:T(8,128)(2,1)S(1)} collective-permute-done((bf16[208,128]{1,0:T(8,128)(2,1)S(1)}, bf16[208,128]{1,0:T(8,128)(2,1)S(1)}, u32[]{:S(2)}, u32[]{:S(2)}) %collective-permute-start.3) | collective-permute-done | bytes 53280 | tf_op jit(solution)/shard_map/ppermute | solution.py:405
  66.7 0.1 collective-permute-start.4
  66.8 1.3 %collective-permute-done.4 = f32[208,128]{1,0:T(8,128)S(1)} collective-permute-done((f32[208,128]{1,0:T(8,128)S(1)}, f32[208,128]{1,0:T(8,128)S(1)}, u32[]{:S(2)}, u32[]{:S(2)}) %collective-permute-start.4) | collective-permute-done | bytes 106528 | tf_op jit(solution)/shard_map/ppermute | solution.py:409
  68.1 0.9 %shard_map.98 = f32[5,5,32,64]{3,2,1,0:T(8,128)} custom-call(f32[416,128]{1,0:T(8,128)S(1)} %maximum_select_fusion.tap_ref), custom_call_target="tpu_custom_call" | custom-call | flops 1000000 | bytes 417792 | tf_op jit(solution)/shard_map/pallas_call | solution.py:58
  (7 shorter events, 0.1 us)
Async XLA Ops:
  6.2 7.6 %copy-start.5 = (f32[2,4,4096]{2,1,0:T(4,128)S(1)}, f32[2,4,4096]{2,1,0:T(4,128)}, u32[]{:S(2)}) copy-start(f32[2,4,4096]{2,1,0:T(4,128)} %param.9) | copy-start | bytes 393220
  6.2 22.6 %all-to-all-start = ((bf16[16,136,128]{2,1,0:T(8,128)(2,1)}), bf16[16,136,128]{2,1,0:T(8,128)(2,1)S(1)}, u32[]{:S(2)}, u32[]{:S(2)}) async-start(bf16[16,136,128]{2,1,0:T(8,128)(2,1)} %get-tuple-element.13), calls=%async_computation | async-start | bytes 1114112 | tf_op jit(solution)/shard_map/all_to_all | solution.py:455
  14.2 14.6 %copy-start.1 = (bf16[512,512]{1,0:T(8,128)(2,1)S(1)}, bf16[512,512]{1,0:T(8,128)(2,1)}, u32[]{:S(2)}) copy-start(bf16[512,512]{1,0:T(8,128)(2,1)} %constant.33.clone.rest_ref) | copy-start | bytes 1572868
  14.2 14.6 %copy-start.2 = (bf16[512,512]{1,0:T(8,128)(2,1)S(1)}, bf16[512,512]{1,0:T(8,128)(2,1)}, u32[]{:S(2)}) copy-start(bf16[512,512]{1,0:T(8,128)(2,1)} %constant.32.clone.high_ref) | copy-start | bytes 1572868
  14.2 14.6 %copy-start.3 = (f32[2,16,256]{2,1,0:T(8,128)S(1)}, f32[2,16,256]{2,1,0:T(8,128)}, u32[]{:S(2)}) copy-start(f32[2,16,256]{2,1,0:T(8,128)} %constant.31.clone.twist_ref) | copy-start | bytes 98308
  34.8 14.8 %all-to-all-start.1 = ((bf16[16,72,128]{2,1,0:T(8,128)(2,1)}), bf16[16,72,128]{2,1,0:T(8,128)(2,1)S(1)}, u32[]{:S(2)}, u32[]{:S(2)}) async-start(bf16[16,72,128]{2,1,0:T(8,128)(2,1)} %get-tuple-element.14), calls=%async_computation.1 | async-start | bytes 589824 | tf_op jit(solution)/shard_map/all_to_all | solution.py:475
  39.4 10.2 %copy-start.4 = (bf16[512,512]{1,0:T(8,128)(2,1)S(1)}, bf16[512,512]{1,0:T(8,128)(2,1)}, u32[]{:S(2)}) copy-start(bf16[512,512]{1,0:T(8,128)(2,1)} %get-tuple-element.17.z_ref) | copy-start | bytes 1572868
  51.2 1.8 %copy-start = (bf16[5,5,64,32]{2,3,1,0:T(8,128)(2,1)S(1)}, bf16[5,5,64,32]{2,3,1,0:T(8,128)(2,1)}, u32[]{:S(2)}) copy-start(bf16[5,5,64,32]{2,3,1,0:T(8,128)(2,1)} %param.8) | copy-start | bytes 307204
  51.2 1.4 %collective-permute-start = (f32[208,128]{1,0:T(8,128)S(1)}, f32[208,128]{1,0:T(8,128)S(1)}, u32[]{:S(2)}, u32[]{:S(2)}) collective-permute-start(f32[208,128]{1,0:T(8,128)S(1)} %constant_dynamic-slice_fusion), channel_id=1, source_target_pairs={{0,1},{1,0},{2,3},{3,2},{4,5},{5,4},{6,7},{7,6},{8,9},{9,8},{10,11... | collective-permute-start | bytes 319496 | tf_op jit(solution)/shard_map/ppermute | solution.py:401
  52.6 4.2 %collective-permute-start.1 = (bf16[208,128]{1,0:T(8,128)(2,1)S(1)}, bf16[208,128]{1,0:T(8,128)(2,1)S(1)}, u32[]{:S(2)}, u32[]{:S(2)}) collective-permute-start(bf16[208,128]{1,0:T(8,128)(2,1)S(1)} %add_convert_fusion.1), channel_id=1, source_target_pairs={{0,2},{1,3},{2,0},{3,1},{4,6},{5,7},{6,4},{7,5},{8,10},{9,11},{10,... | collective-permute-start | bytes 159752 | tf_op jit(solution)/shard_map/ppermute | solution.py:405
  56.8 4.2 %collective-permute-start.2 = (bf16[208,128]{1,0:T(8,128)(2,1)S(1)}, bf16[208,128]{1,0:T(8,128)(2,1)S(1)}, u32[]{:S(2)}, u32[]{:S(2)}) collective-permute-start(bf16[208,128]{1,0:T(8,128)(2,1)S(1)} %convert_add_fusion.1), channel_id=1, source_target_pairs={{0,4},{1,5},{2,6},{3,7},{4,0},{5,1},{6,2},{7,3},{8,12},{9,13},{10,... | collective-permute-start | bytes 159752 | tf_op jit(solution)/shard_map/ppermute | solution.py:405
  61.1 5.6 %collective-permute-start.3 = (bf16[208,128]{1,0:T(8,128)(2,1)S(1)}, bf16[208,128]{1,0:T(8,128)(2,1)S(1)}, u32[]{:S(2)}, u32[]{:S(2)}) collective-permute-start(bf16[208,128]{1,0:T(8,128)(2,1)S(1)} %add_convert_fusion), channel_id=1, source_target_pairs={{0,8},{1,9},{2,10},{3,11},{4,12},{5,13},{6,14},{7,15},{8,0},{9,1},... | collective-permute-start | bytes 159752 | tf_op jit(solution)/shard_map/ppermute | solution.py:405
  66.7 1.4 %collective-permute-start.4 = (f32[208,128]{1,0:T(8,128)S(1)}, f32[208,128]{1,0:T(8,128)S(1)}, u32[]{:S(2)}, u32[]{:S(2)}) collective-permute-start(f32[208,128]{1,0:T(8,128)S(1)} %convert_add_fusion), channel_id=1, source_target_pairs={{0,1},{1,0},{2,3},{3,2},{4,5},{5,4},{6,7},{7,6},{8,9},{9,8},{10,11... | collective-permute-start | bytes 319496 | tf_op jit(solution)/shard_map/ppermute | solution.py:409

commit v3 on v2

--- a/solution.py
+++ b/solution.py
@@ -45,6 +45,17 @@
     return b * outer + a
 
 
+def packed_of(r, cout, tout):
+    def place(count):
+        channels, pair = cout // count, tout // 2
+        t, o = split_index(r, cout)
+        owner, channel = split_index(o, channels)
+        late, step = split_index(t, pair)
+        return ((owner * 2 + late) * channels + channel) * pair + step
+
+    return place
+
+
 def one_hot(shape, column_of_row):
     return (iota(shape, 1) == column_of_row(iota((shape[0], 1), 0))).astype(f32).astype(bf16)
 
@@ -53,7 +64,7 @@
     return (iota(shape, 0) == row_of_column(iota((1, shape[1]), 1))).astype(f32).astype(bf16)
 
 
-def call(kernel, outs, scratch, flops, args, left=(), room=48):
+def call(kernel, outs, scratch, flops, args, left=(), left_out=(), room=48):
     moved = sum(a.size * a.dtype.itemsize for a in list(args) + list(outs))
     return pl.pallas_call(
         kernel,
@@ -61,21 +72,48 @@
         in_specs=[
             pl.BlockSpec(memory_space=pltpu.HBM if a in left else pltpu.VMEM) for a in range(len(args))
         ],
-        out_specs=[pl.BlockSpec(memory_space=pltpu.VMEM)] * len(outs),
+        out_specs=[
+            pl.BlockSpec(memory_space=pltpu.HBM if a in left_out else pltpu.VMEM) for a in range(len(outs))
+        ],
         scratch_shapes=scratch,
         compiler_params=pltpu.CompilerParams(vmem_limit_bytes=room << 20),
         cost_estimate=pl.CostEstimate(flops=int(flops), bytes_accessed=moved, transcendentals=0),
     )(*args)
 
 
-def conv_kernel(dims, sig_hbm, cot_hbm, taps_ref, out_ref, z_ref, w_ref, sig_ref, cot_ref, sem):
+def conv_kernel(
+    dims, sig_hbm, cot_hbm, taps_hbm, out_hbm, z_hbm,
+    w_ref, sig_ref, cot_ref, taps_ref, out_ref, z_ref, sem,
+):
     cin, tin, cout, tout, ks, count, rows = dims
     k_in, k_out = cin * tin, cout * tout
     half = sig_ref.shape[1] // 2
-    sig_copy = pltpu.make_async_copy(sig_hbm, sig_ref, sem.at[0])
+    tiles_wide = half // lanes
+    conv_rows = rows * tiles_wide
+    taps_copy = pltpu.make_async_copy(taps_hbm, taps_ref, sem.at[0])
     cot_copy = pltpu.make_async_copy(cot_hbm, cot_ref, sem.at[1])
+    sig_copy = pltpu.make_async_copy(sig_hbm, sig_ref, sem.at[2])
+    at_cot, at_conv = pl.ds(conv_rows, conv_rows), pl.ds(0, conv_rows)
+    at_edge = pl.ds(2 * conv_rows, edge_rows)
+    cot_out = pltpu.make_async_copy(out_ref.at[:, at_cot], out_hbm.at[:, at_cot], sem.at[3])
+    z_out = pltpu.make_async_copy(z_ref, z_hbm, sem.at[4])
+    conv_out = pltpu.make_async_copy(out_ref.at[:, at_conv], out_hbm.at[:, at_conv], sem.at[5])
+    edge_out = pltpu.make_async_copy(out_ref.at[:, at_edge], out_hbm.at[:, at_edge], sem.at[6])
+    taps_copy.start()
+    cot_copy.start()
     sig_copy.start()
-    cot_copy.start()
+    packed = packed_of(iota((1, k_out), 1), cout, tout)(count)
+    from_time = (iota((k_out, k_out), 0) == packed).astype(f32).astype(bf16)
+    natural = packed_of(swapped(iota((1, k_out), 1), cout, tout), cout, tout)(count)
+    from_channel = (iota((k_out, k_out), 0) == natural).astype(f32).astype(bf16)
+    cot_copy.wait()
+    cot = dot(from_channel, cot_ref[...]).astype(bf16)
+    for d in range(count):
+        for b in range(tiles_wide):
+            at = conv_rows + rows * b
+            out_ref[d, at : at + rows] = cot[rows * d : rows * (d + 1), lanes * b : lanes * (b + 1)]
+    cot_out.start()
+    taps_copy.wait()
     blank = jnp.zeros((2 * cin, cout), bf16)
     stacked = []
     for j in range(ks):
@@ -99,6 +137,7 @@
     to_time = one_hot((k_in, k_in), lambda r: swapped(r, tin, cin))
     z = dot(to_time, apart.astype(bf16)).astype(bf16)
     z_ref[...] = z
+    z_out.start()
     even, odd = z[:, :half], z[:, half:]
     left = dot(w_ref[0], even) + dot(w_ref[1], odd)
     right = dot(w_ref[4], even)
@@ -128,19 +167,20 @@
         + pick(4, 0, right_high)
         + pick(5, 0, right_rest)
     ).astype(bf16)
-    to_channel = one_hot((k_out, k_out), lambda r: swapped(r, cout, tout))
-    edges = dot_nt(edges, to_channel)
-    main = dot(to_channel, high).astype(bf16)
-    cot_copy.wait()
+    edges = dot_nt(edges, from_time)
+    main = dot(from_time, high).astype(bf16)
     for d in range(count):
-        for b in range(half // lanes):
+        for b in range(tiles_wide):
             at = slice(lanes * b, lanes * (b + 1))
             out_ref[d, rows * b : rows * (b + 1)] = main[rows * d : rows * (d + 1), at]
-            low = rows * (half // lanes + b)
-            out_ref[d, low : low + rows] = cot_ref[d, :, at]
-        low = 2 * rows * (half // lanes)
-        out_ref[d, low:] = jnp.zeros((edge_rows, lanes), bf16)
-        out_ref[d, low:, :rows] = edges[:, rows * d : rows * (d + 1)].astype(bf16)
+        out_ref[d, 2 * conv_rows :] = jnp.zeros((edge_rows, lanes), bf16)
+        out_ref[d, 2 * conv_rows :, :rows] = edges[:, rows * d : rows * (d + 1)].astype(bf16)
+    conv_out.start()
+    edge_out.start()
+    cot_out.wait()
+    z_out.wait()
+    conv_out.wait()
+    edge_out.wait()
 
 
 def transform(real, imag, sign):
@@ -185,11 +225,12 @@
 
 def filter_kernel(
     dims, cols_ref, resp_ref, twist_ref, high_ref, rest_ref,
-    out_ref, fgrad_ref, x_ref, y_ref, spec_ref, grad_ref,
+    out_ref, cross_ref, x_ref, y_ref, spec_ref, grad_ref,
 ):
     count, channels, tout, width = dims
-    rows = channels * tout
-    scale = 1.0 / (count * width)
+    rows, pair = channels * tout, tout // 2
+    packed = rows // 2
+    chunk = min(8, packed)
     edge_row, edge_col = iota((edge_rows, width), 0), iota((edge_rows, width), 1)
     to_low = (edge_col == 0) & ((edge_row == 0) | (edge_row == 2) | (edge_row == 3))
     to_high = (edge_col == width - 1) & ((edge_row == 1) | (edge_row == 4) | (edge_row == 5))
@@ -206,78 +247,75 @@
         whole = jnp.concatenate(blocks, axis=1).astype(f32) + dot_tn(joined.astype(bf16), spread)
         x_ref[d] = whole.astype(bf16).astype(f32)
 
-    def forward_planes(planes, r, h):
-        re, im = transform(planes, None, -1)
+    def forward_planes(real, imag, r, h):
+        re, im = transform(real, imag, -1)
         for k in range(count):
             c = twist_ref[0, k : k + 1, h : h + lanes]
             s = twist_ref[1, k : k + 1, h : h + lanes]
-            at = pl.ds(k * rows + r, tout)
-            if k == 0:
-                y_ref[at, h : h + lanes] = re[k]
-                y_ref[at, width + h : width + h + lanes] = jnp.zeros_like(re[k]) if im[k] is None else im[k]
-            elif im[k] is None:
-                y_ref[at, h : h + lanes] = re[k] * c
-                y_ref[at, width + h : width + h + lanes] = -(re[k] * s)
-            else:
-                y_ref[at, h : h + lanes] = re[k] * c + im[k] * s
-                y_ref[at, width + h : width + h + lanes] = im[k] * c - re[k] * s
+            at = slice(k * packed + r, k * packed + r + chunk)
+            y_ref[at, h : h + lanes] = re[k] * c + im[k] * s if k else re[k]
+            y_ref[at, width + h : width + h + lanes] = im[k] * c - re[k] * s if k else im[k]
 
     def backward_planes(r, h):
         re, im = [], []
         for k in range(count):
             c = twist_ref[0, k : k + 1, h : h + lanes]
             s = twist_ref[1, k : k + 1, h : h + lanes]
-            at = pl.ds(k * rows + r, tout)
+            at = slice(k * packed + r, k * packed + r + chunk)
             a, b = y_ref[at, h : h + lanes], y_ref[at, width + h : width + h + lanes]
             re.append(a * c - b * s if k else a)
             im.append(b * c + a * s if k else b)
-        return transform(re, im, 1)[0]
-
-    def halves(v):
+        return transform(re, im, 1)
+
+    def inner(product):
+        v = y_ref[...]
         high = v.astype(bf16)
-        return high, (v - high.astype(f32)).astype(bf16)
-
-    def inner(product):
-        high, rest = halves(y_ref[...])
-        return (
-            product(high, high_ref[...]) + product(rest, high_ref[...]) + product(high, rest_ref[...])
+        rest = (v - high.astype(f32)).astype(bf16)
+        both = product(jnp.concatenate([high, rest], axis=0), high_ref[...])
+        size = v.shape[0]
+        return both[:size] + both[size:] + product(high, rest_ref[...])
+
+    chunks = [(r, h) for r in range(0, packed, chunk) for h in range(0, width, lanes)]
+    for r, h in chunks:
+        at, to = slice(r, r + chunk), slice(packed + r, packed + r + chunk)
+        forward_planes(
+            [x_ref[d, at, h : h + lanes] for d in range(count)],
+            [x_ref[d, to, h : h + lanes] for d in range(count)],
+            r, h,
         )
-
-    chunks = [(r * tout, h) for r in range(channels) for h in range(0, width, lanes)]
+    spec_ref[...] = inner(dot)
+    sr, si = spec_ref[:, :width], spec_ref[:, width:]
+    rr, ri = resp_ref[0], resp_ref[1]
+    y_ref[:, :width] = rr * sr - ri * si
+    y_ref[:, width:] = rr * si + ri * sr
+    y_ref[...] = inner(dot_nt)
     for r, h in chunks:
-        forward_planes([x_ref[d, r : r + tout, h : h + lanes] for d in range(count)], r, h)
-    spec_ref[...] = inner(dot)
+        real, imag = backward_planes(r, h)
+        at = rows * (width + h) // lanes + r
+        cot = [cols_ref[d, at : at + chunk].astype(f32) for d in range(count)]
+        real = [cot[d] * gelu_slope(real[d]) for d in range(count)]
+        at += packed
+        cot = [cols_ref[d, at : at + chunk].astype(f32) for d in range(count)]
+        imag = [cot[d] * gelu_slope(imag[d]) for d in range(count)]
+        forward_planes(real, imag, r, h)
+    grad_ref[...] = inner(dot)
+    sr, si = spec_ref[:, :width], spec_ref[:, width:]
+    gr, gi = grad_ref[:, :width], grad_ref[:, width:]
+    rr, ri = resp_ref[0], resp_ref[1]
+    y_ref[:, :width] = rr * gr + ri * gi
+    y_ref[:, width:] = rr * gi - ri * gr
+    scale = 1.0 / (count * width)
+    spec_ref[:, :width], spec_ref[:, width:] = (sr * gr + si * gi) * scale, (sr * gi - si * gr) * scale
     for k in range(count):
         for ch in range(channels):
-            at = pl.ds(k * rows + ch * tout, tout)
-            sr, si = spec_ref[at, :width], spec_ref[at, width:]
-            rr, ri = resp_ref[0, ch, k : k + 1], resp_ref[1, ch, k : k + 1]
-            y_ref[at, :width] = rr * sr - ri * si
-            y_ref[at, width:] = rr * si + ri * sr
+            at = k * packed + ch * pair
+            cross_ref[k, ch : ch + 1] = jnp.sum(spec_ref[at : at + pair], axis=0, keepdims=True)
     y_ref[...] = inner(dot_nt)
     for r, h in chunks:
-        planes = backward_planes(r, h)
-        at = rows * (width + h) // lanes + r
-        slopes = [
-            cols_ref[d, at : at + tout].astype(f32) * gelu_slope(planes[d]) for d in range(count)
-        ]
-        forward_planes(slopes, r, h)
-    grad_ref[...] = inner(dot)
-    for k in range(count):
-        for ch in range(channels):
-            at = pl.ds(k * rows + ch * tout, tout)
-            sr, si = spec_ref[at, :width], spec_ref[at, width:]
-            gr, gi = grad_ref[at, :width], grad_ref[at, width:]
-            rr, ri = resp_ref[0, ch, k : k + 1], resp_ref[1, ch, k : k + 1]
-            fgrad_ref[0, ch, k : k + 1] = jnp.sum(sr * gr + si * gi, axis=0, keepdims=True) * scale
-            fgrad_ref[1, ch, k : k + 1] = jnp.sum(sr * gi - si * gr, axis=0, keepdims=True) * scale
-            y_ref[at, :width] = rr * gr + ri * gi
-            y_ref[at, width:] = rr * gi - ri * gr
-    y_ref[...] = inner(dot_nt)
-    for r, h in chunks:
-        planes = backward_planes(r, h)
+        real, imag = backward_planes(r, h)
         for d in range(count):
-            x_ref[d, r : r + tout, h : h + lanes] = planes[d]
+            x_ref[d, r : r + chunk, h : h + lanes] = real[d]
+            x_ref[d, packed + r : packed + r + chunk, h : h + lanes] = imag[d]
     last = ((iota((edge_rows, lanes), 0) == 0) & (iota((edge_rows, lanes), 1) == lanes - 1)).astype(f32).astype(bf16)
     first = ((iota((edge_rows, lanes), 0) == 1) & (iota((edge_rows, lanes), 1) == 0)).astype(f32).astype(bf16)
     for d in range(count):
@@ -304,7 +342,7 @@
         for b in range(half // lanes):
             g_ref[at, lanes * b : lanes * (b + 1)] = grad_ref[d, rows * b : rows * (b + 1)].astype(f32)
         g_ref[at, half:] = dot_tn(grad_ref[d, rows * (half // lanes) :, :rows], spread)
-    to_time = one_hot((k_out, k_out), lambda r: swapped(r, tout, cout))
+    to_time = one_hot((k_out, k_out), lambda r: packed_of(r, cout, tout)(count))
     g = dot(to_time, g_ref[...].astype(bf16)).astype(bf16)
     wide = half + lanes
     later = one_hot_columns((wide, half), lambda n: n + 1)
@@ -402,13 +440,21 @@
     step = 2
     while step < count:
         rounded = rows.astype(bf16)
-        rows = rounded.astype(f32) + lax.ppermute(rounded, axis, pairs(step)).astype(f32)
-        if step == 2:
+        theirs = lambda step: lax.ppermute(rounded, axis, pairs(step)).astype(f32)
+        if step == 2 and 4 * step <= count:
+            rows = (rounded.astype(f32) + theirs(step)) + (theirs(2 * step) + theirs(3 * step))
             rows, beside = lax.optimization_barrier((rows, beside))
-        step *= 2
+            step *= 4
+        else:
+            rows = rounded.astype(f32) + theirs(step)
+            step *= 2
     other = lax.ppermute(rows, axis, pairs(1))
     rows = jnp.where(bit == 0, jnp.concatenate([rows, other]), jnp.concatenate([other, rows]))
     return rows, beside
+
+
+def mirrored(spectrum):
+    return jnp.roll(jnp.flip(spectrum, -1), 1, -1)
 
 
 def tables(count, width):
@@ -444,23 +490,31 @@
         [
             pltpu.VMEM((ks, k_out, k_in), bf16),
             pltpu.VMEM((k_in, fibre_in), bf16),
-            pltpu.VMEM((count, rows, width), bf16),
-            pltpu.SemaphoreType.DMA((2,)),
+            pltpu.VMEM((k_out, width), bf16),
+            pltpu.VMEM(taps.shape, bf16),
+            pltpu.VMEM((count, 2 * rows * tiles + edge_rows, lanes), bf16),
+            pltpu.VMEM((k_in, fibre_in), bf16),
+            pltpu.SemaphoreType.DMA((7,)),
         ],
         2e9,
-        (signal.reshape(k_in, fibre_in), cotangent.reshape(count, rows, width), taps),
-        left=(0, 1),
+        (signal.reshape(k_in, fibre_in), cotangent.reshape(k_out, width), taps),
+        left=(0, 1, 2),
+        left_out=(0, 1),
         room=60,
     )
     cols = lax.all_to_all(conv_part, "fibre", split_axis=0, concat_axis=0, tiled=True)
-    arranged = (response * (1.0 / waves)).reshape(2, channels, width, count).transpose(0, 1, 3, 2)
+    pair = tout // 2
+    back = mirrored(response)
+    real = jnp.stack([response[0] + back[0], response[1] - back[1]]) * (0.5 / waves)
+    real = real.reshape(2, channels, 1, width, count).transpose(0, 4, 1, 2, 3)
+    real = jnp.broadcast_to(real, (2, count, channels, pair, width)).reshape(2, count * rows // 2, width)
     twist, high, rest = tables(count, width)
-    big = count * rows
-    grad_part, fgrad = call(
+    big = count * rows // 2
+    grad_part, cross = call(
         functools.partial(filter_kernel, (count, channels, tout, width)),
         [
             shape((count, rows * tiles + edge_rows, lanes), bf16),
-            shape((2, channels, count, width), f32),
+            shape((count, channels, 2 * width), f32),
         ],
         [
             pltpu.VMEM((count, rows, width), f32),
@@ -469,9 +523,11 @@
             pltpu.VMEM((big, 2 * width), f32),
         ],
         6e9,
-        (cols, arranged, jnp.asarray(twist), jnp.asarray(high), jnp.asarray(rest)),
-    )
-    filter_grad = fgrad.transpose(0, 1, 3, 2).reshape(2, channels, waves)
+        (cols, real, jnp.asarray(twist), jnp.asarray(high), jnp.asarray(rest)),
+    )
+    cross = cross.reshape(count, channels, 2, width).transpose(2, 1, 3, 0).reshape(2, channels, waves)
+    back = mirrored(cross)
+    filter_grad = 0.5 * jnp.stack([cross[0] + back[0], cross[1] - back[1]])
     grad_cols = lax.all_to_all(grad_part, "fibre", split_axis=0, concat_axis=0, tiled=True)
     grad_cols, filter_grad = lax.optimization_barrier((grad_cols, filter_grad))
     taps_part, shifted = call(

time: 69.3 us -> 66.7 us (0.962)
  waiting for transfers between devices: 34.8 us -> 23 us
  local copies, waits for them, and re-layouts: 2.27 us -> 9.71 us
  starting transfers between devices: 14.2 us -> 16.8 us
  Pallas kernels: 16.8 us -> 14.9 us
  other arithmetic: 0.12 us -> 1.06 us
    unnamed x12 -> x16, local copies, waits for them, and re-layouts: 0.04 us -> 6.06 us
    ppermute x3 -> x4, waiting for transfers between devices: 8.98 us -> 4.38 us  [summed_over(): theirs = lambda step: lax.ppermute(rounded, axis, pairs(step)).astype(f32)]
    all_to_all x1, waiting for transfers between devices: 14.3 us -> 9.89 us  [per_device(): lax.all_to_all(conv_part, 'fibre', split_axis=0, concat_axis=0, tiled=True)]
    all_to_all x1, waiting for transfers between devices: 8.99 us -> 6.11 us  [per_device(): lax.all_to_all(grad_part, 'fibre', split_axis=0, concat_axis=0, tiled=True)]
    ppermute x3 -> x4, starting transfers between devices: 2.27 us -> 4.85 us  [summed_over(): theirs = lambda step: lax.ppermute(rounded, axis, pairs(step)).astype(f32)]
    pallas_call x5, Pallas kernels: 16.8 us -> 14.9 us  [call(): pl.pallas_call(kernel, out_shape=outs, in_specs=[pl.BlockSpec(memory_spac...]
    slice x0 -> x6, local copies, waits for them, and re-layouts: none -> 0.88 us  [the longest x5 0.81 us: mirrored(): return jnp.roll(jnp.flip(spectrum, -1), 1, -1)]
    another operation x0 -> x4, local copies, waits for them, and re-layouts: none -> 0.75 us  [per_device(): jnp.stack([response[0] + back[0], response[1] - back[1]]) * (0.5 / waves)]
  transfers between devices with their start and end apart: 7 -> 8, of which waited for: 7 -> 5; matrix products, arithmetic and copies ran while one was open for 3% -> 13% of each run, Pallas kernels for 4% -> 4%
where the time goes in v3:
time: 66.7 us; the launch traced here: 66.4 us
  waiting for transfers between devices  23 us (34%)
  starting transfers between devices  16.8 us (25%)
  Pallas kernels  14.9 us (22%)
  local copies, waits for them, and re-layouts  9.71 us (15%)
  other arithmetic  1.06 us (2%)
  between operations  0.93 us (1%)
    pallas_call x5, Pallas kernels, call(): pl.pallas_call(kernel, out_shape=outs, in_specs=[pl.BlockSpec(memory_spac...  14.9 us
    all_to_all x1, waiting for transfers between devices, per_device(): lax.all_to_all(conv_part, 'fibre', split_axis=0, concat_axis=0, tiled=True)  9.89 us
    all_to_all x1, starting transfers between devices, per_device(): lax.all_to_all(conv_part, 'fibre', split_axis=0, concat_axis=0, tiled=True)  7.53 us
    all_to_all x1, waiting for transfers between devices, per_device(): lax.all_to_all(grad_part, 'fibre', split_axis=0, concat_axis=0, tiled=True)  6.11 us
    unnamed x16, local copies, waits for them, and re-layouts  6.06 us
    ppermute x4, starting transfers between devices, summed_over(): theirs = lambda step: lax.ppermute(rounded, axis, pairs(step)).astype(f32)  4.85 us
    ppermute x4, waiting for transfers between devices, summed_over(): theirs = lambda step: lax.ppermute(rounded, axis, pairs(step)).astype(f32)  4.38 us
    all_to_all x1, starting transfers between devices, per_device(): lax.all_to_all(grad_part, 'fibre', split_axis=0, concat_axis=0, tiled=True)  4.27 us
  transfers between devices with their start and end apart: 8, of which 5 were waited for; matrix products, arithmetic and copies ran while one was open for 13% of the time, Pallas kernels for 4%

profile of v3, /device:TPU:0, one launch (start us, length us, event | category | flops | bytes accessed | tf_op | source)
XLA Modules:
  0.0 66.4 jit_solution(14669635403944347351)
XLA Ops:
  0.6 5.3 %shard_map.94 = (bf16[16,136,128]{2,1,0:T(8,128)(2,1)}, bf16[512,512]{1,0:T(8,128)(2,1)}) custom-call(bf16[512,512]{1,0:T(8,128)(2,1)} %bitcast.25, bf16[512,256]{1,0:T(8,128)(2,1)} %bitcast.26, bf16[5,5,32,64]{3,2,1,0:T(8,128)(2,1)} %bitcast.18), custom_call_target="tpu_custom_call" | custom-call | flops 2000000000 | bytes 1970176 | tf_op jit(solution)/shard_map/pallas_call | solution.py:69
  6.0 0.0 copy-start.5
  6.0 7.5 %all-to-all-start = ((bf16[16,136,128]{2,1,0:T(8,128)(2,1)}), bf16[16,136,128]{2,1,0:T(8,128)(2,1)S(1)}, u32[]{:S(2)}, u32[]{:S(2)}) async-start(bf16[16,136,128]{2,1,0:T(8,128)(2,1)} %get-tuple-element.13), calls=%async_computation | async-start | bytes 1114112 | tf_op jit(solution)/shard_map/all_to_all | solution.py:505
  13.5 0.1 slice.50
  13.7 2.9 %reverse.4 = f32[2,4,4096]{2,1,0:T(4,128)S(1)} reverse(f32[2,4,4096]{2,1,0:T(4,128)S(1)} %bitcast.22), dimensions={2} | reverse | bytes 262144
  16.5 0.1 slice.88
  16.7 0.6 slice-done
  17.3 0.1 fusion.4
  17.4 0.2 stack.15
  17.6 0.2 copy.17
  17.8 0.2 stack.14
  18.0 0.2 copy.16
  18.2 0.1 copy.18
  18.3 0.0 copy-start.3
  18.3 0.1 broadcast_in_dim.8
  18.4 0.0 copy-start.1
  18.4 0.0 copy-start.2
  18.5 0.2 reshape.62.resp_ref
  18.7 9.9 %all-to-all-done.cols_ref = bf16[16,136,128]{2,1,0:T(8,128)(2,1)S(1)} async-done(((bf16[16,136,128]{2,1,0:T(8,128)(2,1)}), bf16[16,136,128]{2,1,0:T(8,128)(2,1)S(1)}, u32[]{:S(2)}, u32[]{:S(2)}) %all-to-all-start) | async-done | bytes 557088 | tf_op jit(solution)/shard_map/all_to_all | solution.py:505
  28.6 4.4 %shard_map.95 = (bf16[16,72,128]{2,1,0:T(8,128)(2,1)}, f32[16,4,512]{2,1,0:T(4,128)S(1)}) custom-call(bf16[16,136,128]{2,1,0:T(8,128)(2,1)S(1)} %all-to-all-done.cols_ref, f32[2,256,256]{2,1,0:T(8,128)S(1)} %reshape.62.resp_ref, f32[2,16,256]{2,1,0:T(8,128)S(1)} %copy-done.3, bf16[512,512]{1,0:T(8,128)(2,1)S(1)} %copy-done.1, bf16[512,512]{1,0:T(8,128)(2,1)S(1)} %copy-done.2), custom_call_target="tpu_custom_call" | custom-call | flops 6000000000 | bytes 2588672 | tf_op jit(solution)/shard_map/pallas_call | solution.py:69
  32.9 0.1 reshape.63
  33.1 0.3 copy.19
  33.4 0.1 fusion.7
  33.5 0.6 reshape.64
  34.0 0.1 slice.66
  34.2 4.3 %all-to-all-start.1 = ((bf16[16,72,128]{2,1,0:T(8,128)(2,1)}), bf16[16,72,128]{2,1,0:T(8,128)(2,1)S(1)}, u32[]{:S(2)}, u32[]{:S(2)}) async-start(bf16[16,72,128]{2,1,0:T(8,128)(2,1)} %get-tuple-element.14), calls=%async_computation.1 | async-start | bytes 589824 | tf_op jit(solution)/shard_map/all_to_all | solution.py:531
  38.5 0.3 squeeze.4
  38.8 2.9 %reverse.5 = f32[2,4,4096]{2,1,0:T(4,128)S(1)} reverse(f32[2,4,4096]{2,1,0:T(4,128)S(1)} %bitcast.23), dimensions={2} | reverse | bytes 262144
  41.6 0.1 slice.89
  41.8 0.0 copy-start.4
  41.8 0.3 squeeze.5
  42.1 0.1 fusion.2
  42.2 0.7 %maximum_multiply_fusion.1 = f32[2,4,4096]{2,1,0:T(4,128)} fusion(f32[1,4,4096]{2,1,0:T(4,128)S(1)} %get-tuple-element.28, f32[1,4,4096]{2,1,0:T(4,128)S(1)} %get-tuple-element.27), kind=kLoop, calls=%fused_computation.7 | loop fusion | flops 65536 | bytes 262144 | tf_op jit(solution)/shard_map/mul | solution.py:530
  42.9 6.1 %all-to-all-done.1.grad_ref = bf16[16,72,128]{2,1,0:T(8,128)(2,1)S(1)} async-done(((bf16[16,72,128]{2,1,0:T(8,128)(2,1)}), bf16[16,72,128]{2,1,0:T(8,128)(2,1)S(1)}, u32[]{:S(2)}, u32[]{:S(2)}) %all-to-all-start.1) | async-done | bytes 294944 | tf_op jit(solution)/shard_map/all_to_all | solution.py:531
  49.0 1.6 %shard_map.96 = (f32[416,128]{1,0:T(8,128)S(1)}, bf16[3,512,256]{2,1,0:T(8,128)(2,1)S(1)}) custom-call(bf16[16,72,128]{2,1,0:T(8,128)(2,1)S(1)} %all-to-all-done.1.grad_ref, bf16[512,512]{1,0:T(8,128)(2,1)S(1)} %copy-done.4), custom_call_target="tpu_custom_call" | custom-call | flops 1000000000 | bytes 1818624 | tf_op jit(solution)/shard_map/pallas_call | solution.py:69
  50.6 0.0 copy-start
  50.6 0.1 collective-permute-start
  50.7 1.3 %collective-permute-done = f32[208,128]{1,0:T(8,128)S(1)} collective-permute-done((f32[208,128]{1,0:T(8,128)S(1)}, f32[208,128]{1,0:T(8,128)S(1)}, u32[]{:S(2)}, u32[]{:S(2)}) %collective-permute-start) | collective-permute-done | bytes 106528 | tf_op jit(solution)/shard_map/ppermute | solution.py:439
  52.0 0.8 %collective-permute-start.3 = (bf16[208,128]{1,0:T(8,128)(2,1)S(1)}, bf16[208,128]{1,0:T(8,128)(2,1)S(1)}, u32[]{:S(2)}, u32[]{:S(2)}) collective-permute-start(bf16[208,128]{1,0:T(8,128)(2,1)S(1)} %add_convert_fusion), channel_id=1, source_target_pairs={{0,6},{1,7},{2,4},{3,5},{4,2},{5,3},{6,0},{7,1},{8,14},{9,15},{10,... | collective-permute-start | bytes 159752 | tf_op jit(solution)/shard_map/ppermute | solution.py:443
  52.9 1.0 %collective-permute-start.2 = (bf16[208,128]{1,0:T(8,128)(2,1)S(1)}, bf16[208,128]{1,0:T(8,128)(2,1)S(1)}, u32[]{:S(2)}, u32[]{:S(2)}) collective-permute-start(bf16[208,128]{1,0:T(8,128)(2,1)S(1)} %add_convert_fusion), channel_id=1, source_target_pairs={{0,4},{1,5},{2,6},{3,7},{4,0},{5,1},{6,2},{7,3},{8,12},{9,13},{10,... | collective-permute-start | bytes 159752 | tf_op jit(solution)/shard_map/ppermute | solution.py:443
  53.9 1.7 %collective-permute-start.1 = (bf16[208,128]{1,0:T(8,128)(2,1)S(1)}, bf16[208,128]{1,0:T(8,128)(2,1)S(1)}, u32[]{:S(2)}, u32[]{:S(2)}) collective-permute-start(bf16[208,128]{1,0:T(8,128)(2,1)S(1)} %add_convert_fusion), channel_id=1, source_target_pairs={{0,2},{1,3},{2,0},{3,1},{4,6},{5,7},{6,4},{7,5},{8,10},{9,11},{10,... | collective-permute-start | bytes 159752 | tf_op jit(solution)/shard_map/ppermute | solution.py:443
  55.6 2.8 %shard_map.97 = bf16[512,512]{1,0:T(8,128)(2,1)} custom-call(bf16[3,512,256]{2,1,0:T(8,128)(2,1)S(1)} %get-tuple-element.19.shifted_ref, bf16[5,5,32,64]{3,2,1,0:T(8,128)(2,1)S(1)} %bitcast.19), custom_call_target="tpu_custom_call" | custom-call | flops 2000000000 | bytes 1413120 | tf_op jit(solution)/shard_map/pallas_call | solution.py:69
  58.4 0.0 collective-permute-done.3
  58.4 1.3 %collective-permute-start.4 = (bf16[208,128]{1,0:T(8,128)(2,1)S(1)}, bf16[208,128]{1,0:T(8,128)(2,1)S(1)}, u32[]{:S(2)}, u32[]{:S(2)}) collective-permute-start(bf16[208,128]{1,0:T(8,128)(2,1)S(1)} %add_add_fusion), channel_id=1, source_target_pairs={{0,8},{1,9},{2,10},{3,11},{4,12},{5,13},{6,14},{7,15},{8,0},{9,1},... | collective-permute-start | bytes 159752 | tf_op jit(solution)/shard_map/ppermute | solution.py:443
  59.7 4.4 %collective-permute-done.4 = bf16[208,128]{1,0:T(8,128)(2,1)S(1)} collective-permute-done((bf16[208,128]{1,0:T(8,128)(2,1)S(1)}, bf16[208,128]{1,0:T(8,128)(2,1)S(1)}, u32[]{:S(2)}, u32[]{:S(2)}) %collective-permute-start.4) | collective-permute-done | bytes 53280 | tf_op jit(solution)/shard_map/ppermute | solution.py:443
  64.1 0.1 collective-permute-start.5
  64.2 1.3 %collective-permute-done.5 = f32[208,128]{1,0:T(8,128)S(1)} collective-permute-done((f32[208,128]{1,0:T(8,128)S(1)}, f32[208,128]{1,0:T(8,128)S(1)}, u32[]{:S(2)}, u32[]{:S(2)}) %collective-permute-start.5) | collective-permute-done | bytes 106528 | tf_op jit(solution)/shard_map/ppermute | solution.py:451
  65.5 0.9 %shard_map.98 = f32[5,5,32,64]{3,2,1,0:T(8,128)} custom-call(f32[416,128]{1,0:T(8,128)S(1)} %maximum_select_fusion.tap_ref), custom_call_target="tpu_custom_call" | custom-call | flops 1000000 | bytes 417792 | tf_op jit(solution)/shard_map/pallas_call | solution.py:69
  (16 shorter events, 0.1 us)
Async XLA Ops:
  6.0 7.6 %copy-start.5 = (f32[2,4,4096]{2,1,0:T(4,128)S(1)}, f32[2,4,4096]{2,1,0:T(4,128)}, u32[]{:S(2)}) copy-start(f32[2,4,4096]{2,1,0:T(4,128)} %param.9) | copy-start | bytes 393220
  6.0 22.6 %all-to-all-start = ((bf16[16,136,128]{2,1,0:T(8,128)(2,1)}), bf16[16,136,128]{2,1,0:T(8,128)(2,1)S(1)}, u32[]{:S(2)}, u32[]{:S(2)}) async-start(bf16[16,136,128]{2,1,0:T(8,128)(2,1)} %get-tuple-element.13), calls=%async_computation | async-start | bytes 1114112 | tf_op jit(solution)/shard_map/all_to_all | solution.py:505
  16.5 0.7 %slice-start = ((f32[2,4,4096]{2,1,0:T(4,128)}), f32[2,4,1]{2,1,0:T(4,128)S(1)}, s32[]{:S(2)}) async-start(f32[2,4,4096]{2,1,0:T(4,128)} %param.9), calls=%async_computation.2 | async-start | bytes 8192 | tf_op jit(solution)/shard_map/jit(_roll_static)/slice | solution.py:457
  18.3 10.3 %copy-start.3 = (f32[2,16,256]{2,1,0:T(8,128)S(1)}, f32[2,16,256]{2,1,0:T(8,128)}, u32[]{:S(2)}) copy-start(f32[2,16,256]{2,1,0:T(8,128)} %constant.33.clone.twist_ref) | copy-start | bytes 98308
  18.4 10.1 %copy-start.1 = (bf16[512,512]{1,0:T(8,128)(2,1)S(1)}, bf16[512,512]{1,0:T(8,128)(2,1)}, u32[]{:S(2)}) copy-start(bf16[512,512]{1,0:T(8,128)(2,1)} %constant.34.clone.high_ref) | copy-start | bytes 1572868
  18.4 10.1 %copy-start.2 = (bf16[512,512]{1,0:T(8,128)(2,1)S(1)}, bf16[512,512]{1,0:T(8,128)(2,1)}, u32[]{:S(2)}) copy-start(bf16[512,512]{1,0:T(8,128)(2,1)} %constant.35.clone.rest_ref) | copy-start | bytes 1572868
  34.2 14.8 %all-to-all-start.1 = ((bf16[16,72,128]{2,1,0:T(8,128)(2,1)}), bf16[16,72,128]{2,1,0:T(8,128)(2,1)S(1)}, u32[]{:S(2)}, u32[]{:S(2)}) async-start(bf16[16,72,128]{2,1,0:T(8,128)(2,1)} %get-tuple-element.14), calls=%async_computation.1 | async-start | bytes 589824 | tf_op jit(solution)/shard_map/all_to_all | solution.py:531
  41.8 7.3 %copy-start.4 = (bf16[512,512]{1,0:T(8,128)(2,1)S(1)}, bf16[512,512]{1,0:T(8,128)(2,1)}, u32[]{:S(2)}) copy-start(bf16[512,512]{1,0:T(8,128)(2,1)} %get-tuple-element.17.z_ref) | copy-start | bytes 1572868
  50.6 5.0 %copy-start = (bf16[5,5,64,32]{2,3,1,0:T(8,128)(2,1)S(1)}, bf16[5,5,64,32]{2,3,1,0:T(8,128)(2,1)}, u32[]{:S(2)}) copy-start(bf16[5,5,64,32]{2,3,1,0:T(8,128)(2,1)} %param.8) | copy-start | bytes 307204
  50.6 1.4 %collective-permute-start = (f32[208,128]{1,0:T(8,128)S(1)}, f32[208,128]{1,0:T(8,128)S(1)}, u32[]{:S(2)}, u32[]{:S(2)}) collective-permute-start(f32[208,128]{1,0:T(8,128)S(1)} %constant_dynamic-slice_fusion), channel_id=1, source_target_pairs={{0,1},{1,0},{2,3},{3,2},{4,5},{5,4},{6,7},{7,6},{8,9},{9,8},{10,11... | collective-permute-start | bytes 319496 | tf_op jit(solution)/shard_map/ppermute | solution.py:439
  52.0 6.3 %collective-permute-start.3 = (bf16[208,128]{1,0:T(8,128)(2,1)S(1)}, bf16[208,128]{1,0:T(8,128)(2,1)S(1)}, u32[]{:S(2)}, u32[]{:S(2)}) collective-permute-start(bf16[208,128]{1,0:T(8,128)(2,1)S(1)} %add_convert_fusion), channel_id=1, source_target_pairs={{0,6},{1,7},{2,4},{3,5},{4,2},{5,3},{6,0},{7,1},{8,14},{9,15},{10,... | collective-permute-start | bytes 159752 | tf_op jit(solution)/shard_map/ppermute | solution.py:443
  52.9 5.5 %collective-permute-start.2 = (bf16[208,128]{1,0:T(8,128)(2,1)S(1)}, bf16[208,128]{1,0:T(8,128)(2,1)S(1)}, u32[]{:S(2)}, u32[]{:S(2)}) collective-permute-start(bf16[208,128]{1,0:T(8,128)(2,1)S(1)} %add_convert_fusion), channel_id=1, source_target_pairs={{0,4},{1,5},{2,6},{3,7},{4,0},{5,1},{6,2},{7,3},{8,12},{9,13},{10,... | collective-permute-start | bytes 159752 | tf_op jit(solution)/shard_map/ppermute | solution.py:443
  53.9 4.5 %collective-permute-start.1 = (bf16[208,128]{1,0:T(8,128)(2,1)S(1)}, bf16[208,128]{1,0:T(8,128)(2,1)S(1)}, u32[]{:S(2)}, u32[]{:S(2)}) collective-permute-start(bf16[208,128]{1,0:T(8,128)(2,1)S(1)} %add_convert_fusion), channel_id=1, source_target_pairs={{0,2},{1,3},{2,0},{3,1},{4,6},{5,7},{6,4},{7,5},{8,10},{9,11},{10,... | collective-permute-start | bytes 159752 | tf_op jit(solution)/shard_map/ppermute | solution.py:443
  58.4 5.7 %collective-permute-start.4 = (bf16[208,128]{1,0:T(8,128)(2,1)S(1)}, bf16[208,128]{1,0:T(8,128)(2,1)S(1)}, u32[]{:S(2)}, u32[]{:S(2)}) collective-permute-start(bf16[208,128]{1,0:T(8,128)(2,1)S(1)} %add_add_fusion), channel_id=1, source_target_pairs={{0,8},{1,9},{2,10},{3,11},{4,12},{5,13},{6,14},{7,15},{8,0},{9,1},... | collective-permute-start | bytes 159752 | tf_op jit(solution)/shard_map/ppermute | solution.py:443
  64.1 1.4 %collective-permute-start.5 = (f32[208,128]{1,0:T(8,128)S(1)}, f32[208,128]{1,0:T(8,128)S(1)}, u32[]{:S(2)}, u32[]{:S(2)}) collective-permute-start(f32[208,128]{1,0:T(8,128)S(1)} %convert_add_fusion), channel_id=1, source_target_pairs={{0,1},{1,0},{2,3},{3,2},{4,5},{5,4},{6,7},{7,6},{8,9},{9,8},{10,11... | collective-permute-start | bytes 319496 | tf_op jit(solution)/shard_map/ppermute | solution.py:451

commit v4 on v3

--- a/solution.py
+++ b/solution.py
@@ -43,17 +43,6 @@
 def swapped(x, outer, inner):
     a, b = split_index(x, inner)
     return b * outer + a
-
-
-def packed_of(r, cout, tout):
-    def place(count):
-        channels, pair = cout // count, tout // 2
-        t, o = split_index(r, cout)
-        owner, channel = split_index(o, channels)
-        late, step = split_index(t, pair)
-        return ((owner * 2 + late) * channels + channel) * pair + step
-
-    return place
 
 
 def one_hot(shape, column_of_row):
@@ -83,7 +72,7 @@
 
 def conv_kernel(
     dims, sig_hbm, cot_hbm, taps_hbm, out_hbm, z_hbm,
-    w_ref, sig_ref, cot_ref, taps_ref, out_ref, z_ref, sem,
+    w_ref, sig_ref, taps_ref, out_ref, z_ref, sem,
 ):
     cin, tin, cout, tout, ks, count, rows = dims
     k_in, k_out = cin * tin, cout * tout
@@ -91,28 +80,23 @@
     tiles_wide = half // lanes
     conv_rows = rows * tiles_wide
     taps_copy = pltpu.make_async_copy(taps_hbm, taps_ref, sem.at[0])
-    cot_copy = pltpu.make_async_copy(cot_hbm, cot_ref, sem.at[1])
-    sig_copy = pltpu.make_async_copy(sig_hbm, sig_ref, sem.at[2])
-    at_cot, at_conv = pl.ds(conv_rows, conv_rows), pl.ds(0, conv_rows)
-    at_edge = pl.ds(2 * conv_rows, edge_rows)
-    cot_out = pltpu.make_async_copy(out_ref.at[:, at_cot], out_hbm.at[:, at_cot], sem.at[3])
-    z_out = pltpu.make_async_copy(z_ref, z_hbm, sem.at[4])
-    conv_out = pltpu.make_async_copy(out_ref.at[:, at_conv], out_hbm.at[:, at_conv], sem.at[5])
-    edge_out = pltpu.make_async_copy(out_ref.at[:, at_edge], out_hbm.at[:, at_edge], sem.at[6])
+    sig_copy = pltpu.make_async_copy(sig_hbm, sig_ref, sem.at[1])
+    cot_copies = [
+        pltpu.make_async_copy(
+            cot_hbm.at[:, :, pl.ds(lanes * b, lanes)],
+            out_hbm.at[:, pl.ds(conv_rows + rows * b, rows)],
+            sem.at[5 + b],
+        )
+        for b in range(tiles_wide)
+    ]
+    at_conv, at_edge = pl.ds(0, conv_rows), pl.ds(2 * conv_rows, edge_rows)
+    z_out = pltpu.make_async_copy(z_ref, z_hbm, sem.at[2])
+    conv_out = pltpu.make_async_copy(out_ref.at[:, at_conv], out_hbm.at[:, at_conv], sem.at[3])
+    edge_out = pltpu.make_async_copy(out_ref.at[:, at_edge], out_hbm.at[:, at_edge], sem.at[4])
     taps_copy.start()
-    cot_copy.start()
     sig_copy.start()
-    packed = packed_of(iota((1, k_out), 1), cout, tout)(count)
-    from_time = (iota((k_out, k_out), 0) == packed).astype(f32).astype(bf16)
-    natural = packed_of(swapped(iota((1, k_out), 1), cout, tout), cout, tout)(count)
-    from_channel = (iota((k_out, k_out), 0) == natural).astype(f32).astype(bf16)
-    cot_copy.wait()
-    cot = dot(from_channel, cot_ref[...]).astype(bf16)
-    for d in range(count):
-        for b in range(tiles_wide):
-            at = conv_rows + rows * b
-            out_ref[d, at : at + rows] = cot[rows * d : rows * (d + 1), lanes * b : lanes * (b + 1)]
-    cot_out.start()
+    for copy in cot_copies:
+        copy.start()
     taps_copy.wait()
     blank = jnp.zeros((2 * cin, cout), bf16)
     stacked = []
@@ -149,25 +133,21 @@
         + jnp.where(lane == half - 1, 0.0, pltpu.roll(right, half - 1, 1))
     )
     high = own.astype(bf16)
-    rest = (own - high.astype(f32)).astype(bf16)
-    left_edge, right_edge = left[:, half - lanes :], right[:, :lanes]
-    left_high, right_high = left_edge.astype(bf16), right_edge.astype(bf16)
-    left_rest = (left_edge - left_high.astype(f32)).astype(bf16)
-    right_rest = (right_edge - right_high.astype(f32)).astype(bf16)
-
-    def pick(row, column, tile):
-        at = (iota((edge_rows, lanes), 0) == row) & (iota((edge_rows, lanes), 1) == column)
-        return dot_nt(at.astype(f32).astype(bf16), tile)
-
-    edges = (
-        pick(0, 0, rest[:, :lanes])
-        + pick(1, lanes - 1, rest[:, half - lanes :])
-        + pick(2, lanes - 1, left_high)
-        + pick(3, lanes - 1, left_rest)
-        + pick(4, 0, right_high)
-        + pick(5, 0, right_rest)
-    ).astype(bf16)
-    edges = dot_nt(edges, from_time)
+    first = iota((k_out, lanes), 1) == 0
+
+    def parts_of(v):
+        top = v.astype(bf16)
+        return top, (v - top.astype(f32)).astype(bf16)
+
+    _, own_rest = parts_of(jnp.where(first, own[:, :lanes], own[:, half - lanes :]))
+    next_high, next_rest = parts_of(jnp.where(first, right[:, :lanes], left[:, half - lanes :]))
+    row, col = iota((edge_rows, 3 * lanes), 0), iota((edge_rows, 3 * lanes), 1)
+    pick = jnp.zeros((edge_rows, 3 * lanes), f32)
+    for at, column in enumerate((0, lanes - 1, 2 * lanes - 1, 3 * lanes - 1, lanes, 2 * lanes)):
+        pick = jnp.where((row == at) & (col == column), 1.0, pick)
+    edges = dot_nt(pick.astype(bf16), jnp.concatenate([own_rest, next_high, next_rest], axis=1))
+    from_time = one_hot((k_out, k_out), lambda r: swapped(r, cout, tout))
+    edges = dot_nt(edges.astype(bf16), from_time)
     main = dot(from_time, high).astype(bf16)
     for d in range(count):
         for b in range(tiles_wide):
@@ -177,7 +157,8 @@
         out_ref[d, 2 * conv_rows :, :rows] = edges[:, rows * d : rows * (d + 1)].astype(bf16)
     conv_out.start()
     edge_out.start()
-    cot_out.wait()
+    for copy in cot_copies:
+        copy.wait()
     z_out.wait()
     conv_out.wait()
     edge_out.wait()
@@ -230,7 +211,8 @@
     count, channels, tout, width = dims
     rows, pair = channels * tout, tout // 2
     packed = rows // 2
-    chunk = min(8, packed)
+    group = min(2, channels)
+    chunk = group * pair
     edge_row, edge_col = iota((edge_rows, width), 0), iota((edge_rows, width), 1)
     to_low = (edge_col == 0) & ((edge_row == 0) | (edge_row == 2) | (edge_row == 3))
     to_high = (edge_col == width - 1) & ((edge_row == 1) | (edge_row == 4) | (edge_row == 5))
@@ -275,14 +257,19 @@
         size = v.shape[0]
         return both[:size] + both[size:] + product(high, rest_ref[...])
 
+    def paired(tiles):
+        return (
+            jnp.concatenate([tile[:pair] for tile in tiles], axis=0),
+            jnp.concatenate([tile[pair:] for tile in tiles], axis=0),
+        )
+
     chunks = [(r, h) for r in range(0, packed, chunk) for h in range(0, width, lanes)]
     for r, h in chunks:
-        at, to = slice(r, r + chunk), slice(packed + r, packed + r + chunk)
-        forward_planes(
-            [x_ref[d, at, h : h + lanes] for d in range(count)],
-            [x_ref[d, to, h : h + lanes] for d in range(count)],
-            r, h,
-        )
+        planes = [
+            paired([x_ref[d, 2 * r + tout * g : 2 * r + tout * (g + 1), h : h + lanes] for g in range(group)])
+            for d in range(count)
+        ]
+        forward_planes([re for re, im in planes], [im for re, im in planes], r, h)
     spec_ref[...] = inner(dot)
     sr, si = spec_ref[:, :width], spec_ref[:, width:]
     rr, ri = resp_ref[0], resp_ref[1]
@@ -291,12 +278,11 @@
     y_ref[...] = inner(dot_nt)
     for r, h in chunks:
         real, imag = backward_planes(r, h)
-        at = rows * (width + h) // lanes + r
-        cot = [cols_ref[d, at : at + chunk].astype(f32) for d in range(count)]
-        real = [cot[d] * gelu_slope(real[d]) for d in range(count)]
-        at += packed
-        cot = [cols_ref[d, at : at + chunk].astype(f32) for d in range(count)]
-        imag = [cot[d] * gelu_slope(imag[d]) for d in range(count)]
+        at = rows * (width + h) // lanes + 2 * r
+        for d in range(count):
+            cot = cols_ref[d, at : at + tout * group].astype(f32)
+            re, im = paired([cot[tout * g : tout * (g + 1)] for g in range(group)])
+            real[d], imag[d] = re * gelu_slope(real[d]), im * gelu_slope(imag[d])
         forward_planes(real, imag, r, h)
     grad_ref[...] = inner(dot)
     sr, si = spec_ref[:, :width], spec_ref[:, width:]
@@ -314,8 +300,10 @@
     for r, h in chunks:
         real, imag = backward_planes(r, h)
         for d in range(count):
-            x_ref[d, r : r + chunk, h : h + lanes] = real[d]
-            x_ref[d, packed + r : packed + r + chunk, h : h + lanes] = imag[d]
+            for g in range(group):
+                at = slice(pair * g, pair * (g + 1))
+                tile = jnp.concatenate([real[d][at], imag[d][at]], axis=0)
+                x_ref[d, 2 * r + tout * g : 2 * r + tout * (g + 1), h : h + lanes] = tile
     last = ((iota((edge_rows, lanes), 0) == 0) & (iota((edge_rows, lanes), 1) == lanes - 1)).astype(f32).astype(bf16)
     first = ((iota((edge_rows, lanes), 0) == 1) & (iota((edge_rows, lanes), 1) == 0)).astype(f32).astype(bf16)
     for d in range(count):
@@ -331,6 +319,29 @@
         out_ref[d, low:, :rows] = edge.astype(bf16)
 
 
+def hermitian_kernel(cross_ref, out_ref):
+    count, channels, wide = cross_ref.shape
+    width = wide // 2
+    row, col = iota((width, width), 0), iota((width, width), 1)
+    flip = (row + col == width - 1).astype(f32).astype(bf16)
+    flip_first = ((row + col == width) | ((row == 0) & (col == 0))).astype(f32).astype(bf16)
+
+    def moved(v, by):
+        total = None
+        for _ in range(3):
+            part = v.astype(bf16)
+            v = v - part.astype(f32)
+            term = dot(part, by)
+            total = term if total is None else total + term
+        return total
+
+    for k in range(count):
+        own, other = cross_ref[k], cross_ref[(count - k) % count]
+        by = flip if k else flip_first
+        out_ref[0, :, k] = 0.5 * (own[:, :width] + moved(other[:, :width], by))
+        out_ref[1, :, k] = 0.5 * (own[:, width:] - moved(other[:, width:], by))
+
+
 def tap_kernel(dims, grad_ref, z_ref, tap_ref, shifted_ref, g_ref, zp_ref):
     cin, tin, cout, tout, ks, count, rows = dims
     half = zp_ref.shape[1] // 2
@@ -342,7 +353,7 @@
         for b in range(half // lanes):
             g_ref[at, lanes * b : lanes * (b + 1)] = grad_ref[d, rows * b : rows * (b + 1)].astype(f32)
         g_ref[at, half:] = dot_tn(grad_ref[d, rows * (half // lanes) :, :rows], spread)
-    to_time = one_hot((k_out, k_out), lambda r: packed_of(r, cout, tout)(count))
+    to_time = one_hot((k_out, k_out), lambda r: swapped(r, tout, cout))
     g = dot(to_time, g_ref[...].astype(bf16)).astype(bf16)
     wide = half + lanes
     later = one_hot_columns((wide, half), lambda n: n + 1)
@@ -490,14 +501,13 @@
         [
             pltpu.VMEM((ks, k_out, k_in), bf16),
             pltpu.VMEM((k_in, fibre_in), bf16),
-            pltpu.VMEM((k_out, width), bf16),
             pltpu.VMEM(taps.shape, bf16),
             pltpu.VMEM((count, 2 * rows * tiles + edge_rows, lanes), bf16),
             pltpu.VMEM((k_in, fibre_in), bf16),
-            pltpu.SemaphoreType.DMA((7,)),
+            pltpu.SemaphoreType.DMA((5 + tiles,)),
         ],
         2e9,
-        (signal.reshape(k_in, fibre_in), cotangent.reshape(k_out, width), taps),
+        (signal.reshape(k_in, fibre_in), cotangent.reshape(count, rows, width), taps),
         left=(0, 1, 2),
         left_out=(0, 1),
         room=60,
@@ -525,9 +535,8 @@
         6e9,
         (cols, real, jnp.asarray(twist), jnp.asarray(high), jnp.asarray(rest)),
     )
-    cross = cross.reshape(count, channels, 2, width).transpose(2, 1, 3, 0).reshape(2, channels, waves)
-    back = mirrored(cross)
-    filter_grad = 0.5 * jnp.stack([cross[0] + back[0], cross[1] - back[1]])
+    (cross,) = call(hermitian_kernel, [shape((2, channels, count, width), f32)], [], 1e6, (cross,))
+    filter_grad = cross.transpose(0, 1, 3, 2).reshape(2, channels, waves)
     grad_cols = lax.all_to_all(grad_part, "fibre", split_axis=0, concat_axis=0, tiled=True)
     grad_cols, filter_grad = lax.optimization_barrier((grad_cols, filter_grad))
     taps_part, shifted = call(

time: 66.7 us -> 69.3 us (1.039)
  Pallas kernels: 14.9 us -> 20.5 us
  local copies, waits for them, and re-layouts: 9.71 us -> 6.45 us
  waiting for transfers between devices: 23 us -> 24.1 us
  other arithmetic: 1.06 us -> 0.23 us
    pallas_call x5 -> x6, Pallas kernels: 14.9 us -> 20.5 us  [call(): pl.pallas_call(kernel, out_shape=outs, in_specs=[pl.BlockSpec(memory_spac...]
    unnamed x16 -> x14, local copies, waits for them, and re-layouts: 6.06 us -> 3.05 us
    all_to_all x1, waiting for transfers between devices: 6.11 us -> 7.23 us  [per_device(): lax.all_to_all(grad_part, 'fibre', split_axis=0, concat_axis=0, tiled=True)]
  transfers between devices with their start and end apart: 8 -> 8, of which waited for: 5 -> 5; matrix products, arithmetic and copies ran while one was open for 13% -> 9% of each run, Pallas kernels for 4% -> 7%
where the time goes in v4:
time: 69.3 us; the launch traced here: 69 us
  waiting for transfers between devices  24.1 us (35%)
  Pallas kernels  20.5 us (30%)
  starting transfers between devices  16.8 us (24%)
  local copies, waits for them, and re-layouts  6.45 us (9%)
  between operations  0.89 us (1%)
    pallas_call x6, Pallas kernels, call(): pl.pallas_call(kernel, out_shape=outs, in_specs=[pl.BlockSpec(memory_spac...  20.5 us
    all_to_all x1, waiting for transfers between devices, per_device(): lax.all_to_all(conv_part, 'fibre', split_axis=0, concat_axis=0, tiled=True)  9.91 us
    all_to_all x1, starting transfers between devices, per_device(): lax.all_to_all(conv_part, 'fibre', split_axis=0, concat_axis=0, tiled=True)  7.53 us
    all_to_all x1, waiting for transfers between devices, per_device(): lax.all_to_all(grad_part, 'fibre', split_axis=0, concat_axis=0, tiled=True)  7.23 us
    ppermute x4, starting transfers between devices, summed_over(): theirs = lambda step: lax.ppermute(rounded, axis, pairs(step)).astype(f32)  4.85 us
    ppermute x4, waiting for transfers between devices, summed_over(): theirs = lambda step: lax.ppermute(rounded, axis, pairs(step)).astype(f32)  4.38 us
    all_to_all x1, starting transfers between devices, per_device(): lax.all_to_all(grad_part, 'fibre', split_axis=0, concat_axis=0, tiled=True)  4.25 us
    unnamed x14, local copies, waits for them, and re-layouts  3.05 us
  transfers between devices with their start and end apart: 8, of which 5 were waited for; matrix products, arithmetic and copies ran while one was open for 9% of the time, Pallas kernels for 7%

profile of v4, /device:TPU:0, one launch (start us, length us, event | category | flops | bytes accessed | tf_op | source)
XLA Modules:
  0.0 69.0 jit_solution(4005630705517406178)
XLA Ops:
  0.6 9.1 %shard_map.94 = (bf16[16,136,128]{2,1,0:T(8,128)(2,1)}, bf16[512,512]{1,0:T(8,128)(2,1)}) custom-call(bf16[512,512]{1,0:T(8,128)(2,1)} %bitcast.18, bf16[16,32,256]{2,1,0:T(8,128)(2,1)} %bitcast.19, bf16[5,5,32,64]{3,2,1,0:T(8,128)(2,1)} %bitcast.14), custom_call_target="tpu_custom_call" | custom-call | flops 2000000000 | bytes 1970176 | tf_op jit(solution)/shard_map/pallas_call | solution.py:58
  9.8 0.0 copy-start.5
  9.8 7.5 %all-to-all-start = ((bf16[16,136,128]{2,1,0:T(8,128)(2,1)}), bf16[16,136,128]{2,1,0:T(8,128)(2,1)S(1)}, u32[]{:S(2)}, u32[]{:S(2)}) async-start(bf16[16,136,128]{2,1,0:T(8,128)(2,1)} %get-tuple-element.13), calls=%async_computation | async-start | bytes 1114112 | tf_op jit(solution)/shard_map/all_to_all | solution.py:515
  17.3 0.0 copy-done.5
  17.3 0.1 slice.26
  17.4 2.9 %reverse.2 = f32[2,4,4096]{2,1,0:T(4,128)S(1)} reverse(f32[2,4,4096]{2,1,0:T(4,128)S(1)} %bitcast.16), dimensions={2} | reverse | bytes 262144
  20.3 0.1 slice.43
  20.5 0.6 slice-done
  21.0 0.1 fusion.2
  21.2 0.2 stack.10
  21.4 0.2 copy.14
  21.5 0.2 stack.9
  21.8 0.2 copy.13
  22.0 0.1 copy.15
  22.0 0.0 copy-start.3
  22.1 0.1 broadcast_in_dim.8
  22.2 0.0 copy-start.1
  22.2 0.0 copy-start.2
  22.2 0.2 reshape.53.resp_ref
  22.4 9.9 %all-to-all-done.cols_ref = bf16[16,136,128]{2,1,0:T(8,128)(2,1)S(1)} async-done(((bf16[16,136,128]{2,1,0:T(8,128)(2,1)}), bf16[16,136,128]{2,1,0:T(8,128)(2,1)S(1)}, u32[]{:S(2)}, u32[]{:S(2)}) %all-to-all-start) | async-done | bytes 557088 | tf_op jit(solution)/shard_map/all_to_all | solution.py:515
  32.3 0.0 copy-done.3
  32.3 0.0 copy-done.1
  32.3 0.0 copy-done.2
  32.3 4.5 %shard_map.95 = (bf16[16,72,128]{2,1,0:T(8,128)(2,1)}, f32[16,4,512]{2,1,0:T(4,128)S(1)}) custom-call(bf16[16,136,128]{2,1,0:T(8,128)(2,1)S(1)} %all-to-all-done.cols_ref, f32[2,256,256]{2,1,0:T(8,128)S(1)} %reshape.53.resp_ref, f32[2,16,256]{2,1,0:T(8,128)S(1)} %copy-done.3, bf16[512,512]{1,0:T(8,128)(2,1)S(1)} %copy-done.1, bf16[512,512]{1,0:T(8,128)(2,1)S(1)} %copy-done.2), custom_call_target="tpu_custom_call" | custom-call | flops 6000000000 | bytes 2588672 | tf_op jit(solution)/shard_map/pallas_call | solution.py:58
  36.8 4.2 %all-to-all-start.1 = ((bf16[16,72,128]{2,1,0:T(8,128)(2,1)}), bf16[16,72,128]{2,1,0:T(8,128)(2,1)S(1)}, u32[]{:S(2)}, u32[]{:S(2)}) async-start(bf16[16,72,128]{2,1,0:T(8,128)(2,1)} %get-tuple-element.14), calls=%async_computation.1 | async-start | bytes 589824 | tf_op jit(solution)/shard_map/all_to_all | solution.py:540
  41.1 1.7 %shard_map.96 = f32[2,4,16,256]{3,2,1,0:T(8,128)S(1)} custom-call(f32[16,4,512]{2,1,0:T(4,128)S(1)} %get-tuple-element.15.cross_ref), custom_call_target="tpu_custom_call" | custom-call | flops 1000000 | bytes 262144 | tf_op jit(solution)/shard_map/pallas_call | solution.py:58
  42.8 0.3 copy.16
  43.2 0.0 copy-start.4
  43.2 1.2 %reshape.54 = f32[2,4,4096]{2,1,0:T(4,128)} reshape(f32[2,4,256,16]{3,2,1,0:T(8,128)S(1)} %copy.16) | data formatting | bytes 262144 | tf_op jit(solution)/shard_map/reshape | solution.py:539
  44.4 7.2 %all-to-all-done.1.grad_ref = bf16[16,72,128]{2,1,0:T(8,128)(2,1)S(1)} async-done(((bf16[16,72,128]{2,1,0:T(8,128)(2,1)}), bf16[16,72,128]{2,1,0:T(8,128)(2,1)S(1)}, u32[]{:S(2)}, u32[]{:S(2)}) %all-to-all-start.1) | async-done | bytes 294944 | tf_op jit(solution)/shard_map/all_to_all | solution.py:540
  51.6 0.0 copy-done.4
  51.6 1.6 %shard_map.97 = (f32[416,128]{1,0:T(8,128)S(1)}, bf16[3,512,256]{2,1,0:T(8,128)(2,1)S(1)}) custom-call(bf16[16,72,128]{2,1,0:T(8,128)(2,1)S(1)} %all-to-all-done.1.grad_ref, bf16[512,512]{1,0:T(8,128)(2,1)S(1)} %copy-done.4), custom_call_target="tpu_custom_call" | custom-call | flops 1000000000 | bytes 1818624 | tf_op jit(solution)/shard_map/pallas_call | solution.py:58
  53.2 0.0 copy-start
  53.2 0.1 collective-permute-start
  53.3 1.3 %collective-permute-done = f32[208,128]{1,0:T(8,128)S(1)} collective-permute-done((f32[208,128]{1,0:T(8,128)S(1)}, f32[208,128]{1,0:T(8,128)S(1)}, u32[]{:S(2)}, u32[]{:S(2)}) %collective-permute-start) | collective-permute-done | bytes 106528 | tf_op jit(solution)/shard_map/ppermute | solution.py:450
  54.6 0.8 %collective-permute-start.3 = (bf16[208,128]{1,0:T(8,128)(2,1)S(1)}, bf16[208,128]{1,0:T(8,128)(2,1)S(1)}, u32[]{:S(2)}, u32[]{:S(2)}) collective-permute-start(bf16[208,128]{1,0:T(8,128)(2,1)S(1)} %add_convert_fusion), channel_id=1, source_target_pairs={{0,6},{1,7},{2,4},{3,5},{4,2},{5,3},{6,0},{7,1},{8,14},{9,15},{10,... | collective-permute-start | bytes 159752 | tf_op jit(solution)/shard_map/ppermute | solution.py:454
  55.5 1.0 %collective-permute-start.2 = (bf16[208,128]{1,0:T(8,128)(2,1)S(1)}, bf16[208,128]{1,0:T(8,128)(2,1)S(1)}, u32[]{:S(2)}, u32[]{:S(2)}) collective-permute-start(bf16[208,128]{1,0:T(8,128)(2,1)S(1)} %add_convert_fusion), channel_id=1, source_target_pairs={{0,4},{1,5},{2,6},{3,7},{4,0},{5,1},{6,2},{7,3},{8,12},{9,13},{10,... | collective-permute-start | bytes 159752 | tf_op jit(solution)/shard_map/ppermute | solution.py:454
  56.5 1.7 %collective-permute-start.1 = (bf16[208,128]{1,0:T(8,128)(2,1)S(1)}, bf16[208,128]{1,0:T(8,128)(2,1)S(1)}, u32[]{:S(2)}, u32[]{:S(2)}) collective-permute-start(bf16[208,128]{1,0:T(8,128)(2,1)S(1)} %add_convert_fusion), channel_id=1, source_target_pairs={{0,2},{1,3},{2,0},{3,1},{4,6},{5,7},{6,4},{7,5},{8,10},{9,11},{10,... | collective-permute-start | bytes 159752 | tf_op jit(solution)/shard_map/ppermute | solution.py:454
  58.2 0.0 copy-done
  58.2 2.8 %shard_map.98 = bf16[512,512]{1,0:T(8,128)(2,1)} custom-call(bf16[3,512,256]{2,1,0:T(8,128)(2,1)S(1)} %get-tuple-element.19.shifted_ref, bf16[5,5,32,64]{3,2,1,0:T(8,128)(2,1)S(1)} %bitcast.15), custom_call_target="tpu_custom_call" | custom-call | flops 2000000000 | bytes 1413120 | tf_op jit(solution)/shard_map/pallas_call | solution.py:58
  61.0 0.0 collective-permute-done.3
  61.0 0.0 collective-permute-done.2
  61.0 0.0 collective-permute-done.1
  61.0 1.3 %collective-permute-start.4 = (bf16[208,128]{1,0:T(8,128)(2,1)S(1)}, bf16[208,128]{1,0:T(8,128)(2,1)S(1)}, u32[]{:S(2)}, u32[]{:S(2)}) collective-permute-start(bf16[208,128]{1,0:T(8,128)(2,1)S(1)} %add_add_fusion), channel_id=1, source_target_pairs={{0,8},{1,9},{2,10},{3,11},{4,12},{5,13},{6,14},{7,15},{8,0},{9,1},... | collective-permute-start | bytes 159752 | tf_op jit(solution)/shard_map/ppermute | solution.py:454
  62.3 4.4 %collective-permute-done.4 = bf16[208,128]{1,0:T(8,128)(2,1)S(1)} collective-permute-done((bf16[208,128]{1,0:T(8,128)(2,1)S(1)}, bf16[208,128]{1,0:T(8,128)(2,1)S(1)}, u32[]{:S(2)}, u32[]{:S(2)}) %collective-permute-start.4) | collective-permute-done | bytes 53280 | tf_op jit(solution)/shard_map/ppermute | solution.py:454
  66.7 0.1 collective-permute-start.5
  66.8 1.3 %collective-permute-done.5 = f32[208,128]{1,0:T(8,128)S(1)} collective-permute-done((f32[208,128]{1,0:T(8,128)S(1)}, f32[208,128]{1,0:T(8,128)S(1)}, u32[]{:S(2)}, u32[]{:S(2)}) %collective-permute-start.5) | collective-permute-done | bytes 106528 | tf_op jit(solution)/shard_map/ppermute | solution.py:462
  68.1 0.9 %shard_map.99 = f32[5,5,32,64]{3,2,1,0:T(8,128)} custom-call(f32[416,128]{1,0:T(8,128)S(1)} %maximum_select_fusion.tap_ref), custom_call_target="tpu_custom_call" | custom-call | flops 1000000 | bytes 417792 | tf_op jit(solution)/shard_map/pallas_call | solution.py:58
  (7 shorter events, 0.1 us)
Async XLA Ops:
  9.8 7.6 %copy-start.5 = (f32[2,4,4096]{2,1,0:T(4,128)S(1)}, f32[2,4,4096]{2,1,0:T(4,128)}, u32[]{:S(2)}) copy-start(f32[2,4,4096]{2,1,0:T(4,128)} %param.9) | copy-start | bytes 393220
  9.8 22.6 %all-to-all-start = ((bf16[16,136,128]{2,1,0:T(8,128)(2,1)}), bf16[16,136,128]{2,1,0:T(8,128)(2,1)S(1)}, u32[]{:S(2)}, u32[]{:S(2)}) async-start(bf16[16,136,128]{2,1,0:T(8,128)(2,1)} %get-tuple-element.13), calls=%async_computation | async-start | bytes 1114112 | tf_op jit(solution)/shard_map/all_to_all | solution.py:515
  20.3 0.7 %slice-start = ((f32[2,4,4096]{2,1,0:T(4,128)}), f32[2,4,1]{2,1,0:T(4,128)S(1)}, s32[]{:S(2)}) async-start(f32[2,4,4096]{2,1,0:T(4,128)} %param.9), calls=%async_computation.2 | async-start | bytes 8192 | tf_op jit(solution)/shard_map/jit(_roll_static)/slice | solution.py:468
  22.0 10.3 %copy-start.3 = (f32[2,16,256]{2,1,0:T(8,128)S(1)}, f32[2,16,256]{2,1,0:T(8,128)}, u32[]{:S(2)}) copy-start(f32[2,16,256]{2,1,0:T(8,128)} %constant.31.clone.twist_ref) | copy-start | bytes 98308
  22.2 10.1 %copy-start.1 = (bf16[512,512]{1,0:T(8,128)(2,1)S(1)}, bf16[512,512]{1,0:T(8,128)(2,1)}, u32[]{:S(2)}) copy-start(bf16[512,512]{1,0:T(8,128)(2,1)} %constant.32.clone.high_ref) | copy-start | bytes 1572868
  22.2 10.1 %copy-start.2 = (bf16[512,512]{1,0:T(8,128)(2,1)S(1)}, bf16[512,512]{1,0:T(8,128)(2,1)}, u32[]{:S(2)}) copy-start(bf16[512,512]{1,0:T(8,128)(2,1)} %constant.33.clone.rest_ref) | copy-start | bytes 1572868
  36.8 14.8 %all-to-all-start.1 = ((bf16[16,72,128]{2,1,0:T(8,128)(2,1)}), bf16[16,72,128]{2,1,0:T(8,128)(2,1)S(1)}, u32[]{:S(2)}, u32[]{:S(2)}) async-start(bf16[16,72,128]{2,1,0:T(8,128)(2,1)} %get-tuple-element.14), calls=%async_computation.1 | async-start | bytes 589824 | tf_op jit(solution)/shard_map/all_to_all | solution.py:540
  43.2 8.5 %copy-start.4 = (bf16[512,512]{1,0:T(8,128)(2,1)S(1)}, bf16[512,512]{1,0:T(8,128)(2,1)}, u32[]{:S(2)}) copy-start(bf16[512,512]{1,0:T(8,128)(2,1)} %get-tuple-element.17.z_ref) | copy-start | bytes 1572868
  53.2 5.0 %copy-start = (bf16[5,5,64,32]{2,3,1,0:T(8,128)(2,1)S(1)}, bf16[5,5,64,32]{2,3,1,0:T(8,128)(2,1)}, u32[]{:S(2)}) copy-start(bf16[5,5,64,32]{2,3,1,0:T(8,128)(2,1)} %param.8) | copy-start | bytes 307204
  53.2 1.4 %collective-permute-start = (f32[208,128]{1,0:T(8,128)S(1)}, f32[208,128]{1,0:T(8,128)S(1)}, u32[]{:S(2)}, u32[]{:S(2)}) collective-permute-start(f32[208,128]{1,0:T(8,128)S(1)} %constant_dynamic-slice_fusion), channel_id=1, source_target_pairs={{0,1},{1,0},{2,3},{3,2},{4,5},{5,4},{6,7},{7,6},{8,9},{9,8},{10,11... | collective-permute-start | bytes 319496 | tf_op jit(solution)/shard_map/ppermute | solution.py:450
  54.6 6.3 %collective-permute-start.3 = (bf16[208,128]{1,0:T(8,128)(2,1)S(1)}, bf16[208,128]{1,0:T(8,128)(2,1)S(1)}, u32[]{:S(2)}, u32[]{:S(2)}) collective-permute-start(bf16[208,128]{1,0:T(8,128)(2,1)S(1)} %add_convert_fusion), channel_id=1, source_target_pairs={{0,6},{1,7},{2,4},{3,5},{4,2},{5,3},{6,0},{7,1},{8,14},{9,15},{10,... | collective-permute-start | bytes 159752 | tf_op jit(solution)/shard_map/ppermute | solution.py:454
  55.5 5.5 %collective-permute-start.2 = (bf16[208,128]{1,0:T(8,128)(2,1)S(1)}, bf16[208,128]{1,0:T(8,128)(2,1)S(1)}, u32[]{:S(2)}, u32[]{:S(2)}) collective-permute-start(bf16[208,128]{1,0:T(8,128)(2,1)S(1)} %add_convert_fusion), channel_id=1, source_target_pairs={{0,4},{1,5},{2,6},{3,7},{4,0},{5,1},{6,2},{7,3},{8,12},{9,13},{10,... | collective-permute-start | bytes 159752 | tf_op jit(solution)/shard_map/ppermute | solution.py:454
  56.5 4.5 %collective-permute-start.1 = (bf16[208,128]{1,0:T(8,128)(2,1)S(1)}, bf16[208,128]{1,0:T(8,128)(2,1)S(1)}, u32[]{:S(2)}, u32[]{:S(2)}) collective-permute-start(bf16[208,128]{1,0:T(8,128)(2,1)S(1)} %add_convert_fusion), channel_id=1, source_target_pairs={{0,2},{1,3},{2,0},{3,1},{4,6},{5,7},{6,4},{7,5},{8,10},{9,11},{10,... | collective-permute-start | bytes 159752 | tf_op jit(solution)/shard_map/ppermute | solution.py:454
  61.0 5.7 %collective-permute-start.4 = (bf16[208,128]{1,0:T(8,128)(2,1)S(1)}, bf16[208,128]{1,0:T(8,128)(2,1)S(1)}, u32[]{:S(2)}, u32[]{:S(2)}) collective-permute-start(bf16[208,128]{1,0:T(8,128)(2,1)S(1)} %add_add_fusion), channel_id=1, source_target_pairs={{0,8},{1,9},{2,10},{3,11},{4,12},{5,13},{6,14},{7,15},{8,0},{9,1},... | collective-permute-start | bytes 159752 | tf_op jit(solution)/shard_map/ppermute | solution.py:454
  66.7 1.4 %collective-permute-start.5 = (f32[208,128]{1,0:T(8,128)S(1)}, f32[208,128]{1,0:T(8,128)S(1)}, u32[]{:S(2)}, u32[]{:S(2)}) collective-permute-start(f32[208,128]{1,0:T(8,128)S(1)} %convert_add_fusion), channel_id=1, source_target_pairs={{0,1},{1,0},{2,3},{3,2},{4,5},{5,4},{6,7},{7,6},{8,9},{9,8},{10,11... | collective-permute-start | bytes 319496 | tf_op jit(solution)/shard_map/ppermute | solution.py:462

commit v5 on v4

--- a/solution.py
+++ b/solution.py
@@ -84,12 +84,14 @@
     cot_copies = [
         pltpu.make_async_copy(
             cot_hbm.at[:, :, pl.ds(lanes * b, lanes)],
-            out_hbm.at[:, pl.ds(conv_rows + rows * b, rows)],
-            sem.at[5 + b],
+            out_ref.at[:, pl.ds(conv_rows + rows * b, rows)],
+            sem.at[6 + b],
         )
         for b in range(tiles_wide)
     ]
     at_conv, at_edge = pl.ds(0, conv_rows), pl.ds(2 * conv_rows, edge_rows)
+    at_cot = pl.ds(conv_rows, conv_rows)
+    cot_out = pltpu.make_async_copy(out_ref.at[:, at_cot], out_hbm.at[:, at_cot], sem.at[5])
     z_out = pltpu.make_async_copy(z_ref, z_hbm, sem.at[2])
     conv_out = pltpu.make_async_copy(out_ref.at[:, at_conv], out_hbm.at[:, at_conv], sem.at[3])
     edge_out = pltpu.make_async_copy(out_ref.at[:, at_edge], out_hbm.at[:, at_edge], sem.at[4])
@@ -122,6 +124,9 @@
     z = dot(to_time, apart.astype(bf16)).astype(bf16)
     z_ref[...] = z
     z_out.start()
+    for copy in cot_copies:
+        copy.wait()
+    cot_out.start()
     even, odd = z[:, :half], z[:, half:]
     left = dot(w_ref[0], even) + dot(w_ref[1], odd)
     right = dot(w_ref[4], even)
@@ -157,8 +162,7 @@
         out_ref[d, 2 * conv_rows :, :rows] = edges[:, rows * d : rows * (d + 1)].astype(bf16)
     conv_out.start()
     edge_out.start()
-    for copy in cot_copies:
-        copy.wait()
+    cot_out.wait()
     z_out.wait()
     conv_out.wait()
     edge_out.wait()
@@ -504,7 +508,7 @@
             pltpu.VMEM(taps.shape, bf16),
             pltpu.VMEM((count, 2 * rows * tiles + edge_rows, lanes), bf16),
             pltpu.VMEM((k_in, fibre_in), bf16),
-            pltpu.SemaphoreType.DMA((5 + tiles,)),
+            pltpu.SemaphoreType.DMA((6 + tiles,)),
         ],
         2e9,
         (signal.reshape(k_in, fibre_in), cotangent.reshape(count, rows, width), taps),

time: 69.3 us -> 64.7 us (0.934)
  Pallas kernels: 20.5 us -> 15.9 us
    pallas_call x6, Pallas kernels: 20.5 us -> 15.9 us  [call(): pl.pallas_call(kernel, out_shape=outs, in_specs=[pl.BlockSpec(memory_spac...]
where the time goes in v5:
time: 64.7 us; the launch traced here: 64.4 us
  waiting for transfers between devices  24.1 us (37%)
  starting transfers between devices  16.8 us (26%)
  Pallas kernels  15.9 us (25%)
  local copies, waits for them, and re-layouts  6.45 us (10%)
  between operations  0.89 us (1%)
    pallas_call x6, Pallas kernels, call(): pl.pallas_call(kernel, out_shape=outs, in_specs=[pl.BlockSpec(memory_spac...  15.9 us
    all_to_all x1, waiting for transfers between devices, per_device(): lax.all_to_all(conv_part, 'fibre', split_axis=0, concat_axis=0, tiled=True)  9.91 us
    all_to_all x1, starting transfers between devices, per_device(): lax.all_to_all(conv_part, 'fibre', split_axis=0, concat_axis=0, tiled=True)  7.53 us
    all_to_all x1, waiting for transfers between devices, per_device(): lax.all_to_all(grad_part, 'fibre', split_axis=0, concat_axis=0, tiled=True)  7.23 us
    ppermute x4, starting transfers between devices, summed_over(): theirs = lambda step: lax.ppermute(rounded, axis, pairs(step)).astype(f32)  4.85 us
    ppermute x4, waiting for transfers between devices, summed_over(): theirs = lambda step: lax.ppermute(rounded, axis, pairs(step)).astype(f32)  4.38 us
    all_to_all x1, starting transfers between devices, per_device(): lax.all_to_all(grad_part, 'fibre', split_axis=0, concat_axis=0, tiled=True)  4.25 us
    unnamed x14, local copies, waits for them, and re-layouts  3.05 us
  transfers between devices with their start and end apart: 8, of which 5 were waited for; matrix products, arithmetic and copies ran while one was open for 9% of the time, Pallas kernels for 7%

profile of v5, /device:TPU:0, one launch (start us, length us, event | category | flops | bytes accessed | tf_op | source)
XLA Modules:
  0.0 64.4 jit_solution(18278456433390305029)
XLA Ops:
  0.6 4.5 %shard_map.94 = (bf16[16,136,128]{2,1,0:T(8,128)(2,1)}, bf16[512,512]{1,0:T(8,128)(2,1)}) custom-call(bf16[512,512]{1,0:T(8,128)(2,1)} %bitcast.18, bf16[16,32,256]{2,1,0:T(8,128)(2,1)} %bitcast.19, bf16[5,5,32,64]{3,2,1,0:T(8,128)(2,1)} %bitcast.14), custom_call_target="tpu_custom_call" | custom-call | flops 2000000000 | bytes 1970176 | tf_op jit(solution)/shard_map/pallas_call | solution.py:58
  5.2 0.0 copy-start.5
  5.2 7.5 %all-to-all-start = ((bf16[16,136,128]{2,1,0:T(8,128)(2,1)}), bf16[16,136,128]{2,1,0:T(8,128)(2,1)S(1)}, u32[]{:S(2)}, u32[]{:S(2)}) async-start(bf16[16,136,128]{2,1,0:T(8,128)(2,1)} %get-tuple-element.13), calls=%async_computation | async-start | bytes 1114112 | tf_op jit(solution)/shard_map/all_to_all | solution.py:519
  12.7 0.0 copy-done.5
  12.7 0.1 slice.26
  12.8 2.9 %reverse.2 = f32[2,4,4096]{2,1,0:T(4,128)S(1)} reverse(f32[2,4,4096]{2,1,0:T(4,128)S(1)} %bitcast.16), dimensions={2} | reverse | bytes 262144
  15.7 0.1 slice.43
  15.9 0.6 slice-done
  16.4 0.1 fusion.2
  16.6 0.2 stack.10
  16.8 0.2 copy.14
  16.9 0.2 stack.9
  17.2 0.2 copy.13
  17.3 0.1 copy.15
  17.4 0.0 copy-start.3
  17.5 0.1 broadcast_in_dim.8
  17.6 0.0 copy-start.1
  17.6 0.0 copy-start.2
  17.6 0.2 reshape.53.resp_ref
  17.8 9.9 %all-to-all-done.cols_ref = bf16[16,136,128]{2,1,0:T(8,128)(2,1)S(1)} async-done(((bf16[16,136,128]{2,1,0:T(8,128)(2,1)}), bf16[16,136,128]{2,1,0:T(8,128)(2,1)S(1)}, u32[]{:S(2)}, u32[]{:S(2)}) %all-to-all-start) | async-done | bytes 557088 | tf_op jit(solution)/shard_map/all_to_all | solution.py:519
  27.7 0.0 copy-done.3
  27.7 0.0 copy-done.1
  27.7 0.0 copy-done.2
  27.7 4.5 %shard_map.95 = (bf16[16,72,128]{2,1,0:T(8,128)(2,1)}, f32[16,4,512]{2,1,0:T(4,128)S(1)}) custom-call(bf16[16,136,128]{2,1,0:T(8,128)(2,1)S(1)} %all-to-all-done.cols_ref, f32[2,256,256]{2,1,0:T(8,128)S(1)} %reshape.53.resp_ref, f32[2,16,256]{2,1,0:T(8,128)S(1)} %copy-done.3, bf16[512,512]{1,0:T(8,128)(2,1)S(1)} %copy-done.1, bf16[512,512]{1,0:T(8,128)(2,1)S(1)} %copy-done.2), custom_call_target="tpu_custom_call" | custom-call | flops 6000000000 | bytes 2588672 | tf_op jit(solution)/shard_map/pallas_call | solution.py:58
  32.2 4.2 %all-to-all-start.1 = ((bf16[16,72,128]{2,1,0:T(8,128)(2,1)}), bf16[16,72,128]{2,1,0:T(8,128)(2,1)S(1)}, u32[]{:S(2)}, u32[]{:S(2)}) async-start(bf16[16,72,128]{2,1,0:T(8,128)(2,1)} %get-tuple-element.14), calls=%async_computation.1 | async-start | bytes 589824 | tf_op jit(solution)/shard_map/all_to_all | solution.py:544
  36.5 1.7 %shard_map.96 = f32[2,4,16,256]{3,2,1,0:T(8,128)S(1)} custom-call(f32[16,4,512]{2,1,0:T(4,128)S(1)} %get-tuple-element.15.cross_ref), custom_call_target="tpu_custom_call" | custom-call | flops 1000000 | bytes 262144 | tf_op jit(solution)/shard_map/pallas_call | solution.py:58
  38.2 0.3 copy.16
  38.6 0.0 copy-start.4
  38.6 1.2 %reshape.54 = f32[2,4,4096]{2,1,0:T(4,128)} reshape(f32[2,4,256,16]{3,2,1,0:T(8,128)S(1)} %copy.16) | data formatting | bytes 262144 | tf_op jit(solution)/shard_map/reshape | solution.py:543
  39.8 7.2 %all-to-all-done.1.grad_ref = bf16[16,72,128]{2,1,0:T(8,128)(2,1)S(1)} async-done(((bf16[16,72,128]{2,1,0:T(8,128)(2,1)}), bf16[16,72,128]{2,1,0:T(8,128)(2,1)S(1)}, u32[]{:S(2)}, u32[]{:S(2)}) %all-to-all-start.1) | async-done | bytes 294944 | tf_op jit(solution)/shard_map/all_to_all | solution.py:544
  47.0 0.0 copy-done.4
  47.0 1.6 %shard_map.97 = (f32[416,128]{1,0:T(8,128)S(1)}, bf16[3,512,256]{2,1,0:T(8,128)(2,1)S(1)}) custom-call(bf16[16,72,128]{2,1,0:T(8,128)(2,1)S(1)} %all-to-all-done.1.grad_ref, bf16[512,512]{1,0:T(8,128)(2,1)S(1)} %copy-done.4), custom_call_target="tpu_custom_call" | custom-call | flops 1000000000 | bytes 1818624 | tf_op jit(solution)/shard_map/pallas_call | solution.py:58
  48.6 0.0 copy-start
  48.6 0.1 collective-permute-start
  48.7 1.3 %collective-permute-done = f32[208,128]{1,0:T(8,128)S(1)} collective-permute-done((f32[208,128]{1,0:T(8,128)S(1)}, f32[208,128]{1,0:T(8,128)S(1)}, u32[]{:S(2)}, u32[]{:S(2)}) %collective-permute-start) | collective-permute-done | bytes 106528 | tf_op jit(solution)/shard_map/ppermute | solution.py:454
  50.0 0.8 %collective-permute-start.3 = (bf16[208,128]{1,0:T(8,128)(2,1)S(1)}, bf16[208,128]{1,0:T(8,128)(2,1)S(1)}, u32[]{:S(2)}, u32[]{:S(2)}) collective-permute-start(bf16[208,128]{1,0:T(8,128)(2,1)S(1)} %add_convert_fusion), channel_id=1, source_target_pairs={{0,6},{1,7},{2,4},{3,5},{4,2},{5,3},{6,0},{7,1},{8,14},{9,15},{10,... | collective-permute-start | bytes 159752 | tf_op jit(solution)/shard_map/ppermute | solution.py:458
  50.8 1.0 %collective-permute-start.2 = (bf16[208,128]{1,0:T(8,128)(2,1)S(1)}, bf16[208,128]{1,0:T(8,128)(2,1)S(1)}, u32[]{:S(2)}, u32[]{:S(2)}) collective-permute-start(bf16[208,128]{1,0:T(8,128)(2,1)S(1)} %add_convert_fusion), channel_id=1, source_target_pairs={{0,4},{1,5},{2,6},{3,7},{4,0},{5,1},{6,2},{7,3},{8,12},{9,13},{10,... | collective-permute-start | bytes 159752 | tf_op jit(solution)/shard_map/ppermute | solution.py:458
  51.9 1.7 %collective-permute-start.1 = (bf16[208,128]{1,0:T(8,128)(2,1)S(1)}, bf16[208,128]{1,0:T(8,128)(2,1)S(1)}, u32[]{:S(2)}, u32[]{:S(2)}) collective-permute-start(bf16[208,128]{1,0:T(8,128)(2,1)S(1)} %add_convert_fusion), channel_id=1, source_target_pairs={{0,2},{1,3},{2,0},{3,1},{4,6},{5,7},{6,4},{7,5},{8,10},{9,11},{10,... | collective-permute-start | bytes 159752 | tf_op jit(solution)/shard_map/ppermute | solution.py:458
  53.6 0.0 copy-done
  53.6 2.8 %shard_map.98 = bf16[512,512]{1,0:T(8,128)(2,1)} custom-call(bf16[3,512,256]{2,1,0:T(8,128)(2,1)S(1)} %get-tuple-element.19.shifted_ref, bf16[5,5,32,64]{3,2,1,0:T(8,128)(2,1)S(1)} %bitcast.15), custom_call_target="tpu_custom_call" | custom-call | flops 2000000000 | bytes 1413120 | tf_op jit(solution)/shard_map/pallas_call | solution.py:58
  56.3 0.0 collective-permute-done.3
  56.4 0.0 collective-permute-done.2
  56.4 0.0 collective-permute-done.1
  56.4 1.3 %collective-permute-start.4 = (bf16[208,128]{1,0:T(8,128)(2,1)S(1)}, bf16[208,128]{1,0:T(8,128)(2,1)S(1)}, u32[]{:S(2)}, u32[]{:S(2)}) collective-permute-start(bf16[208,128]{1,0:T(8,128)(2,1)S(1)} %add_add_fusion), channel_id=1, source_target_pairs={{0,8},{1,9},{2,10},{3,11},{4,12},{5,13},{6,14},{7,15},{8,0},{9,1},... | collective-permute-start | bytes 159752 | tf_op jit(solution)/shard_map/ppermute | solution.py:458
  57.7 4.4 %collective-permute-done.4 = bf16[208,128]{1,0:T(8,128)(2,1)S(1)} collective-permute-done((bf16[208,128]{1,0:T(8,128)(2,1)S(1)}, bf16[208,128]{1,0:T(8,128)(2,1)S(1)}, u32[]{:S(2)}, u32[]{:S(2)}) %collective-permute-start.4) | collective-permute-done | bytes 53280 | tf_op jit(solution)/shard_map/ppermute | solution.py:458
  62.1 0.1 collective-permute-start.5
  62.2 1.3 %collective-permute-done.5 = f32[208,128]{1,0:T(8,128)S(1)} collective-permute-done((f32[208,128]{1,0:T(8,128)S(1)}, f32[208,128]{1,0:T(8,128)S(1)}, u32[]{:S(2)}, u32[]{:S(2)}) %collective-permute-start.5) | collective-permute-done | bytes 106528 | tf_op jit(solution)/shard_map/ppermute | solution.py:466
  63.5 0.9 %shard_map.99 = f32[5,5,32,64]{3,2,1,0:T(8,128)} custom-call(f32[416,128]{1,0:T(8,128)S(1)} %maximum_select_fusion.tap_ref), custom_call_target="tpu_custom_call" | custom-call | flops 1000000 | bytes 417792 | tf_op jit(solution)/shard_map/pallas_call | solution.py:58
  (7 shorter events, 0.1 us)
Async XLA Ops:
  5.2 7.5 %copy-start.5 = (f32[2,4,4096]{2,1,0:T(4,128)S(1)}, f32[2,4,4096]{2,1,0:T(4,128)}, u32[]{:S(2)}) copy-start(f32[2,4,4096]{2,1,0:T(4,128)} %param.9) | copy-start | bytes 393220
  5.2 22.6 %all-to-all-start = ((bf16[16,136,128]{2,1,0:T(8,128)(2,1)}), bf16[16,136,128]{2,1,0:T(8,128)(2,1)S(1)}, u32[]{:S(2)}, u32[]{:S(2)}) async-start(bf16[16,136,128]{2,1,0:T(8,128)(2,1)} %get-tuple-element.13), calls=%async_computation | async-start | bytes 1114112 | tf_op jit(solution)/shard_map/all_to_all | solution.py:519
  15.7 0.7 %slice-start = ((f32[2,4,4096]{2,1,0:T(4,128)}), f32[2,4,1]{2,1,0:T(4,128)S(1)}, s32[]{:S(2)}) async-start(f32[2,4,4096]{2,1,0:T(4,128)} %param.9), calls=%async_computation.2 | async-start | bytes 8192 | tf_op jit(solution)/shard_map/jit(_roll_static)/slice | solution.py:472
  17.4 10.3 %copy-start.3 = (f32[2,16,256]{2,1,0:T(8,128)S(1)}, f32[2,16,256]{2,1,0:T(8,128)}, u32[]{:S(2)}) copy-start(f32[2,16,256]{2,1,0:T(8,128)} %constant.31.clone.twist_ref) | copy-start | bytes 98308
  17.6 10.1 %copy-start.1 = (bf16[512,512]{1,0:T(8,128)(2,1)S(1)}, bf16[512,512]{1,0:T(8,128)(2,1)}, u32[]{:S(2)}) copy-start(bf16[512,512]{1,0:T(8,128)(2,1)} %constant.32.clone.high_ref) | copy-start | bytes 1572868
  17.6 10.1 %copy-start.2 = (bf16[512,512]{1,0:T(8,128)(2,1)S(1)}, bf16[512,512]{1,0:T(8,128)(2,1)}, u32[]{:S(2)}) copy-start(bf16[512,512]{1,0:T(8,128)(2,1)} %constant.33.clone.rest_ref) | copy-start | bytes 1572868
  32.2 14.8 %all-to-all-start.1 = ((bf16[16,72,128]{2,1,0:T(8,128)(2,1)}), bf16[16,72,128]{2,1,0:T(8,128)(2,1)S(1)}, u32[]{:S(2)}, u32[]{:S(2)}) async-start(bf16[16,72,128]{2,1,0:T(8,128)(2,1)} %get-tuple-element.14), calls=%async_computation.1 | async-start | bytes 589824 | tf_op jit(solution)/shard_map/all_to_all | solution.py:544
  38.6 8.5 %copy-start.4 = (bf16[512,512]{1,0:T(8,128)(2,1)S(1)}, bf16[512,512]{1,0:T(8,128)(2,1)}, u32[]{:S(2)}) copy-start(bf16[512,512]{1,0:T(8,128)(2,1)} %get-tuple-element.17.z_ref) | copy-start | bytes 1572868
  48.6 5.0 %copy-start = (bf16[5,5,64,32]{2,3,1,0:T(8,128)(2,1)S(1)}, bf16[5,5,64,32]{2,3,1,0:T(8,128)(2,1)}, u32[]{:S(2)}) copy-start(bf16[5,5,64,32]{2,3,1,0:T(8,128)(2,1)} %param.8) | copy-start | bytes 307204
  48.6 1.4 %collective-permute-start = (f32[208,128]{1,0:T(8,128)S(1)}, f32[208,128]{1,0:T(8,128)S(1)}, u32[]{:S(2)}, u32[]{:S(2)}) collective-permute-start(f32[208,128]{1,0:T(8,128)S(1)} %constant_dynamic-slice_fusion), channel_id=1, source_target_pairs={{0,1},{1,0},{2,3},{3,2},{4,5},{5,4},{6,7},{7,6},{8,9},{9,8},{10,11... | collective-permute-start | bytes 319496 | tf_op jit(solution)/shard_map/ppermute | solution.py:454
  50.0 6.3 %collective-permute-start.3 = (bf16[208,128]{1,0:T(8,128)(2,1)S(1)}, bf16[208,128]{1,0:T(8,128)(2,1)S(1)}, u32[]{:S(2)}, u32[]{:S(2)}) collective-permute-start(bf16[208,128]{1,0:T(8,128)(2,1)S(1)} %add_convert_fusion), channel_id=1, source_target_pairs={{0,6},{1,7},{2,4},{3,5},{4,2},{5,3},{6,0},{7,1},{8,14},{9,15},{10,... | collective-permute-start | bytes 159752 | tf_op jit(solution)/shard_map/ppermute | solution.py:458
  50.8 5.5 %collective-permute-start.2 = (bf16[208,128]{1,0:T(8,128)(2,1)S(1)}, bf16[208,128]{1,0:T(8,128)(2,1)S(1)}, u32[]{:S(2)}, u32[]{:S(2)}) collective-permute-start(bf16[208,128]{1,0:T(8,128)(2,1)S(1)} %add_convert_fusion), channel_id=1, source_target_pairs={{0,4},{1,5},{2,6},{3,7},{4,0},{5,1},{6,2},{7,3},{8,12},{9,13},{10,... | collective-permute-start | bytes 159752 | tf_op jit(solution)/shard_map/ppermute | solution.py:458
  51.9 4.5 %collective-permute-start.1 = (bf16[208,128]{1,0:T(8,128)(2,1)S(1)}, bf16[208,128]{1,0:T(8,128)(2,1)S(1)}, u32[]{:S(2)}, u32[]{:S(2)}) collective-permute-start(bf16[208,128]{1,0:T(8,128)(2,1)S(1)} %add_convert_fusion), channel_id=1, source_target_pairs={{0,2},{1,3},{2,0},{3,1},{4,6},{5,7},{6,4},{7,5},{8,10},{9,11},{10,... | collective-permute-start | bytes 159752 | tf_op jit(solution)/shard_map/ppermute | solution.py:458
  56.4 5.7 %collective-permute-start.4 = (bf16[208,128]{1,0:T(8,128)(2,1)S(1)}, bf16[208,128]{1,0:T(8,128)(2,1)S(1)}, u32[]{:S(2)}, u32[]{:S(2)}) collective-permute-start(bf16[208,128]{1,0:T(8,128)(2,1)S(1)} %add_add_fusion), channel_id=1, source_target_pairs={{0,8},{1,9},{2,10},{3,11},{4,12},{5,13},{6,14},{7,15},{8,0},{9,1},... | collective-permute-start | bytes 159752 | tf_op jit(solution)/shard_map/ppermute | solution.py:458
  62.1 1.4 %collective-permute-start.5 = (f32[208,128]{1,0:T(8,128)S(1)}, f32[208,128]{1,0:T(8,128)S(1)}, u32[]{:S(2)}, u32[]{:S(2)}) collective-permute-start(f32[208,128]{1,0:T(8,128)S(1)} %convert_add_fusion), channel_id=1, source_target_pairs={{0,1},{1,0},{2,3},{3,2},{4,5},{5,4},{6,7},{7,6},{8,9},{9,8},{10,11... | collective-permute-start | bytes 319496 | tf_op jit(solution)/shard_map/ppermute | solution.py:466

commit v6 on v5

--- a/solution.py
+++ b/solution.py
@@ -15,7 +15,7 @@
 inv_root_tau = 1.0 / math.sqrt(2.0 * math.pi)
 lanes = 128
 edge_rows = 8
-tap_rows = 416
+cores = 2
 
 
 def dot(a, b):
@@ -53,13 +53,16 @@
     return (iota(shape, 0) == row_of_column(iota((1, shape[1]), 1))).astype(f32).astype(bf16)
 
 
-def call(kernel, outs, scratch, flops, args, left=(), left_out=(), room=48):
+def call(kernel, outs, scratch, flops, args, left=(), left_out=(), small=(), room=48):
     moved = sum(a.size * a.dtype.itemsize for a in list(args) + list(outs))
     return pl.pallas_call(
         kernel,
         out_shape=outs,
         in_specs=[
-            pl.BlockSpec(memory_space=pltpu.HBM if a in left else pltpu.VMEM) for a in range(len(args))
+            pl.BlockSpec(
+                memory_space=pltpu.HBM if a in left else pltpu.SMEM if a in small else pltpu.VMEM
+            )
+            for a in range(len(args))
         ],
         out_specs=[
             pl.BlockSpec(memory_space=pltpu.HBM if a in left_out else pltpu.VMEM) for a in range(len(outs))
@@ -310,17 +313,19 @@
                 x_ref[d, 2 * r + tout * g : 2 * r + tout * (g + 1), h : h + lanes] = tile
     last = ((iota((edge_rows, lanes), 0) == 0) & (iota((edge_rows, lanes), 1) == lanes - 1)).astype(f32).astype(bf16)
     first = ((iota((edge_rows, lanes), 0) == 1) & (iota((edge_rows, lanes), 1) == 0)).astype(f32).astype(bf16)
-    for d in range(count):
-        for b in range(width // lanes):
-            out_ref[d, rows * b : rows * (b + 1)] = x_ref[d, :, lanes * b : lanes * (b + 1)].astype(bf16)
-        low = rows * (width // lanes)
-        out_ref[d, low:] = jnp.zeros((edge_rows, lanes), bf16)
+    for chip in range(count // cores):
+        at = 0
+        for d in range(cores * chip, cores * (chip + 1)):
+            for b in range(0, width, lanes):
+                out_ref[chip, at : at + rows] = x_ref[d, :, b : b + lanes].astype(bf16)
+                at += rows
+        out_ref[chip, at:] = jnp.zeros((edge_rows, lanes), bf16)
         edge = none
-        if d > 0:
-            edge = edge + dot_nt(last, x_ref[d - 1, :, width - lanes :].astype(bf16))
-        if d < count - 1:
-            edge = edge + dot_nt(first, x_ref[d + 1, :, :lanes].astype(bf16))
-        out_ref[d, low:, :rows] = edge.astype(bf16)
+        if chip > 0:
+            edge = edge + dot_nt(last, x_ref[cores * chip - 1, :, width - lanes :].astype(bf16))
+        if chip < count // cores - 1:
+            edge = edge + dot_nt(first, x_ref[cores * (chip + 1), :, :lanes].astype(bf16))
+        out_ref[chip, at:, :rows] = edge.astype(bf16)
 
 
 def hermitian_kernel(cross_ref, out_ref):
@@ -346,74 +351,100 @@
         out_ref[1, :, k] = 0.5 * (own[:, width:] - moved(other[:, width:], by))
 
 
-def tap_kernel(dims, grad_ref, z_ref, tap_ref, shifted_ref, g_ref, zp_ref):
+def gather_kernel(core_ref, own_ref, other_ref, out_ref):
+    k_in, wide = own_ref.shape
+    width = wide // 2
+    pad = (out_ref.shape[0] - k_in) // 2
+    core = core_ref[0]
+    out_ref[:pad] = jnp.zeros((pad, cores * wide), bf16)
+    out_ref[pad + k_in :] = jnp.zeros((pad, cores * wide), bf16)
+    for phase in range(2):
+        at = slice(width * phase, width * (phase + 1))
+        own_at = pl.multiple_of(wide * phase + width * core, lanes)
+        other_at = pl.multiple_of(wide * phase + width * (1 - core), lanes)
+        out_ref[pad : pad + k_in, pl.ds(own_at, width)] = own_ref[:, at]
+        out_ref[pad : pad + k_in, pl.ds(other_at, width)] = other_ref[:, at]
+
+
+def tap_kernel(dims, core_ref, grad_ref, z_ref, tap_ref, keep_ref, send_ref, g_ref, shifted_ref):
     cin, tin, cout, tout, ks, count, rows = dims
-    half = zp_ref.shape[1] // 2
-    k_out = cout * tout
-    row, col = iota((edge_rows, lanes), 0), iota((edge_rows, lanes), 1)
-    spread = (((row == 1) & (col == 0)) | ((row == 0) & (col == 1))).astype(f32).astype(bf16)
-    for d in range(count):
-        at = slice(rows * d, rows * (d + 1))
-        for b in range(half // lanes):
-            g_ref[at, lanes * b : lanes * (b + 1)] = grad_ref[d, rows * b : rows * (b + 1)].astype(f32)
-        g_ref[at, half:] = dot_tn(grad_ref[d, rows * (half // lanes) :, :rows], spread)
-    to_time = one_hot((k_out, k_out), lambda r: swapped(r, tout, cout))
-    g = dot(to_time, g_ref[...].astype(bf16)).astype(bf16)
-    wide = half + lanes
-    later = one_hot_columns((wide, half), lambda n: n + 1)
-    sooner = one_hot_columns((wide, half), lambda n: jnp.where(n == 0, half + 1, n - 1))
-    shifted_ref[0] = dot(g, later).astype(bf16)
-    shifted_ref[1] = g[:, :half]
-    shifted_ref[2] = dot(g, sooner).astype(bf16)
-    k_in = cin * tin
-    pad = 2 * cin
-    zp_ref[:pad] = jnp.zeros((pad, 2 * half), bf16)
-    zp_ref[pad + k_in :] = jnp.zeros((zp_ref.shape[0] - pad - k_in, 2 * half), bf16)
-    zp_ref[pad : pad + k_in] = z_ref[...]
-    both, lone = None, None
+    some = cout // cores
+    width = keep_ref.shape[2]
+    wide = cores * width
+    core = core_ref[0]
+    row, col = iota((edge_rows, 2 * lanes), 0), iota((edge_rows, 2 * lanes), 1)
+    spread = (((row == 0) & (col == lanes - 1)) | ((row == 1) & (col == lanes))).astype(f32).astype(bf16)
+    for chip in range(count // cores):
+        at = slice(rows * chip, rows * (chip + 1))
+        low = 0
+        for b in range(0, wide, lanes):
+            g_ref[at, lanes + b : 2 * lanes + b] = grad_ref[chip, low : low + rows].astype(f32)
+            low += rows
+        edge = dot_tn(grad_ref[chip, low:, :rows], spread)
+        g_ref[at, :lanes] = edge[:, :lanes]
+        g_ref[at, lanes + wide :] = edge[:, lanes:]
+    to_time = one_hot((some * tout, some * tout), lambda r: swapped(r, tout, some))
+    g = dot(to_time, g_ref[...].astype(bf16))
+    inside = slice(lanes, lanes + wide)
+    shifted_ref[0] = pltpu.roll(g, wide + 2 * lanes - 1, 1)[:, inside].astype(bf16)
+    shifted_ref[1] = g[:, inside].astype(bf16)
+    shifted_ref[2] = pltpu.roll(g, 1, 1)[:, inside].astype(bf16)
+    for shift in range(3):
+        keep_ref[shift] = shifted_ref[shift, :, pl.ds(pl.multiple_of(width * core, lanes), width)]
+        send_ref[shift] = shifted_ref[shift, :, pl.ds(pl.multiple_of(width * (1 - core), lanes), width)]
+    blank = jnp.zeros((lanes - 3 * some, wide), bf16)
+    total = None
     for t in range(tout):
-        at = slice(cout * t, cout * (t + 1))
-        band = zp_ref[2 * cin * t : 2 * cin * t + ks * cin]
-        pair = jnp.concatenate([shifted_ref[0, at], shifted_ref[1, at]], axis=0)
-        even, odd = band[:, :half], band[:, half:]
-        term = jnp.concatenate([dot_nt(even, pair), dot_nt(odd, pair)], axis=0)
-        both = term if both is None else both + term
-        blank = jnp.zeros((cout, half), bf16)
-        mid = ks * cin // 2
-        term = dot_nt(even[:mid], jnp.concatenate([shifted_ref[2, at], blank], axis=0)) + dot_nt(
-            even[mid:], jnp.concatenate([blank, shifted_ref[2, at]], axis=0)
-        )
-        lone = term if lone is None else lone + term
-    top = both.shape[0]
-    tap_ref[:top] = both
-    tap_ref[top : top + lone.shape[0]] = lone
-    tap_ref[top + lone.shape[0] :] = jnp.zeros((tap_ref.shape[0] - top - lone.shape[0], lanes), f32)
-
-
-def input_kernel(dims, shifted_ref, taps_ref, out_ref, w_ref):
+        at = slice(some * t, some * (t + 1))
+        band = slice(2 * cin * t, 2 * cin * t + ks * cin)
+        taken = jnp.concatenate([shifted_ref[shift, at] for shift in range(3)] + [blank], axis=0)
+        samples = jnp.concatenate([z_ref[band, :wide], z_ref[band, wide:]], axis=0)
+        term = dot_nt(samples, taken)
+        total = term if total is None else total + term
+    size = ks * cin
+    even, odd = total[:size], total[size:]
+    tap_ref[:size] = jnp.where(iota((size, lanes), 1) < 3 * some, even, pltpu.roll(odd, 3 * some, 1))
+    fold = size * some // lanes
+    folded = jnp.zeros((fold, lanes), f32)
+    for part in range(lanes // some):
+        moved = pltpu.roll(odd[fold * part : fold * (part + 1)], (some * (part - 1)) % lanes, 1)
+        here = split_index(iota((fold, lanes), 1), some)[0] == part
+        folded = jnp.where(here, moved, folded)
+    tap_ref[size:] = folded
+
+
+def input_kernel(dims, core_ref, own_ref, other_ref, taps_ref, out_ref, w_ref):
     cin, tin, cout, tout, ks, count, rows = dims
     k_in = cin * tin
-    half = shifted_ref.shape[2]
+    half = own_ref.shape[2]
+    some, channels = cout // cores, cout // count
+    steps = lanes // some
+    kinds = ks + 2 * (steps - 1)
     blank = jnp.zeros((cin, cout), bf16)
-    firsts, seconds = [], []
-    for j in range(ks):
-        for i in range(ks + 2):
-            firsts.append(taps_ref[i, j] if i < ks else blank)
-            seconds.append(taps_ref[i - 2, j] if i >= 2 else blank)
-    to_first = one_hot((cout, lanes), lambda r: r)
-    to_second = one_hot((cout, lanes), lambda r: r + cout)
-    tiles = (
-        dot(jnp.concatenate(firsts, axis=0), to_first) + dot(jnp.concatenate(seconds, axis=0), to_second)
-    ).astype(bf16)
-    empty = jnp.zeros((cin, lanes), bf16)
-    for j in range(ks):
-        for s in range(tin):
-            for q in range(cout * tout // lanes):
-                i = s - 4 * q + 2
-                at = (j * (ks + 2) + i) * cin
-                tile = tiles[at : at + cin] if 0 <= i < ks + 2 else empty
-                w_ref[j, cin * s : cin * (s + 1), lanes * q : lanes * (q + 1)] = tile
-    later, same, sooner = shifted_ref[0], shifted_ref[1], shifted_ref[2]
+    core = core_ref[0]
+    o, lane = iota((cout, lanes), 0), iota((cout, lanes), 1)
+    device, channel = split_index(o, channels)
+    chip, core_of = split_index(device, cores)
+    for part in range(cores):
+        wanted = core if part == 0 else 1 - core
+        tiles = None
+        for step in range(steps):
+            picked = [taps_ref[i - 2 * step, j] if 0 <= i - 2 * step < ks else blank
+                      for j in range(ks) for i in range(kinds)]
+            place = (core_of == wanted) & (lane == some * step + chip * channels + channel)
+            term = dot(jnp.concatenate(picked, axis=0), place.astype(f32).astype(bf16))
+            tiles = term if tiles is None else tiles + term
+        tiles = tiles.astype(bf16)
+        empty = jnp.zeros((cin, lanes), bf16)
+        for j in range(ks):
+            for s in range(tin):
+                for q in range(some * tout // lanes):
+                    i = s - 2 * steps * q + 2
+                    at = (j * kinds + i) * cin
+                    tile = tiles[at : at + cin] if 0 <= i < kinds else empty
+                    low = some * tout * part + lanes * q
+                    w_ref[j, cin * s : cin * (s + 1), low : low + lanes] = tile
+    later, same, sooner = (jnp.concatenate([own_ref[k], other_ref[k]], axis=0) for k in range(3))
     even = dot(w_ref[0], later) + dot(w_ref[2], same) + dot(w_ref[4], sooner)
     odd = dot(w_ref[1], later) + dot(w_ref[3], same)
     both = jnp.concatenate([even.astype(bf16), odd.astype(bf16)], axis=1)
@@ -429,43 +460,44 @@
 
 def unpack_kernel(dims, scale, tap_ref, out_ref):
     cin, tin, cout, tout, ks, count, rows = dims
-    band = ks * cin
-    for i in range(ks):
-        at = slice(cin * i, cin * (i + 1))
-        even, odd = tap_ref[at] * scale, tap_ref[band + cin * i : band + cin * (i + 1)] * scale
-        out_ref[i, 0] = even[:, :cout]
-        out_ref[i, 2] = even[:, cout:]
-        out_ref[i, 1] = odd[:, :cout]
-        out_ref[i, 3] = odd[:, cout:]
-        for c in range(0, cin, 8):
-            at = cin * i + c
-            low = at < band // 2
-            packed = tap_ref[2 * band + at % (band // 2) : 2 * band + at % (band // 2) + 8] * scale
-            out_ref[i, 4, c : c + 8] = packed[:, :cout] if low else packed[:, cout:]
-
-
-def summed_over(rows, axis, beside):
+    some, channels = cout // cores, cout // count
+    size, folds = ks * cin, lanes // some
+    fold = size // folds
+    packed = size + fold
+    both = jnp.concatenate([tap_ref[:packed], tap_ref[packed:]], axis=1)
+
+    wide = cores * lanes
+    source, target = iota((wide, folds * cout), 0), iota((wide, folds * cout), 1)
+    slot, o = split_index(target, cout)
+    device, channel = split_index(o, channels)
+    chip, core_of = split_index(device, cores)
+    place = (source == core_of * lanes + slot * some + chip * channels + channel).astype(f32).astype(bf16)
+    total, rest = None, both
+    for _ in range(3):
+        part = rest.astype(bf16)
+        rest = rest - part.astype(f32)
+        term = dot(part, place)
+        total = term if total is None else total + term
+    total = total * scale
+    for slot, j in enumerate((0, 2, 4, 1)):
+        for i in range(ks):
+            out_ref[i, j] = total[cin * i : cin * (i + 1), cout * slot : cout * (slot + 1)]
+    for at in range(0, size, 8):
+        slot, low = at // fold, size + at % fold
+        out_ref[at // cin, 3, at % cin : at % cin + 8] = total[low : low + 8, cout * slot : cout * (slot + 1)]
+
+
+def summed_over_chips(rows, axis, steps):
     count = lax.axis_size(axis)
-    bit = lax.axis_index(axis) % 2
-    pairs = lambda step: [(i, i ^ step) for i in range(count)]
-    size = rows.shape[0] // 2
-    kept = lax.dynamic_slice_in_dim(rows, bit * size, size)
-    sent = lax.dynamic_slice_in_dim(rows, (1 - bit) * size, size)
-    rows = kept + lax.ppermute(sent, axis, pairs(1))
-    step = 2
-    while step < count:
-        rounded = rows.astype(bf16)
-        theirs = lambda step: lax.ppermute(rounded, axis, pairs(step)).astype(f32)
-        if step == 2 and 4 * step <= count:
-            rows = (rounded.astype(f32) + theirs(step)) + (theirs(2 * step) + theirs(3 * step))
-            rows, beside = lax.optimization_barrier((rows, beside))
-            step *= 4
-        else:
-            rows = rounded.astype(f32) + theirs(step)
-            step *= 2
-    other = lax.ppermute(rows, axis, pairs(1))
-    rows = jnp.where(bit == 0, jnp.concatenate([rows, other]), jnp.concatenate([other, rows]))
-    return rows, beside
+    rounded = rows.astype(bf16)
+    theirs = [lax.ppermute(rounded, axis, partners(count, step)).astype(f32) for step in steps]
+    if len(steps) == 1:
+        return rounded.astype(f32) + theirs[0]
+    return (rounded.astype(f32) + theirs[0]) + (theirs[1] + theirs[2])
+
+
+def partners(count, step):
+    return [(i, i ^ step) for i in range(count)]
 
 
 def mirrored(spectrum):
@@ -516,6 +548,7 @@
         left_out=(0, 1),
         room=60,
     )
+    other_z = lax.ppermute(z, "fibre", partners(count, 1))
     cols = lax.all_to_all(conv_part, "fibre", split_axis=0, concat_axis=0, tiled=True)
     pair = tout // 2
     back = mirrored(response)
@@ -527,7 +560,7 @@
     grad_part, cross = call(
         functools.partial(filter_kernel, (count, channels, tout, width)),
         [
-            shape((count, rows * tiles + edge_rows, lanes), bf16),
+            shape((count // cores, cores * rows * tiles + edge_rows, lanes), bf16),
             shape((count, channels, 2 * width), f32),
         ],
         [
@@ -541,23 +574,57 @@
     )
     (cross,) = call(hermitian_kernel, [shape((2, channels, count, width), f32)], [], 1e6, (cross,))
     filter_grad = cross.transpose(0, 1, 3, 2).reshape(2, channels, waves)
-    grad_cols = lax.all_to_all(grad_part, "fibre", split_axis=0, concat_axis=0, tiled=True)
-    grad_cols, filter_grad = lax.optimization_barrier((grad_cols, filter_grad))
-    taps_part, shifted = call(
+    chips = [[core + cores * chip for chip in range(count // cores)] for core in range(cores)]
+    grad_cols = lax.all_to_all(
+        grad_part, "fibre", split_axis=0, concat_axis=0, tiled=True, axis_index_groups=chips
+    )
+    core = (lax.axis_index("fibre") % cores).astype(jnp.int32).reshape(1)
+    (samples,) = call(
+        gather_kernel,
+        [shape((k_in + 4 * cin, cores * fibre_in), bf16)],
+        [],
+        1e6,
+        (core, z, other_z),
+        small=(0,),
+    )
+    grad_cols, filter_grad, samples = lax.optimization_barrier((grad_cols, filter_grad, samples))
+    some = k_out // cores
+    taps_part, keep, send = call(
         functools.partial(tap_kernel, dims),
-        [shape((tap_rows, lanes), f32), shape((3, k_out, width), bf16)],
-        [pltpu.VMEM((k_out, width + lanes), f32), pltpu.VMEM((k_in + 4 * cin, fibre_in), bf16)],
+        [
+            shape((ks * cin + ks * cin * (cout // cores) // lanes, lanes), f32),
+            shape((3, some, width), bf16),
+            shape((3, some, width), bf16),
+        ],
+        [
+            pltpu.VMEM((some, cores * width + 2 * lanes), f32),
+            pltpu.VMEM((3, some, cores * width), bf16),
+        ],
         1e9,
-        (grad_cols, z),
-    )
+        (core, grad_cols, samples),
+        small=(0,),
+    )
+    got = lax.ppermute(send, "fibre", partners(count, 1))
+    chips = count // cores
+    step = 4 if chips % 4 == 0 else 1
+    total = taps_part
+    if step == 4:
+        total = summed_over_chips(total, "fibre", (cores, 2 * cores, 3 * cores))
+    total, keep, got = lax.optimization_barrier((total, keep, got))
     (input_grad,) = call(
         functools.partial(input_kernel, dims),
         [shape((k_in, fibre_in), bf16)],
         [pltpu.VMEM((ks, k_in, k_out), bf16)],
         2e9,
-        (shifted, taps),
-    )
-    total, input_grad = summed_over(taps_part, "fibre", input_grad)
+        (core, keep, got, taps),
+        small=(0,),
+    )
+    while step < chips:
+        total = summed_over_chips(total, "fibre", (cores * step,))
+        step *= 2
+    total, input_grad = lax.optimization_barrier((total, input_grad))
+    other = lax.ppermute(total, "fibre", partners(count, 1))
+    total = jnp.where(core[0] == 0, jnp.concatenate([total, other]), jnp.concatenate([other, total]))
     (tap_grad,) = call(
         functools.partial(unpack_kernel, dims, 1.0 / math.sqrt(tout * waves)),
         [shape((ks, ks, cin, cout), f32)],

time: 64.7 us -> 63.9 us (0.988)
  waiting for transfers between devices: 24.1 us -> 20.5 us
  local copies, waits for them, and re-layouts: 6.45 us -> 9.16 us
  starting transfers between devices: 16.8 us -> 15.8 us
  Pallas kernels: 15.9 us -> 16.9 us
    all_to_all x1, waiting for transfers between devices: 7.23 us -> 3.95 us  [per_device(): lax.all_to_all(grad_part, 'fibre', split_axis=0, concat_axis=0, tiled=Tru...]
    reshape x1, local copies, waits for them, and re-layouts: 1.21 us -> 2.44 us  [per_device(): filter_grad = cross.transpose(0, 1, 3, 2).reshape(2, channels, waves)]
    unnamed x14, local copies, waits for them, and re-layouts: 3.05 us -> 4.09 us
    transpose x1, local copies, waits for them, and re-layouts: 0.34 us -> 1.35 us  [per_device(): filter_grad = cross.transpose(0, 1, 3, 2).reshape(2, channels, waves)]
    pallas_call x6 -> x7, Pallas kernels: 15.9 us -> 16.9 us  [call(): pl.pallas_call(kernel, out_shape=outs, in_specs=[pl.BlockSpec(memory_spac...]
    ppermute x6 -> x7, starting transfers between devices: 5 us -> 4.3 us  [the longest x4 3.75 us: summed_over_chips(): lax.ppermute(rounded, axis, partners(count, step)).astype(f32)]
    ppermute x6 -> x7, waiting for transfers between devices: 6.96 us -> 6.49 us  [the longest x4 5.19 us: summed_over_chips(): lax.ppermute(rounded, axis, partners(count, step)).astype(f32)]
  transfers between devices with their start and end apart: 8 -> 9, of which waited for: 5 -> 7; matrix products, arithmetic and copies ran while one was open for 9% -> 13% of each run, Pallas kernels for 7% -> 15%
where the time goes in v6:
time: 63.9 us; the launch traced here: 63.4 us
  waiting for transfers between devices  20.5 us (32%)
  Pallas kernels  16.9 us (26%)
  starting transfers between devices  15.8 us (25%)
  local copies, waits for them, and re-layouts  9.16 us (14%)
  between operations  0.85 us (1%)
    pallas_call x7, Pallas kernels, call(): pl.pallas_call(kernel, out_shape=outs, in_specs=[pl.BlockSpec(memory_spac...  16.9 us
    all_to_all x1, waiting for transfers between devices, per_device(): lax.all_to_all(conv_part, 'fibre', split_axis=0, concat_axis=0, tiled=True)  10 us
    all_to_all x1, starting transfers between devices, per_device(): lax.all_to_all(conv_part, 'fibre', split_axis=0, concat_axis=0, tiled=True)  7.4 us
    ppermute x4, waiting for transfers between devices, summed_over_chips(): lax.ppermute(rounded, axis, partners(count, step)).astype(f32)  5.19 us
    all_to_all x1, starting transfers between devices, per_device(): lax.all_to_all(grad_part, 'fibre', split_axis=0, concat_axis=0, tiled=Tru...  4.14 us
    unnamed x14, local copies, waits for them, and re-layouts  4.09 us
    all_to_all x1, waiting for transfers between devices, per_device(): lax.all_to_all(grad_part, 'fibre', split_axis=0, concat_axis=0, tiled=Tru...  3.95 us
    ppermute x4, starting transfers between devices, summed_over_chips(): lax.ppermute(rounded, axis, partners(count, step)).astype(f32)  3.75 us
  transfers between devices with their start and end apart: 9, of which 7 were waited for; matrix products, arithmetic and copies ran while one was open for 13% of the time, Pallas kernels for 15%

profile of v6, /device:TPU:0, one launch (start us, length us, event | category | flops | bytes accessed | tf_op | source)
XLA Modules:
  0.0 63.4 jit_solution(16344767955065397318)
XLA Ops:
  0.6 0.0 copy-start.5
  0.6 4.5 %shard_map.94 = (bf16[16,136,128]{2,1,0:T(8,128)(2,1)}, bf16[512,512]{1,0:T(8,128)(2,1)}) custom-call(bf16[512,512]{1,0:T(8,128)(2,1)} %bitcast.19, bf16[16,32,256]{2,1,0:T(8,128)(2,1)} %bitcast.20, bf16[5,5,32,64]{3,2,1,0:T(8,128)(2,1)} %bitcast.15), custom_call_target="tpu_custom_call" | custom-call | flops 2000000000 | bytes 1970176 | tf_op jit(solution)/shard_map/pallas_call | solution.py:58
  5.2 0.0 slice-start
  5.2 7.4 %all-to-all-start = ((bf16[16,136,128]{2,1,0:T(8,128)(2,1)}), bf16[16,136,128]{2,1,0:T(8,128)(2,1)S(1)}, u32[]{:S(2)}, u32[]{:S(2)}) async-start(bf16[16,136,128]{2,1,0:T(8,128)(2,1)} %get-tuple-element.18), calls=%async_computation | async-start | bytes 1114112 | tf_op jit(solution)/shard_map/all_to_all | solution.py:552
  12.6 0.4 collective-permute-start
  13.0 0.0 copy-done.5
  13.0 0.1 slice.26
  13.2 2.9 %reverse.2 = f32[2,4,4096]{2,1,0:T(4,128)S(1)} reverse(f32[2,4,4096]{2,1,0:T(4,128)S(1)} %bitcast.17), dimensions={2} | reverse | bytes 262144
  16.0 0.1 slice.43
  16.2 0.0 slice-done
  16.2 0.1 fusion.2
  16.3 0.2 stack.10
  16.5 0.2 copy.14
  16.7 0.2 stack.9
  16.9 0.0 copy-start.2
  16.9 0.0 copy-start.4
  17.0 0.2 copy.13
  17.1 0.1 copy.15
  17.2 0.1 broadcast_in_dim.8
  17.4 0.2 reshape.57.resp_ref
  17.6 0.0 copy-start
  17.6 10.0 %all-to-all-done.cols_ref = bf16[16,136,128]{2,1,0:T(8,128)(2,1)S(1)} async-done(((bf16[16,136,128]{2,1,0:T(8,128)(2,1)}), bf16[16,136,128]{2,1,0:T(8,128)(2,1)S(1)}, u32[]{:S(2)}, u32[]{:S(2)}) %all-to-all-start) | async-done | bytes 557088 | tf_op jit(solution)/shard_map/all_to_all | solution.py:552
  27.6 0.0 copy-done.2
  27.6 1.0 %copy-done.3 = bf16[512,512]{1,0:T(8,128)(2,1)S(1)} copy-done((bf16[512,512]{1,0:T(8,128)(2,1)S(1)}, bf16[512,512]{1,0:T(8,128)(2,1)}, u32[]{:S(2)}) %copy-start.3) | copy-done | bytes 524312
  28.7 4.4 %shard_map.95 = (bf16[8,136,128]{2,1,0:T(8,128)(2,1)}, f32[16,4,512]{2,1,0:T(4,128)S(1)}) custom-call(bf16[16,136,128]{2,1,0:T(8,128)(2,1)S(1)} %all-to-all-done.cols_ref, f32[2,256,256]{2,1,0:T(8,128)S(1)} %reshape.57.resp_ref, f32[2,16,256]{2,1,0:T(8,128)S(1)} %copy-done.4, bf16[512,512]{1,0:T(8,128)(2,1)S(1)} %copy-done.2, bf16[512,512]{1,0:T(8,128)(2,1)S(1)} %copy-done.3), custom_call_target="tpu_custom_call" | custom-call | flops 6000000000 | bytes 2572288 | tf_op jit(solution)/shard_map/pallas_call | solution.py:58
  33.1 4.1 %all-to-all-start.1 = ((bf16[8,136,128]{2,1,0:T(8,128)(2,1)}), bf16[8,136,128]{2,1,0:T(8,128)(2,1)S(1)}, u32[]{:S(2)}, u32[]{:S(2)}) async-start(bf16[8,136,128]{2,1,0:T(8,128)(2,1)} %get-tuple-element.19), calls=%async_computation.1 | async-start | bytes 557056 | tf_op jit(solution)/shard_map/all_to_all | solution.py:578
  37.3 0.0 collective-permute-done.other_ref
  37.3 0.0 copy-done
  37.3 0.1 shard_map.97.z_ref
  37.4 1.8 %shard_map.96 = f32[2,4,16,256]{3,2,1,0:T(8,128)S(1)} custom-call(f32[16,4,512]{2,1,0:T(4,128)S(1)} %get-tuple-element.20.cross_ref), custom_call_target="tpu_custom_call" | custom-call | flops 1000000 | bytes 262144 | tf_op jit(solution)/shard_map/pallas_call | solution.py:58
  39.2 1.3 %copy.16 = f32[2,4,256,16]{3,2,1,0:T(8,128)} copy(f32[2,4,256,16]{2,3,1,0:T(8,128)S(1)} %bitcast.14) | data formatting | bytes 262144 | tf_op jit(solution)/shard_map/transpose | solution.py:576
  40.5 2.4 %reshape.58 = f32[2,4,4096]{2,1,0:T(4,128)} reshape(f32[2,4,256,16]{3,2,1,0:T(8,128)} %copy.16) | data formatting | bytes 262144 | tf_op jit(solution)/shard_map/reshape | solution.py:576
  43.0 4.0 %all-to-all-done.1.grad_ref = bf16[8,136,128]{2,1,0:T(8,128)(2,1)S(1)} async-done(((bf16[8,136,128]{2,1,0:T(8,128)(2,1)}), bf16[8,136,128]{2,1,0:T(8,128)(2,1)S(1)}, u32[]{:S(2)}, u32[]{:S(2)}) %all-to-all-start.1) | async-done | bytes 278560 | tf_op jit(solution)/shard_map/all_to_all | solution.py:578
  46.9 1.5 %shard_map.98 = (f32[200,128]{1,0:T(8,128)S(1)}, bf16[3,256,256]{2,1,0:T(8,128)(2,1)S(1)}, bf16[3,256,256]{2,1,0:T(8,128)(2,1)S(1)}) custom-call(s32[1]{0:T(128)} %bitcast.core_ref, bf16[8,136,128]{2,1,0:T(8,128)(2,1)S(1)} %all-to-all-done.1.grad_ref, bf16[640,1024]{1,0:T(8,128)(2,1)S(1)} %shard_map.97.z_ref), custom_call_target="tpu_custom_call" | custom-call | flops 1000000000 | bytes 2478084 | tf_op jit(solution)/shard_map/pallas_call | solution.py:58
  48.4 0.1 collective-permute-start.4
  48.5 0.9 %collective-permute-start.3 = (bf16[200,128]{1,0:T(8,128)(2,1)S(1)}, bf16[200,128]{1,0:T(8,128)(2,1)S(1)}, u32[]{:S(2)}, u32[]{:S(2)}) collective-permute-start(bf16[200,128]{1,0:T(8,128)(2,1)S(1)} %convert_element_type.24), channel_id=1, source_target_pairs={{0,6},{1,7},{2,4},{3,5},{4,2},{5,3},{6,0},{7,1},{8,14},{9,15},{10,... | collective-permute-start | bytes 153608 | tf_op jit(solution)/shard_map/ppermute | solution.py:493
  49.4 2.0 %collective-permute-start.2 = (bf16[200,128]{1,0:T(8,128)(2,1)S(1)}, bf16[200,128]{1,0:T(8,128)(2,1)S(1)}, u32[]{:S(2)}, u32[]{:S(2)}) collective-permute-start(bf16[200,128]{1,0:T(8,128)(2,1)S(1)} %convert_element_type.24), channel_id=1, source_target_pairs={{0,4},{1,5},{2,6},{3,7},{4,0},{5,1},{6,2},{7,3},{8,12},{9,13},{10,... | collective-permute-start | bytes 153608 | tf_op jit(solution)/shard_map/ppermute | solution.py:493
  51.5 0.6 collective-permute-start.1
  52.0 1.9 %collective-permute-done.3 = bf16[200,128]{1,0:T(8,128)(2,1)S(1)} collective-permute-done((bf16[200,128]{1,0:T(8,128)(2,1)S(1)}, bf16[200,128]{1,0:T(8,128)(2,1)S(1)}, u32[]{:S(2)}, u32[]{:S(2)}) %collective-permute-start.3) | collective-permute-done | bytes 51232 | tf_op jit(solution)/shard_map/ppermute | solution.py:493
  53.9 0.8 %collective-permute-done.2 = bf16[200,128]{1,0:T(8,128)(2,1)S(1)} collective-permute-done((bf16[200,128]{1,0:T(8,128)(2,1)S(1)}, bf16[200,128]{1,0:T(8,128)(2,1)S(1)}, u32[]{:S(2)}, u32[]{:S(2)}) %collective-permute-start.2) | collective-permute-done | bytes 51232 | tf_op jit(solution)/shard_map/ppermute | solution.py:493
  54.7 0.9 %collective-permute-done.1 = bf16[200,128]{1,0:T(8,128)(2,1)S(1)} collective-permute-done((bf16[200,128]{1,0:T(8,128)(2,1)S(1)}, bf16[200,128]{1,0:T(8,128)(2,1)S(1)}, u32[]{:S(2)}, u32[]{:S(2)}) %collective-permute-start.1) | collective-permute-done | bytes 51232 | tf_op jit(solution)/shard_map/ppermute | solution.py:493
  55.6 0.0 collective-permute-done.4.other_ref
  55.6 0.2 collective-permute-start.5
  55.8 3.4 %shard_map.99 = bf16[512,512]{1,0:T(8,128)(2,1)} custom-call(s32[1]{0:T(128)} %bitcast.core_ref, bf16[3,256,256]{2,1,0:T(8,128)(2,1)S(1)} %get-tuple-element.28.own_ref, bf16[3,256,256]{2,1,0:T(8,128)(2,1)S(1)} %collective-permute-done.4.other_ref, bf16[5,5,32,64]{3,2,1,0:T(8,128)(2,1)S(1)} %bitcast.16), custom_call_target="tpu_custom_call" | custom-call | flops 2000000000 | bytes 1413124 | tf_op jit(solution)/shard_map/pallas_call | solution.py:58
  59.3 1.7 %collective-permute-done.5 = bf16[200,128]{1,0:T(8,128)(2,1)S(1)} collective-permute-done((bf16[200,128]{1,0:T(8,128)(2,1)S(1)}, bf16[200,128]{1,0:T(8,128)(2,1)S(1)}, u32[]{:S(2)}, u32[]{:S(2)}) %collective-permute-start.5) | collective-permute-done | bytes 51232 | tf_op jit(solution)/shard_map/ppermute | solution.py:493
  60.9 0.1 collective-permute-start.6
  61.0 1.3 %collective-permute-done.6 = f32[200,128]{1,0:T(8,128)S(1)} collective-permute-done((f32[200,128]{1,0:T(8,128)S(1)}, f32[200,128]{1,0:T(8,128)S(1)}, u32[]{:S(2)}, u32[]{:S(2)}) %collective-permute-start.6) | collective-permute-done | bytes 102432 | tf_op jit(solution)/shard_map/ppermute | solution.py:626
  62.3 1.1 %shard_map.100 = f32[5,5,32,64]{3,2,1,0:T(8,128)} custom-call(f32[400,128]{1,0:T(8,128)S(1)} %maximum_select_fusion.tap_ref), custom_call_target="tpu_custom_call" | custom-call | flops 1000000 | bytes 409600 | tf_op jit(solution)/shard_map/pallas_call | solution.py:58
  (9 shorter events, 0.1 us)
Async XLA Ops:
  0.6 12.4 %copy-start.5 = (f32[2,4,4096]{2,1,0:T(4,128)S(1)}, f32[2,4,4096]{2,1,0:T(4,128)}, u32[]{:S(2)}) copy-start(f32[2,4,4096]{2,1,0:T(4,128)} %param.9) | copy-start | bytes 393220
  5.2 11.0 %slice-start = ((f32[2,4,4096]{2,1,0:T(4,128)}), f32[2,4,1]{2,1,0:T(4,128)S(1)}, s32[]{:S(2)}) async-start(f32[2,4,4096]{2,1,0:T(4,128)} %param.9), calls=%async_computation.2 | async-start | bytes 8192 | tf_op jit(solution)/shard_map/jit(_roll_static)/slice | solution.py:504
  5.2 22.4 %all-to-all-start = ((bf16[16,136,128]{2,1,0:T(8,128)(2,1)}), bf16[16,136,128]{2,1,0:T(8,128)(2,1)S(1)}, u32[]{:S(2)}, u32[]{:S(2)}) async-start(bf16[16,136,128]{2,1,0:T(8,128)(2,1)} %get-tuple-element.18), calls=%async_computation | async-start | bytes 1114112 | tf_op jit(solution)/shard_map/all_to_all | solution.py:552
  12.6 24.6 %collective-permute-start = (bf16[512,512]{1,0:T(8,128)(2,1)}, bf16[512,512]{1,0:T(8,128)(2,1)S(1)}, u32[]{:S(2)}, u32[]{:S(2)}) collective-permute-start(bf16[512,512]{1,0:T(8,128)(2,1)} %get-tuple-element.21.own_ref), channel_id=1, source_target_pairs={{0,1},{1,0},{2,3},{3,2},{4,5},{5,4},{6,7},{7,6},{8,9},{9,8},{10,11... | collective-permute-start | bytes 1572872 | tf_op jit(solution)/shard_map/ppermute | solution.py:551
  16.9 10.7 %copy-start.2 = (bf16[512,512]{1,0:T(8,128)(2,1)S(1)}, bf16[512,512]{1,0:T(8,128)(2,1)}, u32[]{:S(2)}) copy-start(bf16[512,512]{1,0:T(8,128)(2,1)} %constant.27.clone.high_ref) | copy-start | bytes 1572868
  16.9 10.7 %copy-start.4 = (f32[2,16,256]{2,1,0:T(8,128)S(1)}, f32[2,16,256]{2,1,0:T(8,128)}, u32[]{:S(2)}) copy-start(f32[2,16,256]{2,1,0:T(8,128)} %constant.26.clone.twist_ref) | copy-start | bytes 98308
  17.6 19.7 %copy-start = (bf16[512,512]{1,0:T(8,128)(2,1)S(1)}, bf16[512,512]{1,0:T(8,128)(2,1)}, u32[]{:S(2)}) copy-start(bf16[512,512]{1,0:T(8,128)(2,1)} %get-tuple-element.21.own_ref) | copy-start | bytes 1572868
  27.6 1.0 %copy-start.3 = (bf16[512,512]{1,0:T(8,128)(2,1)S(1)}, bf16[512,512]{1,0:T(8,128)(2,1)}, u32[]{:S(2)}) copy-start(bf16[512,512]{1,0:T(8,128)(2,1)} %constant.28.clone.rest_ref) | copy-start | bytes 1572868
  33.1 13.8 %all-to-all-start.1 = ((bf16[8,136,128]{2,1,0:T(8,128)(2,1)}), bf16[8,136,128]{2,1,0:T(8,128)(2,1)S(1)}, u32[]{:S(2)}, u32[]{:S(2)}) async-start(bf16[8,136,128]{2,1,0:T(8,128)(2,1)} %get-tuple-element.19), calls=%async_computation.1 | async-start | bytes 557056 | tf_op jit(solution)/shard_map/all_to_all | solution.py:578
  43.0 12.9 %copy-start.1 = (bf16[5,5,64,32]{2,3,1,0:T(8,128)(2,1)S(1)}, bf16[5,5,64,32]{2,3,1,0:T(8,128)(2,1)}, u32[]{:S(2)}) copy-start(bf16[5,5,64,32]{2,3,1,0:T(8,128)(2,1)} %param.8) | copy-start | bytes 307204
  48.4 7.2 %collective-permute-start.4 = (bf16[3,256,256]{2,1,0:T(8,128)(2,1)S(1)}, bf16[3,256,256]{2,1,0:T(8,128)(2,1)S(1)}, u32[]{:S(2)}, u32[]{:S(2)}) collective-permute-start(bf16[3,256,256]{2,1,0:T(8,128)(2,1)S(1)} %get-tuple-element.26), channel_id=1, source_target_pairs={{0,1},{1,0},{2,3},{3,2},{4,5},{5,4},{6,7},{7,6},{8,9},{9,8},{10,11... | collective-permute-start | bytes 1179656 | tf_op jit(solution)/shard_map/ppermute | solution.py:607
  48.5 5.4 %collective-permute-start.3 = (bf16[200,128]{1,0:T(8,128)(2,1)S(1)}, bf16[200,128]{1,0:T(8,128)(2,1)S(1)}, u32[]{:S(2)}, u32[]{:S(2)}) collective-permute-start(bf16[200,128]{1,0:T(8,128)(2,1)S(1)} %convert_element_type.24), channel_id=1, source_target_pairs={{0,6},{1,7},{2,4},{3,5},{4,2},{5,3},{6,0},{7,1},{8,14},{9,15},{10,... | collective-permute-start | bytes 153608 | tf_op jit(solution)/shard_map/ppermute | solution.py:493
  49.4 5.3 %collective-permute-start.2 = (bf16[200,128]{1,0:T(8,128)(2,1)S(1)}, bf16[200,128]{1,0:T(8,128)(2,1)S(1)}, u32[]{:S(2)}, u32[]{:S(2)}) collective-permute-start(bf16[200,128]{1,0:T(8,128)(2,1)S(1)} %convert_element_type.24), channel_id=1, source_target_pairs={{0,4},{1,5},{2,6},{3,7},{4,0},{5,1},{6,2},{7,3},{8,12},{9,13},{10,... | collective-permute-start | bytes 153608 | tf_op jit(solution)/shard_map/ppermute | solution.py:493
  51.5 4.1 %collective-permute-start.1 = (bf16[200,128]{1,0:T(8,128)(2,1)S(1)}, bf16[200,128]{1,0:T(8,128)(2,1)S(1)}, u32[]{:S(2)}, u32[]{:S(2)}) collective-permute-start(bf16[200,128]{1,0:T(8,128)(2,1)S(1)} %convert_element_type.24), channel_id=1, source_target_pairs={{0,2},{1,3},{2,0},{3,1},{4,6},{5,7},{6,4},{7,5},{8,10},{9,11},{10,... | collective-permute-start | bytes 153608 | tf_op jit(solution)/shard_map/ppermute | solution.py:493
  55.6 5.3 %collective-permute-start.5 = (bf16[200,128]{1,0:T(8,128)(2,1)S(1)}, bf16[200,128]{1,0:T(8,128)(2,1)S(1)}, u32[]{:S(2)}, u32[]{:S(2)}) collective-permute-start(bf16[200,128]{1,0:T(8,128)(2,1)S(1)} %add_add_fusion), channel_id=1, source_target_pairs={{0,8},{1,9},{2,10},{3,11},{4,12},{5,13},{6,14},{7,15},{8,0},{9,1},... | collective-permute-start | bytes 153608 | tf_op jit(solution)/shard_map/ppermute | solution.py:493
  60.9 1.4 %collective-permute-start.6 = (f32[200,128]{1,0:T(8,128)S(1)}, f32[200,128]{1,0:T(8,128)S(1)}, u32[]{:S(2)}, u32[]{:S(2)}) collective-permute-start(f32[200,128]{1,0:T(8,128)S(1)} %convert_add_fusion), channel_id=1, source_target_pairs={{0,1},{1,0},{2,3},{3,2},{4,5},{5,4},{6,7},{7,6},{8,9},{9,8},{10,11... | collective-permute-start | bytes 307208 | tf_op jit(solution)/shard_map/ppermute | solution.py:626

commit v7 on v6

--- a/solution.py
+++ b/solution.py
@@ -53,7 +53,7 @@
     return (iota(shape, 0) == row_of_column(iota((1, shape[1]), 1))).astype(f32).astype(bf16)
 
 
-def call(kernel, outs, scratch, flops, args, left=(), left_out=(), small=(), room=48):
+def call(kernel, outs, scratch, flops, args, left=(), left_out=(), small=(), room=24):
     moved = sum(a.size * a.dtype.itemsize for a in list(args) + list(outs))
     return pl.pallas_call(
         kernel,
@@ -213,7 +213,7 @@
 
 def filter_kernel(
     dims, cols_ref, resp_ref, twist_ref, high_ref, rest_ref,
-    out_ref, cross_ref, x_ref, y_ref, spec_ref, grad_ref,
+    out_ref, cross_ref, x_ref, y_ref, spec_ref, grad_ref, prod_ref,
 ):
     count, channels, tout, width = dims
     rows, pair = channels * tout, tout // 2
@@ -298,11 +298,16 @@
     y_ref[:, :width] = rr * gr + ri * gi
     y_ref[:, width:] = rr * gi - ri * gr
     scale = 1.0 / (count * width)
-    spec_ref[:, :width], spec_ref[:, width:] = (sr * gr + si * gi) * scale, (sr * gi - si * gr) * scale
-    for k in range(count):
-        for ch in range(channels):
-            at = k * packed + ch * pair
-            cross_ref[k, ch : ch + 1] = jnp.sum(spec_ref[at : at + pair], axis=0, keepdims=True)
+    crossed = ((sr * gr + si * gi) * scale, (sr * gi - si * gr) * scale)
+    wide = width // lanes
+    for b in range(2 * wide):
+        prod_ref[b] = crossed[b // wide][:, lanes * (b % wide) : lanes * (b % wide + 1)]
+    groups = count * channels
+    for b in range(2 * wide):
+        summed = prod_ref[b, pl.ds(0, groups, stride=pair), :]
+        for step in range(1, pair):
+            summed = summed + prod_ref[b, pl.ds(step, groups, stride=pair), :]
+        cross_ref[:, lanes * b : lanes * (b + 1)] = summed
     y_ref[...] = inner(dot_nt)
     for r, h in chunks:
         real, imag = backward_planes(r, h)
@@ -329,8 +334,7 @@
 
 
 def hermitian_kernel(cross_ref, out_ref):
-    count, channels, wide = cross_ref.shape
-    width = wide // 2
+    _, channels, count, width = out_ref.shape
     row, col = iota((width, width), 0), iota((width, width), 1)
     flip = (row + col == width - 1).astype(f32).astype(bf16)
     flip_first = ((row + col == width) | ((row == 0) & (col == 0))).astype(f32).astype(bf16)
@@ -345,13 +349,15 @@
         return total
 
     for k in range(count):
-        own, other = cross_ref[k], cross_ref[(count - k) % count]
+        from_k = channels * ((count - k) % count)
+        own = cross_ref[channels * k : channels * (k + 1)]
+        other = cross_ref[from_k : from_k + channels]
         by = flip if k else flip_first
         out_ref[0, :, k] = 0.5 * (own[:, :width] + moved(other[:, :width], by))
         out_ref[1, :, k] = 0.5 * (own[:, width:] - moved(other[:, width:], by))
 
 
-def gather_kernel(core_ref, own_ref, other_ref, out_ref):
+def gather_kernel(core_ref, own_ref, other_ref, wave_ref, out_ref, high_ref, rest_ref):
     k_in, wide = own_ref.shape
     width = wide // 2
     pad = (out_ref.shape[0] - k_in) // 2
@@ -364,6 +370,10 @@
         other_at = pl.multiple_of(wide * phase + width * (1 - core), lanes)
         out_ref[pad : pad + k_in, pl.ds(own_at, width)] = own_ref[:, at]
         out_ref[pad : pad + k_in, pl.ds(other_at, width)] = other_ref[:, at]
+    for at, table_ref in ((0, high_ref), (width, rest_ref)):
+        cosine, sine = wave_ref[at : at + width, :width], wave_ref[at : at + width, width:]
+        table_ref[:width, :width], table_ref[:width, width:] = cosine, -sine
+        table_ref[width:, :width], table_ref[width:, width:] = sine, cosine
 
 
 def tap_kernel(dims, core_ref, grad_ref, z_ref, tap_ref, keep_ref, send_ref, g_ref, shifted_ref):
@@ -506,13 +516,12 @@
 
 def tables(count, width):
     inner = np.outer(np.arange(width), np.arange(width)) % width * (2.0 * np.pi / width)
-    c, s = np.cos(inner), np.sin(inner)
-    table = np.block([[c, -s], [s, c]]).astype(np.float32)
+    table = np.concatenate([np.cos(inner), np.sin(inner)], axis=1).astype(np.float32)
     high = table.astype(bf16)
     rest = (table - high.astype(np.float32)).astype(bf16)
     outer = np.outer(np.arange(count), np.arange(width)) * (2.0 * np.pi / (count * width))
     twist = np.stack([np.cos(outer), np.sin(outer)]).astype(np.float32)
-    return twist, high, rest
+    return twist, np.concatenate([high, rest])
 
 
 def per_device(signal, conv_taps, response, cotangent):
@@ -550,27 +559,39 @@
     )
     other_z = lax.ppermute(z, "fibre", partners(count, 1))
     cols = lax.all_to_all(conv_part, "fibre", split_axis=0, concat_axis=0, tiled=True)
+    core = (lax.axis_index("fibre") % cores).astype(jnp.int32).reshape(1)
+    twist, waves_table = tables(count, width)
+    matrix = shape((2 * width, 2 * width), bf16)
+    samples, high, rest = call(
+        gather_kernel,
+        [shape((k_in + 4 * cin, cores * fibre_in), bf16), matrix, matrix],
+        [],
+        1e6,
+        (core, z, other_z, jnp.asarray(waves_table)),
+        small=(0,),
+    )
+    cols, samples, high, rest = lax.optimization_barrier((cols, samples, high, rest))
     pair = tout // 2
     back = mirrored(response)
     real = jnp.stack([response[0] + back[0], response[1] - back[1]]) * (0.5 / waves)
     real = real.reshape(2, channels, 1, width, count).transpose(0, 4, 1, 2, 3)
     real = jnp.broadcast_to(real, (2, count, channels, pair, width)).reshape(2, count * rows // 2, width)
-    twist, high, rest = tables(count, width)
     big = count * rows // 2
     grad_part, cross = call(
         functools.partial(filter_kernel, (count, channels, tout, width)),
         [
             shape((count // cores, cores * rows * tiles + edge_rows, lanes), bf16),
-            shape((count, channels, 2 * width), f32),
+            shape((count * channels, 2 * width), f32),
         ],
         [
             pltpu.VMEM((count, rows, width), f32),
             pltpu.VMEM((big, 2 * width), f32),
             pltpu.VMEM((big, 2 * width), f32),
             pltpu.VMEM((big, 2 * width), f32),
+            pltpu.VMEM((2 * tiles, big, lanes), f32),
         ],
         6e9,
-        (cols, real, jnp.asarray(twist), jnp.asarray(high), jnp.asarray(rest)),
+        (cols, real, jnp.asarray(twist), high, rest),
     )
     (cross,) = call(hermitian_kernel, [shape((2, channels, count, width), f32)], [], 1e6, (cross,))
     filter_grad = cross.transpose(0, 1, 3, 2).reshape(2, channels, waves)
@@ -578,16 +599,7 @@
     grad_cols = lax.all_to_all(
         grad_part, "fibre", split_axis=0, concat_axis=0, tiled=True, axis_index_groups=chips
     )
-    core = (lax.axis_index("fibre") % cores).astype(jnp.int32).reshape(1)
-    (samples,) = call(
-        gather_kernel,
-        [shape((k_in + 4 * cin, cores * fibre_in), bf16)],
-        [],
-        1e6,
-        (core, z, other_z),
-        small=(0,),
-    )
-    grad_cols, filter_grad, samples = lax.optimization_barrier((grad_cols, filter_grad, samples))
+    grad_cols, filter_grad = lax.optimization_barrier((grad_cols, filter_grad))
     some = k_out // cores
     taps_part, keep, send = call(
         functools.partial(tap_kernel, dims),

time: 63.9 us -> 63.5 us (level)
    all_to_all x1, waiting for transfers between devices: 10 us -> 7.39 us  [per_device(): lax.all_to_all(conv_part, 'fibre', split_axis=0, concat_axis=0, tiled=True)]
    all_to_all x1, waiting for transfers between devices: 3.95 us -> 6.35 us  [per_device(): lax.all_to_all(grad_part, 'fibre', split_axis=0, concat_axis=0, tiled=Tru...]
    unnamed x14 -> x20, local copies, waits for them, and re-layouts: 4.09 us -> 6.48 us
    reshape x1, local copies, waits for them, and re-layouts: 2.44 us -> 1.22 us  [per_device(): filter_grad = cross.transpose(0, 1, 3, 2).reshape(2, channels, waves)]
    transpose x1, local copies, waits for them, and re-layouts: 1.35 us -> 0.33 us  [per_device(): filter_grad = cross.transpose(0, 1, 3, 2).reshape(2, channels, waves)]
  transfers between devices with their start and end apart: 9 -> 9, of which waited for: 7 -> 7; matrix products, arithmetic and copies ran while one was open for 13% -> 10% of each run, Pallas kernels for 15% -> 9%
where the time goes in v7:
time: 63.5 us; the launch traced here: 63.1 us
  waiting for transfers between devices  20.2 us (32%)
  Pallas kernels  16.6 us (26%)
  starting transfers between devices  15.9 us (25%)
  local copies, waits for them, and re-layouts  9.31 us (15%)
  between operations  0.89 us (1%)
    pallas_call x7, Pallas kernels, call(): pl.pallas_call(kernel, out_shape=outs, in_specs=[pl.BlockSpec(memory_spac...  16.6 us
    all_to_all x1, starting transfers between devices, per_device(): lax.all_to_all(conv_part, 'fibre', split_axis=0, concat_axis=0, tiled=True)  7.4 us
    all_to_all x1, waiting for transfers between devices, per_device(): lax.all_to_all(conv_part, 'fibre', split_axis=0, concat_axis=0, tiled=True)  7.39 us
    unnamed x20, local copies, waits for them, and re-layouts  6.48 us
    all_to_all x1, waiting for transfers between devices, per_device(): lax.all_to_all(grad_part, 'fibre', split_axis=0, concat_axis=0, tiled=Tru...  6.35 us
    ppermute x4, waiting for transfers between devices, summed_over_chips(): lax.ppermute(rounded, axis, partners(count, step)).astype(f32)  5.19 us
    all_to_all x1, starting transfers between devices, per_device(): lax.all_to_all(grad_part, 'fibre', split_axis=0, concat_axis=0, tiled=Tru...  4.15 us
    ppermute x4, starting transfers between devices, summed_over_chips(): lax.ppermute(rounded, axis, partners(count, step)).astype(f32)  3.75 us
  transfers between devices with their start and end apart: 9, of which 7 were waited for; matrix products, arithmetic and copies ran while one was open for 10% of the time, Pallas kernels for 9%

profile of v7, /device:TPU:0, one launch (start us, length us, event | category | flops | bytes accessed | tf_op | source)
XLA Modules:
  0.0 63.1 jit_solution(3578659863931868097)
XLA Ops:
  0.6 0.0 copy-start.8
  0.6 4.5 %shard_map.85 = (bf16[16,136,128]{2,1,0:T(8,128)(2,1)}, bf16[512,512]{1,0:T(8,128)(2,1)}) custom-call(bf16[512,512]{1,0:T(8,128)(2,1)} %bitcast.19, bf16[16,32,256]{2,1,0:T(8,128)(2,1)} %bitcast.20, bf16[5,5,32,64]{3,2,1,0:T(8,128)(2,1)} %bitcast.15), custom_call_target="tpu_custom_call" | custom-call | flops 2000000000 | bytes 1970176 | tf_op jit(solution)/shard_map/pallas_call | solution.py:58
  5.2 0.0 slice-start
  5.2 7.4 %all-to-all-start = ((bf16[16,136,128]{2,1,0:T(8,128)(2,1)}), bf16[16,136,128]{2,1,0:T(8,128)(2,1)S(1)}, u32[]{:S(2)}, u32[]{:S(2)}) async-start(bf16[16,136,128]{2,1,0:T(8,128)(2,1)} %get-tuple-element.24), calls=%async_computation | async-start | bytes 1114112 | tf_op jit(solution)/shard_map/all_to_all | solution.py:561
  12.6 0.4 collective-permute-start
  13.0 0.1 slice.26
  13.2 2.9 %reverse.2 = f32[2,4,4096]{2,1,0:T(4,128)S(1)} reverse(f32[2,4,4096]{2,1,0:T(4,128)S(1)} %bitcast.17), dimensions={2} | reverse | bytes 262144
  16.0 0.1 slice.43
  16.2 0.1 fusion.2
  16.3 0.2 stack.10
  16.6 0.2 copy.13
  16.7 0.2 stack.9
  16.9 0.0 copy-start
  17.0 0.0 copy-start.1
  17.0 0.2 copy.12
  17.2 0.1 copy.14
  17.2 0.1 broadcast_in_dim.8
  17.4 0.0 copy-start.7
  17.4 0.2 reshape.57.resp_ref
  17.6 0.0 collective-permute-done.other_ref
  17.6 0.4 copy-done
  18.0 0.2 copy-done.1
  18.1 0.2 shard_map.86
  18.4 1.1 %copy-done.2 = bf16[640,1024]{1,0:T(8,128)(2,1)} copy-done((bf16[640,1024]{1,0:T(8,128)(2,1)}, bf16[640,1024]{1,0:T(8,128)(2,1)S(1)}, u32[]{:S(2)}) %copy-start.2) | copy-done | bytes 1310744
  19.5 0.8 %copy-done.4 = bf16[512,512]{1,0:T(8,128)(2,1)} copy-done((bf16[512,512]{1,0:T(8,128)(2,1)}, bf16[512,512]{1,0:T(8,128)(2,1)S(1)}, u32[]{:S(2)}) %copy-start.4) | copy-done | bytes 524312
  20.2 7.4 %all-to-all-done.cols_ref = bf16[16,136,128]{2,1,0:T(8,128)(2,1)S(1)} async-done(((bf16[16,136,128]{2,1,0:T(8,128)(2,1)}), bf16[16,136,128]{2,1,0:T(8,128)(2,1)S(1)}, u32[]{:S(2)}, u32[]{:S(2)}) %all-to-all-start) | async-done | bytes 557088 | tf_op jit(solution)/shard_map/all_to_all | solution.py:561
  27.6 1.0 %copy-done.5 = bf16[512,512]{1,0:T(8,128)(2,1)S(1)} copy-done((bf16[512,512]{1,0:T(8,128)(2,1)S(1)}, bf16[512,512]{1,0:T(8,128)(2,1)}, u32[]{:S(2)}) %copy-start.5) | copy-done | bytes 524312
  28.7 4.0 %shard_map.87 = (bf16[8,136,128]{2,1,0:T(8,128)(2,1)}, f32[64,512]{1,0:T(8,128)S(1)}) custom-call(bf16[16,136,128]{2,1,0:T(8,128)(2,1)S(1)} %all-to-all-done.cols_ref, f32[2,256,256]{2,1,0:T(8,128)S(1)} %reshape.57.resp_ref, f32[2,16,256]{2,1,0:T(8,128)S(1)} %copy-done.7, bf16[512,512]{1,0:T(8,128)(2,1)S(1)} %get-tuple-element.30.high_ref, ...), custom_call_target="tpu_custom_call" | custom-call | flops 6000000000 | bytes 2572288 | tf_op jit(solution)/shard_map/pallas_call | solution.py:58
  32.7 4.2 %all-to-all-start.1 = ((bf16[8,136,128]{2,1,0:T(8,128)(2,1)}), bf16[8,136,128]{2,1,0:T(8,128)(2,1)S(1)}, u32[]{:S(2)}, u32[]{:S(2)}) async-start(bf16[8,136,128]{2,1,0:T(8,128)(2,1)} %get-tuple-element.32), calls=%async_computation.1 | async-start | bytes 557056 | tf_op jit(solution)/shard_map/all_to_all | solution.py:599
  36.9 1.8 %shard_map.88 = f32[2,4,16,256]{3,2,1,0:T(8,128)S(1)} custom-call(f32[64,512]{1,0:T(8,128)S(1)} %get-tuple-element.33.cross_ref), custom_call_target="tpu_custom_call" | custom-call | flops 1000000 | bytes 262144 | tf_op jit(solution)/shard_map/pallas_call | solution.py:58
  38.6 0.3 copy.15
  39.0 1.2 %reshape.58 = f32[2,4,4096]{2,1,0:T(4,128)} reshape(f32[2,4,256,16]{3,2,1,0:T(8,128)S(1)} %copy.15) | data formatting | bytes 262144 | tf_op jit(solution)/shard_map/reshape | solution.py:597
  40.2 6.4 %all-to-all-done.1.grad_ref = bf16[8,136,128]{2,1,0:T(8,128)(2,1)S(1)} async-done(((bf16[8,136,128]{2,1,0:T(8,128)(2,1)}), bf16[8,136,128]{2,1,0:T(8,128)(2,1)S(1)}, u32[]{:S(2)}, u32[]{:S(2)}) %all-to-all-start.1) | async-done | bytes 278560 | tf_op jit(solution)/shard_map/all_to_all | solution.py:599
  46.5 1.5 %shard_map.89 = (f32[200,128]{1,0:T(8,128)S(1)}, bf16[3,256,256]{2,1,0:T(8,128)(2,1)S(1)}, bf16[3,256,256]{2,1,0:T(8,128)(2,1)S(1)}) custom-call(s32[1]{0:T(128)} %bitcast.core_ref, bf16[8,136,128]{2,1,0:T(8,128)(2,1)S(1)} %all-to-all-done.1.grad_ref, bf16[640,1024]{1,0:T(8,128)(2,1)S(1)} %copy-done.3), custom_call_target="tpu_custom_call" | custom-call | flops 1000000000 | bytes 2478084 | tf_op jit(solution)/shard_map/pallas_call | solution.py:58
  48.0 0.1 collective-permute-start.4
  48.1 0.9 %collective-permute-start.3 = (bf16[200,128]{1,0:T(8,128)(2,1)S(1)}, bf16[200,128]{1,0:T(8,128)(2,1)S(1)}, u32[]{:S(2)}, u32[]{:S(2)}) collective-permute-start(bf16[200,128]{1,0:T(8,128)(2,1)S(1)} %convert_element_type.24), channel_id=1, source_target_pairs={{0,6},{1,7},{2,4},{3,5},{4,2},{5,3},{6,0},{7,1},{8,14},{9,15},{10,... | collective-permute-start | bytes 153608 | tf_op jit(solution)/shard_map/ppermute | solution.py:503
  49.0 2.0 %collective-permute-start.2 = (bf16[200,128]{1,0:T(8,128)(2,1)S(1)}, bf16[200,128]{1,0:T(8,128)(2,1)S(1)}, u32[]{:S(2)}, u32[]{:S(2)}) collective-permute-start(bf16[200,128]{1,0:T(8,128)(2,1)S(1)} %convert_element_type.24), channel_id=1, source_target_pairs={{0,4},{1,5},{2,6},{3,7},{4,0},{5,1},{6,2},{7,3},{8,12},{9,13},{10,... | collective-permute-start | bytes 153608 | tf_op jit(solution)/shard_map/ppermute | solution.py:503
  51.1 0.6 collective-permute-start.1
  51.7 1.9 %collective-permute-done.3 = bf16[200,128]{1,0:T(8,128)(2,1)S(1)} collective-permute-done((bf16[200,128]{1,0:T(8,128)(2,1)S(1)}, bf16[200,128]{1,0:T(8,128)(2,1)S(1)}, u32[]{:S(2)}, u32[]{:S(2)}) %collective-permute-start.3) | collective-permute-done | bytes 51232 | tf_op jit(solution)/shard_map/ppermute | solution.py:503
  53.5 0.8 %collective-permute-done.2 = bf16[200,128]{1,0:T(8,128)(2,1)S(1)} collective-permute-done((bf16[200,128]{1,0:T(8,128)(2,1)S(1)}, bf16[200,128]{1,0:T(8,128)(2,1)S(1)}, u32[]{:S(2)}, u32[]{:S(2)}) %collective-permute-start.2) | collective-permute-done | bytes 51232 | tf_op jit(solution)/shard_map/ppermute | solution.py:503
  54.3 0.9 %collective-permute-done.1 = bf16[200,128]{1,0:T(8,128)(2,1)S(1)} collective-permute-done((bf16[200,128]{1,0:T(8,128)(2,1)S(1)}, bf16[200,128]{1,0:T(8,128)(2,1)S(1)}, u32[]{:S(2)}, u32[]{:S(2)}) %collective-permute-start.1) | collective-permute-done | bytes 51232 | tf_op jit(solution)/shard_map/ppermute | solution.py:503
  55.2 0.0 collective-permute-done.4.other_ref
  55.2 0.2 collective-permute-start.5
  55.4 3.4 %shard_map.90 = bf16[512,512]{1,0:T(8,128)(2,1)} custom-call(s32[1]{0:T(128)} %bitcast.core_ref, bf16[3,256,256]{2,1,0:T(8,128)(2,1)S(1)} %get-tuple-element.40.own_ref, bf16[3,256,256]{2,1,0:T(8,128)(2,1)S(1)} %collective-permute-done.4.other_ref, bf16[5,5,32,64]{3,2,1,0:T(8,128)(2,1)S(1)} %bitcast.16), custom_call_target="tpu_custom_call" | custom-call | flops 2000000000 | bytes 1413124 | tf_op jit(solution)/shard_map/pallas_call | solution.py:58
  58.9 1.7 %collective-permute-done.5 = bf16[200,128]{1,0:T(8,128)(2,1)S(1)} collective-permute-done((bf16[200,128]{1,0:T(8,128)(2,1)S(1)}, bf16[200,128]{1,0:T(8,128)(2,1)S(1)}, u32[]{:S(2)}, u32[]{:S(2)}) %collective-permute-start.5) | collective-permute-done | bytes 51232 | tf_op jit(solution)/shard_map/ppermute | solution.py:503
  60.6 0.1 collective-permute-start.6
  60.6 1.3 %collective-permute-done.6 = f32[200,128]{1,0:T(8,128)S(1)} collective-permute-done((f32[200,128]{1,0:T(8,128)S(1)}, f32[200,128]{1,0:T(8,128)S(1)}, u32[]{:S(2)}, u32[]{:S(2)}) %collective-permute-start.6) | collective-permute-done | bytes 102432 | tf_op jit(solution)/shard_map/ppermute | solution.py:638
  62.0 1.1 %shard_map.91 = f32[5,5,32,64]{3,2,1,0:T(8,128)} custom-call(f32[400,128]{1,0:T(8,128)S(1)} %maximum_select_fusion.tap_ref), custom_call_target="tpu_custom_call" | custom-call | flops 1000000 | bytes 409600 | tf_op jit(solution)/shard_map/pallas_call | solution.py:58
  (15 shorter events, 0.1 us)
Async XLA Ops:
  0.6 12.4 %copy-start.8 = (f32[2,4,4096]{2,1,0:T(4,128)S(1)}, f32[2,4,4096]{2,1,0:T(4,128)}, u32[]{:S(2)}) copy-start(f32[2,4,4096]{2,1,0:T(4,128)} %param.8) | copy-start | bytes 393220
  5.2 11.0 %slice-start = ((f32[2,4,4096]{2,1,0:T(4,128)}), f32[2,4,1]{2,1,0:T(4,128)S(1)}, s32[]{:S(2)}) async-start(f32[2,4,4096]{2,1,0:T(4,128)} %param.8), calls=%async_computation.2 | async-start | bytes 8192 | tf_op jit(solution)/shard_map/jit(_roll_static)/slice | solution.py:514
  5.2 22.4 %all-to-all-start = ((bf16[16,136,128]{2,1,0:T(8,128)(2,1)}), bf16[16,136,128]{2,1,0:T(8,128)(2,1)S(1)}, u32[]{:S(2)}, u32[]{:S(2)}) async-start(bf16[16,136,128]{2,1,0:T(8,128)(2,1)} %get-tuple-element.24), calls=%async_computation | async-start | bytes 1114112 | tf_op jit(solution)/shard_map/all_to_all | solution.py:561
  12.6 5.0 %collective-permute-start = (bf16[512,512]{1,0:T(8,128)(2,1)}, bf16[512,512]{1,0:T(8,128)(2,1)S(1)}, u32[]{:S(2)}, u32[]{:S(2)}) collective-permute-start(bf16[512,512]{1,0:T(8,128)(2,1)} %get-tuple-element.25.own_ref), channel_id=1, source_target_pairs={{0,1},{1,0},{2,3},{3,2},{4,5},{5,4},{6,7},{7,6},{8,9},{9,8},{10,11... | collective-permute-start | bytes 1572872 | tf_op jit(solution)/shard_map/ppermute | solution.py:560
  16.9 1.0 %copy-start = (bf16[512,512]{1,0:T(8,128)(2,1)S(1)}, bf16[512,512]{1,0:T(8,128)(2,1)}, u32[]{:S(2)}) copy-start(bf16[512,512]{1,0:T(8,128)(2,1)} %constant.24.clone.wave_ref) | copy-start | bytes 1572868
  17.0 1.2 %copy-start.1 = (bf16[512,512]{1,0:T(8,128)(2,1)S(1)}, bf16[512,512]{1,0:T(8,128)(2,1)}, u32[]{:S(2)}) copy-start(bf16[512,512]{1,0:T(8,128)(2,1)} %get-tuple-element.25.own_ref) | copy-start | bytes 1572868
  17.4 10.3 %copy-start.7 = (f32[2,16,256]{2,1,0:T(8,128)S(1)}, f32[2,16,256]{2,1,0:T(8,128)}, u32[]{:S(2)}) copy-start(f32[2,16,256]{2,1,0:T(8,128)} %constant.25.clone.twist_ref) | copy-start | bytes 98308
  18.4 1.1 %copy-start.2 = (bf16[640,1024]{1,0:T(8,128)(2,1)}, bf16[640,1024]{1,0:T(8,128)(2,1)S(1)}, u32[]{:S(2)}) copy-start(bf16[640,1024]{1,0:T(8,128)(2,1)S(1)} %get-tuple-element.35.z_ref) | copy-start | bytes 3932164
  19.5 0.8 %copy-start.4 = (bf16[512,512]{1,0:T(8,128)(2,1)}, bf16[512,512]{1,0:T(8,128)(2,1)S(1)}, u32[]{:S(2)}) copy-start(bf16[512,512]{1,0:T(8,128)(2,1)S(1)} %get-tuple-element.31.rest_ref) | copy-start | bytes 1572868
  27.6 1.0 %copy-start.5 = (bf16[512,512]{1,0:T(8,128)(2,1)S(1)}, bf16[512,512]{1,0:T(8,128)(2,1)}, u32[]{:S(2)}) copy-start(bf16[512,512]{1,0:T(8,128)(2,1)} %copy-done.4) | copy-start | bytes 1572868
  32.7 13.8 %all-to-all-start.1 = ((bf16[8,136,128]{2,1,0:T(8,128)(2,1)}), bf16[8,136,128]{2,1,0:T(8,128)(2,1)S(1)}, u32[]{:S(2)}, u32[]{:S(2)}) async-start(bf16[8,136,128]{2,1,0:T(8,128)(2,1)} %get-tuple-element.32), calls=%async_computation.1 | async-start | bytes 557056 | tf_op jit(solution)/shard_map/all_to_all | solution.py:599
  36.9 9.7 %copy-start.3 = (bf16[640,1024]{1,0:T(8,128)(2,1)S(1)}, bf16[640,1024]{1,0:T(8,128)(2,1)}, u32[]{:S(2)}) copy-start(bf16[640,1024]{1,0:T(8,128)(2,1)} %copy-done.2) | copy-start | bytes 3932164
  40.2 15.3 %copy-start.6 = (bf16[5,5,64,32]{2,3,1,0:T(8,128)(2,1)S(1)}, bf16[5,5,64,32]{2,3,1,0:T(8,128)(2,1)}, u32[]{:S(2)}) copy-start(bf16[5,5,64,32]{2,3,1,0:T(8,128)(2,1)} %param.7) | copy-start | bytes 307204
  48.0 7.2 %collective-permute-start.4 = (bf16[3,256,256]{2,1,0:T(8,128)(2,1)S(1)}, bf16[3,256,256]{2,1,0:T(8,128)(2,1)S(1)}, u32[]{:S(2)}, u32[]{:S(2)}) collective-permute-start(bf16[3,256,256]{2,1,0:T(8,128)(2,1)S(1)} %get-tuple-element.38), channel_id=1, source_target_pairs={{0,1},{1,0},{2,3},{3,2},{4,5},{5,4},{6,7},{7,6},{8,9},{9,8},{10,11... | collective-permute-start | bytes 1179656 | tf_op jit(solution)/shard_map/ppermute | solution.py:619
  48.1 5.4 %collective-permute-start.3 = (bf16[200,128]{1,0:T(8,128)(2,1)S(1)}, bf16[200,128]{1,0:T(8,128)(2,1)S(1)}, u32[]{:S(2)}, u32[]{:S(2)}) collective-permute-start(bf16[200,128]{1,0:T(8,128)(2,1)S(1)} %convert_element_type.24), channel_id=1, source_target_pairs={{0,6},{1,7},{2,4},{3,5},{4,2},{5,3},{6,0},{7,1},{8,14},{9,15},{10,... | collective-permute-start | bytes 153608 | tf_op jit(solution)/shard_map/ppermute | solution.py:503
  49.0 5.3 %collective-permute-start.2 = (bf16[200,128]{1,0:T(8,128)(2,1)S(1)}, bf16[200,128]{1,0:T(8,128)(2,1)S(1)}, u32[]{:S(2)}, u32[]{:S(2)}) collective-permute-start(bf16[200,128]{1,0:T(8,128)(2,1)S(1)} %convert_element_type.24), channel_id=1, source_target_pairs={{0,4},{1,5},{2,6},{3,7},{4,0},{5,1},{6,2},{7,3},{8,12},{9,13},{10,... | collective-permute-start | bytes 153608 | tf_op jit(solution)/shard_map/ppermute | solution.py:503
  51.1 4.1 %collective-permute-start.1 = (bf16[200,128]{1,0:T(8,128)(2,1)S(1)}, bf16[200,128]{1,0:T(8,128)(2,1)S(1)}, u32[]{:S(2)}, u32[]{:S(2)}) collective-permute-start(bf16[200,128]{1,0:T(8,128)(2,1)S(1)} %convert_element_type.24), channel_id=1, source_target_pairs={{0,2},{1,3},{2,0},{3,1},{4,6},{5,7},{6,4},{7,5},{8,10},{9,11},{10,... | collective-permute-start | bytes 153608 | tf_op jit(solution)/shard_map/ppermute | solution.py:503
  55.2 5.3 %collective-permute-start.5 = (bf16[200,128]{1,0:T(8,128)(2,1)S(1)}, bf16[200,128]{1,0:T(8,128)(2,1)S(1)}, u32[]{:S(2)}, u32[]{:S(2)}) collective-permute-start(bf16[200,128]{1,0:T(8,128)(2,1)S(1)} %add_add_fusion), channel_id=1, source_target_pairs={{0,8},{1,9},{2,10},{3,11},{4,12},{5,13},{6,14},{7,15},{8,0},{9,1},... | collective-permute-start | bytes 153608 | tf_op jit(solution)/shard_map/ppermute | solution.py:503
  60.6 1.4 %collective-permute-start.6 = (f32[200,128]{1,0:T(8,128)S(1)}, f32[200,128]{1,0:T(8,128)S(1)}, u32[]{:S(2)}, u32[]{:S(2)}) collective-permute-start(f32[200,128]{1,0:T(8,128)S(1)} %convert_add_fusion), channel_id=1, source_target_pairs={{0,1},{1,0},{2,3},{3,2},{4,5},{5,4},{6,7},{7,6},{8,9},{9,8},{10,11... | collective-permute-start | bytes 307208 | tf_op jit(solution)/shard_map/ppermute | solution.py:638

commit v8 on v7

--- a/solution.py
+++ b/solution.py
@@ -212,11 +212,20 @@
 
 
 def filter_kernel(
-    dims, cols_ref, resp_ref, twist_ref, high_ref, rest_ref,
-    out_ref, cross_ref, x_ref, y_ref, spec_ref, grad_ref, prod_ref,
+    dims, cols_ref, own_ref, twist_ref, wave_ref,
+    out_ref, cross_ref, x_ref, y_ref, spec_ref, grad_ref, prod_ref, resp_ref, high_ref, rest_ref,
 ):
     count, channels, tout, width = dims
     rows, pair = channels * tout, tout // 2
+    wide, groups = width // lanes, count * channels
+    for at, table_ref in ((0, high_ref), (width, rest_ref)):
+        cosine, sine = wave_ref[at : at + width, :width], wave_ref[at : at + width, width:]
+        table_ref[:width, :width], table_ref[:width, width:] = cosine, -sine
+        table_ref[width:, :width], table_ref[width:, width:] = sine, cosine
+    for b in range(2 * wide):
+        own = own_ref[b // wide, :, lanes * (b % wide) : lanes * (b % wide + 1)]
+        for step in range(pair):
+            resp_ref[b, pl.ds(step, groups, stride=pair), :] = own
     packed = rows // 2
     group = min(2, channels)
     chunk = group * pair
@@ -279,7 +288,7 @@
         forward_planes([re for re, im in planes], [im for re, im in planes], r, h)
     spec_ref[...] = inner(dot)
     sr, si = spec_ref[:, :width], spec_ref[:, width:]
-    rr, ri = resp_ref[0], resp_ref[1]
+    rr, ri = (jnp.concatenate([resp_ref[p * wide + b] for b in range(wide)], axis=1) for p in range(2))
     y_ref[:, :width] = rr * sr - ri * si
     y_ref[:, width:] = rr * si + ri * sr
     y_ref[...] = inner(dot_nt)
@@ -294,15 +303,13 @@
     grad_ref[...] = inner(dot)
     sr, si = spec_ref[:, :width], spec_ref[:, width:]
     gr, gi = grad_ref[:, :width], grad_ref[:, width:]
-    rr, ri = resp_ref[0], resp_ref[1]
+    rr, ri = (jnp.concatenate([resp_ref[p * wide + b] for b in range(wide)], axis=1) for p in range(2))
     y_ref[:, :width] = rr * gr + ri * gi
     y_ref[:, width:] = rr * gi - ri * gr
     scale = 1.0 / (count * width)
     crossed = ((sr * gr + si * gi) * scale, (sr * gi - si * gr) * scale)
-    wide = width // lanes
     for b in range(2 * wide):
         prod_ref[b] = crossed[b // wide][:, lanes * (b % wide) : lanes * (b % wide + 1)]
-    groups = count * channels
     for b in range(2 * wide):
         summed = prod_ref[b, pl.ds(0, groups, stride=pair), :]
         for step in range(1, pair):
@@ -357,7 +364,7 @@
         out_ref[1, :, k] = 0.5 * (own[:, width:] - moved(other[:, width:], by))
 
 
-def gather_kernel(core_ref, own_ref, other_ref, wave_ref, out_ref, high_ref, rest_ref):
+def gather_kernel(core_ref, own_ref, other_ref, out_ref):
     k_in, wide = own_ref.shape
     width = wide // 2
     pad = (out_ref.shape[0] - k_in) // 2
@@ -370,10 +377,6 @@
         other_at = pl.multiple_of(wide * phase + width * (1 - core), lanes)
         out_ref[pad : pad + k_in, pl.ds(own_at, width)] = own_ref[:, at]
         out_ref[pad : pad + k_in, pl.ds(other_at, width)] = other_ref[:, at]
-    for at, table_ref in ((0, high_ref), (width, rest_ref)):
-        cosine, sine = wave_ref[at : at + width, :width], wave_ref[at : at + width, width:]
-        table_ref[:width, :width], table_ref[:width, width:] = cosine, -sine
-        table_ref[width:, :width], table_ref[width:, width:] = sine, cosine
 
 
 def tap_kernel(dims, core_ref, grad_ref, z_ref, tap_ref, keep_ref, send_ref, g_ref, shifted_ref):
@@ -559,23 +562,11 @@
     )
     other_z = lax.ppermute(z, "fibre", partners(count, 1))
     cols = lax.all_to_all(conv_part, "fibre", split_axis=0, concat_axis=0, tiled=True)
-    core = (lax.axis_index("fibre") % cores).astype(jnp.int32).reshape(1)
-    twist, waves_table = tables(count, width)
-    matrix = shape((2 * width, 2 * width), bf16)
-    samples, high, rest = call(
-        gather_kernel,
-        [shape((k_in + 4 * cin, cores * fibre_in), bf16), matrix, matrix],
-        [],
-        1e6,
-        (core, z, other_z, jnp.asarray(waves_table)),
-        small=(0,),
-    )
-    cols, samples, high, rest = lax.optimization_barrier((cols, samples, high, rest))
-    pair = tout // 2
     back = mirrored(response)
     real = jnp.stack([response[0] + back[0], response[1] - back[1]]) * (0.5 / waves)
-    real = real.reshape(2, channels, 1, width, count).transpose(0, 4, 1, 2, 3)
-    real = jnp.broadcast_to(real, (2, count, channels, pair, width)).reshape(2, count * rows // 2, width)
+    real = real.reshape(2, channels, width, count).transpose(0, 3, 1, 2)
+    real = real.reshape(2, count * channels, width)
+    twist, waves_table = tables(count, width)
     big = count * rows // 2
     grad_part, cross = call(
         functools.partial(filter_kernel, (count, channels, tout, width)),
@@ -589,9 +580,12 @@
             pltpu.VMEM((big, 2 * width), f32),
             pltpu.VMEM((big, 2 * width), f32),
             pltpu.VMEM((2 * tiles, big, lanes), f32),
+            pltpu.VMEM((2 * tiles, big, lanes), f32),
+            pltpu.VMEM((2 * width, 2 * width), bf16),
+            pltpu.VMEM((2 * width, 2 * width), bf16),
         ],
         6e9,
-        (cols, real, jnp.asarray(twist), high, rest),
+        (cols, real, jnp.asarray(twist), jnp.asarray(waves_table)),
     )
     (cross,) = call(hermitian_kernel, [shape((2, channels, count, width), f32)], [], 1e6, (cross,))
     filter_grad = cross.transpose(0, 1, 3, 2).reshape(2, channels, waves)
@@ -599,7 +593,16 @@
     grad_cols = lax.all_to_all(
         grad_part, "fibre", split_axis=0, concat_axis=0, tiled=True, axis_index_groups=chips
     )
-    grad_cols, filter_grad = lax.optimization_barrier((grad_cols, filter_grad))
+    core = (lax.axis_index("fibre") % cores).astype(jnp.int32).reshape(1)
+    (samples,) = call(
+        gather_kernel,
+        [shape((k_in + 4 * cin, cores * fibre_in), bf16)],
+        [],
+        1e6,
+        (core, z, other_z),
+        small=(0,),
+    )
+    grad_cols, filter_grad, samples = lax.optimization_barrier((grad_cols, filter_grad, samples))
     some = k_out // cores
     taps_part, keep, send = call(
         functools.partial(tap_kernel, dims),

time: 63.5 us -> 62.5 us (0.984)
  local copies, waits for them, and re-layouts: 9.31 us -> 7.82 us
    unnamed x20 -> x12, local copies, waits for them, and re-layouts: 6.48 us -> 3.04 us
    all_to_all x1, waiting for transfers between devices: 7.39 us -> 10.3 us  [per_device(): lax.all_to_all(conv_part, 'fibre', split_axis=0, concat_axis=0, tiled=True)]
    all_to_all x1, waiting for transfers between devices: 6.35 us -> 3.96 us  [per_device(): lax.all_to_all(grad_part, 'fibre', split_axis=0, concat_axis=0, tiled=Tru...]
    reshape x1, local copies, waits for them, and re-layouts: 1.22 us -> 2.44 us  [per_device(): filter_grad = cross.transpose(0, 1, 3, 2).reshape(2, channels, waves)]
    transpose x1, local copies, waits for them, and re-layouts: 0.33 us -> 1.33 us  [per_device(): filter_grad = cross.transpose(0, 1, 3, 2).reshape(2, channels, waves)]
  transfers between devices with their start and end apart: 9 -> 9, of which waited for: 7 -> 7; matrix products, arithmetic and copies ran while one was open for 10% -> 13% of each run, Pallas kernels for 9% -> 15%
where the time goes in v8:
time: 62.5 us; the launch traced here: 62.1 us
  waiting for transfers between devices  20.8 us (33%)
  Pallas kernels  16.5 us (26%)
  starting transfers between devices  15.9 us (25%)
  local copies, waits for them, and re-layouts  7.82 us (13%)
  between operations  0.84 us (1%)
    pallas_call x7, Pallas kernels, call(): pl.pallas_call(kernel, out_shape=outs, in_specs=[pl.BlockSpec(memory_spac...  16.5 us
    all_to_all x1, waiting for transfers between devices, per_device(): lax.all_to_all(conv_part, 'fibre', split_axis=0, concat_axis=0, tiled=True)  10.3 us
    all_to_all x1, starting transfers between devices, per_device(): lax.all_to_all(conv_part, 'fibre', split_axis=0, concat_axis=0, tiled=True)  7.4 us
    ppermute x4, waiting for transfers between devices, summed_over_chips(): lax.ppermute(rounded, axis, partners(count, step)).astype(f32)  5.2 us
    all_to_all x1, starting transfers between devices, per_device(): lax.all_to_all(grad_part, 'fibre', split_axis=0, concat_axis=0, tiled=Tru...  4.16 us
    all_to_all x1, waiting for transfers between devices, per_device(): lax.all_to_all(grad_part, 'fibre', split_axis=0, concat_axis=0, tiled=Tru...  3.96 us
    ppermute x4, starting transfers between devices, summed_over_chips(): lax.ppermute(rounded, axis, partners(count, step)).astype(f32)  3.75 us
    unnamed x12, local copies, waits for them, and re-layouts  3.04 us
  transfers between devices with their start and end apart: 9, of which 7 were waited for; matrix products, arithmetic and copies ran while one was open for 13% of the time, Pallas kernels for 15%

profile of v8, /device:TPU:0, one launch (start us, length us, event | category | flops | bytes accessed | tf_op | source)
XLA Modules:
  0.0 62.1 jit_solution(18163438053008188492)
XLA Ops:
  0.6 0.0 copy-start.4
  0.6 4.5 %shard_map.85 = (bf16[16,136,128]{2,1,0:T(8,128)(2,1)}, bf16[512,512]{1,0:T(8,128)(2,1)}) custom-call(bf16[512,512]{1,0:T(8,128)(2,1)} %bitcast.17, bf16[16,32,256]{2,1,0:T(8,128)(2,1)} %bitcast.18, bf16[5,5,32,64]{3,2,1,0:T(8,128)(2,1)} %bitcast.13), custom_call_target="tpu_custom_call" | custom-call | flops 2000000000 | bytes 1970176 | tf_op jit(solution)/shard_map/pallas_call | solution.py:58
  5.2 0.0 slice-start
  5.2 7.4 %all-to-all-start = ((bf16[16,136,128]{2,1,0:T(8,128)(2,1)}), bf16[16,136,128]{2,1,0:T(8,128)(2,1)S(1)}, u32[]{:S(2)}, u32[]{:S(2)}) async-start(bf16[16,136,128]{2,1,0:T(8,128)(2,1)} %get-tuple-element.18), calls=%async_computation | async-start | bytes 1114112 | tf_op jit(solution)/shard_map/all_to_all | solution.py:564
  12.6 0.4 collective-permute-start
  13.0 0.0 copy-done.4
  13.0 0.1 slice.26
  13.2 2.9 %reverse.2 = f32[2,4,4096]{2,1,0:T(4,128)S(1)} reverse(f32[2,4,4096]{2,1,0:T(4,128)S(1)} %bitcast.15), dimensions={2} | reverse | bytes 262144
  16.0 0.1 slice.43
  16.2 0.0 slice-done
  16.2 0.1 fusion.2
  16.3 0.2 stack.10
  16.5 0.0 copy-start.2
  16.6 0.0 copy-start.3
  16.6 0.2 copy.14
  16.7 0.2 stack.9
  17.0 0.2 copy.13
  17.1 0.1 copy.15
  17.3 0.0 copy-start
  17.3 10.3 %all-to-all-done.cols_ref = bf16[16,136,128]{2,1,0:T(8,128)(2,1)S(1)} async-done(((bf16[16,136,128]{2,1,0:T(8,128)(2,1)}), bf16[16,136,128]{2,1,0:T(8,128)(2,1)S(1)}, u32[]{:S(2)}, u32[]{:S(2)}) %all-to-all-start) | async-done | bytes 557088 | tf_op jit(solution)/shard_map/all_to_all | solution.py:564
  27.6 0.0 copy-done.2
  27.6 0.0 copy-done.3
  27.6 4.1 %shard_map.86 = (bf16[8,136,128]{2,1,0:T(8,128)(2,1)}, f32[64,512]{1,0:T(8,128)S(1)}) custom-call(bf16[16,136,128]{2,1,0:T(8,128)(2,1)S(1)} %all-to-all-done.cols_ref, f32[2,64,256]{2,1,0:T(8,128)S(1)} %reshape.30.own_ref, f32[2,16,256]{2,1,0:T(8,128)S(1)} %copy-done.3, bf16[512,512]{1,0:T(8,128)(2,1)S(1)} %copy-done.2), custom_call_target="tpu_custom_call" | custom-call | flops 6000000000 | bytes 1654784 | tf_op jit(solution)/shard_map/pallas_call | solution.py:58
  31.7 4.2 %all-to-all-start.1 = ((bf16[8,136,128]{2,1,0:T(8,128)(2,1)}), bf16[8,136,128]{2,1,0:T(8,128)(2,1)S(1)}, u32[]{:S(2)}, u32[]{:S(2)}) async-start(bf16[8,136,128]{2,1,0:T(8,128)(2,1)} %get-tuple-element.19), calls=%async_computation.1 | async-start | bytes 557056 | tf_op jit(solution)/shard_map/all_to_all | solution.py:593
  35.9 0.0 collective-permute-done.other_ref
  35.9 0.0 copy-done
  35.9 0.1 shard_map.88.z_ref
  36.1 1.8 %shard_map.87 = f32[2,4,16,256]{3,2,1,0:T(8,128)S(1)} custom-call(f32[64,512]{1,0:T(8,128)S(1)} %get-tuple-element.20.cross_ref), custom_call_target="tpu_custom_call" | custom-call | flops 1000000 | bytes 262144 | tf_op jit(solution)/shard_map/pallas_call | solution.py:58
  37.8 1.3 %copy.16 = f32[2,4,256,16]{3,2,1,0:T(8,128)} copy(f32[2,4,256,16]{2,3,1,0:T(8,128)S(1)} %bitcast.12) | data formatting | bytes 262144 | tf_op jit(solution)/shard_map/transpose | solution.py:591
  39.2 2.4 %reshape.31 = f32[2,4,4096]{2,1,0:T(4,128)} reshape(f32[2,4,256,16]{3,2,1,0:T(8,128)} %copy.16) | data formatting | bytes 262144 | tf_op jit(solution)/shard_map/reshape | solution.py:591
  41.6 0.0 copy-start.1
  41.6 4.0 %all-to-all-done.1.grad_ref = bf16[8,136,128]{2,1,0:T(8,128)(2,1)S(1)} async-done(((bf16[8,136,128]{2,1,0:T(8,128)(2,1)}), bf16[8,136,128]{2,1,0:T(8,128)(2,1)S(1)}, u32[]{:S(2)}, u32[]{:S(2)}) %all-to-all-start.1) | async-done | bytes 278560 | tf_op jit(solution)/shard_map/all_to_all | solution.py:593
  45.5 1.5 %shard_map.89 = (f32[200,128]{1,0:T(8,128)S(1)}, bf16[3,256,256]{2,1,0:T(8,128)(2,1)S(1)}, bf16[3,256,256]{2,1,0:T(8,128)(2,1)S(1)}) custom-call(s32[1]{0:T(128)} %bitcast.core_ref, bf16[8,136,128]{2,1,0:T(8,128)(2,1)S(1)} %all-to-all-done.1.grad_ref, bf16[640,1024]{1,0:T(8,128)(2,1)S(1)} %shard_map.88.z_ref), custom_call_target="tpu_custom_call" | custom-call | flops 1000000000 | bytes 2478084 | tf_op jit(solution)/shard_map/pallas_call | solution.py:58
  47.0 0.1 collective-permute-start.4
  47.1 0.9 %collective-permute-start.3 = (bf16[200,128]{1,0:T(8,128)(2,1)S(1)}, bf16[200,128]{1,0:T(8,128)(2,1)S(1)}, u32[]{:S(2)}, u32[]{:S(2)}) collective-permute-start(bf16[200,128]{1,0:T(8,128)(2,1)S(1)} %convert_element_type.24), channel_id=1, source_target_pairs={{0,6},{1,7},{2,4},{3,5},{4,2},{5,3},{6,0},{7,1},{8,14},{9,15},{10,... | collective-permute-start | bytes 153608 | tf_op jit(solution)/shard_map/ppermute | solution.py:506
  48.1 2.0 %collective-permute-start.2 = (bf16[200,128]{1,0:T(8,128)(2,1)S(1)}, bf16[200,128]{1,0:T(8,128)(2,1)S(1)}, u32[]{:S(2)}, u32[]{:S(2)}) collective-permute-start(bf16[200,128]{1,0:T(8,128)(2,1)S(1)} %convert_element_type.24), channel_id=1, source_target_pairs={{0,4},{1,5},{2,6},{3,7},{4,0},{5,1},{6,2},{7,3},{8,12},{9,13},{10,... | collective-permute-start | bytes 153608 | tf_op jit(solution)/shard_map/ppermute | solution.py:506
  50.1 0.6 collective-permute-start.1
  50.7 1.9 %collective-permute-done.3 = bf16[200,128]{1,0:T(8,128)(2,1)S(1)} collective-permute-done((bf16[200,128]{1,0:T(8,128)(2,1)S(1)}, bf16[200,128]{1,0:T(8,128)(2,1)S(1)}, u32[]{:S(2)}, u32[]{:S(2)}) %collective-permute-start.3) | collective-permute-done | bytes 51232 | tf_op jit(solution)/shard_map/ppermute | solution.py:506
  52.5 0.8 %collective-permute-done.2 = bf16[200,128]{1,0:T(8,128)(2,1)S(1)} collective-permute-done((bf16[200,128]{1,0:T(8,128)(2,1)S(1)}, bf16[200,128]{1,0:T(8,128)(2,1)S(1)}, u32[]{:S(2)}, u32[]{:S(2)}) %collective-permute-start.2) | collective-permute-done | bytes 51232 | tf_op jit(solution)/shard_map/ppermute | solution.py:506
  53.3 0.9 %collective-permute-done.1 = bf16[200,128]{1,0:T(8,128)(2,1)S(1)} collective-permute-done((bf16[200,128]{1,0:T(8,128)(2,1)S(1)}, bf16[200,128]{1,0:T(8,128)(2,1)S(1)}, u32[]{:S(2)}, u32[]{:S(2)}) %collective-permute-start.1) | collective-permute-done | bytes 51232 | tf_op jit(solution)/shard_map/ppermute | solution.py:506
  54.2 0.0 collective-permute-done.4.other_ref
  54.3 0.2 collective-permute-start.5
  54.5 0.0 copy-done.1
  54.5 3.4 %shard_map.90 = bf16[512,512]{1,0:T(8,128)(2,1)} custom-call(s32[1]{0:T(128)} %bitcast.core_ref, bf16[3,256,256]{2,1,0:T(8,128)(2,1)S(1)} %get-tuple-element.28.own_ref, bf16[3,256,256]{2,1,0:T(8,128)(2,1)S(1)} %collective-permute-done.4.other_ref, bf16[5,5,32,64]{3,2,1,0:T(8,128)(2,1)S(1)} %bitcast.14), custom_call_target="tpu_custom_call" | custom-call | flops 2000000000 | bytes 1413124 | tf_op jit(solution)/shard_map/pallas_call | solution.py:58
  57.9 1.6 %collective-permute-done.5 = bf16[200,128]{1,0:T(8,128)(2,1)S(1)} collective-permute-done((bf16[200,128]{1,0:T(8,128)(2,1)S(1)}, bf16[200,128]{1,0:T(8,128)(2,1)S(1)}, u32[]{:S(2)}, u32[]{:S(2)}) %collective-permute-start.5) | collective-permute-done | bytes 51232 | tf_op jit(solution)/shard_map/ppermute | solution.py:506
  59.6 0.1 collective-permute-start.6
  59.6 1.3 %collective-permute-done.6 = f32[200,128]{1,0:T(8,128)S(1)} collective-permute-done((f32[200,128]{1,0:T(8,128)S(1)}, f32[200,128]{1,0:T(8,128)S(1)}, u32[]{:S(2)}, u32[]{:S(2)}) %collective-permute-start.6) | collective-permute-done | bytes 102432 | tf_op jit(solution)/shard_map/ppermute | solution.py:641
  60.9 1.1 %shard_map.91 = f32[5,5,32,64]{3,2,1,0:T(8,128)} custom-call(f32[400,128]{1,0:T(8,128)S(1)} %maximum_select_fusion.tap_ref), custom_call_target="tpu_custom_call" | custom-call | flops 1000000 | bytes 409600 | tf_op jit(solution)/shard_map/pallas_call | solution.py:58
  (6 shorter events, 0.1 us)
Async XLA Ops:
  0.6 12.4 %copy-start.4 = (f32[2,4,4096]{2,1,0:T(4,128)S(1)}, f32[2,4,4096]{2,1,0:T(4,128)}, u32[]{:S(2)}) copy-start(f32[2,4,4096]{2,1,0:T(4,128)} %param.8) | copy-start | bytes 393220
  5.2 11.0 %slice-start = ((f32[2,4,4096]{2,1,0:T(4,128)}), f32[2,4,1]{2,1,0:T(4,128)S(1)}, s32[]{:S(2)}) async-start(f32[2,4,4096]{2,1,0:T(4,128)} %param.8), calls=%async_computation.2 | async-start | bytes 8192 | tf_op jit(solution)/shard_map/jit(_roll_static)/slice | solution.py:517
  5.2 22.4 %all-to-all-start = ((bf16[16,136,128]{2,1,0:T(8,128)(2,1)}), bf16[16,136,128]{2,1,0:T(8,128)(2,1)S(1)}, u32[]{:S(2)}, u32[]{:S(2)}) async-start(bf16[16,136,128]{2,1,0:T(8,128)(2,1)} %get-tuple-element.18), calls=%async_computation | async-start | bytes 1114112 | tf_op jit(solution)/shard_map/all_to_all | solution.py:564
  12.6 23.3 %collective-permute-start = (bf16[512,512]{1,0:T(8,128)(2,1)}, bf16[512,512]{1,0:T(8,128)(2,1)S(1)}, u32[]{:S(2)}, u32[]{:S(2)}) collective-permute-start(bf16[512,512]{1,0:T(8,128)(2,1)} %get-tuple-element.21.own_ref), channel_id=1, source_target_pairs={{0,1},{1,0},{2,3},{3,2},{4,5},{5,4},{6,7},{7,6},{8,9},{9,8},{10,11... | collective-permute-start | bytes 1572872 | tf_op jit(solution)/shard_map/ppermute | solution.py:563
  16.5 11.1 %copy-start.2 = (bf16[512,512]{1,0:T(8,128)(2,1)S(1)}, bf16[512,512]{1,0:T(8,128)(2,1)}, u32[]{:S(2)}) copy-start(bf16[512,512]{1,0:T(8,128)(2,1)} %constant.25.clone.wave_ref) | copy-start | bytes 1572868
  16.6 11.1 %copy-start.3 = (f32[2,16,256]{2,1,0:T(8,128)S(1)}, f32[2,16,256]{2,1,0:T(8,128)}, u32[]{:S(2)}) copy-start(f32[2,16,256]{2,1,0:T(8,128)} %constant.24.clone.twist_ref) | copy-start | bytes 98308
  17.3 18.6 %copy-start = (bf16[512,512]{1,0:T(8,128)(2,1)S(1)}, bf16[512,512]{1,0:T(8,128)(2,1)}, u32[]{:S(2)}) copy-start(bf16[512,512]{1,0:T(8,128)(2,1)} %get-tuple-element.21.own_ref) | copy-start | bytes 1572868
  31.7 13.8 %all-to-all-start.1 = ((bf16[8,136,128]{2,1,0:T(8,128)(2,1)}), bf16[8,136,128]{2,1,0:T(8,128)(2,1)S(1)}, u32[]{:S(2)}, u32[]{:S(2)}) async-start(bf16[8,136,128]{2,1,0:T(8,128)(2,1)} %get-tuple-element.19), calls=%async_computation.1 | async-start | bytes 557056 | tf_op jit(solution)/shard_map/all_to_all | solution.py:593
  41.6 12.9 %copy-start.1 = (bf16[5,5,64,32]{2,3,1,0:T(8,128)(2,1)S(1)}, bf16[5,5,64,32]{2,3,1,0:T(8,128)(2,1)}, u32[]{:S(2)}) copy-start(bf16[5,5,64,32]{2,3,1,0:T(8,128)(2,1)} %param.7) | copy-start | bytes 307204
  47.0 7.2 %collective-permute-start.4 = (bf16[3,256,256]{2,1,0:T(8,128)(2,1)S(1)}, bf16[3,256,256]{2,1,0:T(8,128)(2,1)S(1)}, u32[]{:S(2)}, u32[]{:S(2)}) collective-permute-start(bf16[3,256,256]{2,1,0:T(8,128)(2,1)S(1)} %get-tuple-element.26), channel_id=1, source_target_pairs={{0,1},{1,0},{2,3},{3,2},{4,5},{5,4},{6,7},{7,6},{8,9},{9,8},{10,11... | collective-permute-start | bytes 1179656 | tf_op jit(solution)/shard_map/ppermute | solution.py:622
  47.1 5.4 %collective-permute-start.3 = (bf16[200,128]{1,0:T(8,128)(2,1)S(1)}, bf16[200,128]{1,0:T(8,128)(2,1)S(1)}, u32[]{:S(2)}, u32[]{:S(2)}) collective-permute-start(bf16[200,128]{1,0:T(8,128)(2,1)S(1)} %convert_element_type.24), channel_id=1, source_target_pairs={{0,6},{1,7},{2,4},{3,5},{4,2},{5,3},{6,0},{7,1},{8,14},{9,15},{10,... | collective-permute-start | bytes 153608 | tf_op jit(solution)/shard_map/ppermute | solution.py:506
  48.1 5.3 %collective-permute-start.2 = (bf16[200,128]{1,0:T(8,128)(2,1)S(1)}, bf16[200,128]{1,0:T(8,128)(2,1)S(1)}, u32[]{:S(2)}, u32[]{:S(2)}) collective-permute-start(bf16[200,128]{1,0:T(8,128)(2,1)S(1)} %convert_element_type.24), channel_id=1, source_target_pairs={{0,4},{1,5},{2,6},{3,7},{4,0},{5,1},{6,2},{7,3},{8,12},{9,13},{10,... | collective-permute-start | bytes 153608 | tf_op jit(solution)/shard_map/ppermute | solution.py:506
  50.1 4.1 %collective-permute-start.1 = (bf16[200,128]{1,0:T(8,128)(2,1)S(1)}, bf16[200,128]{1,0:T(8,128)(2,1)S(1)}, u32[]{:S(2)}, u32[]{:S(2)}) collective-permute-start(bf16[200,128]{1,0:T(8,128)(2,1)S(1)} %convert_element_type.24), channel_id=1, source_target_pairs={{0,2},{1,3},{2,0},{3,1},{4,6},{5,7},{6,4},{7,5},{8,10},{9,11},{10,... | collective-permute-start | bytes 153608 | tf_op jit(solution)/shard_map/ppermute | solution.py:506
  54.3 5.3 %collective-permute-start.5 = (bf16[200,128]{1,0:T(8,128)(2,1)S(1)}, bf16[200,128]{1,0:T(8,128)(2,1)S(1)}, u32[]{:S(2)}, u32[]{:S(2)}) collective-permute-start(bf16[200,128]{1,0:T(8,128)(2,1)S(1)} %add_add_fusion), channel_id=1, source_target_pairs={{0,8},{1,9},{2,10},{3,11},{4,12},{5,13},{6,14},{7,15},{8,0},{9,1},... | collective-permute-start | bytes 153608 | tf_op jit(solution)/shard_map/ppermute | solution.py:506
  59.6 1.4 %collective-permute-start.6 = (f32[200,128]{1,0:T(8,128)S(1)}, f32[200,128]{1,0:T(8,128)S(1)}, u32[]{:S(2)}, u32[]{:S(2)}) collective-permute-start(f32[200,128]{1,0:T(8,128)S(1)} %convert_add_fusion), channel_id=1, source_target_pairs={{0,1},{1,0},{2,3},{3,2},{4,5},{5,4},{6,7},{7,6},{8,9},{9,8},{10,11... | collective-permute-start | bytes 307208 | tf_op jit(solution)/shard_map/ppermute | solution.py:641

commit v9 on v8

--- a/solution.py
+++ b/solution.py
@@ -379,10 +379,12 @@
         out_ref[pad : pad + k_in, pl.ds(other_at, width)] = other_ref[:, at]
 
 
-def tap_kernel(dims, core_ref, grad_ref, z_ref, tap_ref, keep_ref, send_ref, g_ref, shifted_ref):
+def tap_kernel(
+    dims, core_ref, grad_ref, z_ref, tap_ref, keep_ref, send_ref, g_ref, exact_ref, shifted_ref
+):
     cin, tin, cout, tout, ks, count, rows = dims
     some = cout // cores
-    width = keep_ref.shape[2]
+    width = keep_ref.shape[1] - lanes
     wide = cores * width
     core = core_ref[0]
     row, col = iota((edge_rows, 2 * lanes), 0), iota((edge_rows, 2 * lanes), 1)
@@ -402,9 +404,17 @@
     shifted_ref[0] = pltpu.roll(g, wide + 2 * lanes - 1, 1)[:, inside].astype(bf16)
     shifted_ref[1] = g[:, inside].astype(bf16)
     shifted_ref[2] = pltpu.roll(g, 1, 1)[:, inside].astype(bf16)
-    for shift in range(3):
-        keep_ref[shift] = shifted_ref[shift, :, pl.ds(pl.multiple_of(width * core, lanes), width)]
-        send_ref[shift] = shifted_ref[shift, :, pl.ds(pl.multiple_of(width * (1 - core), lanes), width)]
+    exact_ref[...] = g.astype(bf16)
+    lane = iota((some * tout, lanes), 1)
+    for block, block_ref in ((core, keep_ref), (1 - core, send_ref)):
+        at = width * block
+        before, inner, after = (
+            exact_ref[:, pl.ds(pl.multiple_of(at + low, lanes), size)]
+            for low, size in ((0, lanes), (lanes, width), (lanes + width, lanes))
+        )
+        edge = jnp.where(lane == 0, after.astype(f32), before.astype(f32))
+        block_ref[:, :width] = inner
+        block_ref[:, width:] = jnp.where((lane == 0) | (lane == lanes - 1), edge, 0.0).astype(bf16)
     blank = jnp.zeros((lanes - 3 * some, wide), bf16)
     total = None
     for t in range(tout):
@@ -429,7 +439,7 @@
 def input_kernel(dims, core_ref, own_ref, other_ref, taps_ref, out_ref, w_ref):
     cin, tin, cout, tout, ks, count, rows = dims
     k_in = cin * tin
-    half = own_ref.shape[2]
+    half = own_ref.shape[1] - lanes
     some, channels = cout // cores, cout // count
     steps = lanes // some
     kinds = ks + 2 * (steps - 1)
@@ -457,7 +467,11 @@
                     tile = tiles[at : at + cin] if 0 <= i < kinds else empty
                     low = some * tout * part + lanes * q
                     w_ref[j, cin * s : cin * (s + 1), low : low + lanes] = tile
-    later, same, sooner = (jnp.concatenate([own_ref[k], other_ref[k]], axis=0) for k in range(3))
+    g = jnp.concatenate([own_ref[...], other_ref[...]], axis=0)
+    wide = half + lanes
+    same = g[:, :half]
+    later = dot(g, one_hot_columns((wide, half), lambda n: n + 1)).astype(bf16)
+    sooner = dot(g, one_hot_columns((wide, half), lambda n: jnp.where(n == 0, wide - 1, n - 1))).astype(bf16)
     even = dot(w_ref[0], later) + dot(w_ref[2], same) + dot(w_ref[4], sooner)
     odd = dot(w_ref[1], later) + dot(w_ref[3], same)
     both = jnp.concatenate([even.astype(bf16), odd.astype(bf16)], axis=1)
@@ -608,11 +622,12 @@
         functools.partial(tap_kernel, dims),
         [
             shape((ks * cin + ks * cin * (cout // cores) // lanes, lanes), f32),
-            shape((3, some, width), bf16),
-            shape((3, some, width), bf16),
+            shape((some, width + lanes), bf16),
+            shape((some, width + lanes), bf16),
         ],
         [
             pltpu.VMEM((some, cores * width + 2 * lanes), f32),
+            pltpu.VMEM((some, cores * width + 2 * lanes), bf16),
             pltpu.VMEM((3, some, cores * width), bf16),
         ],
         1e9,

time: 62.5 us -> 62.2 us (level)
  transfers between devices with their start and end apart: 9 -> 9, of which waited for: 7 -> 7; matrix products, arithmetic and copies ran while one was open for 13% -> 13% of each run, Pallas kernels for 15% -> 16%
where the time goes in v9:
time: 62.2 us; the launch traced here: 61.8 us
  waiting for transfers between devices  20.4 us (33%)
  Pallas kernels  16.8 us (27%)
  starting transfers between devices  15.7 us (25%)
  local copies, waits for them, and re-layouts  7.82 us (13%)
  between operations  0.85 us (1%)
    pallas_call x7, Pallas kernels, call(): pl.pallas_call(kernel, out_shape=outs, in_specs=[pl.BlockSpec(memory_spac...  16.8 us
    all_to_all x1, waiting for transfers between devices, per_device(): lax.all_to_all(conv_part, 'fibre', split_axis=0, concat_axis=0, tiled=True)  10.3 us
    all_to_all x1, starting transfers between devices, per_device(): lax.all_to_all(conv_part, 'fibre', split_axis=0, concat_axis=0, tiled=True)  7.4 us
    ppermute x4, waiting for transfers between devices, summed_over_chips(): lax.ppermute(rounded, axis, partners(count, step)).astype(f32)  4.86 us
    all_to_all x1, starting transfers between devices, per_device(): lax.all_to_all(grad_part, 'fibre', split_axis=0, concat_axis=0, tiled=Tru...  4.16 us
    all_to_all x1, waiting for transfers between devices, per_device(): lax.all_to_all(grad_part, 'fibre', split_axis=0, concat_axis=0, tiled=Tru...  3.96 us
    ppermute x4, starting transfers between devices, summed_over_chips(): lax.ppermute(rounded, axis, partners(count, step)).astype(f32)  3.62 us
    unnamed x12, local copies, waits for them, and re-layouts  3.04 us
  transfers between devices with their start and end apart: 9, of which 7 were waited for; matrix products, arithmetic and copies ran while one was open for 13% of the time, Pallas kernels for 16%

profile of v9, /device:TPU:0, one launch (start us, length us, event | category | flops | bytes accessed | tf_op | source)
XLA Modules:
  0.0 61.8 jit_solution(3357402632766006216)
XLA Ops:
  0.6 0.0 copy-start.4
  0.6 4.5 %shard_map.85 = (bf16[16,136,128]{2,1,0:T(8,128)(2,1)}, bf16[512,512]{1,0:T(8,128)(2,1)}) custom-call(bf16[512,512]{1,0:T(8,128)(2,1)} %bitcast.17, bf16[16,32,256]{2,1,0:T(8,128)(2,1)} %bitcast.18, bf16[5,5,32,64]{3,2,1,0:T(8,128)(2,1)} %bitcast.13), custom_call_target="tpu_custom_call" | custom-call | flops 2000000000 | bytes 1970176 | tf_op jit(solution)/shard_map/pallas_call | solution.py:58
  5.2 0.0 slice-start
  5.2 7.4 %all-to-all-start = ((bf16[16,136,128]{2,1,0:T(8,128)(2,1)}), bf16[16,136,128]{2,1,0:T(8,128)(2,1)S(1)}, u32[]{:S(2)}, u32[]{:S(2)}) async-start(bf16[16,136,128]{2,1,0:T(8,128)(2,1)} %get-tuple-element.18), calls=%async_computation | async-start | bytes 1114112 | tf_op jit(solution)/shard_map/all_to_all | solution.py:578
  12.6 0.4 collective-permute-start
  13.0 0.0 copy-done.4
  13.0 0.1 slice.26
  13.2 2.9 %reverse.2 = f32[2,4,4096]{2,1,0:T(4,128)S(1)} reverse(f32[2,4,4096]{2,1,0:T(4,128)S(1)} %bitcast.15), dimensions={2} | reverse | bytes 262144
  16.0 0.1 slice.43
  16.2 0.0 slice-done
  16.2 0.1 fusion.2
  16.3 0.2 stack.10
  16.5 0.0 copy-start.2
  16.6 0.0 copy-start.3
  16.6 0.2 copy.14
  16.7 0.2 stack.9
  17.0 0.2 copy.13
  17.1 0.1 copy.15
  17.3 0.0 copy-start
  17.3 10.3 %all-to-all-done.cols_ref = bf16[16,136,128]{2,1,0:T(8,128)(2,1)S(1)} async-done(((bf16[16,136,128]{2,1,0:T(8,128)(2,1)}), bf16[16,136,128]{2,1,0:T(8,128)(2,1)S(1)}, u32[]{:S(2)}, u32[]{:S(2)}) %all-to-all-start) | async-done | bytes 557088 | tf_op jit(solution)/shard_map/all_to_all | solution.py:578
  27.6 0.0 copy-done.2
  27.6 0.0 copy-done.3
  27.6 4.1 %shard_map.86 = (bf16[8,136,128]{2,1,0:T(8,128)(2,1)}, f32[64,512]{1,0:T(8,128)S(1)}) custom-call(bf16[16,136,128]{2,1,0:T(8,128)(2,1)S(1)} %all-to-all-done.cols_ref, f32[2,64,256]{2,1,0:T(8,128)S(1)} %reshape.30.own_ref, f32[2,16,256]{2,1,0:T(8,128)S(1)} %copy-done.3, bf16[512,512]{1,0:T(8,128)(2,1)S(1)} %copy-done.2), custom_call_target="tpu_custom_call" | custom-call | flops 6000000000 | bytes 1654784 | tf_op jit(solution)/shard_map/pallas_call | solution.py:58
  31.7 4.2 %all-to-all-start.1 = ((bf16[8,136,128]{2,1,0:T(8,128)(2,1)}), bf16[8,136,128]{2,1,0:T(8,128)(2,1)S(1)}, u32[]{:S(2)}, u32[]{:S(2)}) async-start(bf16[8,136,128]{2,1,0:T(8,128)(2,1)} %get-tuple-element.19), calls=%async_computation.1 | async-start | bytes 557056 | tf_op jit(solution)/shard_map/all_to_all | solution.py:607
  35.9 0.0 collective-permute-done.other_ref
  35.9 0.0 copy-done
  35.9 0.1 shard_map.88.z_ref
  36.1 1.8 %shard_map.87 = f32[2,4,16,256]{3,2,1,0:T(8,128)S(1)} custom-call(f32[64,512]{1,0:T(8,128)S(1)} %get-tuple-element.20.cross_ref), custom_call_target="tpu_custom_call" | custom-call | flops 1000000 | bytes 262144 | tf_op jit(solution)/shard_map/pallas_call | solution.py:58
  37.8 1.3 %copy.16 = f32[2,4,256,16]{3,2,1,0:T(8,128)} copy(f32[2,4,256,16]{2,3,1,0:T(8,128)S(1)} %bitcast.12) | data formatting | bytes 262144 | tf_op jit(solution)/shard_map/transpose | solution.py:605
  39.2 2.4 %reshape.31 = f32[2,4,4096]{2,1,0:T(4,128)} reshape(f32[2,4,256,16]{3,2,1,0:T(8,128)} %copy.16) | data formatting | bytes 262144 | tf_op jit(solution)/shard_map/reshape | solution.py:605
  41.6 0.0 copy-start.1
  41.6 4.0 %all-to-all-done.1.grad_ref = bf16[8,136,128]{2,1,0:T(8,128)(2,1)S(1)} async-done(((bf16[8,136,128]{2,1,0:T(8,128)(2,1)}), bf16[8,136,128]{2,1,0:T(8,128)(2,1)S(1)}, u32[]{:S(2)}, u32[]{:S(2)}) %all-to-all-start.1) | async-done | bytes 278560 | tf_op jit(solution)/shard_map/all_to_all | solution.py:607
  45.5 1.5 %shard_map.89 = (f32[200,128]{1,0:T(8,128)S(1)}, bf16[256,384]{1,0:T(8,128)(2,1)S(1)}, bf16[256,384]{1,0:T(8,128)(2,1)S(1)}) custom-call(s32[1]{0:T(128)} %bitcast.core_ref, bf16[8,136,128]{2,1,0:T(8,128)(2,1)S(1)} %all-to-all-done.1.grad_ref, bf16[640,1024]{1,0:T(8,128)(2,1)S(1)} %shard_map.88.z_ref), custom_call_target="tpu_custom_call" | custom-call | flops 1000000000 | bytes 2084868 | tf_op jit(solution)/shard_map/pallas_call | solution.py:58
  47.1 0.9 %collective-permute-start.3 = (bf16[200,128]{1,0:T(8,128)(2,1)S(1)}, bf16[200,128]{1,0:T(8,128)(2,1)S(1)}, u32[]{:S(2)}, u32[]{:S(2)}) collective-permute-start(bf16[200,128]{1,0:T(8,128)(2,1)S(1)} %convert_element_type.24), channel_id=1, source_target_pairs={{0,6},{1,7},{2,4},{3,5},{4,2},{5,3},{6,0},{7,1},{8,14},{9,15},{10,... | collective-permute-start | bytes 153608 | tf_op jit(solution)/shard_map/ppermute | solution.py:520
  48.0 2.0 %collective-permute-start.2 = (bf16[200,128]{1,0:T(8,128)(2,1)S(1)}, bf16[200,128]{1,0:T(8,128)(2,1)S(1)}, u32[]{:S(2)}, u32[]{:S(2)}) collective-permute-start(bf16[200,128]{1,0:T(8,128)(2,1)S(1)} %convert_element_type.24), channel_id=1, source_target_pairs={{0,4},{1,5},{2,6},{3,7},{4,0},{5,1},{6,2},{7,3},{8,12},{9,13},{10,... | collective-permute-start | bytes 153608 | tf_op jit(solution)/shard_map/ppermute | solution.py:520
  50.0 0.6 collective-permute-start.1
  50.6 0.0 collective-permute-start.4
  50.6 1.5 %collective-permute-done.3 = bf16[200,128]{1,0:T(8,128)(2,1)S(1)} collective-permute-done((bf16[200,128]{1,0:T(8,128)(2,1)S(1)}, bf16[200,128]{1,0:T(8,128)(2,1)S(1)}, u32[]{:S(2)}, u32[]{:S(2)}) %collective-permute-start.3) | collective-permute-done | bytes 51232 | tf_op jit(solution)/shard_map/ppermute | solution.py:520
  52.1 0.6 collective-permute-done.2
  52.7 1.5 %collective-permute-done.1 = bf16[200,128]{1,0:T(8,128)(2,1)S(1)} collective-permute-done((bf16[200,128]{1,0:T(8,128)(2,1)S(1)}, bf16[200,128]{1,0:T(8,128)(2,1)S(1)}, u32[]{:S(2)}, u32[]{:S(2)}) %collective-permute-start.1) | collective-permute-done | bytes 51232 | tf_op jit(solution)/shard_map/ppermute | solution.py:520
  54.2 0.0 collective-permute-done.4.other_ref
  54.2 0.1 collective-permute-start.5
  54.3 0.0 copy-done.1
  54.3 3.7 %shard_map.90 = bf16[512,512]{1,0:T(8,128)(2,1)} custom-call(s32[1]{0:T(128)} %bitcast.core_ref, bf16[256,384]{1,0:T(8,128)(2,1)S(1)} %get-tuple-element.28.own_ref, bf16[256,384]{1,0:T(8,128)(2,1)S(1)} %collective-permute-done.4.other_ref, bf16[5,5,32,64]{3,2,1,0:T(8,128)(2,1)S(1)} %bitcast.14), custom_call_target="tpu_custom_call" | custom-call | flops 2000000000 | bytes 1019908 | tf_op jit(solution)/shard_map/pallas_call | solution.py:58
  58.0 1.3 %collective-permute-done.5 = bf16[200,128]{1,0:T(8,128)(2,1)S(1)} collective-permute-done((bf16[200,128]{1,0:T(8,128)(2,1)S(1)}, bf16[200,128]{1,0:T(8,128)(2,1)S(1)}, u32[]{:S(2)}, u32[]{:S(2)}) %collective-permute-start.5) | collective-permute-done | bytes 51232 | tf_op jit(solution)/shard_map/ppermute | solution.py:520
  59.3 0.1 collective-permute-start.6
  59.4 1.3 %collective-permute-done.6 = f32[200,128]{1,0:T(8,128)S(1)} collective-permute-done((f32[200,128]{1,0:T(8,128)S(1)}, f32[200,128]{1,0:T(8,128)S(1)}, u32[]{:S(2)}, u32[]{:S(2)}) %collective-permute-start.6) | collective-permute-done | bytes 102432 | tf_op jit(solution)/shard_map/ppermute | solution.py:656
  60.7 1.1 %shard_map.91 = f32[5,5,32,64]{3,2,1,0:T(8,128)} custom-call(f32[400,128]{1,0:T(8,128)S(1)} %maximum_select_fusion.tap_ref), custom_call_target="tpu_custom_call" | custom-call | flops 1000000 | bytes 409600 | tf_op jit(solution)/shard_map/pallas_call | solution.py:58
  (6 shorter events, 0.1 us)
Async XLA Ops:
  0.6 12.4 %copy-start.4 = (f32[2,4,4096]{2,1,0:T(4,128)S(1)}, f32[2,4,4096]{2,1,0:T(4,128)}, u32[]{:S(2)}) copy-start(f32[2,4,4096]{2,1,0:T(4,128)} %param.8) | copy-start | bytes 393220
  5.2 11.0 %slice-start = ((f32[2,4,4096]{2,1,0:T(4,128)}), f32[2,4,1]{2,1,0:T(4,128)S(1)}, s32[]{:S(2)}) async-start(f32[2,4,4096]{2,1,0:T(4,128)} %param.8), calls=%async_computation.2 | async-start | bytes 8192 | tf_op jit(solution)/shard_map/jit(_roll_static)/slice | solution.py:531
  5.2 22.4 %all-to-all-start = ((bf16[16,136,128]{2,1,0:T(8,128)(2,1)}), bf16[16,136,128]{2,1,0:T(8,128)(2,1)S(1)}, u32[]{:S(2)}, u32[]{:S(2)}) async-start(bf16[16,136,128]{2,1,0:T(8,128)(2,1)} %get-tuple-element.18), calls=%async_computation | async-start | bytes 1114112 | tf_op jit(solution)/shard_map/all_to_all | solution.py:578
  12.6 23.3 %collective-permute-start = (bf16[512,512]{1,0:T(8,128)(2,1)}, bf16[512,512]{1,0:T(8,128)(2,1)S(1)}, u32[]{:S(2)}, u32[]{:S(2)}) collective-permute-start(bf16[512,512]{1,0:T(8,128)(2,1)} %get-tuple-element.21.own_ref), channel_id=1, source_target_pairs={{0,1},{1,0},{2,3},{3,2},{4,5},{5,4},{6,7},{7,6},{8,9},{9,8},{10,11... | collective-permute-start | bytes 1572872 | tf_op jit(solution)/shard_map/ppermute | solution.py:577
  16.5 11.1 %copy-start.2 = (bf16[512,512]{1,0:T(8,128)(2,1)S(1)}, bf16[512,512]{1,0:T(8,128)(2,1)}, u32[]{:S(2)}) copy-start(bf16[512,512]{1,0:T(8,128)(2,1)} %constant.25.clone.wave_ref) | copy-start | bytes 1572868
  16.6 11.1 %copy-start.3 = (f32[2,16,256]{2,1,0:T(8,128)S(1)}, f32[2,16,256]{2,1,0:T(8,128)}, u32[]{:S(2)}) copy-start(f32[2,16,256]{2,1,0:T(8,128)} %constant.24.clone.twist_ref) | copy-start | bytes 98308
  17.3 18.6 %copy-start = (bf16[512,512]{1,0:T(8,128)(2,1)S(1)}, bf16[512,512]{1,0:T(8,128)(2,1)}, u32[]{:S(2)}) copy-start(bf16[512,512]{1,0:T(8,128)(2,1)} %get-tuple-element.21.own_ref) | copy-start | bytes 1572868
  31.7 13.8 %all-to-all-start.1 = ((bf16[8,136,128]{2,1,0:T(8,128)(2,1)}), bf16[8,136,128]{2,1,0:T(8,128)(2,1)S(1)}, u32[]{:S(2)}, u32[]{:S(2)}) async-start(bf16[8,136,128]{2,1,0:T(8,128)(2,1)} %get-tuple-element.19), calls=%async_computation.1 | async-start | bytes 557056 | tf_op jit(solution)/shard_map/all_to_all | solution.py:607
  41.6 12.7 %copy-start.1 = (bf16[5,5,64,32]{2,3,1,0:T(8,128)(2,1)S(1)}, bf16[5,5,64,32]{2,3,1,0:T(8,128)(2,1)}, u32[]{:S(2)}) copy-start(bf16[5,5,64,32]{2,3,1,0:T(8,128)(2,1)} %param.7) | copy-start | bytes 307204
  47.1 5.1 %collective-permute-start.3 = (bf16[200,128]{1,0:T(8,128)(2,1)S(1)}, bf16[200,128]{1,0:T(8,128)(2,1)S(1)}, u32[]{:S(2)}, u32[]{:S(2)}) collective-permute-start(bf16[200,128]{1,0:T(8,128)(2,1)S(1)} %convert_element_type.24), channel_id=1, source_target_pairs={{0,6},{1,7},{2,4},{3,5},{4,2},{5,3},{6,0},{7,1},{8,14},{9,15},{10,... | collective-permute-start | bytes 153608 | tf_op jit(solution)/shard_map/ppermute | solution.py:520
  48.0 4.7 %collective-permute-start.2 = (bf16[200,128]{1,0:T(8,128)(2,1)S(1)}, bf16[200,128]{1,0:T(8,128)(2,1)S(1)}, u32[]{:S(2)}, u32[]{:S(2)}) collective-permute-start(bf16[200,128]{1,0:T(8,128)(2,1)S(1)} %convert_element_type.24), channel_id=1, source_target_pairs={{0,4},{1,5},{2,6},{3,7},{4,0},{5,1},{6,2},{7,3},{8,12},{9,13},{10,... | collective-permute-start | bytes 153608 | tf_op jit(solution)/shard_map/ppermute | solution.py:520
  50.0 4.1 %collective-permute-start.1 = (bf16[200,128]{1,0:T(8,128)(2,1)S(1)}, bf16[200,128]{1,0:T(8,128)(2,1)S(1)}, u32[]{:S(2)}, u32[]{:S(2)}) collective-permute-start(bf16[200,128]{1,0:T(8,128)(2,1)S(1)} %convert_element_type.24), channel_id=1, source_target_pairs={{0,2},{1,3},{2,0},{3,1},{4,6},{5,7},{6,4},{7,5},{8,10},{9,11},{10,... | collective-permute-start | bytes 153608 | tf_op jit(solution)/shard_map/ppermute | solution.py:520
  50.6 3.6 %collective-permute-start.4 = (bf16[256,384]{1,0:T(8,128)(2,1)S(1)}, bf16[256,384]{1,0:T(8,128)(2,1)S(1)}, u32[]{:S(2)}, u32[]{:S(2)}) collective-permute-start(bf16[256,384]{1,0:T(8,128)(2,1)S(1)} %get-tuple-element.26), channel_id=1, source_target_pairs={{0,1},{1,0},{2,3},{3,2},{4,5},{5,4},{6,7},{7,6},{8,9},{9,8},{10,11... | collective-permute-start | bytes 589832 | tf_op jit(solution)/shard_map/ppermute | solution.py:637
  54.2 5.1 %collective-permute-start.5 = (bf16[200,128]{1,0:T(8,128)(2,1)S(1)}, bf16[200,128]{1,0:T(8,128)(2,1)S(1)}, u32[]{:S(2)}, u32[]{:S(2)}) collective-permute-start(bf16[200,128]{1,0:T(8,128)(2,1)S(1)} %add_add_fusion), channel_id=1, source_target_pairs={{0,8},{1,9},{2,10},{3,11},{4,12},{5,13},{6,14},{7,15},{8,0},{9,1},... | collective-permute-start | bytes 153608 | tf_op jit(solution)/shard_map/ppermute | solution.py:520
  59.3 1.4 %collective-permute-start.6 = (f32[200,128]{1,0:T(8,128)S(1)}, f32[200,128]{1,0:T(8,128)S(1)}, u32[]{:S(2)}, u32[]{:S(2)}) collective-permute-start(f32[200,128]{1,0:T(8,128)S(1)} %convert_add_fusion), channel_id=1, source_target_pairs={{0,1},{1,0},{2,3},{3,2},{4,5},{5,4},{6,7},{7,6},{8,9},{9,8},{10,11... | collective-permute-start | bytes 307208 | tf_op jit(solution)/shard_map/ppermute | solution.py:656

commit v10 on v9

--- a/solution.py
+++ b/solution.py
@@ -96,7 +96,13 @@
     at_cot = pl.ds(conv_rows, conv_rows)
     cot_out = pltpu.make_async_copy(out_ref.at[:, at_cot], out_hbm.at[:, at_cot], sem.at[5])
     z_out = pltpu.make_async_copy(z_ref, z_hbm, sem.at[2])
-    conv_out = pltpu.make_async_copy(out_ref.at[:, at_conv], out_hbm.at[:, at_conv], sem.at[3])
+    half_count = count // 2
+    conv_outs = [
+        pltpu.make_async_copy(
+            out_ref.at[pl.ds(low, half_count), at_conv], out_hbm.at[pl.ds(low, half_count), at_conv], sem.at[at]
+        )
+        for at, low in ((3, 0), (6 + tiles_wide, half_count))
+    ]
     edge_out = pltpu.make_async_copy(out_ref.at[:, at_edge], out_hbm.at[:, at_edge], sem.at[4])
     taps_copy.start()
     sig_copy.start()
@@ -156,18 +162,22 @@
     edges = dot_nt(pick.astype(bf16), jnp.concatenate([own_rest, next_high, next_rest], axis=1))
     from_time = one_hot((k_out, k_out), lambda r: swapped(r, cout, tout))
     edges = dot_nt(edges.astype(bf16), from_time)
-    main = dot(from_time, high).astype(bf16)
     for d in range(count):
-        for b in range(tiles_wide):
-            at = slice(lanes * b, lanes * (b + 1))
-            out_ref[d, rows * b : rows * (b + 1)] = main[rows * d : rows * (d + 1), at]
         out_ref[d, 2 * conv_rows :] = jnp.zeros((edge_rows, lanes), bf16)
         out_ref[d, 2 * conv_rows :, :rows] = edges[:, rows * d : rows * (d + 1)].astype(bf16)
-    conv_out.start()
     edge_out.start()
+    for part, conv_out in enumerate(conv_outs):
+        low = half_count * part
+        main = dot(from_time[rows * low : rows * (low + half_count)], high).astype(bf16)
+        for d in range(half_count):
+            for b in range(tiles_wide):
+                at = slice(lanes * b, lanes * (b + 1))
+                out_ref[low + d, rows * b : rows * (b + 1)] = main[rows * d : rows * (d + 1), at]
+        conv_out.start()
     cot_out.wait()
     z_out.wait()
-    conv_out.wait()
+    for conv_out in conv_outs:
+        conv_out.wait()
     edge_out.wait()
 
 
@@ -416,16 +426,19 @@
         block_ref[:, :width] = inner
         block_ref[:, width:] = jnp.where((lane == 0) | (lane == lanes - 1), edge, 0.0).astype(bf16)
     blank = jnp.zeros((lanes - 3 * some, wide), bf16)
-    total = None
-    for t in range(tout):
-        at = slice(some * t, some * (t + 1))
-        band = slice(2 * cin * t, 2 * cin * t + ks * cin)
-        taken = jnp.concatenate([shifted_ref[shift, at] for shift in range(3)] + [blank], axis=0)
+    size, reach = ks * cin, (ks + 2) * cin
+    even, odd = None, None
+    for t in range(0, tout, 2):
+        band = slice(2 * cin * t, 2 * cin * t + reach)
+        taken = []
+        for at in (slice(some * t, some * (t + 1)), slice(some * (t + 1), some * (t + 2))):
+            taken += [shifted_ref[shift, at] for shift in range(3)] + [blank]
         samples = jnp.concatenate([z_ref[band, :wide], z_ref[band, wide:]], axis=0)
-        term = dot_nt(samples, taken)
-        total = term if total is None else total + term
-    size = ks * cin
-    even, odd = total[:size], total[size:]
+        both = dot_nt(samples, jnp.concatenate(taken, axis=0))
+        first = both[:size, :lanes] + both[reach - size : reach, lanes:]
+        second = both[reach : reach + size, :lanes] + both[2 * reach - size :, lanes:]
+        even = first if even is None else even + first
+        odd = second if odd is None else odd + second
     tap_ref[:size] = jnp.where(iota((size, lanes), 1) < 3 * some, even, pltpu.roll(odd, 3 * some, 1))
     fold = size * some // lanes
     folded = jnp.zeros((fold, lanes), f32)
@@ -566,7 +579,7 @@
             pltpu.VMEM(taps.shape, bf16),
             pltpu.VMEM((count, 2 * rows * tiles + edge_rows, lanes), bf16),
             pltpu.VMEM((k_in, fibre_in), bf16),
-            pltpu.SemaphoreType.DMA((6 + tiles,)),
+            pltpu.SemaphoreType.DMA((7 + tiles,)),
         ],
         2e9,
         (signal.reshape(k_in, fibre_in), cotangent.reshape(count, rows, width), taps),

time: 62.2 us -> 61.8 us (level)
  no operation moved by 1% of the time
where the time goes in v10:
time: 61.8 us; the launch traced here: 61.4 us
  waiting for transfers between devices  20.5 us (33%)
  Pallas kernels  16.4 us (27%)
  starting transfers between devices  15.6 us (25%)
  local copies, waits for them, and re-layouts  7.82 us (13%)
  between operations  0.85 us (1%)
    pallas_call x7, Pallas kernels, call(): pl.pallas_call(kernel, out_shape=outs, in_specs=[pl.BlockSpec(memory_spac...  16.4 us
    all_to_all x1, waiting for transfers between devices, per_device(): lax.all_to_all(conv_part, 'fibre', split_axis=0, concat_axis=0, tiled=True)  10.3 us
    all_to_all x1, starting transfers between devices, per_device(): lax.all_to_all(conv_part, 'fibre', split_axis=0, concat_axis=0, tiled=True)  7.4 us
    ppermute x4, waiting for transfers between devices, summed_over_chips(): lax.ppermute(rounded, axis, partners(count, step)).astype(f32)  4.87 us
    all_to_all x1, starting transfers between devices, per_device(): lax.all_to_all(grad_part, 'fibre', split_axis=0, concat_axis=0, tiled=Tru...  4.12 us
    all_to_all x1, waiting for transfers between devices, per_device(): lax.all_to_all(grad_part, 'fibre', split_axis=0, concat_axis=0, tiled=Tru...  3.98 us
    ppermute x4, starting transfers between devices, summed_over_chips(): lax.ppermute(rounded, axis, partners(count, step)).astype(f32)  3.62 us
    unnamed x12, local copies, waits for them, and re-layouts  3.04 us
  transfers between devices with their start and end apart: 9, of which 7 were waited for; matrix products, arithmetic and copies ran while one was open for 13% of the time, Pallas kernels for 16%

profile of v10, /device:TPU:0, one launch (start us, length us, event | category | flops | bytes accessed | tf_op | source)
XLA Modules:
  0.0 61.4 jit_solution(13818496795301802236)
XLA Ops:
  0.6 0.0 copy-start.4
  0.6 4.3 %shard_map.85 = (bf16[16,136,128]{2,1,0:T(8,128)(2,1)}, bf16[512,512]{1,0:T(8,128)(2,1)}) custom-call(bf16[512,512]{1,0:T(8,128)(2,1)} %bitcast.17, bf16[16,32,256]{2,1,0:T(8,128)(2,1)} %bitcast.18, bf16[5,5,32,64]{3,2,1,0:T(8,128)(2,1)} %bitcast.13), custom_call_target="tpu_custom_call" | custom-call | flops 2000000000 | bytes 1970176 | tf_op jit(solution)/shard_map/pallas_call | solution.py:58
  5.0 0.0 slice-start
  5.0 7.4 %all-to-all-start = ((bf16[16,136,128]{2,1,0:T(8,128)(2,1)}), bf16[16,136,128]{2,1,0:T(8,128)(2,1)S(1)}, u32[]{:S(2)}, u32[]{:S(2)}) async-start(bf16[16,136,128]{2,1,0:T(8,128)(2,1)} %get-tuple-element.18), calls=%async_computation | async-start | bytes 1114112 | tf_op jit(solution)/shard_map/all_to_all | solution.py:591
  12.4 0.4 collective-permute-start
  12.8 0.0 copy-done.4
  12.8 0.1 slice.26
  12.9 2.9 %reverse.2 = f32[2,4,4096]{2,1,0:T(4,128)S(1)} reverse(f32[2,4,4096]{2,1,0:T(4,128)S(1)} %bitcast.15), dimensions={2} | reverse | bytes 262144
  15.8 0.1 slice.43
  16.0 0.0 slice-done
  16.0 0.1 fusion.2
  16.1 0.2 stack.10
  16.3 0.0 copy-start.2
  16.3 0.0 copy-start.3
  16.3 0.2 copy.14
  16.5 0.2 stack.9
  16.7 0.2 copy.13
  16.9 0.1 copy.15
  17.1 0.0 copy-start
  17.1 10.3 %all-to-all-done.cols_ref = bf16[16,136,128]{2,1,0:T(8,128)(2,1)S(1)} async-done(((bf16[16,136,128]{2,1,0:T(8,128)(2,1)}), bf16[16,136,128]{2,1,0:T(8,128)(2,1)S(1)}, u32[]{:S(2)}, u32[]{:S(2)}) %all-to-all-start) | async-done | bytes 557088 | tf_op jit(solution)/shard_map/all_to_all | solution.py:591
  27.4 0.0 copy-done.2
  27.4 0.0 copy-done.3
  27.4 4.1 %shard_map.86 = (bf16[8,136,128]{2,1,0:T(8,128)(2,1)}, f32[64,512]{1,0:T(8,128)S(1)}) custom-call(bf16[16,136,128]{2,1,0:T(8,128)(2,1)S(1)} %all-to-all-done.cols_ref, f32[2,64,256]{2,1,0:T(8,128)S(1)} %reshape.30.own_ref, f32[2,16,256]{2,1,0:T(8,128)S(1)} %copy-done.3, bf16[512,512]{1,0:T(8,128)(2,1)S(1)} %copy-done.2), custom_call_target="tpu_custom_call" | custom-call | flops 6000000000 | bytes 1654784 | tf_op jit(solution)/shard_map/pallas_call | solution.py:58
  31.5 4.1 %all-to-all-start.1 = ((bf16[8,136,128]{2,1,0:T(8,128)(2,1)}), bf16[8,136,128]{2,1,0:T(8,128)(2,1)S(1)}, u32[]{:S(2)}, u32[]{:S(2)}) async-start(bf16[8,136,128]{2,1,0:T(8,128)(2,1)} %get-tuple-element.19), calls=%async_computation.1 | async-start | bytes 557056 | tf_op jit(solution)/shard_map/all_to_all | solution.py:620
  35.6 0.0 collective-permute-done.other_ref
  35.6 0.0 copy-done
  35.7 0.1 shard_map.88.z_ref
  35.8 1.8 %shard_map.87 = f32[2,4,16,256]{3,2,1,0:T(8,128)S(1)} custom-call(f32[64,512]{1,0:T(8,128)S(1)} %get-tuple-element.20.cross_ref), custom_call_target="tpu_custom_call" | custom-call | flops 1000000 | bytes 262144 | tf_op jit(solution)/shard_map/pallas_call | solution.py:58
  37.6 1.3 %copy.16 = f32[2,4,256,16]{3,2,1,0:T(8,128)} copy(f32[2,4,256,16]{2,3,1,0:T(8,128)S(1)} %bitcast.12) | data formatting | bytes 262144 | tf_op jit(solution)/shard_map/transpose | solution.py:618
  38.9 2.4 %reshape.31 = f32[2,4,4096]{2,1,0:T(4,128)} reshape(f32[2,4,256,16]{3,2,1,0:T(8,128)} %copy.16) | data formatting | bytes 262144 | tf_op jit(solution)/shard_map/reshape | solution.py:618
  41.3 0.0 copy-start.1
  41.3 4.0 %all-to-all-done.1.grad_ref = bf16[8,136,128]{2,1,0:T(8,128)(2,1)S(1)} async-done(((bf16[8,136,128]{2,1,0:T(8,128)(2,1)}), bf16[8,136,128]{2,1,0:T(8,128)(2,1)S(1)}, u32[]{:S(2)}, u32[]{:S(2)}) %all-to-all-start.1) | async-done | bytes 278560 | tf_op jit(solution)/shard_map/all_to_all | solution.py:620
  45.3 1.3 %shard_map.89 = (f32[200,128]{1,0:T(8,128)S(1)}, bf16[256,384]{1,0:T(8,128)(2,1)S(1)}, bf16[256,384]{1,0:T(8,128)(2,1)S(1)}) custom-call(s32[1]{0:T(128)} %bitcast.core_ref, bf16[8,136,128]{2,1,0:T(8,128)(2,1)S(1)} %all-to-all-done.1.grad_ref, bf16[640,1024]{1,0:T(8,128)(2,1)S(1)} %shard_map.88.z_ref), custom_call_target="tpu_custom_call" | custom-call | flops 1000000000 | bytes 2084868 | tf_op jit(solution)/shard_map/pallas_call | solution.py:58
  46.6 0.9 %collective-permute-start.3 = (bf16[200,128]{1,0:T(8,128)(2,1)S(1)}, bf16[200,128]{1,0:T(8,128)(2,1)S(1)}, u32[]{:S(2)}, u32[]{:S(2)}) collective-permute-start(bf16[200,128]{1,0:T(8,128)(2,1)S(1)} %convert_element_type.24), channel_id=1, source_target_pairs={{0,6},{1,7},{2,4},{3,5},{4,2},{5,3},{6,0},{7,1},{8,14},{9,15},{10,... | collective-permute-start | bytes 153608 | tf_op jit(solution)/shard_map/ppermute | solution.py:533
  47.6 2.0 %collective-permute-start.2 = (bf16[200,128]{1,0:T(8,128)(2,1)S(1)}, bf16[200,128]{1,0:T(8,128)(2,1)S(1)}, u32[]{:S(2)}, u32[]{:S(2)}) collective-permute-start(bf16[200,128]{1,0:T(8,128)(2,1)S(1)} %convert_element_type.24), channel_id=1, source_target_pairs={{0,4},{1,5},{2,6},{3,7},{4,0},{5,1},{6,2},{7,3},{8,12},{9,13},{10,... | collective-permute-start | bytes 153608 | tf_op jit(solution)/shard_map/ppermute | solution.py:533
  49.6 0.6 collective-permute-start.1
  50.2 0.0 collective-permute-start.4
  50.2 1.5 %collective-permute-done.3 = bf16[200,128]{1,0:T(8,128)(2,1)S(1)} collective-permute-done((bf16[200,128]{1,0:T(8,128)(2,1)S(1)}, bf16[200,128]{1,0:T(8,128)(2,1)S(1)}, u32[]{:S(2)}, u32[]{:S(2)}) %collective-permute-start.3) | collective-permute-done | bytes 51232 | tf_op jit(solution)/shard_map/ppermute | solution.py:533
  51.7 0.6 collective-permute-done.2
  52.2 1.5 %collective-permute-done.1 = bf16[200,128]{1,0:T(8,128)(2,1)S(1)} collective-permute-done((bf16[200,128]{1,0:T(8,128)(2,1)S(1)}, bf16[200,128]{1,0:T(8,128)(2,1)S(1)}, u32[]{:S(2)}, u32[]{:S(2)}) %collective-permute-start.1) | collective-permute-done | bytes 51232 | tf_op jit(solution)/shard_map/ppermute | solution.py:533
  53.8 0.0 collective-permute-done.4.other_ref
  53.8 0.1 collective-permute-start.5
  53.8 0.0 copy-done.1
  53.9 3.7 %shard_map.90 = bf16[512,512]{1,0:T(8,128)(2,1)} custom-call(s32[1]{0:T(128)} %bitcast.core_ref, bf16[256,384]{1,0:T(8,128)(2,1)S(1)} %get-tuple-element.28.own_ref, bf16[256,384]{1,0:T(8,128)(2,1)S(1)} %collective-permute-done.4.other_ref, bf16[5,5,32,64]{3,2,1,0:T(8,128)(2,1)S(1)} %bitcast.14), custom_call_target="tpu_custom_call" | custom-call | flops 2000000000 | bytes 1019908 | tf_op jit(solution)/shard_map/pallas_call | solution.py:58
  57.5 1.3 %collective-permute-done.5 = bf16[200,128]{1,0:T(8,128)(2,1)S(1)} collective-permute-done((bf16[200,128]{1,0:T(8,128)(2,1)S(1)}, bf16[200,128]{1,0:T(8,128)(2,1)S(1)}, u32[]{:S(2)}, u32[]{:S(2)}) %collective-permute-start.5) | collective-permute-done | bytes 51232 | tf_op jit(solution)/shard_map/ppermute | solution.py:533
  58.9 0.1 collective-permute-start.6
  58.9 1.3 %collective-permute-done.6 = f32[200,128]{1,0:T(8,128)S(1)} collective-permute-done((f32[200,128]{1,0:T(8,128)S(1)}, f32[200,128]{1,0:T(8,128)S(1)}, u32[]{:S(2)}, u32[]{:S(2)}) %collective-permute-start.6) | collective-permute-done | bytes 102432 | tf_op jit(solution)/shard_map/ppermute | solution.py:669
  60.3 1.1 %shard_map.91 = f32[5,5,32,64]{3,2,1,0:T(8,128)} custom-call(f32[400,128]{1,0:T(8,128)S(1)} %maximum_select_fusion.tap_ref), custom_call_target="tpu_custom_call" | custom-call | flops 1000000 | bytes 409600 | tf_op jit(solution)/shard_map/pallas_call | solution.py:58
  (6 shorter events, 0.1 us)
Async XLA Ops:
  0.6 12.2 %copy-start.4 = (f32[2,4,4096]{2,1,0:T(4,128)S(1)}, f32[2,4,4096]{2,1,0:T(4,128)}, u32[]{:S(2)}) copy-start(f32[2,4,4096]{2,1,0:T(4,128)} %param.8) | copy-start | bytes 393220
  5.0 11.0 %slice-start = ((f32[2,4,4096]{2,1,0:T(4,128)}), f32[2,4,1]{2,1,0:T(4,128)S(1)}, s32[]{:S(2)}) async-start(f32[2,4,4096]{2,1,0:T(4,128)} %param.8), calls=%async_computation.2 | async-start | bytes 8192 | tf_op jit(solution)/shard_map/jit(_roll_static)/slice | solution.py:544
  5.0 22.4 %all-to-all-start = ((bf16[16,136,128]{2,1,0:T(8,128)(2,1)}), bf16[16,136,128]{2,1,0:T(8,128)(2,1)S(1)}, u32[]{:S(2)}, u32[]{:S(2)}) async-start(bf16[16,136,128]{2,1,0:T(8,128)(2,1)} %get-tuple-element.18), calls=%async_computation | async-start | bytes 1114112 | tf_op jit(solution)/shard_map/all_to_all | solution.py:591
  12.4 23.2 %collective-permute-start = (bf16[512,512]{1,0:T(8,128)(2,1)}, bf16[512,512]{1,0:T(8,128)(2,1)S(1)}, u32[]{:S(2)}, u32[]{:S(2)}) collective-permute-start(bf16[512,512]{1,0:T(8,128)(2,1)} %get-tuple-element.21.own_ref), channel_id=1, source_target_pairs={{0,1},{1,0},{2,3},{3,2},{4,5},{5,4},{6,7},{7,6},{8,9},{9,8},{10,11... | collective-permute-start | bytes 1572872 | tf_op jit(solution)/shard_map/ppermute | solution.py:590
  16.3 11.1 %copy-start.2 = (bf16[512,512]{1,0:T(8,128)(2,1)S(1)}, bf16[512,512]{1,0:T(8,128)(2,1)}, u32[]{:S(2)}) copy-start(bf16[512,512]{1,0:T(8,128)(2,1)} %constant.25.clone.wave_ref) | copy-start | bytes 1572868
  16.3 11.1 %copy-start.3 = (f32[2,16,256]{2,1,0:T(8,128)S(1)}, f32[2,16,256]{2,1,0:T(8,128)}, u32[]{:S(2)}) copy-start(f32[2,16,256]{2,1,0:T(8,128)} %constant.24.clone.twist_ref) | copy-start | bytes 98308
  17.1 18.6 %copy-start = (bf16[512,512]{1,0:T(8,128)(2,1)S(1)}, bf16[512,512]{1,0:T(8,128)(2,1)}, u32[]{:S(2)}) copy-start(bf16[512,512]{1,0:T(8,128)(2,1)} %get-tuple-element.21.own_ref) | copy-start | bytes 1572868
  31.5 13.8 %all-to-all-start.1 = ((bf16[8,136,128]{2,1,0:T(8,128)(2,1)}), bf16[8,136,128]{2,1,0:T(8,128)(2,1)S(1)}, u32[]{:S(2)}, u32[]{:S(2)}) async-start(bf16[8,136,128]{2,1,0:T(8,128)(2,1)} %get-tuple-element.19), calls=%async_computation.1 | async-start | bytes 557056 | tf_op jit(solution)/shard_map/all_to_all | solution.py:620
  41.3 12.5 %copy-start.1 = (bf16[5,5,64,32]{2,3,1,0:T(8,128)(2,1)S(1)}, bf16[5,5,64,32]{2,3,1,0:T(8,128)(2,1)}, u32[]{:S(2)}) copy-start(bf16[5,5,64,32]{2,3,1,0:T(8,128)(2,1)} %param.7) | copy-start | bytes 307204
  46.6 5.1 %collective-permute-start.3 = (bf16[200,128]{1,0:T(8,128)(2,1)S(1)}, bf16[200,128]{1,0:T(8,128)(2,1)S(1)}, u32[]{:S(2)}, u32[]{:S(2)}) collective-permute-start(bf16[200,128]{1,0:T(8,128)(2,1)S(1)} %convert_element_type.24), channel_id=1, source_target_pairs={{0,6},{1,7},{2,4},{3,5},{4,2},{5,3},{6,0},{7,1},{8,14},{9,15},{10,... | collective-permute-start | bytes 153608 | tf_op jit(solution)/shard_map/ppermute | solution.py:533
  47.6 4.7 %collective-permute-start.2 = (bf16[200,128]{1,0:T(8,128)(2,1)S(1)}, bf16[200,128]{1,0:T(8,128)(2,1)S(1)}, u32[]{:S(2)}, u32[]{:S(2)}) collective-permute-start(bf16[200,128]{1,0:T(8,128)(2,1)S(1)} %convert_element_type.24), channel_id=1, source_target_pairs={{0,4},{1,5},{2,6},{3,7},{4,0},{5,1},{6,2},{7,3},{8,12},{9,13},{10,... | collective-permute-start | bytes 153608 | tf_op jit(solution)/shard_map/ppermute | solution.py:533
  49.6 4.1 %collective-permute-start.1 = (bf16[200,128]{1,0:T(8,128)(2,1)S(1)}, bf16[200,128]{1,0:T(8,128)(2,1)S(1)}, u32[]{:S(2)}, u32[]{:S(2)}) collective-permute-start(bf16[200,128]{1,0:T(8,128)(2,1)S(1)} %convert_element_type.24), channel_id=1, source_target_pairs={{0,2},{1,3},{2,0},{3,1},{4,6},{5,7},{6,4},{7,5},{8,10},{9,11},{10,... | collective-permute-start | bytes 153608 | tf_op jit(solution)/shard_map/ppermute | solution.py:533
  50.2 3.6 %collective-permute-start.4 = (bf16[256,384]{1,0:T(8,128)(2,1)S(1)}, bf16[256,384]{1,0:T(8,128)(2,1)S(1)}, u32[]{:S(2)}, u32[]{:S(2)}) collective-permute-start(bf16[256,384]{1,0:T(8,128)(2,1)S(1)} %get-tuple-element.26), channel_id=1, source_target_pairs={{0,1},{1,0},{2,3},{3,2},{4,5},{5,4},{6,7},{7,6},{8,9},{9,8},{10,11... | collective-permute-start | bytes 589832 | tf_op jit(solution)/shard_map/ppermute | solution.py:650
  53.8 5.1 %collective-permute-start.5 = (bf16[200,128]{1,0:T(8,128)(2,1)S(1)}, bf16[200,128]{1,0:T(8,128)(2,1)S(1)}, u32[]{:S(2)}, u32[]{:S(2)}) collective-permute-start(bf16[200,128]{1,0:T(8,128)(2,1)S(1)} %add_add_fusion), channel_id=1, source_target_pairs={{0,8},{1,9},{2,10},{3,11},{4,12},{5,13},{6,14},{7,15},{8,0},{9,1},... | collective-permute-start | bytes 153608 | tf_op jit(solution)/shard_map/ppermute | solution.py:533
  58.9 1.4 %collective-permute-start.6 = (f32[200,128]{1,0:T(8,128)S(1)}, f32[200,128]{1,0:T(8,128)S(1)}, u32[]{:S(2)}, u32[]{:S(2)}) collective-permute-start(f32[200,128]{1,0:T(8,128)S(1)} %convert_add_fusion), channel_id=1, source_target_pairs={{0,1},{1,0},{2,3},{3,2},{4,5},{5,4},{6,7},{7,6},{8,9},{9,8},{10,11... | collective-permute-start | bytes 307208 | tf_op jit(solution)/shard_map/ppermute | solution.py:669

commit v11 on v10

--- a/solution.py
+++ b/solution.py
@@ -649,10 +649,8 @@
     )
     got = lax.ppermute(send, "fibre", partners(count, 1))
     chips = count // cores
-    step = 4 if chips % 4 == 0 else 1
-    total = taps_part
-    if step == 4:
-        total = summed_over_chips(total, "fibre", (cores, 2 * cores, 3 * cores))
+    total = summed_over_chips(taps_part, "fibre", (cores,))
+    step = 2
     total, keep, got = lax.optimization_barrier((total, keep, got))
     (input_grad,) = call(
         functools.partial(input_kernel, dims),
@@ -662,6 +660,9 @@
         (core, keep, got, taps),
         small=(0,),
     )
+    if chips % 8 == 0:
+        total = summed_over_chips(total, "fibre", (2 * cores, 4 * cores, 6 * cores))
+        step = 8
     while step < chips:
         total = summed_over_chips(total, "fibre", (cores * step,))
         step *= 2

time: 61.8 us -> 61.9 us (level)
  starting transfers between devices: 15.6 us -> 18 us
  waiting for transfers between devices: 20.5 us -> 18.2 us
    ppermute x4, starting transfers between devices: 3.62 us -> 5.99 us  [summed_over_chips(): lax.ppermute(rounded, axis, partners(count, step)).astype(f32)]
    ppermute x4, waiting for transfers between devices: 4.87 us -> 2.65 us  [summed_over_chips(): lax.ppermute(rounded, axis, partners(count, step)).astype(f32)]
  transfers between devices with their start and end apart: 9 -> 9, of which waited for: 7 -> 4; matrix products, arithmetic and copies ran while one was open for 13% -> 13% of each run, Pallas kernels for 16% -> 16%
where the time goes in v11:
time: 61.9 us; the launch traced here: 61.5 us
  waiting for transfers between devices  18.2 us (29%)
  starting transfers between devices  18 us (29%)
  Pallas kernels  16.4 us (26%)
  local copies, waits for them, and re-layouts  7.82 us (13%)
  between operations  0.84 us (1%)
    pallas_call x7, Pallas kernels, call(): pl.pallas_call(kernel, out_shape=outs, in_specs=[pl.BlockSpec(memory_spac...  16.4 us
    all_to_all x1, waiting for transfers between devices, per_device(): lax.all_to_all(conv_part, 'fibre', split_axis=0, concat_axis=0, tiled=True)  10.3 us
    all_to_all x1, starting transfers between devices, per_device(): lax.all_to_all(conv_part, 'fibre', split_axis=0, concat_axis=0, tiled=True)  7.4 us
    ppermute x4, starting transfers between devices, summed_over_chips(): lax.ppermute(rounded, axis, partners(count, step)).astype(f32)  5.99 us
    all_to_all x1, starting transfers between devices, per_device(): lax.all_to_all(grad_part, 'fibre', split_axis=0, concat_axis=0, tiled=Tru...  4.12 us
    all_to_all x1, waiting for transfers between devices, per_device(): lax.all_to_all(grad_part, 'fibre', split_axis=0, concat_axis=0, tiled=Tru...  3.98 us
    unnamed x12, local copies, waits for them, and re-layouts  3.04 us
    ppermute x4, waiting for transfers between devices, summed_over_chips(): lax.ppermute(rounded, axis, partners(count, step)).astype(f32)  2.65 us
  transfers between devices with their start and end apart: 9, of which 4 were waited for; matrix products, arithmetic and copies ran while one was open for 13% of the time, Pallas kernels for 16%

profile of v11, /device:TPU:0, one launch (start us, length us, event | category | flops | bytes accessed | tf_op | source)
XLA Modules:
  0.0 61.5 jit_solution(14977906490101016214)
XLA Ops:
  0.6 0.0 copy-start.4
  0.6 4.3 %shard_map.85 = (bf16[16,136,128]{2,1,0:T(8,128)(2,1)}, bf16[512,512]{1,0:T(8,128)(2,1)}) custom-call(bf16[512,512]{1,0:T(8,128)(2,1)} %bitcast.17, bf16[16,32,256]{2,1,0:T(8,128)(2,1)} %bitcast.18, bf16[5,5,32,64]{3,2,1,0:T(8,128)(2,1)} %bitcast.13), custom_call_target="tpu_custom_call" | custom-call | flops 2000000000 | bytes 1970176 | tf_op jit(solution)/shard_map/pallas_call | solution.py:58
  5.0 0.0 slice-start
  5.0 7.4 %all-to-all-start = ((bf16[16,136,128]{2,1,0:T(8,128)(2,1)}), bf16[16,136,128]{2,1,0:T(8,128)(2,1)S(1)}, u32[]{:S(2)}, u32[]{:S(2)}) async-start(bf16[16,136,128]{2,1,0:T(8,128)(2,1)} %get-tuple-element.18), calls=%async_computation | async-start | bytes 1114112 | tf_op jit(solution)/shard_map/all_to_all | solution.py:591
  12.4 0.4 collective-permute-start
  12.8 0.0 copy-done.4
  12.8 0.1 slice.26
  12.9 2.9 %reverse.2 = f32[2,4,4096]{2,1,0:T(4,128)S(1)} reverse(f32[2,4,4096]{2,1,0:T(4,128)S(1)} %bitcast.15), dimensions={2} | reverse | bytes 262144
  15.8 0.1 slice.43
  16.0 0.0 slice-done
  16.0 0.1 fusion.2
  16.1 0.2 stack.10
  16.3 0.0 copy-start.2
  16.3 0.0 copy-start.3
  16.3 0.2 copy.14
  16.5 0.2 stack.9
  16.7 0.2 copy.13
  16.9 0.1 copy.15
  17.1 0.0 copy-start
  17.1 10.3 %all-to-all-done.cols_ref = bf16[16,136,128]{2,1,0:T(8,128)(2,1)S(1)} async-done(((bf16[16,136,128]{2,1,0:T(8,128)(2,1)}), bf16[16,136,128]{2,1,0:T(8,128)(2,1)S(1)}, u32[]{:S(2)}, u32[]{:S(2)}) %all-to-all-start) | async-done | bytes 557088 | tf_op jit(solution)/shard_map/all_to_all | solution.py:591
  27.4 0.0 copy-done.2
  27.4 0.0 copy-done.3
  27.4 4.1 %shard_map.86 = (bf16[8,136,128]{2,1,0:T(8,128)(2,1)}, f32[64,512]{1,0:T(8,128)S(1)}) custom-call(bf16[16,136,128]{2,1,0:T(8,128)(2,1)S(1)} %all-to-all-done.cols_ref, f32[2,64,256]{2,1,0:T(8,128)S(1)} %reshape.30.own_ref, f32[2,16,256]{2,1,0:T(8,128)S(1)} %copy-done.3, bf16[512,512]{1,0:T(8,128)(2,1)S(1)} %copy-done.2), custom_call_target="tpu_custom_call" | custom-call | flops 6000000000 | bytes 1654784 | tf_op jit(solution)/shard_map/pallas_call | solution.py:58
  31.5 4.1 %all-to-all-start.1 = ((bf16[8,136,128]{2,1,0:T(8,128)(2,1)}), bf16[8,136,128]{2,1,0:T(8,128)(2,1)S(1)}, u32[]{:S(2)}, u32[]{:S(2)}) async-start(bf16[8,136,128]{2,1,0:T(8,128)(2,1)} %get-tuple-element.19), calls=%async_computation.1 | async-start | bytes 557056 | tf_op jit(solution)/shard_map/all_to_all | solution.py:620
  35.6 0.0 collective-permute-done.other_ref
  35.6 0.0 copy-done
  35.7 0.1 shard_map.88.z_ref
  35.8 1.8 %shard_map.87 = f32[2,4,16,256]{3,2,1,0:T(8,128)S(1)} custom-call(f32[64,512]{1,0:T(8,128)S(1)} %get-tuple-element.20.cross_ref), custom_call_target="tpu_custom_call" | custom-call | flops 1000000 | bytes 262144 | tf_op jit(solution)/shard_map/pallas_call | solution.py:58
  37.6 1.3 %copy.16 = f32[2,4,256,16]{3,2,1,0:T(8,128)} copy(f32[2,4,256,16]{2,3,1,0:T(8,128)S(1)} %bitcast.12) | data formatting | bytes 262144 | tf_op jit(solution)/shard_map/transpose | solution.py:618
  38.9 2.4 %reshape.31 = f32[2,4,4096]{2,1,0:T(4,128)} reshape(f32[2,4,256,16]{3,2,1,0:T(8,128)} %copy.16) | data formatting | bytes 262144 | tf_op jit(solution)/shard_map/reshape | solution.py:618
  41.3 0.0 copy-start.1
  41.3 4.0 %all-to-all-done.1.grad_ref = bf16[8,136,128]{2,1,0:T(8,128)(2,1)S(1)} async-done(((bf16[8,136,128]{2,1,0:T(8,128)(2,1)}), bf16[8,136,128]{2,1,0:T(8,128)(2,1)S(1)}, u32[]{:S(2)}, u32[]{:S(2)}) %all-to-all-start.1) | async-done | bytes 278560 | tf_op jit(solution)/shard_map/all_to_all | solution.py:620
  45.3 1.3 %shard_map.89 = (f32[200,128]{1,0:T(8,128)S(1)}, bf16[256,384]{1,0:T(8,128)(2,1)S(1)}, bf16[256,384]{1,0:T(8,128)(2,1)S(1)}) custom-call(s32[1]{0:T(128)} %bitcast.core_ref, bf16[8,136,128]{2,1,0:T(8,128)(2,1)S(1)} %all-to-all-done.1.grad_ref, bf16[640,1024]{1,0:T(8,128)(2,1)S(1)} %shard_map.88.z_ref), custom_call_target="tpu_custom_call" | custom-call | flops 1000000000 | bytes 2084868 | tf_op jit(solution)/shard_map/pallas_call | solution.py:58
  46.6 1.5 %collective-permute-start.1 = (bf16[200,128]{1,0:T(8,128)(2,1)S(1)}, bf16[200,128]{1,0:T(8,128)(2,1)S(1)}, u32[]{:S(2)}, u32[]{:S(2)}) collective-permute-start(bf16[200,128]{1,0:T(8,128)(2,1)S(1)} %convert_element_type.24), channel_id=1, source_target_pairs={{0,2},{1,3},{2,0},{3,1},{4,6},{5,7},{6,4},{7,5},{8,10},{9,11},{10,... | collective-permute-start | bytes 153608 | tf_op jit(solution)/shard_map/ppermute | solution.py:533
  48.1 0.0 collective-permute-start.2
  48.1 2.6 %collective-permute-done.1 = bf16[200,128]{1,0:T(8,128)(2,1)S(1)} collective-permute-done((bf16[200,128]{1,0:T(8,128)(2,1)S(1)}, bf16[200,128]{1,0:T(8,128)(2,1)S(1)}, u32[]{:S(2)}, u32[]{:S(2)}) %collective-permute-start.1) | collective-permute-done | bytes 51232 | tf_op jit(solution)/shard_map/ppermute | solution.py:533
  50.8 0.0 collective-permute-done.2.other_ref
  50.8 1.2 %collective-permute-start.5 = (bf16[200,128]{1,0:T(8,128)(2,1)S(1)}, bf16[200,128]{1,0:T(8,128)(2,1)S(1)}, u32[]{:S(2)}, u32[]{:S(2)}) collective-permute-start(bf16[200,128]{1,0:T(8,128)(2,1)S(1)} %convert_add_fusion), channel_id=1, source_target_pairs={{0,12},{1,13},{2,14},{3,15},{4,8},{5,9},{6,10},{7,11},{8,4},{9,5},... | collective-permute-start | bytes 153608 | tf_op jit(solution)/shard_map/ppermute | solution.py:533
  52.1 1.4 %collective-permute-start.4 = (bf16[200,128]{1,0:T(8,128)(2,1)S(1)}, bf16[200,128]{1,0:T(8,128)(2,1)S(1)}, u32[]{:S(2)}, u32[]{:S(2)}) collective-permute-start(bf16[200,128]{1,0:T(8,128)(2,1)S(1)} %convert_add_fusion), channel_id=1, source_target_pairs={{0,8},{1,9},{2,10},{3,11},{4,12},{5,13},{6,14},{7,15},{8,0},{9,1},... | collective-permute-start | bytes 153608 | tf_op jit(solution)/shard_map/ppermute | solution.py:533
  53.4 1.8 %collective-permute-start.3 = (bf16[200,128]{1,0:T(8,128)(2,1)S(1)}, bf16[200,128]{1,0:T(8,128)(2,1)S(1)}, u32[]{:S(2)}, u32[]{:S(2)}) collective-permute-start(bf16[200,128]{1,0:T(8,128)(2,1)S(1)} %convert_add_fusion), channel_id=1, source_target_pairs={{0,4},{1,5},{2,6},{3,7},{4,0},{5,1},{6,2},{7,3},{8,12},{9,13},{10,... | collective-permute-start | bytes 153608 | tf_op jit(solution)/shard_map/ppermute | solution.py:533
  55.3 0.0 copy-done.1
  55.3 3.7 %shard_map.90 = bf16[512,512]{1,0:T(8,128)(2,1)} custom-call(s32[1]{0:T(128)} %bitcast.core_ref, bf16[256,384]{1,0:T(8,128)(2,1)S(1)} %get-tuple-element.28.own_ref, bf16[256,384]{1,0:T(8,128)(2,1)S(1)} %collective-permute-done.2.other_ref, bf16[5,5,32,64]{3,2,1,0:T(8,128)(2,1)S(1)} %bitcast.14), custom_call_target="tpu_custom_call" | custom-call | flops 2000000000 | bytes 1019908 | tf_op jit(solution)/shard_map/pallas_call | solution.py:58
  58.9 0.0 collective-permute-done.5
  58.9 0.0 collective-permute-done.4
  58.9 0.0 collective-permute-done.3
  59.0 0.1 collective-permute-start.6
  59.1 1.3 %collective-permute-done.6 = f32[200,128]{1,0:T(8,128)S(1)} collective-permute-done((f32[200,128]{1,0:T(8,128)S(1)}, f32[200,128]{1,0:T(8,128)S(1)}, u32[]{:S(2)}, u32[]{:S(2)}) %collective-permute-start.6) | collective-permute-done | bytes 102432 | tf_op jit(solution)/shard_map/ppermute | solution.py:670
  60.4 1.1 %shard_map.91 = f32[5,5,32,64]{3,2,1,0:T(8,128)} custom-call(f32[400,128]{1,0:T(8,128)S(1)} %maximum_select_fusion.tap_ref), custom_call_target="tpu_custom_call" | custom-call | flops 1000000 | bytes 409600 | tf_op jit(solution)/shard_map/pallas_call | solution.py:58
  (6 shorter events, 0.1 us)
Async XLA Ops:
  0.6 12.2 %copy-start.4 = (f32[2,4,4096]{2,1,0:T(4,128)S(1)}, f32[2,4,4096]{2,1,0:T(4,128)}, u32[]{:S(2)}) copy-start(f32[2,4,4096]{2,1,0:T(4,128)} %param.8) | copy-start | bytes 393220
  5.0 11.0 %slice-start = ((f32[2,4,4096]{2,1,0:T(4,128)}), f32[2,4,1]{2,1,0:T(4,128)S(1)}, s32[]{:S(2)}) async-start(f32[2,4,4096]{2,1,0:T(4,128)} %param.8), calls=%async_computation.2 | async-start | bytes 8192 | tf_op jit(solution)/shard_map/jit(_roll_static)/slice | solution.py:544
  5.0 22.4 %all-to-all-start = ((bf16[16,136,128]{2,1,0:T(8,128)(2,1)}), bf16[16,136,128]{2,1,0:T(8,128)(2,1)S(1)}, u32[]{:S(2)}, u32[]{:S(2)}) async-start(bf16[16,136,128]{2,1,0:T(8,128)(2,1)} %get-tuple-element.18), calls=%async_computation | async-start | bytes 1114112 | tf_op jit(solution)/shard_map/all_to_all | solution.py:591
  12.4 23.2 %collective-permute-start = (bf16[512,512]{1,0:T(8,128)(2,1)}, bf16[512,512]{1,0:T(8,128)(2,1)S(1)}, u32[]{:S(2)}, u32[]{:S(2)}) collective-permute-start(bf16[512,512]{1,0:T(8,128)(2,1)} %get-tuple-element.21.own_ref), channel_id=1, source_target_pairs={{0,1},{1,0},{2,3},{3,2},{4,5},{5,4},{6,7},{7,6},{8,9},{9,8},{10,11... | collective-permute-start | bytes 1572872 | tf_op jit(solution)/shard_map/ppermute | solution.py:590
  16.3 11.1 %copy-start.2 = (bf16[512,512]{1,0:T(8,128)(2,1)S(1)}, bf16[512,512]{1,0:T(8,128)(2,1)}, u32[]{:S(2)}) copy-start(bf16[512,512]{1,0:T(8,128)(2,1)} %constant.25.clone.wave_ref) | copy-start | bytes 1572868
  16.3 11.1 %copy-start.3 = (f32[2,16,256]{2,1,0:T(8,128)S(1)}, f32[2,16,256]{2,1,0:T(8,128)}, u32[]{:S(2)}) copy-start(f32[2,16,256]{2,1,0:T(8,128)} %constant.24.clone.twist_ref) | copy-start | bytes 98308
  17.1 18.6 %copy-start = (bf16[512,512]{1,0:T(8,128)(2,1)S(1)}, bf16[512,512]{1,0:T(8,128)(2,1)}, u32[]{:S(2)}) copy-start(bf16[512,512]{1,0:T(8,128)(2,1)} %get-tuple-element.21.own_ref) | copy-start | bytes 1572868
  31.5 13.8 %all-to-all-start.1 = ((bf16[8,136,128]{2,1,0:T(8,128)(2,1)}), bf16[8,136,128]{2,1,0:T(8,128)(2,1)S(1)}, u32[]{:S(2)}, u32[]{:S(2)}) async-start(bf16[8,136,128]{2,1,0:T(8,128)(2,1)} %get-tuple-element.19), calls=%async_computation.1 | async-start | bytes 557056 | tf_op jit(solution)/shard_map/all_to_all | solution.py:620
  41.3 13.9 %copy-start.1 = (bf16[5,5,64,32]{2,3,1,0:T(8,128)(2,1)S(1)}, bf16[5,5,64,32]{2,3,1,0:T(8,128)(2,1)}, u32[]{:S(2)}) copy-start(bf16[5,5,64,32]{2,3,1,0:T(8,128)(2,1)} %param.7) | copy-start | bytes 307204
  46.6 4.2 %collective-permute-start.1 = (bf16[200,128]{1,0:T(8,128)(2,1)S(1)}, bf16[200,128]{1,0:T(8,128)(2,1)S(1)}, u32[]{:S(2)}, u32[]{:S(2)}) collective-permute-start(bf16[200,128]{1,0:T(8,128)(2,1)S(1)} %convert_element_type.24), channel_id=1, source_target_pairs={{0,2},{1,3},{2,0},{3,1},{4,6},{5,7},{6,4},{7,5},{8,10},{9,11},{10,... | collective-permute-start | bytes 153608 | tf_op jit(solution)/shard_map/ppermute | solution.py:533
  48.1 2.7 %collective-permute-start.2 = (bf16[256,384]{1,0:T(8,128)(2,1)S(1)}, bf16[256,384]{1,0:T(8,128)(2,1)S(1)}, u32[]{:S(2)}, u32[]{:S(2)}) collective-permute-start(bf16[256,384]{1,0:T(8,128)(2,1)S(1)} %get-tuple-element.26), channel_id=1, source_target_pairs={{0,1},{1,0},{2,3},{3,2},{4,5},{5,4},{6,7},{7,6},{8,9},{9,8},{10,11... | collective-permute-start | bytes 589832 | tf_op jit(solution)/shard_map/ppermute | solution.py:650
  50.8 8.1 %collective-permute-start.5 = (bf16[200,128]{1,0:T(8,128)(2,1)S(1)}, bf16[200,128]{1,0:T(8,128)(2,1)S(1)}, u32[]{:S(2)}, u32[]{:S(2)}) collective-permute-start(bf16[200,128]{1,0:T(8,128)(2,1)S(1)} %convert_add_fusion), channel_id=1, source_target_pairs={{0,12},{1,13},{2,14},{3,15},{4,8},{5,9},{6,10},{7,11},{8,4},{9,5},... | collective-permute-start | bytes 153608 | tf_op jit(solution)/shard_map/ppermute | solution.py:533
  52.1 6.9 %collective-permute-start.4 = (bf16[200,128]{1,0:T(8,128)(2,1)S(1)}, bf16[200,128]{1,0:T(8,128)(2,1)S(1)}, u32[]{:S(2)}, u32[]{:S(2)}) collective-permute-start(bf16[200,128]{1,0:T(8,128)(2,1)S(1)} %convert_add_fusion), channel_id=1, source_target_pairs={{0,8},{1,9},{2,10},{3,11},{4,12},{5,13},{6,14},{7,15},{8,0},{9,1},... | collective-permute-start | bytes 153608 | tf_op jit(solution)/shard_map/ppermute | solution.py:533
  53.4 5.5 %collective-permute-start.3 = (bf16[200,128]{1,0:T(8,128)(2,1)S(1)}, bf16[200,128]{1,0:T(8,128)(2,1)S(1)}, u32[]{:S(2)}, u32[]{:S(2)}) collective-permute-start(bf16[200,128]{1,0:T(8,128)(2,1)S(1)} %convert_add_fusion), channel_id=1, source_target_pairs={{0,4},{1,5},{2,6},{3,7},{4,0},{5,1},{6,2},{7,3},{8,12},{9,13},{10,... | collective-permute-start | bytes 153608 | tf_op jit(solution)/shard_map/ppermute | solution.py:533
  59.0 1.4 %collective-permute-start.6 = (f32[200,128]{1,0:T(8,128)S(1)}, f32[200,128]{1,0:T(8,128)S(1)}, u32[]{:S(2)}, u32[]{:S(2)}) collective-permute-start(f32[200,128]{1,0:T(8,128)S(1)} %add_add_fusion), channel_id=1, source_target_pairs={{0,1},{1,0},{2,3},{3,2},{4,5},{5,4},{6,7},{7,6},{8,9},{9,8},{10,11... | collective-permute-start | bytes 307208 | tf_op jit(solution)/shard_map/ppermute | solution.py:670

commit v12 on v11

--- a/solution.py
+++ b/solution.py
@@ -449,53 +449,55 @@
     tap_ref[size:] = folded
 
 
-def input_kernel(dims, core_ref, own_ref, other_ref, taps_ref, out_ref, w_ref):
+def input_kernel(dims, part, core_ref, g_ref, *refs):
+    *started, taps_ref, out_ref, w_ref = refs
     cin, tin, cout, tout, ks, count, rows = dims
     k_in = cin * tin
-    half = own_ref.shape[1] - lanes
+    half = g_ref.shape[1] - lanes
     some, channels = cout // cores, cout // count
     steps = lanes // some
     kinds = ks + 2 * (steps - 1)
     blank = jnp.zeros((cin, cout), bf16)
-    core = core_ref[0]
+    wanted = core_ref[0] if part == 0 else 1 - core_ref[0]
     o, lane = iota((cout, lanes), 0), iota((cout, lanes), 1)
     device, channel = split_index(o, channels)
     chip, core_of = split_index(device, cores)
-    for part in range(cores):
-        wanted = core if part == 0 else 1 - core
-        tiles = None
-        for step in range(steps):
-            picked = [taps_ref[i - 2 * step, j] if 0 <= i - 2 * step < ks else blank
-                      for j in range(ks) for i in range(kinds)]
-            place = (core_of == wanted) & (lane == some * step + chip * channels + channel)
-            term = dot(jnp.concatenate(picked, axis=0), place.astype(f32).astype(bf16))
-            tiles = term if tiles is None else tiles + term
-        tiles = tiles.astype(bf16)
-        empty = jnp.zeros((cin, lanes), bf16)
-        for j in range(ks):
-            for s in range(tin):
-                for q in range(some * tout // lanes):
-                    i = s - 2 * steps * q + 2
-                    at = (j * kinds + i) * cin
-                    tile = tiles[at : at + cin] if 0 <= i < kinds else empty
-                    low = some * tout * part + lanes * q
-                    w_ref[j, cin * s : cin * (s + 1), low : low + lanes] = tile
-    g = jnp.concatenate([own_ref[...], other_ref[...]], axis=0)
+    tiles = None
+    for step in range(steps):
+        picked = [taps_ref[i - 2 * step, j] if 0 <= i - 2 * step < ks else blank
+                  for j in range(ks) for i in range(kinds)]
+        place = (core_of == wanted) & (lane == some * step + chip * channels + channel)
+        term = dot(jnp.concatenate(picked, axis=0), place.astype(f32).astype(bf16))
+        tiles = term if tiles is None else tiles + term
+    tiles = tiles.astype(bf16)
+    empty = jnp.zeros((cin, lanes), bf16)
+    for j in range(ks):
+        for s in range(tin):
+            for q in range(some * tout // lanes):
+                i = s - 2 * steps * q + 2
+                at = (j * kinds + i) * cin
+                tile = tiles[at : at + cin] if 0 <= i < kinds else empty
+                w_ref[j, cin * s : cin * (s + 1), lanes * q : lanes * (q + 1)] = tile
+    g = g_ref[...]
     wide = half + lanes
     same = g[:, :half]
     later = dot(g, one_hot_columns((wide, half), lambda n: n + 1)).astype(bf16)
     sooner = dot(g, one_hot_columns((wide, half), lambda n: jnp.where(n == 0, wide - 1, n - 1))).astype(bf16)
     even = dot(w_ref[0], later) + dot(w_ref[2], same) + dot(w_ref[4], sooner)
     odd = dot(w_ref[1], later) + dot(w_ref[3], same)
+    if not started:
+        out_ref[:, :half], out_ref[:, half:] = even, odd
+        return
+    even, odd = even + started[0][:, :half], odd + started[0][:, half:]
     both = jnp.concatenate([even.astype(bf16), odd.astype(bf16)], axis=1)
     to_channel = one_hot((k_in, k_in), lambda r: swapped(r, cin, tin))
     both = dot(to_channel, both).astype(bf16)
     merge = one_hot((2 * lanes, 2 * lanes), lambda r: swapped(r, 2, lanes))
     for b in range(half // lanes):
-        part = jnp.concatenate(
+        piece = jnp.concatenate(
             [both[:, lanes * b : lanes * (b + 1)], both[:, half + lanes * b : half + lanes * (b + 1)]], axis=1
         )
-        out_ref[:, 2 * lanes * b : 2 * lanes * (b + 1)] = dot(part, merge).astype(bf16)
+        out_ref[:, 2 * lanes * b : 2 * lanes * (b + 1)] = dot(piece, merge).astype(bf16)
 
 
 def unpack_kernel(dims, scale, tap_ref, out_ref):
@@ -651,13 +653,21 @@
     chips = count // cores
     total = summed_over_chips(taps_part, "fibre", (cores,))
     step = 2
-    total, keep, got = lax.optimization_barrier((total, keep, got))
+    (started,) = call(
+        functools.partial(input_kernel, dims, 0),
+        [shape((k_in, fibre_in), f32)],
+        [pltpu.VMEM((ks, k_in, some), bf16)],
+        1e9,
+        (core, keep, taps),
+        small=(0,),
+    )
+    total, started, got = lax.optimization_barrier((total, started, got))
     (input_grad,) = call(
-        functools.partial(input_kernel, dims),
+        functools.partial(input_kernel, dims, 1),
         [shape((k_in, fibre_in), bf16)],
-        [pltpu.VMEM((ks, k_in, k_out), bf16)],
-        2e9,
-        (core, keep, got, taps),
+        [pltpu.VMEM((ks, k_in, some), bf16)],
+        1e9,
+        (core, got, started, taps),
         small=(0,),
     )
     if chips % 8 == 0:

time: 61.9 us -> 61.8 us (level)
  waiting for transfers between devices: 18.2 us -> 16.9 us
  Pallas kernels: 16.4 us -> 17.6 us
    ppermute x4, waiting for transfers between devices: 2.65 us -> 1.3 us  [summed_over_chips(): lax.ppermute(rounded, axis, partners(count, step)).astype(f32)]
    pallas_call x7 -> x8, Pallas kernels: 16.4 us -> 17.6 us  [call(): pl.pallas_call(kernel, out_shape=outs, in_specs=[pl.BlockSpec(memory_spac...]
  transfers between devices with their start and end apart: 9 -> 9, of which waited for: 4 -> 5; matrix products, arithmetic and copies ran while one was open for 13% -> 13% of each run, Pallas kernels for 16% -> 18%
where the time goes in v12:
time: 61.8 us; the launch traced here: 61.4 us
  starting transfers between devices  18 us (29%)
  Pallas kernels  17.6 us (28%)
  waiting for transfers between devices  16.9 us (27%)
  local copies, waits for them, and re-layouts  7.82 us (13%)
  between operations  0.84 us (1%)
    pallas_call x8, Pallas kernels, call(): pl.pallas_call(kernel, out_shape=outs, in_specs=[pl.BlockSpec(memory_spac...  17.6 us
    all_to_all x1, waiting for transfers between devices, per_device(): lax.all_to_all(conv_part, 'fibre', split_axis=0, concat_axis=0, tiled=True)  10.3 us
    all_to_all x1, starting transfers between devices, per_device(): lax.all_to_all(conv_part, 'fibre', split_axis=0, concat_axis=0, tiled=True)  7.4 us
    ppermute x4, starting transfers between devices, summed_over_chips(): lax.ppermute(rounded, axis, partners(count, step)).astype(f32)  5.99 us
    all_to_all x1, starting transfers between devices, per_device(): lax.all_to_all(grad_part, 'fibre', split_axis=0, concat_axis=0, tiled=Tru...  4.12 us
    all_to_all x1, waiting for transfers between devices, per_device(): lax.all_to_all(grad_part, 'fibre', split_axis=0, concat_axis=0, tiled=Tru...  3.98 us
    unnamed x12, local copies, waits for them, and re-layouts  3.04 us
    reshape x1, local copies, waits for them, and re-layouts, per_device(): filter_grad = cross.transpose(0, 1, 3, 2).reshape(2, channels, waves)  2.44 us
  transfers between devices with their start and end apart: 9, of which 5 were waited for; matrix products, arithmetic and copies ran while one was open for 13% of the time, Pallas kernels for 18%

profile of v12, /device:TPU:0, one launch (start us, length us, event | category | flops | bytes accessed | tf_op | source)
XLA Modules:
  0.0 61.4 jit_solution(14302482110748358067)
XLA Ops:
  0.6 0.0 copy-start.4
  0.6 4.3 %shard_map.85 = (bf16[16,136,128]{2,1,0:T(8,128)(2,1)}, bf16[512,512]{1,0:T(8,128)(2,1)}) custom-call(bf16[512,512]{1,0:T(8,128)(2,1)} %bitcast.18, bf16[16,32,256]{2,1,0:T(8,128)(2,1)} %bitcast.19, bf16[5,5,32,64]{3,2,1,0:T(8,128)(2,1)} %bitcast.13), custom_call_target="tpu_custom_call" | custom-call | flops 2000000000 | bytes 1970176 | tf_op jit(solution)/shard_map/pallas_call | solution.py:58
  5.0 0.0 slice-start
  5.0 7.4 %all-to-all-start = ((bf16[16,136,128]{2,1,0:T(8,128)(2,1)}), bf16[16,136,128]{2,1,0:T(8,128)(2,1)S(1)}, u32[]{:S(2)}, u32[]{:S(2)}) async-start(bf16[16,136,128]{2,1,0:T(8,128)(2,1)} %get-tuple-element.18), calls=%async_computation | async-start | bytes 1114112 | tf_op jit(solution)/shard_map/all_to_all | solution.py:593
  12.4 0.4 collective-permute-start
  12.8 0.0 copy-done.4
  12.8 0.1 slice.26
  12.9 2.9 %reverse.2 = f32[2,4,4096]{2,1,0:T(4,128)S(1)} reverse(f32[2,4,4096]{2,1,0:T(4,128)S(1)} %bitcast.16), dimensions={2} | reverse | bytes 262144
  15.8 0.1 slice.43
  16.0 0.0 slice-done
  16.0 0.1 fusion.2
  16.1 0.2 stack.10
  16.3 0.0 copy-start.2
  16.3 0.0 copy-start.3
  16.3 0.2 copy.14
  16.5 0.2 stack.9
  16.7 0.2 copy.13
  16.9 0.1 copy.15
  17.1 0.0 copy-start
  17.1 10.3 %all-to-all-done.cols_ref = bf16[16,136,128]{2,1,0:T(8,128)(2,1)S(1)} async-done(((bf16[16,136,128]{2,1,0:T(8,128)(2,1)}), bf16[16,136,128]{2,1,0:T(8,128)(2,1)S(1)}, u32[]{:S(2)}, u32[]{:S(2)}) %all-to-all-start) | async-done | bytes 557088 | tf_op jit(solution)/shard_map/all_to_all | solution.py:593
  27.4 0.0 copy-done.2
  27.4 0.0 copy-done.3
  27.4 4.1 %shard_map.86 = (bf16[8,136,128]{2,1,0:T(8,128)(2,1)}, f32[64,512]{1,0:T(8,128)S(1)}) custom-call(bf16[16,136,128]{2,1,0:T(8,128)(2,1)S(1)} %all-to-all-done.cols_ref, f32[2,64,256]{2,1,0:T(8,128)S(1)} %reshape.30.own_ref, f32[2,16,256]{2,1,0:T(8,128)S(1)} %copy-done.3, bf16[512,512]{1,0:T(8,128)(2,1)S(1)} %copy-done.2), custom_call_target="tpu_custom_call" | custom-call | flops 6000000000 | bytes 1654784 | tf_op jit(solution)/shard_map/pallas_call | solution.py:58
  31.5 4.1 %all-to-all-start.1 = ((bf16[8,136,128]{2,1,0:T(8,128)(2,1)}), bf16[8,136,128]{2,1,0:T(8,128)(2,1)S(1)}, u32[]{:S(2)}, u32[]{:S(2)}) async-start(bf16[8,136,128]{2,1,0:T(8,128)(2,1)} %get-tuple-element.19), calls=%async_computation.1 | async-start | bytes 557056 | tf_op jit(solution)/shard_map/all_to_all | solution.py:622
  35.6 0.0 collective-permute-done.other_ref
  35.6 0.0 copy-done
  35.7 0.1 shard_map.88.z_ref
  35.8 1.8 %shard_map.87 = f32[2,4,16,256]{3,2,1,0:T(8,128)S(1)} custom-call(f32[64,512]{1,0:T(8,128)S(1)} %get-tuple-element.20.cross_ref), custom_call_target="tpu_custom_call" | custom-call | flops 1000000 | bytes 262144 | tf_op jit(solution)/shard_map/pallas_call | solution.py:58
  37.6 1.3 %copy.16 = f32[2,4,256,16]{3,2,1,0:T(8,128)} copy(f32[2,4,256,16]{2,3,1,0:T(8,128)S(1)} %bitcast.12) | data formatting | bytes 262144 | tf_op jit(solution)/shard_map/transpose | solution.py:620
  38.9 2.4 %reshape.31 = f32[2,4,4096]{2,1,0:T(4,128)} reshape(f32[2,4,256,16]{3,2,1,0:T(8,128)} %copy.16) | data formatting | bytes 262144 | tf_op jit(solution)/shard_map/reshape | solution.py:620
  41.3 4.0 %all-to-all-done.1.grad_ref = bf16[8,136,128]{2,1,0:T(8,128)(2,1)S(1)} async-done(((bf16[8,136,128]{2,1,0:T(8,128)(2,1)}), bf16[8,136,128]{2,1,0:T(8,128)(2,1)S(1)}, u32[]{:S(2)}, u32[]{:S(2)}) %all-to-all-start.1) | async-done | bytes 278560 | tf_op jit(solution)/shard_map/all_to_all | solution.py:622
  45.3 1.3 %shard_map.89 = (f32[200,128]{1,0:T(8,128)S(1)}, bf16[256,384]{1,0:T(8,128)(2,1)S(1)}, bf16[256,384]{1,0:T(8,128)(2,1)S(1)}) custom-call(s32[1]{0:T(128)} %bitcast.core_ref, bf16[8,136,128]{2,1,0:T(8,128)(2,1)S(1)} %all-to-all-done.1.grad_ref, bf16[640,1024]{1,0:T(8,128)(2,1)S(1)} %shard_map.88.z_ref), custom_call_target="tpu_custom_call" | custom-call | flops 1000000000 | bytes 2084868 | tf_op jit(solution)/shard_map/pallas_call | solution.py:58
  46.6 1.5 %collective-permute-start.1 = (bf16[200,128]{1,0:T(8,128)(2,1)S(1)}, bf16[200,128]{1,0:T(8,128)(2,1)S(1)}, u32[]{:S(2)}, u32[]{:S(2)}) collective-permute-start(bf16[200,128]{1,0:T(8,128)(2,1)S(1)} %convert_element_type.24), channel_id=1, source_target_pairs={{0,2},{1,3},{2,0},{3,1},{4,6},{5,7},{6,4},{7,5},{8,10},{9,11},{10,... | collective-permute-start | bytes 153608 | tf_op jit(solution)/shard_map/ppermute | solution.py:535
  48.1 0.0 collective-permute-start.2
  48.1 0.0 copy-done.1
  48.1 1.8 %shard_map.90.refs_0_ = f32[512,512]{1,0:T(8,128)S(1)} custom-call(s32[1]{0:T(128)} %bitcast.core_ref, bf16[256,384]{1,0:T(8,128)(2,1)S(1)} %get-tuple-element.25.g_ref, bf16[5,5,32,64]{3,2,1,0:T(8,128)(2,1)S(1)} %bitcast.14), custom_call_target="tpu_custom_call" | custom-call | flops 1000000000 | bytes 1347588 | tf_op jit(solution)/shard_map/pallas_call | solution.py:58
  50.0 0.8 %collective-permute-done.1 = bf16[200,128]{1,0:T(8,128)(2,1)S(1)} collective-permute-done((bf16[200,128]{1,0:T(8,128)(2,1)S(1)}, bf16[200,128]{1,0:T(8,128)(2,1)S(1)}, u32[]{:S(2)}, u32[]{:S(2)}) %collective-permute-start.1) | collective-permute-done | bytes 51232 | tf_op jit(solution)/shard_map/ppermute | solution.py:535
  50.8 0.0 collective-permute-done.2.g_ref
  50.8 1.2 %collective-permute-start.5 = (bf16[200,128]{1,0:T(8,128)(2,1)S(1)}, bf16[200,128]{1,0:T(8,128)(2,1)S(1)}, u32[]{:S(2)}, u32[]{:S(2)}) collective-permute-start(bf16[200,128]{1,0:T(8,128)(2,1)S(1)} %convert_add_fusion), channel_id=1, source_target_pairs={{0,12},{1,13},{2,14},{3,15},{4,8},{5,9},{6,10},{7,11},{8,4},{9,5},... | collective-permute-start | bytes 153608 | tf_op jit(solution)/shard_map/ppermute | solution.py:535
  52.1 1.4 %collective-permute-start.4 = (bf16[200,128]{1,0:T(8,128)(2,1)S(1)}, bf16[200,128]{1,0:T(8,128)(2,1)S(1)}, u32[]{:S(2)}, u32[]{:S(2)}) collective-permute-start(bf16[200,128]{1,0:T(8,128)(2,1)S(1)} %convert_add_fusion), channel_id=1, source_target_pairs={{0,8},{1,9},{2,10},{3,11},{4,12},{5,13},{6,14},{7,15},{8,0},{9,1},... | collective-permute-start | bytes 153608 | tf_op jit(solution)/shard_map/ppermute | solution.py:535
  53.4 1.8 %collective-permute-start.3 = (bf16[200,128]{1,0:T(8,128)(2,1)S(1)}, bf16[200,128]{1,0:T(8,128)(2,1)S(1)}, u32[]{:S(2)}, u32[]{:S(2)}) collective-permute-start(bf16[200,128]{1,0:T(8,128)(2,1)S(1)} %convert_add_fusion), channel_id=1, source_target_pairs={{0,4},{1,5},{2,6},{3,7},{4,0},{5,1},{6,2},{7,3},{8,12},{9,13},{10,... | collective-permute-start | bytes 153608 | tf_op jit(solution)/shard_map/ppermute | solution.py:535
  55.3 3.1 %shard_map.91 = bf16[512,512]{1,0:T(8,128)(2,1)} custom-call(s32[1]{0:T(128)} %bitcast.core_ref, bf16[256,384]{1,0:T(8,128)(2,1)S(1)} %collective-permute-done.2.g_ref, f32[512,512]{1,0:T(8,128)S(1)} %shard_map.90.refs_0_, bf16[5,5,32,64]{3,2,1,0:T(8,128)(2,1)S(1)} %bitcast.15), custom_call_target="tpu_custom_call" | custom-call | flops 1000000000 | bytes 1871876 | tf_op jit(solution)/shard_map/pallas_call | solution.py:58
  58.3 0.0 collective-permute-done.5
  58.3 0.5 collective-permute-done.4
  58.8 0.0 collective-permute-done.3
  58.9 0.1 collective-permute-start.6
  58.9 1.3 %collective-permute-done.6 = f32[200,128]{1,0:T(8,128)S(1)} collective-permute-done((f32[200,128]{1,0:T(8,128)S(1)}, f32[200,128]{1,0:T(8,128)S(1)}, u32[]{:S(2)}, u32[]{:S(2)}) %collective-permute-start.6) | collective-permute-done | bytes 102432 | tf_op jit(solution)/shard_map/ppermute | solution.py:680
  60.2 1.1 %shard_map.92 = f32[5,5,32,64]{3,2,1,0:T(8,128)} custom-call(f32[400,128]{1,0:T(8,128)S(1)} %maximum_select_fusion.tap_ref), custom_call_target="tpu_custom_call" | custom-call | flops 1000000 | bytes 409600 | tf_op jit(solution)/shard_map/pallas_call | solution.py:58
  (7 shorter events, 0.1 us)
Async XLA Ops:
  0.6 12.2 %copy-start.4 = (f32[2,4,4096]{2,1,0:T(4,128)S(1)}, f32[2,4,4096]{2,1,0:T(4,128)}, u32[]{:S(2)}) copy-start(f32[2,4,4096]{2,1,0:T(4,128)} %param.8) | copy-start | bytes 393220
  5.0 11.0 %slice-start = ((f32[2,4,4096]{2,1,0:T(4,128)}), f32[2,4,1]{2,1,0:T(4,128)S(1)}, s32[]{:S(2)}) async-start(f32[2,4,4096]{2,1,0:T(4,128)} %param.8), calls=%async_computation.2 | async-start | bytes 8192 | tf_op jit(solution)/shard_map/jit(_roll_static)/slice | solution.py:546
  5.0 22.4 %all-to-all-start = ((bf16[16,136,128]{2,1,0:T(8,128)(2,1)}), bf16[16,136,128]{2,1,0:T(8,128)(2,1)S(1)}, u32[]{:S(2)}, u32[]{:S(2)}) async-start(bf16[16,136,128]{2,1,0:T(8,128)(2,1)} %get-tuple-element.18), calls=%async_computation | async-start | bytes 1114112 | tf_op jit(solution)/shard_map/all_to_all | solution.py:593
  12.4 23.2 %collective-permute-start = (bf16[512,512]{1,0:T(8,128)(2,1)}, bf16[512,512]{1,0:T(8,128)(2,1)S(1)}, u32[]{:S(2)}, u32[]{:S(2)}) collective-permute-start(bf16[512,512]{1,0:T(8,128)(2,1)} %get-tuple-element.21.own_ref), channel_id=1, source_target_pairs={{0,1},{1,0},{2,3},{3,2},{4,5},{5,4},{6,7},{7,6},{8,9},{9,8},{10,11... | collective-permute-start | bytes 1572872 | tf_op jit(solution)/shard_map/ppermute | solution.py:592
  16.3 11.1 %copy-start.2 = (bf16[512,512]{1,0:T(8,128)(2,1)S(1)}, bf16[512,512]{1,0:T(8,128)(2,1)}, u32[]{:S(2)}) copy-start(bf16[512,512]{1,0:T(8,128)(2,1)} %constant.25.clone.wave_ref) | copy-start | bytes 1572868
  16.3 11.1 %copy-start.3 = (f32[2,16,256]{2,1,0:T(8,128)S(1)}, f32[2,16,256]{2,1,0:T(8,128)}, u32[]{:S(2)}) copy-start(f32[2,16,256]{2,1,0:T(8,128)} %constant.24.clone.twist_ref) | copy-start | bytes 98308
  17.1 18.6 %copy-start = (bf16[512,512]{1,0:T(8,128)(2,1)S(1)}, bf16[512,512]{1,0:T(8,128)(2,1)}, u32[]{:S(2)}) copy-start(bf16[512,512]{1,0:T(8,128)(2,1)} %get-tuple-element.21.own_ref) | copy-start | bytes 1572868
  31.5 13.8 %all-to-all-start.1 = ((bf16[8,136,128]{2,1,0:T(8,128)(2,1)}), bf16[8,136,128]{2,1,0:T(8,128)(2,1)S(1)}, u32[]{:S(2)}, u32[]{:S(2)}) async-start(bf16[8,136,128]{2,1,0:T(8,128)(2,1)} %get-tuple-element.19), calls=%async_computation.1 | async-start | bytes 557056 | tf_op jit(solution)/shard_map/all_to_all | solution.py:622
  41.3 6.8 %copy-start.1 = (bf16[5,5,64,32]{2,3,1,0:T(8,128)(2,1)S(1)}, bf16[5,5,64,32]{2,3,1,0:T(8,128)(2,1)}, u32[]{:S(2)}) copy-start(bf16[5,5,64,32]{2,3,1,0:T(8,128)(2,1)} %param.7) | copy-start | bytes 307204
  46.6 4.2 %collective-permute-start.1 = (bf16[200,128]{1,0:T(8,128)(2,1)S(1)}, bf16[200,128]{1,0:T(8,128)(2,1)S(1)}, u32[]{:S(2)}, u32[]{:S(2)}) collective-permute-start(bf16[200,128]{1,0:T(8,128)(2,1)S(1)} %convert_element_type.24), channel_id=1, source_target_pairs={{0,2},{1,3},{2,0},{3,1},{4,6},{5,7},{6,4},{7,5},{8,10},{9,11},{10,... | collective-permute-start | bytes 153608 | tf_op jit(solution)/shard_map/ppermute | solution.py:535
  48.1 2.7 %collective-permute-start.2 = (bf16[256,384]{1,0:T(8,128)(2,1)S(1)}, bf16[256,384]{1,0:T(8,128)(2,1)S(1)}, u32[]{:S(2)}, u32[]{:S(2)}) collective-permute-start(bf16[256,384]{1,0:T(8,128)(2,1)S(1)} %get-tuple-element.26), channel_id=1, source_target_pairs={{0,1},{1,0},{2,3},{3,2},{4,5},{5,4},{6,7},{7,6},{8,9},{9,8},{10,11... | collective-permute-start | bytes 589832 | tf_op jit(solution)/shard_map/ppermute | solution.py:652
  50.8 7.5 %collective-permute-start.5 = (bf16[200,128]{1,0:T(8,128)(2,1)S(1)}, bf16[200,128]{1,0:T(8,128)(2,1)S(1)}, u32[]{:S(2)}, u32[]{:S(2)}) collective-permute-start(bf16[200,128]{1,0:T(8,128)(2,1)S(1)} %convert_add_fusion), channel_id=1, source_target_pairs={{0,12},{1,13},{2,14},{3,15},{4,8},{5,9},{6,10},{7,11},{8,4},{9,5},... | collective-permute-start | bytes 153608 | tf_op jit(solution)/shard_map/ppermute | solution.py:535
  52.1 6.8 %collective-permute-start.4 = (bf16[200,128]{1,0:T(8,128)(2,1)S(1)}, bf16[200,128]{1,0:T(8,128)(2,1)S(1)}, u32[]{:S(2)}, u32[]{:S(2)}) collective-permute-start(bf16[200,128]{1,0:T(8,128)(2,1)S(1)} %convert_add_fusion), channel_id=1, source_target_pairs={{0,8},{1,9},{2,10},{3,11},{4,12},{5,13},{6,14},{7,15},{8,0},{9,1},... | collective-permute-start | bytes 153608 | tf_op jit(solution)/shard_map/ppermute | solution.py:535
  53.4 5.4 %collective-permute-start.3 = (bf16[200,128]{1,0:T(8,128)(2,1)S(1)}, bf16[200,128]{1,0:T(8,128)(2,1)S(1)}, u32[]{:S(2)}, u32[]{:S(2)}) collective-permute-start(bf16[200,128]{1,0:T(8,128)(2,1)S(1)} %convert_add_fusion), channel_id=1, source_target_pairs={{0,4},{1,5},{2,6},{3,7},{4,0},{5,1},{6,2},{7,3},{8,12},{9,13},{10,... | collective-permute-start | bytes 153608 | tf_op jit(solution)/shard_map/ppermute | solution.py:535
  58.9 1.4 %collective-permute-start.6 = (f32[200,128]{1,0:T(8,128)S(1)}, f32[200,128]{1,0:T(8,128)S(1)}, u32[]{:S(2)}, u32[]{:S(2)}) collective-permute-start(f32[200,128]{1,0:T(8,128)S(1)} %add_add_fusion), channel_id=1, source_target_pairs={{0,1},{1,0},{2,3},{3,2},{4,5},{5,4},{6,7},{7,6},{8,9},{9,8},{10,11... | collective-permute-start | bytes 307208 | tf_op jit(solution)/shard_map/ppermute | solution.py:680

commit v13 on v12

--- a/solution.py
+++ b/solution.py
@@ -223,7 +223,7 @@
 
 def filter_kernel(
     dims, cols_ref, own_ref, twist_ref, wave_ref,
-    out_ref, cross_ref, x_ref, y_ref, spec_ref, grad_ref, prod_ref, resp_ref, high_ref, rest_ref,
+    out_ref, prod_ref, x_ref, y_ref, spec_ref, grad_ref, resp_ref, high_ref, rest_ref,
 ):
     count, channels, tout, width = dims
     rows, pair = channels * tout, tout // 2
@@ -320,11 +320,6 @@
     crossed = ((sr * gr + si * gi) * scale, (sr * gi - si * gr) * scale)
     for b in range(2 * wide):
         prod_ref[b] = crossed[b // wide][:, lanes * (b % wide) : lanes * (b % wide + 1)]
-    for b in range(2 * wide):
-        summed = prod_ref[b, pl.ds(0, groups, stride=pair), :]
-        for step in range(1, pair):
-            summed = summed + prod_ref[b, pl.ds(step, groups, stride=pair), :]
-        cross_ref[:, lanes * b : lanes * (b + 1)] = summed
     y_ref[...] = inner(dot_nt)
     for r, h in chunks:
         real, imag = backward_planes(r, h)
@@ -350,8 +345,15 @@
         out_ref[chip, at:, :rows] = edge.astype(bf16)
 
 
-def hermitian_kernel(cross_ref, out_ref):
+def hermitian_kernel(prod_ref, out_ref, cross_ref):
     _, channels, count, width = out_ref.shape
+    wide, groups = width // lanes, count * channels
+    pair = prod_ref.shape[1] // groups
+    for b in range(2 * wide):
+        summed = prod_ref[b, pl.ds(0, groups, stride=pair), :]
+        for step in range(1, pair):
+            summed = summed + prod_ref[b, pl.ds(step, groups, stride=pair), :]
+        cross_ref[:, lanes * b : lanes * (b + 1)] = summed
     row, col = iota((width, width), 0), iota((width, width), 1)
     flip = (row + col == width - 1).astype(f32).astype(bf16)
     flip_first = ((row + col == width) | ((row == 0) & (col == 0))).astype(f32).astype(bf16)
@@ -601,7 +603,7 @@
         functools.partial(filter_kernel, (count, channels, tout, width)),
         [
             shape((count // cores, cores * rows * tiles + edge_rows, lanes), bf16),
-            shape((count * channels, 2 * width), f32),
+            shape((2 * tiles, count * rows // 2, lanes), f32),
         ],
         [
             pltpu.VMEM((count, rows, width), f32),
@@ -609,14 +611,19 @@
             pltpu.VMEM((big, 2 * width), f32),
             pltpu.VMEM((big, 2 * width), f32),
             pltpu.VMEM((2 * tiles, big, lanes), f32),
-            pltpu.VMEM((2 * tiles, big, lanes), f32),
             pltpu.VMEM((2 * width, 2 * width), bf16),
             pltpu.VMEM((2 * width, 2 * width), bf16),
         ],
         6e9,
         (cols, real, jnp.asarray(twist), jnp.asarray(waves_table)),
     )
-    (cross,) = call(hermitian_kernel, [shape((2, channels, count, width), f32)], [], 1e6, (cross,))
+    (cross,) = call(
+        hermitian_kernel,
+        [shape((2, channels, count, width), f32)],
+        [pltpu.VMEM((count * channels, 2 * width), f32)],
+        1e6,
+        (cross,),
+    )
     filter_grad = cross.transpose(0, 1, 3, 2).reshape(2, channels, waves)
     chips = [[core + cores * chip for chip in range(count // cores)] for core in range(cores)]
     grad_cols = lax.all_to_all(

time: 61.8 us -> 61.7 us (level)
  local copies, waits for them, and re-layouts: 7.82 us -> 5.6 us
  waiting for transfers between devices: 16.9 us -> 19.1 us
    all_to_all x1, waiting for transfers between devices: 3.98 us -> 6.18 us  [per_device(): lax.all_to_all(grad_part, 'fibre', split_axis=0, concat_axis=0, tiled=Tru...]
    reshape x1, local copies, waits for them, and re-layouts: 2.44 us -> 1.22 us  [per_device(): filter_grad = cross.transpose(0, 1, 3, 2).reshape(2, channels, waves)]
    transpose x1, local copies, waits for them, and re-layouts: 1.33 us -> 0.33 us  [per_device(): filter_grad = cross.transpose(0, 1, 3, 2).reshape(2, channels, waves)]
  transfers between devices with their start and end apart: 9 -> 9, of which waited for: 5 -> 5; matrix products, arithmetic and copies ran while one was open for 13% -> 9% of each run, Pallas kernels for 18% -> 18%
where the time goes in v13:
time: 61.7 us; the launch traced here: 61.3 us
  waiting for transfers between devices  19.1 us (31%)
  starting transfers between devices  18 us (29%)
  Pallas kernels  17.5 us (28%)
  local copies, waits for them, and re-layouts  5.6 us (9%)
  between operations  0.84 us (1%)
    pallas_call x8, Pallas kernels, call(): pl.pallas_call(kernel, out_shape=outs, in_specs=[pl.BlockSpec(memory_spac...  17.5 us
    all_to_all x1, waiting for transfers between devices, per_device(): lax.all_to_all(conv_part, 'fibre', split_axis=0, concat_axis=0, tiled=True)  10.3 us
    all_to_all x1, starting transfers between devices, per_device(): lax.all_to_all(conv_part, 'fibre', split_axis=0, concat_axis=0, tiled=True)  7.4 us
    all_to_all x1, waiting for transfers between devices, per_device(): lax.all_to_all(grad_part, 'fibre', split_axis=0, concat_axis=0, tiled=Tru...  6.18 us
    ppermute x4, starting transfers between devices, summed_over_chips(): lax.ppermute(rounded, axis, partners(count, step)).astype(f32)  5.98 us
    all_to_all x1, starting transfers between devices, per_device(): lax.all_to_all(grad_part, 'fibre', split_axis=0, concat_axis=0, tiled=Tru...  4.13 us
    unnamed x12, local copies, waits for them, and re-layouts  3.04 us
    ppermute x4, waiting for transfers between devices, summed_over_chips(): lax.ppermute(rounded, axis, partners(count, step)).astype(f32)  1.31 us
  transfers between devices with their start and end apart: 9, of which 5 were waited for; matrix products, arithmetic and copies ran while one was open for 9% of the time, Pallas kernels for 18%

profile of v13, /device:TPU:0, one launch (start us, length us, event | category | flops | bytes accessed | tf_op | source)
XLA Modules:
  0.0 61.3 jit_solution(10490284275496364286)
XLA Ops:
  0.6 0.0 copy-start.4
  0.6 4.3 %shard_map.85 = (bf16[16,136,128]{2,1,0:T(8,128)(2,1)}, bf16[512,512]{1,0:T(8,128)(2,1)}) custom-call(bf16[512,512]{1,0:T(8,128)(2,1)} %bitcast.18, bf16[16,32,256]{2,1,0:T(8,128)(2,1)} %bitcast.19, bf16[5,5,32,64]{3,2,1,0:T(8,128)(2,1)} %bitcast.13), custom_call_target="tpu_custom_call" | custom-call | flops 2000000000 | bytes 1970176 | tf_op jit(solution)/shard_map/pallas_call | solution.py:58
  5.0 0.0 slice-start
  5.0 7.4 %all-to-all-start = ((bf16[16,136,128]{2,1,0:T(8,128)(2,1)}), bf16[16,136,128]{2,1,0:T(8,128)(2,1)S(1)}, u32[]{:S(2)}, u32[]{:S(2)}) async-start(bf16[16,136,128]{2,1,0:T(8,128)(2,1)} %get-tuple-element.18), calls=%async_computation | async-start | bytes 1114112 | tf_op jit(solution)/shard_map/all_to_all | solution.py:595
  12.4 0.4 collective-permute-start
  12.8 0.0 copy-done.4
  12.8 0.1 slice.26
  12.9 2.9 %reverse.2 = f32[2,4,4096]{2,1,0:T(4,128)S(1)} reverse(f32[2,4,4096]{2,1,0:T(4,128)S(1)} %bitcast.16), dimensions={2} | reverse | bytes 262144
  15.8 0.1 slice.43
  16.0 0.0 slice-done
  16.0 0.1 fusion.2
  16.1 0.2 stack.10
  16.3 0.0 copy-start.2
  16.3 0.0 copy-start.3
  16.3 0.2 copy.14
  16.5 0.2 stack.9
  16.7 0.2 copy.13
  16.9 0.1 copy.15
  17.1 0.0 copy-start
  17.1 10.3 %all-to-all-done.cols_ref = bf16[16,136,128]{2,1,0:T(8,128)(2,1)S(1)} async-done(((bf16[16,136,128]{2,1,0:T(8,128)(2,1)}), bf16[16,136,128]{2,1,0:T(8,128)(2,1)S(1)}, u32[]{:S(2)}, u32[]{:S(2)}) %all-to-all-start) | async-done | bytes 557088 | tf_op jit(solution)/shard_map/all_to_all | solution.py:595
  27.4 0.0 copy-done.2
  27.4 0.0 copy-done.3
  27.4 4.0 %shard_map.86 = (bf16[8,136,128]{2,1,0:T(8,128)(2,1)}, f32[4,256,128]{2,1,0:T(8,128)S(1)}) custom-call(bf16[16,136,128]{2,1,0:T(8,128)(2,1)S(1)} %all-to-all-done.cols_ref, f32[2,64,256]{2,1,0:T(8,128)S(1)} %reshape.30.own_ref, f32[2,16,256]{2,1,0:T(8,128)S(1)} %copy-done.3, bf16[512,512]{1,0:T(8,128)(2,1)S(1)} %copy-done.2), custom_call_target="tpu_custom_call" | custom-call | flops 6000000000 | bytes 2048000 | tf_op jit(solution)/shard_map/pallas_call | solution.py:58
  31.5 4.1 %all-to-all-start.1 = ((bf16[8,136,128]{2,1,0:T(8,128)(2,1)}), bf16[8,136,128]{2,1,0:T(8,128)(2,1)S(1)}, u32[]{:S(2)}, u32[]{:S(2)}) async-start(bf16[8,136,128]{2,1,0:T(8,128)(2,1)} %get-tuple-element.19), calls=%async_computation.1 | async-start | bytes 557056 | tf_op jit(solution)/shard_map/all_to_all | solution.py:629
  35.6 0.0 collective-permute-done.other_ref
  35.6 0.0 copy-done
  35.6 0.1 shard_map.88.z_ref
  35.8 1.8 %shard_map.87 = f32[2,4,16,256]{3,2,1,0:T(8,128)S(1)} custom-call(f32[4,256,128]{2,1,0:T(8,128)S(1)} %get-tuple-element.20.prod_ref), custom_call_target="tpu_custom_call" | custom-call | flops 1000000 | bytes 655360 | tf_op jit(solution)/shard_map/pallas_call | solution.py:58
  37.5 0.3 copy.16
  37.9 1.2 %reshape.31 = f32[2,4,4096]{2,1,0:T(4,128)} reshape(f32[2,4,256,16]{3,2,1,0:T(8,128)S(1)} %copy.16) | data formatting | bytes 262144 | tf_op jit(solution)/shard_map/reshape | solution.py:627
  39.1 6.2 %all-to-all-done.1.grad_ref = bf16[8,136,128]{2,1,0:T(8,128)(2,1)S(1)} async-done(((bf16[8,136,128]{2,1,0:T(8,128)(2,1)}), bf16[8,136,128]{2,1,0:T(8,128)(2,1)S(1)}, u32[]{:S(2)}, u32[]{:S(2)}) %all-to-all-start.1) | async-done | bytes 278560 | tf_op jit(solution)/shard_map/all_to_all | solution.py:629
  45.3 1.3 %shard_map.89 = (f32[200,128]{1,0:T(8,128)S(1)}, bf16[256,384]{1,0:T(8,128)(2,1)S(1)}, bf16[256,384]{1,0:T(8,128)(2,1)S(1)}) custom-call(s32[1]{0:T(128)} %bitcast.core_ref, bf16[8,136,128]{2,1,0:T(8,128)(2,1)S(1)} %all-to-all-done.1.grad_ref, bf16[640,1024]{1,0:T(8,128)(2,1)S(1)} %shard_map.88.z_ref), custom_call_target="tpu_custom_call" | custom-call | flops 1000000000 | bytes 2084868 | tf_op jit(solution)/shard_map/pallas_call | solution.py:58
  46.6 1.5 %collective-permute-start.1 = (bf16[200,128]{1,0:T(8,128)(2,1)S(1)}, bf16[200,128]{1,0:T(8,128)(2,1)S(1)}, u32[]{:S(2)}, u32[]{:S(2)}) collective-permute-start(bf16[200,128]{1,0:T(8,128)(2,1)S(1)} %convert_element_type.24), channel_id=1, source_target_pairs={{0,2},{1,3},{2,0},{3,1},{4,6},{5,7},{6,4},{7,5},{8,10},{9,11},{10,... | collective-permute-start | bytes 153608 | tf_op jit(solution)/shard_map/ppermute | solution.py:537
  48.1 0.0 collective-permute-start.2
  48.1 0.0 copy-done.1
  48.1 1.8 %shard_map.90.refs_0_ = f32[512,512]{1,0:T(8,128)S(1)} custom-call(s32[1]{0:T(128)} %bitcast.core_ref, bf16[256,384]{1,0:T(8,128)(2,1)S(1)} %get-tuple-element.25.g_ref, bf16[5,5,32,64]{3,2,1,0:T(8,128)(2,1)S(1)} %bitcast.14), custom_call_target="tpu_custom_call" | custom-call | flops 1000000000 | bytes 1347588 | tf_op jit(solution)/shard_map/pallas_call | solution.py:58
  49.9 0.8 %collective-permute-done.1 = bf16[200,128]{1,0:T(8,128)(2,1)S(1)} collective-permute-done((bf16[200,128]{1,0:T(8,128)(2,1)S(1)}, bf16[200,128]{1,0:T(8,128)(2,1)S(1)}, u32[]{:S(2)}, u32[]{:S(2)}) %collective-permute-start.1) | collective-permute-done | bytes 51232 | tf_op jit(solution)/shard_map/ppermute | solution.py:537
  50.8 0.0 collective-permute-done.2.g_ref
  50.8 1.3 %collective-permute-start.5 = (bf16[200,128]{1,0:T(8,128)(2,1)S(1)}, bf16[200,128]{1,0:T(8,128)(2,1)S(1)}, u32[]{:S(2)}, u32[]{:S(2)}) collective-permute-start(bf16[200,128]{1,0:T(8,128)(2,1)S(1)} %convert_add_fusion), channel_id=1, source_target_pairs={{0,12},{1,13},{2,14},{3,15},{4,8},{5,9},{6,10},{7,11},{8,4},{9,5},... | collective-permute-start | bytes 153608 | tf_op jit(solution)/shard_map/ppermute | solution.py:537
  52.0 1.4 %collective-permute-start.4 = (bf16[200,128]{1,0:T(8,128)(2,1)S(1)}, bf16[200,128]{1,0:T(8,128)(2,1)S(1)}, u32[]{:S(2)}, u32[]{:S(2)}) collective-permute-start(bf16[200,128]{1,0:T(8,128)(2,1)S(1)} %convert_add_fusion), channel_id=1, source_target_pairs={{0,8},{1,9},{2,10},{3,11},{4,12},{5,13},{6,14},{7,15},{8,0},{9,1},... | collective-permute-start | bytes 153608 | tf_op jit(solution)/shard_map/ppermute | solution.py:537
  53.4 1.8 %collective-permute-start.3 = (bf16[200,128]{1,0:T(8,128)(2,1)S(1)}, bf16[200,128]{1,0:T(8,128)(2,1)S(1)}, u32[]{:S(2)}, u32[]{:S(2)}) collective-permute-start(bf16[200,128]{1,0:T(8,128)(2,1)S(1)} %convert_add_fusion), channel_id=1, source_target_pairs={{0,4},{1,5},{2,6},{3,7},{4,0},{5,1},{6,2},{7,3},{8,12},{9,13},{10,... | collective-permute-start | bytes 153608 | tf_op jit(solution)/shard_map/ppermute | solution.py:537
  55.2 3.1 %shard_map.91 = bf16[512,512]{1,0:T(8,128)(2,1)} custom-call(s32[1]{0:T(128)} %bitcast.core_ref, bf16[256,384]{1,0:T(8,128)(2,1)S(1)} %collective-permute-done.2.g_ref, f32[512,512]{1,0:T(8,128)S(1)} %shard_map.90.refs_0_, bf16[5,5,32,64]{3,2,1,0:T(8,128)(2,1)S(1)} %bitcast.15), custom_call_target="tpu_custom_call" | custom-call | flops 1000000000 | bytes 1871876 | tf_op jit(solution)/shard_map/pallas_call | solution.py:58
  58.3 0.0 collective-permute-done.5
  58.3 0.5 collective-permute-done.4
  58.8 0.0 collective-permute-done.3
  58.8 0.1 collective-permute-start.6
  58.9 1.3 %collective-permute-done.6 = f32[200,128]{1,0:T(8,128)S(1)} collective-permute-done((f32[200,128]{1,0:T(8,128)S(1)}, f32[200,128]{1,0:T(8,128)S(1)}, u32[]{:S(2)}, u32[]{:S(2)}) %collective-permute-start.6) | collective-permute-done | bytes 102432 | tf_op jit(solution)/shard_map/ppermute | solution.py:687
  60.2 1.1 %shard_map.92 = f32[5,5,32,64]{3,2,1,0:T(8,128)} custom-call(f32[400,128]{1,0:T(8,128)S(1)} %maximum_select_fusion.tap_ref), custom_call_target="tpu_custom_call" | custom-call | flops 1000000 | bytes 409600 | tf_op jit(solution)/shard_map/pallas_call | solution.py:58
  (7 shorter events, 0.1 us)
Async XLA Ops:
  0.6 12.2 %copy-start.4 = (f32[2,4,4096]{2,1,0:T(4,128)S(1)}, f32[2,4,4096]{2,1,0:T(4,128)}, u32[]{:S(2)}) copy-start(f32[2,4,4096]{2,1,0:T(4,128)} %param.8) | copy-start | bytes 393220
  5.0 11.0 %slice-start = ((f32[2,4,4096]{2,1,0:T(4,128)}), f32[2,4,1]{2,1,0:T(4,128)S(1)}, s32[]{:S(2)}) async-start(f32[2,4,4096]{2,1,0:T(4,128)} %param.8), calls=%async_computation.2 | async-start | bytes 8192 | tf_op jit(solution)/shard_map/jit(_roll_static)/slice | solution.py:548
  5.0 22.4 %all-to-all-start = ((bf16[16,136,128]{2,1,0:T(8,128)(2,1)}), bf16[16,136,128]{2,1,0:T(8,128)(2,1)S(1)}, u32[]{:S(2)}, u32[]{:S(2)}) async-start(bf16[16,136,128]{2,1,0:T(8,128)(2,1)} %get-tuple-element.18), calls=%async_computation | async-start | bytes 1114112 | tf_op jit(solution)/shard_map/all_to_all | solution.py:595
  12.4 23.2 %collective-permute-start = (bf16[512,512]{1,0:T(8,128)(2,1)}, bf16[512,512]{1,0:T(8,128)(2,1)S(1)}, u32[]{:S(2)}, u32[]{:S(2)}) collective-permute-start(bf16[512,512]{1,0:T(8,128)(2,1)} %get-tuple-element.21.own_ref), channel_id=1, source_target_pairs={{0,1},{1,0},{2,3},{3,2},{4,5},{5,4},{6,7},{7,6},{8,9},{9,8},{10,11... | collective-permute-start | bytes 1572872 | tf_op jit(solution)/shard_map/ppermute | solution.py:594
  16.3 11.1 %copy-start.2 = (bf16[512,512]{1,0:T(8,128)(2,1)S(1)}, bf16[512,512]{1,0:T(8,128)(2,1)}, u32[]{:S(2)}) copy-start(bf16[512,512]{1,0:T(8,128)(2,1)} %constant.25.clone.wave_ref) | copy-start | bytes 1572868
  16.3 11.1 %copy-start.3 = (f32[2,16,256]{2,1,0:T(8,128)S(1)}, f32[2,16,256]{2,1,0:T(8,128)}, u32[]{:S(2)}) copy-start(f32[2,16,256]{2,1,0:T(8,128)} %constant.24.clone.twist_ref) | copy-start | bytes 98308
  17.1 18.5 %copy-start = (bf16[512,512]{1,0:T(8,128)(2,1)S(1)}, bf16[512,512]{1,0:T(8,128)(2,1)}, u32[]{:S(2)}) copy-start(bf16[512,512]{1,0:T(8,128)(2,1)} %get-tuple-element.21.own_ref) | copy-start | bytes 1572868
  31.5 13.8 %all-to-all-start.1 = ((bf16[8,136,128]{2,1,0:T(8,128)(2,1)}), bf16[8,136,128]{2,1,0:T(8,128)(2,1)S(1)}, u32[]{:S(2)}, u32[]{:S(2)}) async-start(bf16[8,136,128]{2,1,0:T(8,128)(2,1)} %get-tuple-element.19), calls=%async_computation.1 | async-start | bytes 557056 | tf_op jit(solution)/shard_map/all_to_all | solution.py:629
  39.1 9.0 %copy-start.1 = (bf16[5,5,64,32]{2,3,1,0:T(8,128)(2,1)S(1)}, bf16[5,5,64,32]{2,3,1,0:T(8,128)(2,1)}, u32[]{:S(2)}) copy-start(bf16[5,5,64,32]{2,3,1,0:T(8,128)(2,1)} %param.7) | copy-start | bytes 307204
  46.6 4.2 %collective-permute-start.1 = (bf16[200,128]{1,0:T(8,128)(2,1)S(1)}, bf16[200,128]{1,0:T(8,128)(2,1)S(1)}, u32[]{:S(2)}, u32[]{:S(2)}) collective-permute-start(bf16[200,128]{1,0:T(8,128)(2,1)S(1)} %convert_element_type.24), channel_id=1, source_target_pairs={{0,2},{1,3},{2,0},{3,1},{4,6},{5,7},{6,4},{7,5},{8,10},{9,11},{10,... | collective-permute-start | bytes 153608 | tf_op jit(solution)/shard_map/ppermute | solution.py:537
  48.1 2.7 %collective-permute-start.2 = (bf16[256,384]{1,0:T(8,128)(2,1)S(1)}, bf16[256,384]{1,0:T(8,128)(2,1)S(1)}, u32[]{:S(2)}, u32[]{:S(2)}) collective-permute-start(bf16[256,384]{1,0:T(8,128)(2,1)S(1)} %get-tuple-element.26), channel_id=1, source_target_pairs={{0,1},{1,0},{2,3},{3,2},{4,5},{5,4},{6,7},{7,6},{8,9},{9,8},{10,11... | collective-permute-start | bytes 589832 | tf_op jit(solution)/shard_map/ppermute | solution.py:659
  50.8 7.5 %collective-permute-start.5 = (bf16[200,128]{1,0:T(8,128)(2,1)S(1)}, bf16[200,128]{1,0:T(8,128)(2,1)S(1)}, u32[]{:S(2)}, u32[]{:S(2)}) collective-permute-start(bf16[200,128]{1,0:T(8,128)(2,1)S(1)} %convert_add_fusion), channel_id=1, source_target_pairs={{0,12},{1,13},{2,14},{3,15},{4,8},{5,9},{6,10},{7,11},{8,4},{9,5},... | collective-permute-start | bytes 153608 | tf_op jit(solution)/shard_map/ppermute | solution.py:537
  52.0 6.7 %collective-permute-start.4 = (bf16[200,128]{1,0:T(8,128)(2,1)S(1)}, bf16[200,128]{1,0:T(8,128)(2,1)S(1)}, u32[]{:S(2)}, u32[]{:S(2)}) collective-permute-start(bf16[200,128]{1,0:T(8,128)(2,1)S(1)} %convert_add_fusion), channel_id=1, source_target_pairs={{0,8},{1,9},{2,10},{3,11},{4,12},{5,13},{6,14},{7,15},{8,0},{9,1},... | collective-permute-start | bytes 153608 | tf_op jit(solution)/shard_map/ppermute | solution.py:537
  53.4 5.4 %collective-permute-start.3 = (bf16[200,128]{1,0:T(8,128)(2,1)S(1)}, bf16[200,128]{1,0:T(8,128)(2,1)S(1)}, u32[]{:S(2)}, u32[]{:S(2)}) collective-permute-start(bf16[200,128]{1,0:T(8,128)(2,1)S(1)} %convert_add_fusion), channel_id=1, source_target_pairs={{0,4},{1,5},{2,6},{3,7},{4,0},{5,1},{6,2},{7,3},{8,12},{9,13},{10,... | collective-permute-start | bytes 153608 | tf_op jit(solution)/shard_map/ppermute | solution.py:537
  58.8 1.4 %collective-permute-start.6 = (f32[200,128]{1,0:T(8,128)S(1)}, f32[200,128]{1,0:T(8,128)S(1)}, u32[]{:S(2)}, u32[]{:S(2)}) collective-permute-start(f32[200,128]{1,0:T(8,128)S(1)} %add_add_fusion), channel_id=1, source_target_pairs={{0,1},{1,0},{2,3},{3,2},{4,5},{5,4},{6,7},{7,6},{8,9},{9,8},{10,11... | collective-permute-start | bytes 307208 | tf_op jit(solution)/shard_map/ppermute | solution.py:687

commit v14 on v13

--- a/solution.py
+++ b/solution.py
@@ -405,13 +405,13 @@
         at = slice(rows * chip, rows * (chip + 1))
         low = 0
         for b in range(0, wide, lanes):
-            g_ref[at, lanes + b : 2 * lanes + b] = grad_ref[chip, low : low + rows].astype(f32)
+            g_ref[at, lanes + b : 2 * lanes + b] = grad_ref[chip, low : low + rows]
             low += rows
-        edge = dot_tn(grad_ref[chip, low:, :rows], spread)
+        edge = dot_tn(grad_ref[chip, low:, :rows], spread).astype(bf16)
         g_ref[at, :lanes] = edge[:, :lanes]
         g_ref[at, lanes + wide :] = edge[:, lanes:]
     to_time = one_hot((some * tout, some * tout), lambda r: swapped(r, tout, some))
-    g = dot(to_time, g_ref[...].astype(bf16))
+    g = dot(to_time, g_ref[...])
     inside = slice(lanes, lanes + wide)
     shifted_ref[0] = pltpu.roll(g, wide + 2 * lanes - 1, 1)[:, inside].astype(bf16)
     shifted_ref[1] = g[:, inside].astype(bf16)
@@ -648,7 +648,7 @@
             shape((some, width + lanes), bf16),
         ],
         [
-            pltpu.VMEM((some, cores * width + 2 * lanes), f32),
+            pltpu.VMEM((some, cores * width + 2 * lanes), bf16),
             pltpu.VMEM((some, cores * width + 2 * lanes), bf16),
             pltpu.VMEM((3, some, cores * width), bf16),
         ],

time: 61.7 us -> 61.7 us (level)
  no operation moved by 1% of the time
where the time goes in v14:
time: 61.7 us; the launch traced here: 61.3 us
  waiting for transfers between devices  19.1 us (31%)
  starting transfers between devices  18 us (29%)
  Pallas kernels  17.6 us (29%)
  local copies, waits for them, and re-layouts  5.6 us (9%)
  between operations  0.84 us (1%)
    pallas_call x8, Pallas kernels, call(): pl.pallas_call(kernel, out_shape=outs, in_specs=[pl.BlockSpec(memory_spac...  17.6 us
    all_to_all x1, waiting for transfers between devices, per_device(): lax.all_to_all(conv_part, 'fibre', split_axis=0, concat_axis=0, tiled=True)  10.3 us
    all_to_all x1, starting transfers between devices, per_device(): lax.all_to_all(conv_part, 'fibre', split_axis=0, concat_axis=0, tiled=True)  7.4 us
    all_to_all x1, waiting for transfers between devices, per_device(): lax.all_to_all(grad_part, 'fibre', split_axis=0, concat_axis=0, tiled=Tru...  6.18 us
    ppermute x4, starting transfers between devices, summed_over_chips(): lax.ppermute(rounded, axis, partners(count, step)).astype(f32)  5.99 us
    all_to_all x1, starting transfers between devices, per_device(): lax.all_to_all(grad_part, 'fibre', split_axis=0, concat_axis=0, tiled=Tru...  4.13 us
    unnamed x12, local copies, waits for them, and re-layouts  3.04 us
    ppermute x4, waiting for transfers between devices, summed_over_chips(): lax.ppermute(rounded, axis, partners(count, step)).astype(f32)  1.3 us
  transfers between devices with their start and end apart: 9, of which 5 were waited for; matrix products, arithmetic and copies ran while one was open for 9% of the time, Pallas kernels for 18%

profile of v14, /device:TPU:0, one launch (start us, length us, event | category | flops | bytes accessed | tf_op | source)
XLA Modules:
  0.0 61.3 jit_solution(2060927309549314780)
XLA Ops:
  0.6 0.0 copy-start.4
  0.6 4.3 %shard_map.85 = (bf16[16,136,128]{2,1,0:T(8,128)(2,1)}, bf16[512,512]{1,0:T(8,128)(2,1)}) custom-call(bf16[512,512]{1,0:T(8,128)(2,1)} %bitcast.18, bf16[16,32,256]{2,1,0:T(8,128)(2,1)} %bitcast.19, bf16[5,5,32,64]{3,2,1,0:T(8,128)(2,1)} %bitcast.13), custom_call_target="tpu_custom_call" | custom-call | flops 2000000000 | bytes 1970176 | tf_op jit(solution)/shard_map/pallas_call | solution.py:58
  5.0 0.0 slice-start
  5.0 7.4 %all-to-all-start = ((bf16[16,136,128]{2,1,0:T(8,128)(2,1)}), bf16[16,136,128]{2,1,0:T(8,128)(2,1)S(1)}, u32[]{:S(2)}, u32[]{:S(2)}) async-start(bf16[16,136,128]{2,1,0:T(8,128)(2,1)} %get-tuple-element.18), calls=%async_computation | async-start | bytes 1114112 | tf_op jit(solution)/shard_map/all_to_all | solution.py:595
  12.4 0.4 collective-permute-start
  12.8 0.0 copy-done.4
  12.8 0.1 slice.26
  12.9 2.9 %reverse.2 = f32[2,4,4096]{2,1,0:T(4,128)S(1)} reverse(f32[2,4,4096]{2,1,0:T(4,128)S(1)} %bitcast.16), dimensions={2} | reverse | bytes 262144
  15.8 0.1 slice.43
  16.0 0.0 slice-done
  16.0 0.1 fusion.2
  16.1 0.2 stack.10
  16.3 0.0 copy-start.2
  16.3 0.0 copy-start.3
  16.3 0.2 copy.14
  16.5 0.2 stack.9
  16.7 0.2 copy.13
  16.9 0.1 copy.15
  17.1 0.0 copy-start
  17.1 10.3 %all-to-all-done.cols_ref = bf16[16,136,128]{2,1,0:T(8,128)(2,1)S(1)} async-done(((bf16[16,136,128]{2,1,0:T(8,128)(2,1)}), bf16[16,136,128]{2,1,0:T(8,128)(2,1)S(1)}, u32[]{:S(2)}, u32[]{:S(2)}) %all-to-all-start) | async-done | bytes 557088 | tf_op jit(solution)/shard_map/all_to_all | solution.py:595
  27.4 0.0 copy-done.2
  27.4 0.0 copy-done.3
  27.4 4.0 %shard_map.86 = (bf16[8,136,128]{2,1,0:T(8,128)(2,1)}, f32[4,256,128]{2,1,0:T(8,128)S(1)}) custom-call(bf16[16,136,128]{2,1,0:T(8,128)(2,1)S(1)} %all-to-all-done.cols_ref, f32[2,64,256]{2,1,0:T(8,128)S(1)} %reshape.30.own_ref, f32[2,16,256]{2,1,0:T(8,128)S(1)} %copy-done.3, bf16[512,512]{1,0:T(8,128)(2,1)S(1)} %copy-done.2), custom_call_target="tpu_custom_call" | custom-call | flops 6000000000 | bytes 2048000 | tf_op jit(solution)/shard_map/pallas_call | solution.py:58
  31.5 4.1 %all-to-all-start.1 = ((bf16[8,136,128]{2,1,0:T(8,128)(2,1)}), bf16[8,136,128]{2,1,0:T(8,128)(2,1)S(1)}, u32[]{:S(2)}, u32[]{:S(2)}) async-start(bf16[8,136,128]{2,1,0:T(8,128)(2,1)} %get-tuple-element.19), calls=%async_computation.1 | async-start | bytes 557056 | tf_op jit(solution)/shard_map/all_to_all | solution.py:629
  35.6 0.0 collective-permute-done.other_ref
  35.6 0.0 copy-done
  35.6 0.1 shard_map.88.z_ref
  35.8 1.8 %shard_map.87 = f32[2,4,16,256]{3,2,1,0:T(8,128)S(1)} custom-call(f32[4,256,128]{2,1,0:T(8,128)S(1)} %get-tuple-element.20.prod_ref), custom_call_target="tpu_custom_call" | custom-call | flops 1000000 | bytes 655360 | tf_op jit(solution)/shard_map/pallas_call | solution.py:58
  37.5 0.3 copy.16
  37.9 1.2 %reshape.31 = f32[2,4,4096]{2,1,0:T(4,128)} reshape(f32[2,4,256,16]{3,2,1,0:T(8,128)S(1)} %copy.16) | data formatting | bytes 262144 | tf_op jit(solution)/shard_map/reshape | solution.py:627
  39.1 6.2 %all-to-all-done.1.grad_ref = bf16[8,136,128]{2,1,0:T(8,128)(2,1)S(1)} async-done(((bf16[8,136,128]{2,1,0:T(8,128)(2,1)}), bf16[8,136,128]{2,1,0:T(8,128)(2,1)S(1)}, u32[]{:S(2)}, u32[]{:S(2)}) %all-to-all-start.1) | async-done | bytes 278560 | tf_op jit(solution)/shard_map/all_to_all | solution.py:629
  45.3 1.3 %shard_map.89 = (f32[200,128]{1,0:T(8,128)S(1)}, bf16[256,384]{1,0:T(8,128)(2,1)S(1)}, bf16[256,384]{1,0:T(8,128)(2,1)S(1)}) custom-call(s32[1]{0:T(128)} %bitcast.core_ref, bf16[8,136,128]{2,1,0:T(8,128)(2,1)S(1)} %all-to-all-done.1.grad_ref, bf16[640,1024]{1,0:T(8,128)(2,1)S(1)} %shard_map.88.z_ref), custom_call_target="tpu_custom_call" | custom-call | flops 1000000000 | bytes 2084868 | tf_op jit(solution)/shard_map/pallas_call | solution.py:58
  46.6 1.5 %collective-permute-start.1 = (bf16[200,128]{1,0:T(8,128)(2,1)S(1)}, bf16[200,128]{1,0:T(8,128)(2,1)S(1)}, u32[]{:S(2)}, u32[]{:S(2)}) collective-permute-start(bf16[200,128]{1,0:T(8,128)(2,1)S(1)} %convert_element_type.24), channel_id=1, source_target_pairs={{0,2},{1,3},{2,0},{3,1},{4,6},{5,7},{6,4},{7,5},{8,10},{9,11},{10,... | collective-permute-start | bytes 153608 | tf_op jit(solution)/shard_map/ppermute | solution.py:537
  48.1 0.0 collective-permute-start.2
  48.1 0.0 copy-done.1
  48.1 1.8 %shard_map.90.refs_0_ = f32[512,512]{1,0:T(8,128)S(1)} custom-call(s32[1]{0:T(128)} %bitcast.core_ref, bf16[256,384]{1,0:T(8,128)(2,1)S(1)} %get-tuple-element.25.g_ref, bf16[5,5,32,64]{3,2,1,0:T(8,128)(2,1)S(1)} %bitcast.14), custom_call_target="tpu_custom_call" | custom-call | flops 1000000000 | bytes 1347588 | tf_op jit(solution)/shard_map/pallas_call | solution.py:58
  50.0 0.8 %collective-permute-done.1 = bf16[200,128]{1,0:T(8,128)(2,1)S(1)} collective-permute-done((bf16[200,128]{1,0:T(8,128)(2,1)S(1)}, bf16[200,128]{1,0:T(8,128)(2,1)S(1)}, u32[]{:S(2)}, u32[]{:S(2)}) %collective-permute-start.1) | collective-permute-done | bytes 51232 | tf_op jit(solution)/shard_map/ppermute | solution.py:537
  50.8 0.0 collective-permute-done.2.g_ref
  50.8 1.2 %collective-permute-start.5 = (bf16[200,128]{1,0:T(8,128)(2,1)S(1)}, bf16[200,128]{1,0:T(8,128)(2,1)S(1)}, u32[]{:S(2)}, u32[]{:S(2)}) collective-permute-start(bf16[200,128]{1,0:T(8,128)(2,1)S(1)} %convert_add_fusion), channel_id=1, source_target_pairs={{0,12},{1,13},{2,14},{3,15},{4,8},{5,9},{6,10},{7,11},{8,4},{9,5},... | collective-permute-start | bytes 153608 | tf_op jit(solution)/shard_map/ppermute | solution.py:537
  52.0 1.4 %collective-permute-start.4 = (bf16[200,128]{1,0:T(8,128)(2,1)S(1)}, bf16[200,128]{1,0:T(8,128)(2,1)S(1)}, u32[]{:S(2)}, u32[]{:S(2)}) collective-permute-start(bf16[200,128]{1,0:T(8,128)(2,1)S(1)} %convert_add_fusion), channel_id=1, source_target_pairs={{0,8},{1,9},{2,10},{3,11},{4,12},{5,13},{6,14},{7,15},{8,0},{9,1},... | collective-permute-start | bytes 153608 | tf_op jit(solution)/shard_map/ppermute | solution.py:537
  53.4 1.8 %collective-permute-start.3 = (bf16[200,128]{1,0:T(8,128)(2,1)S(1)}, bf16[200,128]{1,0:T(8,128)(2,1)S(1)}, u32[]{:S(2)}, u32[]{:S(2)}) collective-permute-start(bf16[200,128]{1,0:T(8,128)(2,1)S(1)} %convert_add_fusion), channel_id=1, source_target_pairs={{0,4},{1,5},{2,6},{3,7},{4,0},{5,1},{6,2},{7,3},{8,12},{9,13},{10,... | collective-permute-start | bytes 153608 | tf_op jit(solution)/shard_map/ppermute | solution.py:537
  55.3 3.1 %shard_map.91 = bf16[512,512]{1,0:T(8,128)(2,1)} custom-call(s32[1]{0:T(128)} %bitcast.core_ref, bf16[256,384]{1,0:T(8,128)(2,1)S(1)} %collective-permute-done.2.g_ref, f32[512,512]{1,0:T(8,128)S(1)} %shard_map.90.refs_0_, bf16[5,5,32,64]{3,2,1,0:T(8,128)(2,1)S(1)} %bitcast.15), custom_call_target="tpu_custom_call" | custom-call | flops 1000000000 | bytes 1871876 | tf_op jit(solution)/shard_map/pallas_call | solution.py:58
  58.3 0.0 collective-permute-done.5
  58.3 0.5 collective-permute-done.4
  58.8 0.0 collective-permute-done.3
  58.8 0.1 collective-permute-start.6
  58.9 1.3 %collective-permute-done.6 = f32[200,128]{1,0:T(8,128)S(1)} collective-permute-done((f32[200,128]{1,0:T(8,128)S(1)}, f32[200,128]{1,0:T(8,128)S(1)}, u32[]{:S(2)}, u32[]{:S(2)}) %collective-permute-start.6) | collective-permute-done | bytes 102432 | tf_op jit(solution)/shard_map/ppermute | solution.py:687
  60.2 1.1 %shard_map.92 = f32[5,5,32,64]{3,2,1,0:T(8,128)} custom-call(f32[400,128]{1,0:T(8,128)S(1)} %maximum_select_fusion.tap_ref), custom_call_target="tpu_custom_call" | custom-call | flops 1000000 | bytes 409600 | tf_op jit(solution)/shard_map/pallas_call | solution.py:58
  (7 shorter events, 0.1 us)
Async XLA Ops:
  0.6 12.2 %copy-start.4 = (f32[2,4,4096]{2,1,0:T(4,128)S(1)}, f32[2,4,4096]{2,1,0:T(4,128)}, u32[]{:S(2)}) copy-start(f32[2,4,4096]{2,1,0:T(4,128)} %param.8) | copy-start | bytes 393220
  5.0 11.0 %slice-start = ((f32[2,4,4096]{2,1,0:T(4,128)}), f32[2,4,1]{2,1,0:T(4,128)S(1)}, s32[]{:S(2)}) async-start(f32[2,4,4096]{2,1,0:T(4,128)} %param.8), calls=%async_computation.2 | async-start | bytes 8192 | tf_op jit(solution)/shard_map/jit(_roll_static)/slice | solution.py:548
  5.0 22.4 %all-to-all-start = ((bf16[16,136,128]{2,1,0:T(8,128)(2,1)}), bf16[16,136,128]{2,1,0:T(8,128)(2,1)S(1)}, u32[]{:S(2)}, u32[]{:S(2)}) async-start(bf16[16,136,128]{2,1,0:T(8,128)(2,1)} %get-tuple-element.18), calls=%async_computation | async-start | bytes 1114112 | tf_op jit(solution)/shard_map/all_to_all | solution.py:595
  12.4 23.2 %collective-permute-start = (bf16[512,512]{1,0:T(8,128)(2,1)}, bf16[512,512]{1,0:T(8,128)(2,1)S(1)}, u32[]{:S(2)}, u32[]{:S(2)}) collective-permute-start(bf16[512,512]{1,0:T(8,128)(2,1)} %get-tuple-element.21.own_ref), channel_id=1, source_target_pairs={{0,1},{1,0},{2,3},{3,2},{4,5},{5,4},{6,7},{7,6},{8,9},{9,8},{10,11... | collective-permute-start | bytes 1572872 | tf_op jit(solution)/shard_map/ppermute | solution.py:594
  16.3 11.1 %copy-start.2 = (bf16[512,512]{1,0:T(8,128)(2,1)S(1)}, bf16[512,512]{1,0:T(8,128)(2,1)}, u32[]{:S(2)}) copy-start(bf16[512,512]{1,0:T(8,128)(2,1)} %constant.25.clone.wave_ref) | copy-start | bytes 1572868
  16.3 11.1 %copy-start.3 = (f32[2,16,256]{2,1,0:T(8,128)S(1)}, f32[2,16,256]{2,1,0:T(8,128)}, u32[]{:S(2)}) copy-start(f32[2,16,256]{2,1,0:T(8,128)} %constant.24.clone.twist_ref) | copy-start | bytes 98308
  17.1 18.5 %copy-start = (bf16[512,512]{1,0:T(8,128)(2,1)S(1)}, bf16[512,512]{1,0:T(8,128)(2,1)}, u32[]{:S(2)}) copy-start(bf16[512,512]{1,0:T(8,128)(2,1)} %get-tuple-element.21.own_ref) | copy-start | bytes 1572868
  31.5 13.8 %all-to-all-start.1 = ((bf16[8,136,128]{2,1,0:T(8,128)(2,1)}), bf16[8,136,128]{2,1,0:T(8,128)(2,1)S(1)}, u32[]{:S(2)}, u32[]{:S(2)}) async-start(bf16[8,136,128]{2,1,0:T(8,128)(2,1)} %get-tuple-element.19), calls=%async_computation.1 | async-start | bytes 557056 | tf_op jit(solution)/shard_map/all_to_all | solution.py:629
  39.1 9.0 %copy-start.1 = (bf16[5,5,64,32]{2,3,1,0:T(8,128)(2,1)S(1)}, bf16[5,5,64,32]{2,3,1,0:T(8,128)(2,1)}, u32[]{:S(2)}) copy-start(bf16[5,5,64,32]{2,3,1,0:T(8,128)(2,1)} %param.7) | copy-start | bytes 307204
  46.6 4.2 %collective-permute-start.1 = (bf16[200,128]{1,0:T(8,128)(2,1)S(1)}, bf16[200,128]{1,0:T(8,128)(2,1)S(1)}, u32[]{:S(2)}, u32[]{:S(2)}) collective-permute-start(bf16[200,128]{1,0:T(8,128)(2,1)S(1)} %convert_element_type.24), channel_id=1, source_target_pairs={{0,2},{1,3},{2,0},{3,1},{4,6},{5,7},{6,4},{7,5},{8,10},{9,11},{10,... | collective-permute-start | bytes 153608 | tf_op jit(solution)/shard_map/ppermute | solution.py:537
  48.1 2.7 %collective-permute-start.2 = (bf16[256,384]{1,0:T(8,128)(2,1)S(1)}, bf16[256,384]{1,0:T(8,128)(2,1)S(1)}, u32[]{:S(2)}, u32[]{:S(2)}) collective-permute-start(bf16[256,384]{1,0:T(8,128)(2,1)S(1)} %get-tuple-element.26), channel_id=1, source_target_pairs={{0,1},{1,0},{2,3},{3,2},{4,5},{5,4},{6,7},{7,6},{8,9},{9,8},{10,11... | collective-permute-start | bytes 589832 | tf_op jit(solution)/shard_map/ppermute | solution.py:659
  50.8 7.5 %collective-permute-start.5 = (bf16[200,128]{1,0:T(8,128)(2,1)S(1)}, bf16[200,128]{1,0:T(8,128)(2,1)S(1)}, u32[]{:S(2)}, u32[]{:S(2)}) collective-permute-start(bf16[200,128]{1,0:T(8,128)(2,1)S(1)} %convert_add_fusion), channel_id=1, source_target_pairs={{0,12},{1,13},{2,14},{3,15},{4,8},{5,9},{6,10},{7,11},{8,4},{9,5},... | collective-permute-start | bytes 153608 | tf_op jit(solution)/shard_map/ppermute | solution.py:537
  52.0 6.7 %collective-permute-start.4 = (bf16[200,128]{1,0:T(8,128)(2,1)S(1)}, bf16[200,128]{1,0:T(8,128)(2,1)S(1)}, u32[]{:S(2)}, u32[]{:S(2)}) collective-permute-start(bf16[200,128]{1,0:T(8,128)(2,1)S(1)} %convert_add_fusion), channel_id=1, source_target_pairs={{0,8},{1,9},{2,10},{3,11},{4,12},{5,13},{6,14},{7,15},{8,0},{9,1},... | collective-permute-start | bytes 153608 | tf_op jit(solution)/shard_map/ppermute | solution.py:537
  53.4 5.4 %collective-permute-start.3 = (bf16[200,128]{1,0:T(8,128)(2,1)S(1)}, bf16[200,128]{1,0:T(8,128)(2,1)S(1)}, u32[]{:S(2)}, u32[]{:S(2)}) collective-permute-start(bf16[200,128]{1,0:T(8,128)(2,1)S(1)} %convert_add_fusion), channel_id=1, source_target_pairs={{0,4},{1,5},{2,6},{3,7},{4,0},{5,1},{6,2},{7,3},{8,12},{9,13},{10,... | collective-permute-start | bytes 153608 | tf_op jit(solution)/shard_map/ppermute | solution.py:537
  58.8 1.4 %collective-permute-start.6 = (f32[200,128]{1,0:T(8,128)S(1)}, f32[200,128]{1,0:T(8,128)S(1)}, u32[]{:S(2)}, u32[]{:S(2)}) collective-permute-start(f32[200,128]{1,0:T(8,128)S(1)} %add_add_fusion), channel_id=1, source_target_pairs={{0,1},{1,0},{2,3},{3,2},{4,5},{5,4},{6,7},{7,6},{8,9},{9,8},{10,11... | collective-permute-start | bytes 307208 | tf_op jit(solution)/shard_map/ppermute | solution.py:687
